TPU v7x, 32 devices: a whole 2x2x4 slice. The times are simulated.
32 devices in a mesh: groups: 2 (over y), seq: 4 (over z), tower: 2 (over x), mp: 2 (over core).
Axes of the slice: x: 2, y: 2, z: 4, core: 2. Of those that a mesh axis runs over, the one named last changes fastest.
Arguments:
- video_q: bfloat16 [1024, 3072], P(('groups', 'seq'), ('tower', 'mp')), parts along dimension 0, may hold values from -24 to 24
- video_k: bfloat16 [1024, 3072], P(('groups', 'seq'), ('tower', 'mp')), parts along dimension 0, may hold values from -24 to 24
- video_v: bfloat16 [1024, 3072], P(('groups', 'seq'), ('tower', 'mp')), parts along dimension 0, may hold values from -6 to 6
- audio_q: bfloat16 [512, 3072], P(('groups', 'seq'), ('tower', 'mp')), parts along dimension 0, may hold values from -24 to 24
- audio_k: bfloat16 [512, 3072], P(('groups', 'seq'), ('tower', 'mp')), parts along dimension 0, may hold values from -24 to 24
- audio_v: bfloat16 [512, 3072], P(('groups', 'seq'), ('tower', 'mp')), parts along dimension 0, may hold values from -6 to 6
- offsets: int32 [512], P('groups'), parts along dimension 0, may hold values from 0 to 3, as said below
- counts: int32 [8], P('groups'), parts along dimension 0, may hold values from 1 to 128, 384 in all
Outputs:
- video_self: bfloat16 [1024, 3072], P(('groups', 'seq'), ('tower', 'mp')), parts along dimension 0
- video_cross: bfloat16 [1024, 3072], P(('groups', 'seq'), ('tower', 'mp')), parts along dimension 0
- audio_self: bfloat16 [512, 3072], P(('groups', 'seq'), ('tower', 'mp')), parts along dimension 0
- audio_cross: bfloat16 [512, 3072], P(('groups', 'seq'), ('tower', 'mp')), parts along dimension 0
There are 2 independent parts, one for each index of `groups`. A program takes and returns all parts, laid end to end along the dimension named above; each array names one. Nothing has to cross between parts.
Inputs may be any that keep to these rules, and one draw needn't show every extreme that they name: offsets[a] differs from a // 64 by at most 1.
All inputs are finite; a program needn't handle non-finite values.
Results may differ from a plain program's by a relative error of at most 0.0065.
Values may be sent and summed in bfloat16 or wider, within the bound.
No kernel may reach another device: no remote copies, remote signals or barrier semaphores. Data moves between devices by JAX's collectives and lax.ppermute only.
A program may use at most 64 MiB of HBM per device.

v0:
```python
import jax
import jax.numpy as jnp
from jax import lax
from jax.sharding import PartitionSpec as P

HEAD_DIM = 128
SPAN = 1


def empty_state(head_count, row_count):
    return (
        jnp.full((head_count, row_count), -1e30, jnp.float32),
        jnp.zeros((head_count, row_count), jnp.float32),
        jnp.zeros((head_count, row_count, HEAD_DIM), jnp.float32),
    )


def absorb(state_now, queries, key_rows, value_rows, allowed):
    run_peak, run_total, run_sum = state_now
    scores = jnp.einsum(
        "qhe,khe->hqk", queries, key_rows, preferred_element_type=jnp.float32
    ) * HEAD_DIM ** (-0.5)
    scores = jnp.where(allowed[None], scores, -1e30)
    new_peak = jnp.maximum(run_peak, jnp.max(scores, axis=2))
    weights = jnp.where(allowed[None], jnp.exp(scores - new_peak[:, :, None]), 0.0)
    run_total = jnp.sum(weights, axis=2)
    run_sum = jnp.einsum(
        "hqk,khe->hqe", weights.astype(jnp.bfloat16), value_rows, preferred_element_type=jnp.float32
    )
    return (new_peak, run_total, run_sum)


def finish(state_now):
    run_peak, run_total, run_sum = state_now
    blended = run_sum / run_total[:, :, None]
    return jnp.transpose(blended, (1, 0, 2)).reshape(blended.shape[1], -1).astype(jnp.bfloat16)


def shards(video_q, video_k, video_v, audio_q, audio_k, audio_v, offsets, counts):
    frame_total = lax.axis_size("seq")
    my_frame = lax.axis_index("seq")
    video_rows = video_q.shape[0]
    audio_rows = audio_q.shape[0]
    head_count = video_q.shape[1] // HEAD_DIM
    frame_ids = jnp.arange(frame_total, dtype=jnp.int32)
    my_offsets = lax.dynamic_slice_in_dim(offsets, my_frame * audio_rows, audio_rows)
    video_query = video_q.reshape(video_rows, head_count, HEAD_DIM)
    audio_query = audio_q.reshape(audio_rows, head_count, HEAD_DIM)
    video_init = (empty_state(head_count, video_rows), empty_state(head_count, audio_rows))
    audio_init = (empty_state(head_count, audio_rows), empty_state(head_count, video_rows))
    pieces = (
        lax.all_gather(video_k, "seq", axis=0, tiled=True),
        lax.all_gather(video_v, "seq", axis=0, tiled=True),
    )
    key_rows = pieces[0].reshape(-1, head_count, HEAD_DIM)
    value_rows = pieces[1].reshape(-1, head_count, HEAD_DIM)
    key_total = key_rows.shape[0]
    positions = jnp.arange(key_total, dtype=jnp.int32)
    source = positions // video_rows
    is_live = positions % video_rows < jnp.sum(
        jnp.where(source[:, None] == frame_ids[None, :], counts[None, :], 0), axis=1
    )
    self_state = absorb(video_init[0], video_query, key_rows, value_rows, is_live[None, :])
    pieces = (
        lax.all_gather(audio_k, "seq", axis=0, tiled=True),
        lax.all_gather(audio_v, "seq", axis=0, tiled=True),
    )
    audio_key_rows = pieces[0].reshape(-1, head_count, HEAD_DIM)
    audio_value_rows = pieces[1].reshape(-1, head_count, HEAD_DIM)
    key_total = audio_key_rows.shape[0]
    audio_self_state = absorb(
        audio_init[0],
        audio_query,
        audio_key_rows,
        audio_value_rows,
        jnp.ones((1, key_total), jnp.bool_),
    )
    video_self = finish(self_state)
    audio_self = finish(audio_self_state)
    in_reach = (jnp.abs(my_offsets[:, None] - source[None, :]) <= SPAN) & is_live[None, :]
    audio_cross = finish(absorb(video_init[1], audio_query, key_rows, value_rows, in_reach))
    in_reach = jnp.abs(offsets - my_frame) <= SPAN
    video_cross = finish(
        absorb(audio_init[1], video_query, audio_key_rows, audio_value_rows, in_reach[None, :])
    )
    return (video_self, video_cross, audio_self, audio_cross)


def solution(mesh):
    placed = (
        P(("groups", "seq"), ("tower", "mp")),
        P(("groups", "seq"), ("tower", "mp")),
        P(("groups", "seq"), ("tower", "mp")),
        P(("groups", "seq"), ("tower", "mp")),
        P(("groups", "seq"), ("tower", "mp")),
        P(("groups", "seq"), ("tower", "mp")),
        P("groups"),
        P("groups"),
    )
    return jax.shard_map(
        shards,
        mesh=mesh,
        in_specs=placed,
        out_specs=(
            P(("groups", "seq"), ("tower", "mp")),
            P(("groups", "seq"), ("tower", "mp")),
            P(("groups", "seq"), ("tower", "mp")),
            P(("groups", "seq"), ("tower", "mp")),
        ),
        check_vma=False,
    )
```

profile of v0, /device:TPU:0, one launch (start us, length us, event | category | flops | bytes accessed | tf_op | source)
XLA Modules:
  0.0 77.0 jit_solution(14817489283093343876)
XLA Ops:
  0.6 0.0 copy-start
  0.6 0.0 copy-start.1
  0.7 0.0 copy-start.2
  0.7 21.6 %all_gather.13 = bf16[512,768]{1,0:T(8,128)(2,1)S(1)} all-gather(bf16[128,768]{1,0:T(8,128)(2,1)} %param.10), channel_id=1, replica_groups=mesh['groups'=2,'seq'=4,'tower'=2,'mp'=2] {'seq'}, dimensions={0}, use_global_device_ids=true | all-gather | bytes 983040 | tf_op jit(solution)/shard_map/all_gather | solution.py:53
  22.3 0.0 copy-start.6
  22.3 0.3 copy.64
  22.6 0.0 copy-done.1
  22.6 0.2 copy.60
  22.8 0.0 copy-done.2
  22.8 0.2 copy.61
  22.9 17.0 %all_gather.12 = bf16[512,768]{0,1:T(8,128)(2,1)S(1)} all-gather(bf16[128,768]{0,1:T(8,128)(2,1)S(1)} %copy.61), channel_id=1, replica_groups=mesh['groups'=2,'seq'=4,'tower'=2,'mp'=2] {'seq'}, dimensions={0}, use_global_device_ids=true | all-gather | bytes 983040 | tf_op jit(solution)/shard_map/all_gather | solution.py:52
  39.9 0.0 copy-done.6
  39.9 0.1 select_reduce_fusion
  40.0 0.5 fusion.48
  40.5 0.5 fusion.2
  41.0 0.0 copy-start.3
  41.0 0.5 fusion.6
  41.6 0.0 copy-start.4
  41.6 0.0 copy-start.5
  41.6 0.8 %copy.77 = bf16[128,768]{1,0:T(8,128)(2,1)} copy(bf16[128,768]{0,1:T(8,128)(2,1)S(1)} %bitcast.84) | data formatting | bytes 393216
  42.4 0.0 copy-done.3
  42.4 15.2 %all_gather.15 = bf16[256,768]{1,0:T(8,128)(2,1)S(1)} all-gather(bf16[64,768]{1,0:T(8,128)(2,1)S(1)} %copy-done.3), channel_id=1, replica_groups=mesh['groups'=2,'seq'=4,'tower'=2,'mp'=2] {'seq'}, dimensions={0}, use_global_device_ids=true | all-gather | bytes 491520 | tf_op jit(solution)/shard_map/all_gather | solution.py:66
  57.6 0.2 copy.68
  57.8 0.0 copy-done.4
  57.8 14.2 %all_gather.14 = bf16[256,768]{1,0:T(8,128)(2,1)S(1)} all-gather(bf16[64,768]{1,0:T(8,128)(2,1)S(1)} %copy-done.4), channel_id=1, replica_groups=mesh['groups'=2,'seq'=4,'tower'=2,'mp'=2] {'seq'}, dimensions={0}, use_global_device_ids=true | all-gather | bytes 491520 | tf_op jit(solution)/shard_map/all_gather | solution.py:65
  72.0 0.2 copy.65
  72.2 0.0 copy-done.5
  72.2 0.4 fusion.49
  72.6 0.3 fusion.18
  72.9 0.4 fusion.7
  73.3 0.8 %copy.78 = bf16[128,768]{1,0:T(8,128)(2,1)} copy(bf16[128,768]{0,1:T(8,128)(2,1)S(1)} %bitcast.83) | data formatting | bytes 393216
  74.1 0.1 dynamic_slice.3
  74.2 0.1 fusion.34
  74.3 0.0 copy-done
  74.3 0.3 fusion.51
  74.7 0.3 fusion.20
  75.0 0.4 fusion.12
  75.4 0.3 fusion.50
  75.7 0.2 fusion.30
  75.9 0.3 fusion.13
  76.3 0.7 copy_bitcast_fusion
  (7 shorter events, 0.0 us)
Async XLA Ops:
  0.6 73.7 %copy-start = (bf16[64,768]{1,0:T(8,128)(2,1)S(1)}, bf16[64,768]{1,0:T(8,128)(2,1)}, u32[]{:S(2)}) copy-start(bf16[64,768]{1,0:T(8,128)(2,1)} %param.11) | copy-start | bytes 294916
  0.6 22.0 %copy-start.1 = (bf16[128,768]{1,0:T(8,128)(2,1)S(1)}, bf16[128,768]{1,0:T(8,128)(2,1)}, u32[]{:S(2)}) copy-start(bf16[128,768]{1,0:T(8,128)(2,1)} %param.8) | copy-start | bytes 589828
  0.7 22.1 %copy-start.2 = (bf16[128,768]{1,0:T(8,128)(2,1)S(1)}, bf16[128,768]{1,0:T(8,128)(2,1)}, u32[]{:S(2)}) copy-start(bf16[128,768]{1,0:T(8,128)(2,1)} %param.9) | copy-start | bytes 589828
  22.3 17.6 %copy-start.6 = (s32[4]{0:T(128)S(1)}, s32[4]{0:T(128)}, u32[]{:S(2)}) copy-start(s32[4]{0:T(128)} %param.15) | copy-start | bytes 52
  41.0 1.4 %copy-start.3 = (bf16[64,768]{1,0:T(8,128)(2,1)S(1)}, bf16[64,768]{1,0:T(8,128)(2,1)}, u32[]{:S(2)}) copy-start(bf16[64,768]{1,0:T(8,128)(2,1)} %param.13) | copy-start | bytes 294916
  41.6 16.2 %copy-start.4 = (bf16[64,768]{1,0:T(8,128)(2,1)S(1)}, bf16[64,768]{1,0:T(8,128)(2,1)}, u32[]{:S(2)}) copy-start(bf16[64,768]{1,0:T(8,128)(2,1)} %param.12) | copy-start | bytes 294916
  41.6 30.6 %copy-start.5 = (s32[256]{0:T(256)S(1)}, s32[256]{0:T(256)}, u32[]{:S(2)}) copy-start(s32[256]{0:T(256)} %param.14) | copy-start | bytes 3076
where the time goes:
time: 77.2 us; the launch traced here: 77 us
  blocking collectives  68 us (88%)
  local copies, waits for them, and re-layouts  3.4 us (4%)
  matrix products  3.14 us (4%)
  other arithmetic  1.56 us (2%)
  between operations  0.83 us (1%)
    all_gather x1, blocking collectives, shards(): lax.all_gather(video_v, 'seq', axis=0, tiled=True)  21.6 us
    all_gather x1, blocking collectives, shards(): lax.all_gather(video_k, 'seq', axis=0, tiled=True)  17 us
    all_gather x1, blocking collectives, shards(): lax.all_gather(audio_v, 'seq', axis=0, tiled=True)  15.2 us
    all_gather x1, blocking collectives, shards(): lax.all_gather(audio_k, 'seq', axis=0, tiled=True)  14.2 us
    unnamed x18, local copies, waits for them, and re-layouts  2.01 us
    dot_general x4, matrix products, absorb(): jnp.einsum('hqk,khe->hqe', weights.astype(jnp.bfloat16), value_rows, pref...  1.64 us

commit v1 on v0

v1 whole, which is shorter than its diff:
```python
import functools

import jax
import jax.numpy as jnp
from jax import lax
from jax.experimental import pallas as pl
from jax.experimental.pallas import tpu as pltpu
from jax.sharding import PartitionSpec as P


HEAD_DIM = 128
SPAN = 1
MASKED = -1e30
LOG2E = 1.4426950408889634
DEAD = 1 << 20
VMEM = pl.BlockSpec(memory_space=pltpu.VMEM)
SMEM = pl.BlockSpec(memory_space=pltpu.SMEM)
ANY = pl.BlockSpec(memory_space=pl.ANY)
PARAMS = pltpu.CompilerParams(vmem_limit_bytes=16 << 20)


def attend(queries, key_rows, value_rows, allowed):
    scores = jnp.einsum(
        "qhe,khe->hqk", queries, key_rows, preferred_element_type=jnp.float32
    ) * HEAD_DIM ** (-0.5)
    scores = jnp.where(allowed[None], scores, MASKED)
    peak = jnp.max(scores, axis=2)
    weights = jnp.where(allowed[None], jnp.exp(scores - peak[:, :, None]), 0.0)
    total = jnp.sum(weights, axis=2)
    blended = jnp.einsum(
        "hqk,khe->hqe", weights.astype(jnp.bfloat16), value_rows, preferred_element_type=jnp.float32
    )
    blended = blended / total[:, :, None]
    return jnp.transpose(blended, (1, 0, 2)).reshape(blended.shape[1], -1).astype(jnp.bfloat16)


def gathered(video_q, video_k, video_v, audio_q, audio_k, audio_v, offsets, counts):
    my_frame = lax.axis_index("seq")
    video_rows, audio_rows = video_q.shape[0], audio_q.shape[0]

    def heads(rows):
        return rows.reshape(rows.shape[0], -1, HEAD_DIM)

    def everywhere(rows):
        return heads(lax.all_gather(rows, "seq", axis=0, tiled=True))

    my_offsets = lax.dynamic_slice_in_dim(offsets, my_frame * audio_rows, audio_rows)
    keys, values = everywhere(video_k), everywhere(video_v)
    audio_keys, audio_values = everywhere(audio_k), everywhere(audio_v)
    positions = jnp.arange(keys.shape[0], dtype=jnp.int32)
    source = positions // video_rows
    is_live = positions % video_rows < jnp.repeat(counts, video_rows)
    video_self = attend(heads(video_q), keys, values, is_live[None, :])
    in_reach = (jnp.abs(my_offsets[:, None] - source[None, :]) <= SPAN) & is_live[None, :]
    audio_cross = attend(heads(audio_q), keys, values, in_reach)
    every = jnp.ones((1, audio_keys.shape[0]), jnp.bool_)
    audio_self = attend(heads(audio_q), audio_keys, audio_values, every)
    in_reach = jnp.abs(offsets - my_frame) <= SPAN
    video_cross = attend(heads(video_q), audio_keys, audio_values, in_reach[None, :])
    return (video_self, video_cross, audio_self, audio_cross)


def blend(queries, keys, values, allowed):
    scores = lax.dot_general(
        queries, keys, (((1,), (1,)), ((), ())), preferred_element_type=jnp.float32
    )
    if allowed is not None:
        scores = jnp.where(allowed, scores, MASKED)
    peak = jnp.max(scores, axis=1, keepdims=True)
    weights = jnp.exp2((scores - peak) * (HEAD_DIM ** (-0.5) * LOG2E))
    total = jnp.sum(weights, axis=1, keepdims=True)
    mixed = jnp.dot(weights.astype(jnp.bfloat16), values, preferred_element_type=jnp.float32)
    return (mixed * (1.0 / total)).astype(jnp.bfloat16)


def audio_kernel(role_ref, gap_ref, q_own, q_mate, b0, b1, b2, b3, own_ref, mate_ref):
    video_rows = q_own.shape[0] - b0.shape[0] // 2
    audio_rows = b0.shape[0] // 2

    @pl.when(role_ref[0] == 0)
    def _():
        reach = [jnp.abs(gap_ref[i : i + 1, :]) <= SPAN for i in range(2)]
        for head in range(q_own.shape[1] // HEAD_DIM):
            cols = slice(head * HEAD_DIM, (head + 1) * HEAD_DIM)
            keys = jnp.concatenate([b[:audio_rows, cols] for b in (b0, b1, b2, b3)], axis=0)
            values = jnp.concatenate([b[audio_rows:, cols] for b in (b0, b1, b2, b3)], axis=0)
            for who, (q_ref, o_ref) in enumerate(((q_own, own_ref), (q_mate, mate_ref))):
                o_ref[:video_rows, cols] = blend(q_ref[:video_rows, cols], keys, values, reach[who])
            both = jnp.concatenate([q_own[video_rows:, cols], q_mate[video_rows:, cols]], axis=0)
            out = blend(both, keys, values, None)
            own_ref[video_rows:, cols] = out[:audio_rows]
            mate_ref[video_rows:, cols] = out[audio_rows:]


def video_kernel(first, role_ref, frame_ref, off_ref, q_own, q_mate, b0, b1, b2, b3, own_ref, mate_ref):
    video_rows = b0.shape[0] // 2
    audio_rows = q_own.shape[0] - video_rows

    @pl.when(role_ref[0] == 0)
    def _():
        frames = frame_ref[...]
        live = frames < DEAD
        reach = jnp.abs(off_ref[...] - frames) <= SPAN
        for head in range(b0.shape[1] // HEAD_DIM):
            cols = slice(head * HEAD_DIM, (head + 1) * HEAD_DIM)
            q_cols = slice((first + head) * HEAD_DIM, (first + head + 1) * HEAD_DIM)
            keys = jnp.concatenate([b[:video_rows, cols] for b in (b0, b1, b2, b3)], axis=0)
            values = jnp.concatenate([b[video_rows:, cols] for b in (b0, b1, b2, b3)], axis=0)
            for q_ref, o_ref in ((q_own, own_ref), (q_mate, mate_ref)):
                o_ref[:video_rows, cols] = blend(q_ref[:video_rows, q_cols], keys, values, live)
            both = jnp.concatenate([q_own[video_rows:, q_cols], q_mate[video_rows:, q_cols]], axis=0)
            out = blend(both, keys, values, reach)
            own_ref[video_rows:, cols] = out[:audio_rows]
            mate_ref[video_rows:, cols] = out[audio_rows:]


def place_kernel(video_rows, role_ref, *refs):
    n = (len(refs) - 5) // 2
    own, back = refs[:n], refs[n : 2 * n]
    video_self, video_cross, audio_self, audio_cross = refs[2 * n : 2 * n + 4]
    sem = refs[-1]

    def copies(parts):
        yield parts[0].at[:video_rows], video_cross
        yield parts[0].at[video_rows:], audio_self
        at = 0
        for part in parts[1:]:
            cols = pl.ds(at, part.shape[1])
            yield part.at[:video_rows], video_self.at[:, cols]
            yield part.at[video_rows:], audio_cross.at[:, cols]
            at += part.shape[1]

    for role, parts in ((0, own), (1, back)):

        @pl.when(role_ref[0] == role)
        def _(parts=parts):
            moves = [
                pltpu.make_async_copy(src, dst, sem.at[i])
                for i, (src, dst) in enumerate(copies(parts))
            ]
            for move in moves:
                move.start()
            for move in moves:
                move.wait()


def cost(rows, keys, heads):
    scores = rows * keys * heads
    return pl.CostEstimate(flops=4 * scores * HEAD_DIM, bytes_accessed=rows * heads * 512, transcendentals=scores)


def chunks_of(heads):
    tail = max(1, heads // 3)
    return (heads - tail, tail) if heads > tail else (heads,)


def lined(video_q, video_k, video_v, audio_q, audio_k, audio_v, offsets, counts):
    n, cores = lax.axis_size("seq"), lax.axis_size("mp")
    me = lax.axis_index("seq")
    video_rows, audio_rows = video_q.shape[0], audio_q.shape[0]
    width = video_q.shape[1]
    heads = width // HEAD_DIM
    chunks = chunks_of(heads)
    mate_pairs = [(i, i ^ 1) for i in range(n)]
    cross_pairs = []
    for i in range(n):
        for core in range(cores):
            inner = 0 < i < n - 1
            to = (n - 1 - i) * cores + core if inner else i * cores + cores - 1 - core
            cross_pairs.append((i * cores + core, to))

    def mate(rows):
        return lax.ppermute(rows, "seq", mate_pairs)

    def cross(rows):
        return lax.ppermute(rows, ("seq", "mp"), cross_pairs)

    role = jnp.where((me == 0) | (me == n - 1), 1, 0).astype(jnp.int32).reshape(1)
    blocks = jnp.stack([me, me ^ 1, n - 1 - me, (n - 1 - me) ^ 1]).astype(jnp.int32)
    flip = me * 2 >= n

    def by_role(low, high):
        return jnp.where(flip, jnp.concatenate(high), jnp.concatenate(low))

    parts = [offsets[i * audio_rows : (i + 1) * audio_rows] for i in range(n)]
    key_offsets = by_role(
        [parts[1], parts[0], parts[2], parts[3]], [parts[2], parts[3], parts[1], parts[0]]
    )
    gap = key_offsets[None, :] - blocks[:2, None]
    within = jnp.arange(video_rows, dtype=jnp.int32)
    tagged = [jnp.where(within < counts[i], i, DEAD) for i in range(n)]
    frames = by_role(
        [tagged[1], tagged[0], tagged[2], tagged[3]], [tagged[2], tagged[3], tagged[1], tagged[0]]
    ).astype(jnp.int32)[None, :]
    row_offsets = key_offsets[: 2 * audio_rows, None]

    sound = jnp.concatenate([audio_k, audio_v], axis=0)
    asks = jnp.concatenate([video_q, audio_q], axis=0)
    sights, at = [], 0
    for size in chunks:
        cols = slice(at * HEAD_DIM, (at + size) * HEAD_DIM)
        sights.append(jnp.concatenate([video_k[:, cols], video_v[:, cols]], axis=0))
        at += size

    last = len(chunks) - 1
    sound_mate = mate(sound)
    sound_across = cross(sound)
    sight_mate = [mate(sights[i]) for i in range(last + 1)]
    asks_mate = mate(asks)
    sight_across = [cross(sights[i]) for i in range(last + 1)]
    sound_far = cross(sound_mate)
    sight_far = [cross(sight_mate[i]) for i in range(last + 1)]

    rows = video_rows + audio_rows
    shape = jax.ShapeDtypeStruct((rows, width), jnp.bfloat16)
    own, theirs = pl.pallas_call(
        audio_kernel,
        out_shape=(shape, shape),
        in_specs=[SMEM] + [VMEM] * 7,
        out_specs=(VMEM, VMEM),
        cost_estimate=cost(2 * rows, n * audio_rows, heads),
        compiler_params=PARAMS,
        name="audio_keys",
    )(role, gap, asks, asks_mate, sound, sound_mate, sound_across, sound_far)
    mine, back = [own], [mate(theirs)]
    at = 0
    for i, size in enumerate(chunks):
        shape = jax.ShapeDtypeStruct((rows, size * HEAD_DIM), jnp.bfloat16)
        own, theirs = pl.pallas_call(
            functools.partial(video_kernel, at),
            out_shape=(shape, shape),
            in_specs=[SMEM] + [VMEM] * 8,
            out_specs=(VMEM, VMEM),
            cost_estimate=cost(2 * rows, n * video_rows, size),
            compiler_params=PARAMS,
        )(role, frames, row_offsets, asks, asks_mate, sights[i], sight_mate[i], sight_across[i], sight_far[i])
        mine.append(own)
        back.append(mate(theirs))
        at += size

    video_shape = jax.ShapeDtypeStruct((video_rows, width), jnp.bfloat16)
    audio_shape = jax.ShapeDtypeStruct((audio_rows, width), jnp.bfloat16)
    return pl.pallas_call(
        functools.partial(place_kernel, video_rows),
        out_shape=(video_shape, video_shape, audio_shape, audio_shape),
        in_specs=[SMEM] + [VMEM] * (2 * len(mine)),
        out_specs=(ANY,) * 4,
        scratch_shapes=[pltpu.SemaphoreType.DMA((2 * len(mine),))],
        compiler_params=PARAMS,
        name="place",
    )(role, *mine, *back)


def solution(mesh):
    split = P(("groups", "seq"), ("tower", "mp"))
    placed = (split,) * 6 + (P("groups"), P("groups"))
    lined_up = mesh.shape["seq"] == 4 and mesh.shape["mp"] == 2

    def whole(*arrays):
        body = lined if lined_up else gathered
        return jax.shard_map(
            body, mesh=mesh, in_specs=placed, out_specs=(split,) * 4, check_vma=False
        )(*arrays)

    return whole
```

time: 77.2 us -> 49.8 us (0.65)
  blocking collectives: 68 us -> 0 us
  starting transfers between devices: 0 us -> 25.7 us
  waiting for transfers between devices: 0 us -> 14.4 us
  matrix products: 3.14 us -> 0 us
  Pallas kernels: 0 us -> 1.57 us
  other arithmetic: 1.56 us -> 2.83 us
  local copies, waits for them, and re-layouts: 3.4 us -> 4.21 us
    all_gather x4 -> x0, blocking collectives: 68 us -> none  [the longest x1 21.6 us: shards(): lax.all_gather(video_v, 'seq', axis=0, tiled=True)]
    ppermute x0 -> x13, starting transfers between devices: none -> 25.7 us  [the longest x7 24.7 us: mate(): return lax.ppermute(rows, 'seq', mate_pairs)]
    ppermute x0 -> x13, waiting for transfers between devices: none -> 14.4 us  [the longest x7 14.4 us: mate(): return lax.ppermute(rows, 'seq', mate_pairs)]
    dot_general x8 -> x0, matrix products: 3.14 us -> none  [the longest x4 1.64 us: absorb(): jnp.einsum('hqk,khe->hqe', weights.astype(jnp.bfloat16), value_rows, pref...]
    concatenate x0 -> x4, other arithmetic: none -> 2.61 us  [the longest x2 2.58 us: by_role(): return jnp.where(flip, jnp.concatenate(high), jnp.concatenate(low))]
    slice x0 -> x11, local copies, waits for them, and re-layouts: none -> 2.56 us  [the longest x8 1.83 us: lined(): sights.append(jnp.concatenate([video_k[:, cols], video_v[:, cols]], axis=0))]
    pallas_call x0 -> x4, Pallas kernels: none -> 1.57 us  [the longest x1 0.85 us: lined(): pl.pallas_call(functools.partial(place_kernel, video_rows), out_shape=(vi...]
    reduce_sum x5 -> x0, other arithmetic: 1.41 us -> none  [the longest x4 1.32 us: absorb(): run_total = jnp.sum(weights, axis=2)]
  transfers between devices with their start and end apart: 0 -> 13, of which waited for: 0 -> 3; matrix products, arithmetic and copies ran while one was open for 0% -> 7% of each run, Pallas kernels for 0% -> 1%
where the time goes in v1:
time: 49.8 us; the launch traced here: 49.5 us
  starting transfers between devices  25.7 us (52%)
  waiting for transfers between devices  14.4 us (29%)
  local copies, waits for them, and re-layouts  4.21 us (8%)
  other arithmetic  2.83 us (6%)
  Pallas kernels  1.57 us (3%)
  between operations  0.79 us (2%)
    ppermute x7, starting transfers between devices, mate(): return lax.ppermute(rows, 'seq', mate_pairs)  24.7 us
    ppermute x7, waiting for transfers between devices, mate(): return lax.ppermute(rows, 'seq', mate_pairs)  14.4 us
    concatenate x2, other arithmetic, by_role(): return jnp.where(flip, jnp.concatenate(high), jnp.concatenate(low))  2.58 us
    slice x8, local copies, waits for them, and re-layouts, lined(): sights.append(jnp.concatenate([video_k[:, cols], video_v[:, cols]], axis=0))  1.83 us
    unnamed x14, local copies, waits for them, and re-layouts  1.52 us
    ppermute x6, starting transfers between devices, cross(): return lax.ppermute(rows, ('seq', 'mp'), cross_pairs)  1.08 us
  transfers between devices with their start and end apart: 13, of which 3 were waited for; matrix products, arithmetic and copies ran while one was open for 7% of the time, Pallas kernels for 1%

profile of v1, /device:TPU:0, one launch (start us, length us, event | category | flops | bytes accessed | tf_op | source)
XLA Modules:
  0.0 49.5 jit_solution(4828561947445975434)
XLA Ops:
  0.6 0.0 slice-start
  0.6 0.0 slice-start.2
  0.7 0.9 %slice-done = bf16[128,512]{1,0:T(8,128)(2,1)S(1)} async-done(((bf16[128,768]{1,0:T(8,128)(2,1)}), bf16[128,512]{1,0:T(8,128)(2,1)S(1)}, s32[]{:S(2)}) %slice-start) | async-done | bytes 131096 | tf_op jit(solution)/shard_map/slice | solution.py:202
  1.5 0.1 slice-done.2
  1.6 0.0 copy-start
  1.6 0.0 copy-start.1
  1.6 3.1 %collective-permute-start.4 = (bf16[256,512]{1,0:T(8,128)(2,1)S(1)}, bf16[256,512]{1,0:T(8,128)(2,1)S(1)}, u32[]{:S(2)}, u32[]{:S(2)}) collective-permute-start(bf16[256,512]{1,0:T(8,128)(2,1)S(1)} %pad_maximum_fusion.b0), channel_id=1, source_target_pairs={{0,4},{4,0},{8,12},{12,8},{1,5},{5,1},{9,13},{13,9},{2,6},{6,2},{1... | collective-permute-start | bytes 786440 | tf_op jit(solution)/shard_map/ppermute | solution.py:173
  4.8 0.0 collective-permute-start.5
  4.8 0.0 copy-done
  4.8 0.0 copy-done.1
  4.8 3.2 %collective-permute-start = (bf16[192,768]{1,0:T(8,128)(2,1)S(1)}, bf16[192,768]{1,0:T(8,128)(2,1)S(1)}, u32[]{:S(2)}, u32[]{:S(2)}) collective-permute-start(bf16[192,768]{1,0:T(8,128)(2,1)S(1)} %constant_dynamic-update-slice_fusion.q_own), channel_id=1, source_target_pairs={{0,4},{4,0},{8,12},{12,8},{1,5},{5,1},{9,13},{13,9},{2,6},{6,2},{1... | collective-permute-start | bytes 884744 | tf_op jit(solution)/shard_map/ppermute | solution.py:173
  8.0 0.0 slice-start.1
  8.0 0.0 slice-start.3
  8.0 0.8 %slice-done.1 = bf16[128,256]{1,0:T(8,128)(2,1)S(1)} async-done(((bf16[128,768]{1,0:T(8,128)(2,1)}), bf16[128,256]{1,0:T(8,128)(2,1)S(1)}, s32[]{:S(2)}) %slice-start.1) | async-done | bytes 65560 | tf_op jit(solution)/shard_map/slice | solution.py:202
  8.9 0.0 slice-done.3
  8.9 0.0 copy-start.2
  8.9 0.0 copy-start.3
  8.9 0.1 collective-permute-start.7
  9.0 0.8 %copy-done.2 = bf16[64,768]{1,0:T(8,128)(2,1)S(1)} copy-done((bf16[64,768]{1,0:T(8,128)(2,1)S(1)}, bf16[64,768]{1,0:T(8,128)(2,1)}, u32[]{:S(2)}) %copy-start.2) | copy-done | bytes 98328
  9.8 0.0 copy-done.3
  9.8 0.0 copy-start.5
  9.9 1.3 %collective-permute-start.1 = (bf16[128,768]{1,0:T(8,128)(2,1)S(1)}, bf16[128,768]{1,0:T(8,128)(2,1)S(1)}, u32[]{:S(2)}, u32[]{:S(2)}) collective-permute-start(bf16[128,768]{1,0:T(8,128)(2,1)S(1)} %constant_dynamic-update-slice_fusion.2.b0), channel_id=1, source_target_pairs={{0,4},{4,0},{8,12},{12,8},{1,5},{5,1},{9,13},{13,9},{2,6},{6,2},{1... | collective-permute-start | bytes 589832 | tf_op jit(solution)/shard_map/ppermute | solution.py:173
  11.1 0.0 copy-done.5
  11.1 0.1 fusion.4
  11.2 0.1 pad_add_fusion
  11.3 0.1 add_select_fusion
  11.4 0.1 broadcast_subtract_fusion.gap_ref
  11.4 0.0 copy-start.4
  11.4 0.7 %copy-done.4 = s32[4]{0:T(128)S(1)} copy-done((s32[4]{0:T(128)S(1)}, s32[4]{0:T(128)}, u32[]{:S(2)}) %copy-start.4) | copy-done | bytes 40
  12.1 0.7 %fusion.5 = (s32[1]{0:T(128)}, s32[1]{0:T(128)}, s32[1]{0:T(128)}, s32[1]{0:T(128)}) fusion(s32[4]{0:T(128)S(1)} %copy-done.4), kind=kLoop, calls=%fused_computation.20 | loop fusion | bytes 32 | tf_op jit(solution)/shard_map/slice | solution.py:191
  12.8 8.3 %collective-permute-done.7.b1 = bf16[256,256]{1,0:T(8,128)(2,1)S(1)} collective-permute-done((bf16[256,256]{1,0:T(8,128)(2,1)S(1)}, bf16[256,256]{1,0:T(8,128)(2,1)S(1)}, u32[]{:S(2)}, u32[]{:S(2)}) %collective-permute-start.7) | collective-permute-done | bytes 131104 | tf_op jit(solution)/shard_map/ppermute | solution.py:173
  21.0 0.0 collective-permute-start.2
  21.0 3.4 %collective-permute-done.1.b1 = bf16[128,768]{1,0:T(8,128)(2,1)S(1)} collective-permute-done((bf16[128,768]{1,0:T(8,128)(2,1)S(1)}, bf16[128,768]{1,0:T(8,128)(2,1)S(1)}, u32[]{:S(2)}, u32[]{:S(2)}) %collective-permute-start.1) | collective-permute-done | bytes 196640 | tf_op jit(solution)/shard_map/ppermute | solution.py:173
  24.4 0.0 collective-permute-start.3
  24.4 0.0 collective-permute-done.4.b1
  24.4 0.5 %collective-permute-start.6 = (bf16[256,512]{1,0:T(8,128)(2,1)S(1)}, bf16[256,512]{1,0:T(8,128)(2,1)S(1)}, u32[]{:S(2)}, u32[]{:S(2)}) collective-permute-start(bf16[256,512]{1,0:T(8,128)(2,1)S(1)} %collective-permute-done.4.b1), channel_id=1, source_target_pairs={{0,1},{1,0},{4,8},{5,9},{8,4},{9,5},{12,13},{13,12},{2,3},{3,2},{6... | collective-permute-start | bytes 786440 | tf_op jit(solution)/shard_map/ppermute | solution.py:176
  24.9 1.3 %fusion = (s32[1,128]{1,0:T(1,128)S(1)}, s32[1,128]{1,0:T(1,128)S(1)}) fusion(s32[]{:T(128)} %bitcast.3, s32[]{:T(128)} %bitcast.5), kind=kLoop, calls=%fused_computation.13 | loop fusion | flops 512 | bytes 1032 | tf_op jit(solution)/shard_map/concatenate | solution.py:183
  26.2 1.3 %fusion.2 = (s32[1,128]{1,0:T(1,128)S(1)}, s32[1,128]{1,0:T(1,128)S(1)}) fusion(s32[]{:T(128)} %bitcast.7, s32[]{:T(128)} %bitcast.9), kind=kLoop, calls=%fused_computation.15 | loop fusion | flops 512 | bytes 1032 | tf_op jit(solution)/shard_map/concatenate | solution.py:183
  27.5 0.0 collective-permute-done.2.b2
  27.5 0.1 collective-permute-start.8
  27.6 0.0 collective-permute-done.q_mate
  27.6 0.5 collective-permute-start.9
  28.1 0.0 collective-permute-done.3.b3
  28.1 0.7 %audio_keys.1 = (bf16[192,768]{1,0:T(8,128)(2,1)S(1)}, bf16[192,768]{1,0:T(8,128)(2,1)}) custom-call(s32[1]{0:T(128)} %bitcast.role_ref, s32[2,256]{1,0:T(2,128)S(1)} %broadcast_subtract_fusion.gap_ref, bf16[192,768]{1,0:T(8,128)(2,1)S(1)} %constant_dynamic-update-slice_fusion.q_own, bf16[192,768]{1,0:T(8,128)(2,1)S(1)} %collective-permute-done.q_mate, ...), custom_call_target="tpu_custom_call" | custom-call | flops 301989888 | bytes 1179648 | tf_op jit(solution)/shard_map/audio_keys/pallas_call | solution.py:216
  28.8 7.0 %collective-permute-start.10 = (bf16[192,768]{1,0:T(8,128)(2,1)}, bf16[192,768]{1,0:T(8,128)(2,1)S(1)}, u32[]{:S(2)}, u32[]{:S(2)}) collective-permute-start(bf16[192,768]{1,0:T(8,128)(2,1)} %get-tuple-element.13), channel_id=1, source_target_pairs={{0,4},{4,0},{8,12},{12,8},{1,5},{5,1},{9,13},{13,9},{2,6},{6,2},{1... | collective-permute-start | bytes 884744 | tf_op jit(solution)/shard_map/ppermute | solution.py:173
  35.9 0.1 copy.12.off_ref
  36.0 0.0 collective-permute-done.5.b2
  36.0 0.0 collective-permute-done.6.b3
  36.0 6.9 %collective-permute-start.11 = (bf16[192,512]{1,0:T(8,128)(2,1)S(1)}, bf16[192,512]{1,0:T(8,128)(2,1)S(1)}, u32[]{:S(2)}, u32[]{:S(2)}) collective-permute-start(bf16[192,512]{1,0:T(8,128)(2,1)S(1)} %get-tuple-element.14), channel_id=1, source_target_pairs={{0,4},{4,0},{8,12},{12,8},{1,5},{5,1},{9,13},{13,9},{2,6},{6,2},{1... | collective-permute-start | bytes 589832 | tf_op jit(solution)/shard_map/ppermute | solution.py:173
  42.9 0.0 collective-permute-done.8.b2
  42.9 0.0 collective-permute-done.9.b3
  42.9 3.0 %collective-permute-start.12 = (bf16[192,256]{1,0:T(8,128)(2,1)S(1)}, bf16[192,256]{1,0:T(8,128)(2,1)S(1)}, u32[]{:S(2)}, u32[]{:S(2)}) collective-permute-start(bf16[192,256]{1,0:T(8,128)(2,1)S(1)} %get-tuple-element.15), channel_id=1, source_target_pairs={{0,4},{4,0},{8,12},{12,8},{1,5},{5,1},{9,13},{13,9},{2,6},{6,2},{1... | collective-permute-start | bytes 294920 | tf_op jit(solution)/shard_map/ppermute | solution.py:173
  46.0 2.7 %collective-permute-done.12.refs_5_ = bf16[192,256]{1,0:T(8,128)(2,1)S(1)} collective-permute-done((bf16[192,256]{1,0:T(8,128)(2,1)S(1)}, bf16[192,256]{1,0:T(8,128)(2,1)S(1)}, u32[]{:S(2)}, u32[]{:S(2)}) %collective-permute-start.12) | collective-permute-done | bytes 98336 | tf_op jit(solution)/shard_map/ppermute | solution.py:173
  48.7 0.0 collective-permute-done.10.refs_3_
  48.7 0.0 collective-permute-done.11.refs_4_
  48.7 0.8 %place.1 = (bf16[128,768]{1,0:T(8,128)(2,1)}, bf16[128,768]{1,0:T(8,128)(2,1)}, bf16[64,768]{1,0:T(8,128)(2,1)}, bf16[64,768]{1,0:T(8,128)(2,1)}) custom-call(s32[1]{0:T(128)} %bitcast.role_ref, bf16[192,768]{1,0:T(8,128)(2,1)S(1)} %get-tuple-element.10.refs_0_, bf16[192,512]{1,0:T(8,128)(2,1)S(1)} %get-tuple-element.11.refs_1_, ...), custom_call_target="tpu_custom_call" | custom-call | tf_op jit(solution)/shard_map/place/pallas_call | solution.py:243
  (11 shorter events, 0.1 us)
Async XLA Ops:
  0.6 0.9 %slice-start = ((bf16[128,768]{1,0:T(8,128)(2,1)}), bf16[128,512]{1,0:T(8,128)(2,1)S(1)}, s32[]{:S(2)}) async-start(bf16[128,768]{1,0:T(8,128)(2,1)} %param.9), calls=%async_computation | async-start | bytes 262144 | tf_op jit(solution)/shard_map/slice | solution.py:202
  0.6 1.0 %slice-start.2 = ((bf16[128,768]{1,0:T(8,128)(2,1)}), bf16[128,512]{1,0:T(8,128)(2,1)S(1)}, s32[]{:S(2)}) async-start(bf16[128,768]{1,0:T(8,128)(2,1)} %param.10), calls=%async_computation.2 | async-start | bytes 262144 | tf_op jit(solution)/shard_map/slice | solution.py:202
  1.6 3.2 %copy-start = (bf16[128,768]{1,0:T(8,128)(2,1)S(1)}, bf16[128,768]{1,0:T(8,128)(2,1)}, u32[]{:S(2)}) copy-start(bf16[128,768]{1,0:T(8,128)(2,1)} %param.8) | copy-start | bytes 589828
  1.6 3.2 %copy-start.1 = (bf16[64,768]{1,0:T(8,128)(2,1)S(1)}, bf16[64,768]{1,0:T(8,128)(2,1)}, u32[]{:S(2)}) copy-start(bf16[64,768]{1,0:T(8,128)(2,1)} %param.11) | copy-start | bytes 294916
  1.6 22.8 %collective-permute-start.4 = (bf16[256,512]{1,0:T(8,128)(2,1)S(1)}, bf16[256,512]{1,0:T(8,128)(2,1)S(1)}, u32[]{:S(2)}, u32[]{:S(2)}) collective-permute-start(bf16[256,512]{1,0:T(8,128)(2,1)S(1)} %pad_maximum_fusion.b0), channel_id=1, source_target_pairs={{0,4},{4,0},{8,12},{12,8},{1,5},{5,1},{9,13},{13,9},{2,6},{6,2},{1... | collective-permute-start | bytes 786440 | tf_op jit(solution)/shard_map/ppermute | solution.py:173
  4.8 31.2 %collective-permute-start.5 = (bf16[256,512]{1,0:T(8,128)(2,1)S(1)}, bf16[256,512]{1,0:T(8,128)(2,1)S(1)}, u32[]{:S(2)}, u32[]{:S(2)}) collective-permute-start(bf16[256,512]{1,0:T(8,128)(2,1)S(1)} %pad_maximum_fusion.b0), channel_id=1, source_target_pairs={{0,1},{1,0},{4,8},{5,9},{8,4},{9,5},{12,13},{13,12},{2,3},{3,2},{6... | collective-permute-start | bytes 786440 | tf_op jit(solution)/shard_map/ppermute | solution.py:176
  4.8 22.8 %collective-permute-start = (bf16[192,768]{1,0:T(8,128)(2,1)S(1)}, bf16[192,768]{1,0:T(8,128)(2,1)S(1)}, u32[]{:S(2)}, u32[]{:S(2)}) collective-permute-start(bf16[192,768]{1,0:T(8,128)(2,1)S(1)} %constant_dynamic-update-slice_fusion.q_own), channel_id=1, source_target_pairs={{0,4},{4,0},{8,12},{12,8},{1,5},{5,1},{9,13},{13,9},{2,6},{6,2},{1... | collective-permute-start | bytes 884744 | tf_op jit(solution)/shard_map/ppermute | solution.py:173
  8.0 0.8 %slice-start.1 = ((bf16[128,768]{1,0:T(8,128)(2,1)}), bf16[128,256]{1,0:T(8,128)(2,1)S(1)}, s32[]{:S(2)}) async-start(bf16[128,768]{1,0:T(8,128)(2,1)} %param.9), calls=%async_computation.1 | async-start | bytes 131072 | tf_op jit(solution)/shard_map/slice | solution.py:202
  8.0 0.9 %slice-start.3 = ((bf16[128,768]{1,0:T(8,128)(2,1)}), bf16[128,256]{1,0:T(8,128)(2,1)S(1)}, s32[]{:S(2)}) async-start(bf16[128,768]{1,0:T(8,128)(2,1)} %param.10), calls=%async_computation.3 | async-start | bytes 131072 | tf_op jit(solution)/shard_map/slice | solution.py:202
  8.9 0.9 %copy-start.2 = (bf16[64,768]{1,0:T(8,128)(2,1)S(1)}, bf16[64,768]{1,0:T(8,128)(2,1)}, u32[]{:S(2)}) copy-start(bf16[64,768]{1,0:T(8,128)(2,1)} %param.12) | copy-start | bytes 294916
  8.9 0.9 %copy-start.3 = (bf16[64,768]{1,0:T(8,128)(2,1)S(1)}, bf16[64,768]{1,0:T(8,128)(2,1)}, u32[]{:S(2)}) copy-start(bf16[64,768]{1,0:T(8,128)(2,1)} %param.13) | copy-start | bytes 294916
  8.9 12.1 %collective-permute-start.7 = (bf16[256,256]{1,0:T(8,128)(2,1)S(1)}, bf16[256,256]{1,0:T(8,128)(2,1)S(1)}, u32[]{:S(2)}, u32[]{:S(2)}) collective-permute-start(bf16[256,256]{1,0:T(8,128)(2,1)S(1)} %pad_maximum_fusion.1.b0), channel_id=1, source_target_pairs={{0,4},{4,0},{8,12},{12,8},{1,5},{5,1},{9,13},{13,9},{2,6},{6,2},{1... | collective-permute-start | bytes 393224 | tf_op jit(solution)/shard_map/ppermute | solution.py:173
  9.8 1.3 %copy-start.5 = (s32[256]{0:T(256)S(1)}, s32[256]{0:T(256)}, u32[]{:S(2)}) copy-start(s32[256]{0:T(256)} %param.14) | copy-start | bytes 3076
  9.9 14.6 %collective-permute-start.1 = (bf16[128,768]{1,0:T(8,128)(2,1)S(1)}, bf16[128,768]{1,0:T(8,128)(2,1)S(1)}, u32[]{:S(2)}, u32[]{:S(2)}) collective-permute-start(bf16[128,768]{1,0:T(8,128)(2,1)S(1)} %constant_dynamic-update-slice_fusion.2.b0), channel_id=1, source_target_pairs={{0,4},{4,0},{8,12},{12,8},{1,5},{5,1},{9,13},{13,9},{2,6},{6,2},{1... | collective-permute-start | bytes 589832 | tf_op jit(solution)/shard_map/ppermute | solution.py:173
  11.4 0.7 %copy-start.4 = (s32[4]{0:T(128)S(1)}, s32[4]{0:T(128)}, u32[]{:S(2)}) copy-start(s32[4]{0:T(128)} %param.15) | copy-start | bytes 52
  21.0 6.5 %collective-permute-start.2 = (bf16[128,768]{1,0:T(8,128)(2,1)S(1)}, bf16[128,768]{1,0:T(8,128)(2,1)S(1)}, u32[]{:S(2)}, u32[]{:S(2)}) collective-permute-start(bf16[128,768]{1,0:T(8,128)(2,1)S(1)} %constant_dynamic-update-slice_fusion.2.b0), channel_id=1, source_target_pairs={{0,1},{1,0},{4,8},{5,9},{8,4},{9,5},{12,13},{13,12},{2,3},{3,2},{6... | collective-permute-start | bytes 589832 | tf_op jit(solution)/shard_map/ppermute | solution.py:176
  24.4 3.7 %collective-permute-start.3 = (bf16[128,768]{1,0:T(8,128)(2,1)S(1)}, bf16[128,768]{1,0:T(8,128)(2,1)S(1)}, u32[]{:S(2)}, u32[]{:S(2)}) collective-permute-start(bf16[128,768]{1,0:T(8,128)(2,1)S(1)} %collective-permute-done.1.b1), channel_id=1, source_target_pairs={{0,1},{1,0},{4,8},{5,9},{8,4},{9,5},{12,13},{13,12},{2,3},{3,2},{6... | collective-permute-start | bytes 589832 | tf_op jit(solution)/shard_map/ppermute | solution.py:176
  24.4 11.6 %collective-permute-start.6 = (bf16[256,512]{1,0:T(8,128)(2,1)S(1)}, bf16[256,512]{1,0:T(8,128)(2,1)S(1)}, u32[]{:S(2)}, u32[]{:S(2)}) collective-permute-start(bf16[256,512]{1,0:T(8,128)(2,1)S(1)} %collective-permute-done.4.b1), channel_id=1, source_target_pairs={{0,1},{1,0},{4,8},{5,9},{8,4},{9,5},{12,13},{13,12},{2,3},{3,2},{6... | collective-permute-start | bytes 786440 | tf_op jit(solution)/shard_map/ppermute | solution.py:176
  27.5 15.4 %collective-permute-start.8 = (bf16[256,256]{1,0:T(8,128)(2,1)S(1)}, bf16[256,256]{1,0:T(8,128)(2,1)S(1)}, u32[]{:S(2)}, u32[]{:S(2)}) collective-permute-start(bf16[256,256]{1,0:T(8,128)(2,1)S(1)} %pad_maximum_fusion.1.b0), channel_id=1, source_target_pairs={{0,1},{1,0},{4,8},{5,9},{8,4},{9,5},{12,13},{13,12},{2,3},{3,2},{6... | collective-permute-start | bytes 393224 | tf_op jit(solution)/shard_map/ppermute | solution.py:176
  27.6 15.3 %collective-permute-start.9 = (bf16[256,256]{1,0:T(8,128)(2,1)S(1)}, bf16[256,256]{1,0:T(8,128)(2,1)S(1)}, u32[]{:S(2)}, u32[]{:S(2)}) collective-permute-start(bf16[256,256]{1,0:T(8,128)(2,1)S(1)} %collective-permute-done.7.b1), channel_id=1, source_target_pairs={{0,1},{1,0},{4,8},{5,9},{8,4},{9,5},{12,13},{13,12},{2,3},{3,2},{6... | collective-permute-start | bytes 393224 | tf_op jit(solution)/shard_map/ppermute | solution.py:176
  28.8 19.9 %collective-permute-start.10 = (bf16[192,768]{1,0:T(8,128)(2,1)}, bf16[192,768]{1,0:T(8,128)(2,1)S(1)}, u32[]{:S(2)}, u32[]{:S(2)}) collective-permute-start(bf16[192,768]{1,0:T(8,128)(2,1)} %get-tuple-element.13), channel_id=1, source_target_pairs={{0,4},{4,0},{8,12},{12,8},{1,5},{5,1},{9,13},{13,9},{2,6},{6,2},{1... | collective-permute-start | bytes 884744 | tf_op jit(solution)/shard_map/ppermute | solution.py:173
  36.0 12.7 %collective-permute-start.11 = (bf16[192,512]{1,0:T(8,128)(2,1)S(1)}, bf16[192,512]{1,0:T(8,128)(2,1)S(1)}, u32[]{:S(2)}, u32[]{:S(2)}) collective-permute-start(bf16[192,512]{1,0:T(8,128)(2,1)S(1)} %get-tuple-element.14), channel_id=1, source_target_pairs={{0,4},{4,0},{8,12},{12,8},{1,5},{5,1},{9,13},{13,9},{2,6},{6,2},{1... | collective-permute-start | bytes 589832 | tf_op jit(solution)/shard_map/ppermute | solution.py:173
  42.9 5.7 %collective-permute-start.12 = (bf16[192,256]{1,0:T(8,128)(2,1)S(1)}, bf16[192,256]{1,0:T(8,128)(2,1)S(1)}, u32[]{:S(2)}, u32[]{:S(2)}) collective-permute-start(bf16[192,256]{1,0:T(8,128)(2,1)S(1)} %get-tuple-element.15), channel_id=1, source_target_pairs={{0,4},{4,0},{8,12},{12,8},{1,5},{5,1},{9,13},{13,9},{2,6},{6,2},{1... | collective-permute-start | bytes 294920 | tf_op jit(solution)/shard_map/ppermute | solution.py:173

commit v2 on v1

--- a/solution.py
+++ b/solution.py
@@ -73,23 +73,31 @@
     return (mixed * (1.0 / total)).astype(jnp.bfloat16)
 
 
-def audio_kernel(role_ref, gap_ref, q_own, q_mate, b0, b1, b2, b3, own_ref, mate_ref):
-    video_rows = q_own.shape[0] - b0.shape[0] // 2
-    audio_rows = b0.shape[0] // 2
+def audio_kernel(role_ref, gap_ref, q_own, q_mate, b0, b1, inner2, end2, b3, cross_ref, own_ref, mate_ref):
+    video_rows = cross_ref.shape[0]
+    audio_rows = own_ref.shape[0]
+    reach = jnp.abs(gap_ref[...]) <= SPAN
+
+    def run(blocks, alone):
+        for head in range(q_own.shape[1] // HEAD_DIM):
+            cols = slice(head * HEAD_DIM, (head + 1) * HEAD_DIM)
+            keys = jnp.concatenate([b[:audio_rows, cols] for b in blocks], axis=0)
+            values = jnp.concatenate([b[audio_rows:, cols] for b in blocks], axis=0)
+            span = slice(0, keys.shape[0])
+            cross_ref[:, cols] = blend(q_own[:video_rows, cols], keys, values, reach[:, span])
+            if not alone:
+                both = jnp.concatenate([q_own[video_rows:, cols], q_mate[video_rows:, cols]], axis=0)
+                out = blend(both, keys, values, None)
+                own_ref[:, cols] = out[:audio_rows]
+                mate_ref[:, cols] = out[audio_rows:]
 
     @pl.when(role_ref[0] == 0)
     def _():
-        reach = [jnp.abs(gap_ref[i : i + 1, :]) <= SPAN for i in range(2)]
-        for head in range(q_own.shape[1] // HEAD_DIM):
-            cols = slice(head * HEAD_DIM, (head + 1) * HEAD_DIM)
-            keys = jnp.concatenate([b[:audio_rows, cols] for b in (b0, b1, b2, b3)], axis=0)
-            values = jnp.concatenate([b[audio_rows:, cols] for b in (b0, b1, b2, b3)], axis=0)
-            for who, (q_ref, o_ref) in enumerate(((q_own, own_ref), (q_mate, mate_ref))):
-                o_ref[:video_rows, cols] = blend(q_ref[:video_rows, cols], keys, values, reach[who])
-            both = jnp.concatenate([q_own[video_rows:, cols], q_mate[video_rows:, cols]], axis=0)
-            out = blend(both, keys, values, None)
-            own_ref[video_rows:, cols] = out[:audio_rows]
-            mate_ref[video_rows:, cols] = out[audio_rows:]
+        run((b0, b1, inner2, b3), False)
+
+    @pl.when(role_ref[0] == 1)
+    def _():
+        run((b0, b1, end2), True)
 
 
 def video_kernel(first, role_ref, frame_ref, off_ref, q_own, q_mate, b0, b1, b2, b3, own_ref, mate_ref):
@@ -114,15 +122,15 @@
             mate_ref[video_rows:, cols] = out[audio_rows:]
 
 
-def place_kernel(video_rows, role_ref, *refs):
+def place_kernel(video_rows, role_ref, cross, *refs):
     n = (len(refs) - 5) // 2
     own, back = refs[:n], refs[n : 2 * n]
     video_self, video_cross, audio_self, audio_cross = refs[2 * n : 2 * n + 4]
     sem = refs[-1]
 
     def copies(parts):
-        yield parts[0].at[:video_rows], video_cross
-        yield parts[0].at[video_rows:], audio_self
+        yield cross, video_cross
+        yield parts[0], audio_self
         at = 0
         for part in parts[1:]:
             cols = pl.ds(at, part.shape[1])
@@ -176,22 +184,20 @@
         return lax.ppermute(rows, ("seq", "mp"), cross_pairs)
 
     role = jnp.where((me == 0) | (me == n - 1), 1, 0).astype(jnp.int32).reshape(1)
-    blocks = jnp.stack([me, me ^ 1, n - 1 - me, (n - 1 - me) ^ 1]).astype(jnp.int32)
-    flip = me * 2 >= n
-
-    def by_role(low, high):
-        return jnp.where(flip, jnp.concatenate(high), jnp.concatenate(low))
-
-    parts = [offsets[i * audio_rows : (i + 1) * audio_rows] for i in range(n)]
-    key_offsets = by_role(
-        [parts[1], parts[0], parts[2], parts[3]], [parts[2], parts[3], parts[1], parts[0]]
-    )
-    gap = key_offsets[None, :] - blocks[:2, None]
+    upper = me * 2 >= n
+
+    def by_block(parts):
+        own = jnp.where(me % 2 == 0, jnp.concatenate(parts[:2]), jnp.concatenate(parts[1::-1]))
+        other = jnp.where(me % 2 == 0, jnp.concatenate(parts[2:]), jnp.concatenate(parts[:1:-1]))
+        low = jnp.concatenate([own] + parts[2:])
+        high = jnp.concatenate([other] + parts[1::-1])
+        return jnp.where(upper, high, low)
+
+    key_offsets = by_block([offsets[i * audio_rows : (i + 1) * audio_rows] for i in range(n)])
+    gap = (key_offsets - me)[None, :]
     within = jnp.arange(video_rows, dtype=jnp.int32)
-    tagged = [jnp.where(within < counts[i], i, DEAD) for i in range(n)]
-    frames = by_role(
-        [tagged[1], tagged[0], tagged[2], tagged[3]], [tagged[2], tagged[3], tagged[1], tagged[0]]
-    ).astype(jnp.int32)[None, :]
+    frames = by_block([jnp.where(within < counts[i], i, DEAD) for i in range(n)])
+    frames = frames.astype(jnp.int32)[None, :]
     row_offsets = key_offsets[: 2 * audio_rows, None]
 
     sound = jnp.concatenate([audio_k, audio_v], axis=0)
@@ -202,28 +208,18 @@
         sights.append(jnp.concatenate([video_k[:, cols], video_v[:, cols]], axis=0))
         at += size
 
-    last = len(chunks) - 1
+    pieces = range(len(chunks))
+    sight_mate = [mate(sights[i]) for i in pieces]
+    sight_across = [cross(sights[i]) for i in pieces]
+    sight_far = [cross(sight_mate[i]) for i in pieces]
+    asks_mate = mate(asks)
     sound_mate = mate(sound)
     sound_across = cross(sound)
-    sight_mate = [mate(sights[i]) for i in range(last + 1)]
-    asks_mate = mate(asks)
-    sight_across = [cross(sights[i]) for i in range(last + 1)]
     sound_far = cross(sound_mate)
-    sight_far = [cross(sight_mate[i]) for i in range(last + 1)]
+    sound_passed = mate(sound_across)
 
     rows = video_rows + audio_rows
-    shape = jax.ShapeDtypeStruct((rows, width), jnp.bfloat16)
-    own, theirs = pl.pallas_call(
-        audio_kernel,
-        out_shape=(shape, shape),
-        in_specs=[SMEM] + [VMEM] * 7,
-        out_specs=(VMEM, VMEM),
-        cost_estimate=cost(2 * rows, n * audio_rows, heads),
-        compiler_params=PARAMS,
-        name="audio_keys",
-    )(role, gap, asks, asks_mate, sound, sound_mate, sound_across, sound_far)
-    mine, back = [own], [mate(theirs)]
-    at = 0
+    mine, back, at = [], [], 0
     for i, size in enumerate(chunks):
         shape = jax.ShapeDtypeStruct((rows, size * HEAD_DIM), jnp.bfloat16)
         own, theirs = pl.pallas_call(
@@ -237,18 +233,28 @@
         mine.append(own)
         back.append(mate(theirs))
         at += size
-
     video_shape = jax.ShapeDtypeStruct((video_rows, width), jnp.bfloat16)
     audio_shape = jax.ShapeDtypeStruct((audio_rows, width), jnp.bfloat16)
+    video_cross, own, theirs = pl.pallas_call(
+        audio_kernel,
+        out_shape=(video_shape, audio_shape, audio_shape),
+        in_specs=[SMEM] + [VMEM] * 8,
+        out_specs=(VMEM,) * 3,
+        cost_estimate=cost(2 * rows, n * audio_rows, heads),
+        compiler_params=PARAMS,
+        name="audio_keys",
+    )(role, gap, asks, asks_mate, sound, sound_mate, sound_across, sound_passed, sound_far)
+    mine = [own] + mine
+    back = [mate(theirs)] + back
     return pl.pallas_call(
         functools.partial(place_kernel, video_rows),
         out_shape=(video_shape, video_shape, audio_shape, audio_shape),
-        in_specs=[SMEM] + [VMEM] * (2 * len(mine)),
+        in_specs=[SMEM] + [VMEM] * (1 + 2 * len(mine)),
         out_specs=(ANY,) * 4,
         scratch_shapes=[pltpu.SemaphoreType.DMA((2 * len(mine),))],
         compiler_params=PARAMS,
         name="place",
-    )(role, *mine, *back)
+    )(role, video_cross, *mine, *back)
 
 
 def solution(mesh):

time: 49.8 us -> 47.1 us (0.946)
  waiting for transfers between devices: 14.4 us -> 9.09 us
  other arithmetic: 2.83 us -> 5.46 us
  starting transfers between devices: 25.7 us -> 24.2 us
  Pallas kernels: 1.57 us -> 2.33 us
  local copies, waits for them, and re-layouts: 4.21 us -> 4.91 us
    ppermute x7 -> x8, waiting for transfers between devices: 14.4 us -> 9.08 us  [mate(): return lax.ppermute(rows, 'seq', mate_pairs)]
    select_n x2 -> x7, other arithmetic: 0.08 us -> 2.69 us  [the longest x4 2.6 us: lined(): jnp.where(within < counts[i], i, DEAD)]
    ppermute x7 -> x8, starting transfers between devices: 24.7 us -> 23.6 us  [mate(): return lax.ppermute(rows, 'seq', mate_pairs)]
    pallas_call x1, Pallas kernels: 0.71 us -> 1.48 us  [lined(): pl.pallas_call(audio_kernel, out_shape=(video_shape, audio_shape, audio_s...]
    unnamed x14 -> x12, local copies, waits for them, and re-layouts: 1.52 us -> 2.27 us
    ppermute x6, starting transfers between devices: 1.08 us -> 0.57 us  [cross(): return lax.ppermute(rows, ('seq', 'mp'), cross_pairs)]
    concatenate x2 -> x3, other arithmetic: 2.58 us -> 2.67 us  [the longest x1 1.3 us: by_block(): low = jnp.concatenate([own] + parts[2:])]
  transfers between devices with their start and end apart: 13 -> 14, of which waited for: 3 -> 4; matrix products, arithmetic and copies ran while one was open for 7% -> 13% of each run, Pallas kernels for 1% -> 3%
where the time goes in v2:
time: 47.1 us; the launch traced here: 46.8 us
  starting transfers between devices  24.2 us (51%)
  waiting for transfers between devices  9.09 us (19%)
  other arithmetic  5.46 us (12%)
  local copies, waits for them, and re-layouts  4.91 us (10%)
  Pallas kernels  2.33 us (5%)
  between operations  0.81 us (2%)
    ppermute x8, starting transfers between devices, mate(): return lax.ppermute(rows, 'seq', mate_pairs)  23.6 us
    ppermute x8, waiting for transfers between devices, mate(): return lax.ppermute(rows, 'seq', mate_pairs)  9.08 us
    select_n x4, other arithmetic, lined(): jnp.where(within < counts[i], i, DEAD)  2.6 us
    unnamed x12, local copies, waits for them, and re-layouts  2.27 us
    slice x8, local copies, waits for them, and re-layouts, lined(): sights.append(jnp.concatenate([video_k[:, cols], video_v[:, cols]], axis=0))  1.83 us
    pallas_call x1, Pallas kernels, lined(): pl.pallas_call(audio_kernel, out_shape=(video_shape, audio_shape, audio_s...  1.48 us
    concatenate x1, other arithmetic, by_block(): low = jnp.concatenate([own] + parts[2:])  1.3 us
    concatenate x1, other arithmetic, by_block(): high = jnp.concatenate([other] + parts[1::-1])  1.3 us
  transfers between devices with their start and end apart: 14, of which 4 were waited for; matrix products, arithmetic and copies ran while one was open for 13% of the time, Pallas kernels for 3%

profile of v2, /device:TPU:0, one launch (start us, length us, event | category | flops | bytes accessed | tf_op | source)
XLA Modules:
  0.0 46.8 jit_solution(4576706989222551232)
XLA Ops:
  0.6 0.0 copy-start.1
  0.6 0.9 %constant_dynamic-update-slice_fusion.3 = bf16[128,768]{1,0:T(8,128)(2,1)S(1)} fusion(bf16[64,768]{1,0:T(8,128)(2,1)} %param.12), kind=kLoop, calls=%fused_computation.5 | loop fusion | bytes 196608
  1.6 0.0 copy-done.1
  1.6 3.1 %collective-permute-start.1 = (bf16[128,768]{1,0:T(8,128)(2,1)S(1)}, bf16[128,768]{1,0:T(8,128)(2,1)S(1)}, u32[]{:S(2)}, u32[]{:S(2)}) collective-permute-start(bf16[128,768]{1,0:T(8,128)(2,1)S(1)} %constant_dynamic-update-slice_fusion.2.b0), channel_id=1, source_target_pairs={{0,4},{4,0},{8,12},{12,8},{1,5},{5,1},{9,13},{13,9},{2,6},{6,2},{1... | collective-permute-start | bytes 589832 | tf_op jit(solution)/shard_map/ppermute | solution.py:181
  4.7 0.0 collective-permute-start.2
  4.7 0.0 slice-start
  4.7 0.0 slice-start.2
  4.7 0.9 %slice-done = bf16[128,512]{1,0:T(8,128)(2,1)S(1)} async-done(((bf16[128,768]{1,0:T(8,128)(2,1)}), bf16[128,512]{1,0:T(8,128)(2,1)S(1)}, s32[]{:S(2)}) %slice-start) | async-done | bytes 131096 | tf_op jit(solution)/shard_map/slice | solution.py:208
  5.6 0.1 slice-done.2
  5.7 3.2 %collective-permute-start.5 = (bf16[256,512]{1,0:T(8,128)(2,1)S(1)}, bf16[256,512]{1,0:T(8,128)(2,1)S(1)}, u32[]{:S(2)}, u32[]{:S(2)}) collective-permute-start(bf16[256,512]{1,0:T(8,128)(2,1)S(1)} %pad_maximum_fusion.b0), channel_id=1, source_target_pairs={{0,4},{4,0},{8,12},{12,8},{1,5},{5,1},{9,13},{13,9},{2,6},{6,2},{1... | collective-permute-start | bytes 786440 | tf_op jit(solution)/shard_map/ppermute | solution.py:181
  8.9 0.0 collective-permute-start.6
  8.9 0.0 slice-start.1
  8.9 0.0 slice-start.3
  8.9 0.0 copy-start
  8.9 0.8 %slice-done.1 = bf16[128,256]{1,0:T(8,128)(2,1)S(1)} async-done(((bf16[128,768]{1,0:T(8,128)(2,1)}), bf16[128,256]{1,0:T(8,128)(2,1)S(1)}, s32[]{:S(2)}) %slice-start.1) | async-done | bytes 65560 | tf_op jit(solution)/shard_map/slice | solution.py:208
  9.8 0.0 slice-done.3
  9.8 0.5 %collective-permute-start.8 = (bf16[256,256]{1,0:T(8,128)(2,1)S(1)}, bf16[256,256]{1,0:T(8,128)(2,1)S(1)}, u32[]{:S(2)}, u32[]{:S(2)}) collective-permute-start(bf16[256,256]{1,0:T(8,128)(2,1)S(1)} %pad_maximum_fusion.1.b0), channel_id=1, source_target_pairs={{0,4},{4,0},{8,12},{12,8},{1,5},{5,1},{9,13},{13,9},{2,6},{6,2},{1... | collective-permute-start | bytes 393224 | tf_op jit(solution)/shard_map/ppermute | solution.py:181
  10.3 0.0 copy-start.3
  10.3 0.7 %copy-done.3 = s32[256]{0:T(256)S(1)} copy-done((s32[256]{0:T(256)S(1)}, s32[256]{0:T(256)}, u32[]{:S(2)}) %copy-start.3) | copy-done | bytes 1048
  11.0 0.1 fusion.6
  11.1 0.0 copy-done
  11.1 0.0 copy-start.4
  11.1 0.0 copy-start.2
  11.1 0.6 %copy-done.4 = s32[4]{0:T(128)S(1)} copy-done((s32[4]{0:T(128)S(1)}, s32[4]{0:T(128)}, u32[]{:S(2)}) %copy-start.4) | copy-done | bytes 40
  11.7 0.6 %fusion.7 = (s32[1]{0:T(128)}, s32[1]{0:T(128)}, s32[1]{0:T(128)}, s32[1]{0:T(128)}) fusion(s32[4]{0:T(128)S(1)} %copy-done.4), kind=kLoop, calls=%fused_computation.28 | loop fusion | bytes 32 | tf_op jit(solution)/shard_map/slice | solution.py:199
  12.3 0.6 %compare_select_fusion.2 = s32[128]{0:T(128)S(1)} fusion(s32[]{:T(128)} %bitcast.7), kind=kLoop, calls=%fused_computation.9 | loop fusion | flops 256 | bytes 516 | tf_op jit(solution)/shard_map/jit(_where)/select_n | solution.py:199
  13.0 1.3 %fusion.1 = (s32[1,128]{1,0:T(1,128)S(1)}, s32[1,128]{1,0:T(1,128)S(1)}) fusion(s32[]{:T(128)} %bitcast.6, s32[]{:T(128)} %bitcast.7), kind=kLoop, calls=%fused_computation.19 | loop fusion | flops 512 | bytes 1032 | tf_op jit(solution)/shard_map/concatenate | solution.py:192
  14.3 0.1 fusion.5
  14.4 0.1 add_select_fusion.2
  14.5 1.3 %fusion.3 = (s32[1,128]{1,0:T(1,128)S(1)}, s32[1,128]{1,0:T(1,128)S(1)}) fusion(s32[]{:T(128)} %bitcast.9, s32[]{:T(128)} %bitcast.11), kind=kLoop, calls=%fused_computation.21 | loop fusion | flops 512 | bytes 1032 | tf_op jit(solution)/shard_map/concatenate | solution.py:193
  15.8 0.7 %compare_select_fusion.3 = s32[128]{0:T(128)S(1)} fusion(s32[]{:T(128)} %bitcast.6), kind=kLoop, calls=%fused_computation.10 | loop fusion | flops 256 | bytes 516 | tf_op jit(solution)/shard_map/jit(_where)/select_n | solution.py:199
  16.4 0.7 %compare_select_fusion = s32[128]{0:T(128)S(1)} fusion(s32[]{:T(128)} %bitcast.11), kind=kLoop, calls=%fused_computation.7 | loop fusion | flops 256 | bytes 516 | tf_op jit(solution)/shard_map/jit(_where)/select_n | solution.py:199
  17.1 0.0 copy-done.2
  17.1 0.9 %collective-permute-done.8.b1 = bf16[256,256]{1,0:T(8,128)(2,1)S(1)} collective-permute-done((bf16[256,256]{1,0:T(8,128)(2,1)S(1)}, bf16[256,256]{1,0:T(8,128)(2,1)S(1)}, u32[]{:S(2)}, u32[]{:S(2)}) %collective-permute-start.8) | collective-permute-done | bytes 131104 | tf_op jit(solution)/shard_map/ppermute | solution.py:181
  18.0 1.7 %collective-permute-start = (bf16[192,768]{1,0:T(8,128)(2,1)S(1)}, bf16[192,768]{1,0:T(8,128)(2,1)S(1)}, u32[]{:S(2)}, u32[]{:S(2)}) collective-permute-start(bf16[192,768]{1,0:T(8,128)(2,1)S(1)} %constant_dynamic-update-slice_fusion.q_own), channel_id=1, source_target_pairs={{0,4},{4,0},{8,12},{12,8},{1,5},{5,1},{9,13},{13,9},{2,6},{6,2},{1... | collective-permute-start | bytes 884744 | tf_op jit(solution)/shard_map/ppermute | solution.py:181
  19.8 0.0 collective-permute-done.5.b1
  19.8 0.0 collective-permute-start.7
  19.8 0.6 %compare_select_fusion.1 = s32[128]{0:T(128)S(1)} fusion(s32[]{:T(128)} %bitcast.9), kind=kLoop, calls=%fused_computation.8 | loop fusion | flops 256 | bytes 516 | tf_op jit(solution)/shard_map/jit(_where)/select_n | solution.py:199
  20.5 0.0 collective-permute-done.2.inner2
  20.5 3.2 %collective-permute-start.3 = (bf16[128,768]{1,0:T(8,128)(2,1)S(1)}, bf16[128,768]{1,0:T(8,128)(2,1)S(1)}, u32[]{:S(2)}, u32[]{:S(2)}) collective-permute-start(bf16[128,768]{1,0:T(8,128)(2,1)S(1)} %collective-permute-done.2.inner2), channel_id=1, source_target_pairs={{0,4},{4,0},{8,12},{12,8},{1,5},{5,1},{9,13},{13,9},{2,6},{6,2},{1... | collective-permute-start | bytes 589832 | tf_op jit(solution)/shard_map/ppermute | solution.py:181
  23.7 0.0 collective-permute-done.1.b1
  23.7 0.0 collective-permute-start.4
  23.7 0.1 copy.12.off_ref
  23.8 0.0 collective-permute-done.6.b2
  23.8 0.6 %collective-permute-start.9 = (bf16[256,256]{1,0:T(8,128)(2,1)S(1)}, bf16[256,256]{1,0:T(8,128)(2,1)S(1)}, u32[]{:S(2)}, u32[]{:S(2)}) collective-permute-start(bf16[256,256]{1,0:T(8,128)(2,1)S(1)} %pad_maximum_fusion.1.b0), channel_id=1, source_target_pairs={{0,1},{1,0},{4,8},{5,9},{8,4},{9,5},{12,13},{13,12},{2,3},{3,2},{6... | collective-permute-start | bytes 393224 | tf_op jit(solution)/shard_map/ppermute | solution.py:184
  24.4 3.5 %collective-permute-done.q_mate = bf16[192,768]{1,0:T(8,128)(2,1)S(1)} collective-permute-done((bf16[192,768]{1,0:T(8,128)(2,1)S(1)}, bf16[192,768]{1,0:T(8,128)(2,1)S(1)}, u32[]{:S(2)}, u32[]{:S(2)}) %collective-permute-start) | collective-permute-done | bytes 294944 | tf_op jit(solution)/shard_map/ppermute | solution.py:181
  27.9 0.0 collective-permute-start.10
  27.9 0.0 collective-permute-done.7.b3
  27.9 6.7 %collective-permute-start.12 = (bf16[192,512]{1,0:T(8,128)(2,1)S(1)}, bf16[192,512]{1,0:T(8,128)(2,1)S(1)}, u32[]{:S(2)}, u32[]{:S(2)}) collective-permute-start(bf16[192,512]{1,0:T(8,128)(2,1)S(1)} %get-tuple-element.16), channel_id=1, source_target_pairs={{0,4},{4,0},{8,12},{12,8},{1,5},{5,1},{9,13},{13,9},{2,6},{6,2},{1... | collective-permute-start | bytes 589832 | tf_op jit(solution)/shard_map/ppermute | solution.py:181
  34.6 0.1 fusion.gap_ref
  34.7 0.0 collective-permute-done.9.b2
  34.7 0.0 collective-permute-done.10.b3
  34.7 5.1 %collective-permute-start.13 = (bf16[192,256]{1,0:T(8,128)(2,1)S(1)}, bf16[192,256]{1,0:T(8,128)(2,1)S(1)}, u32[]{:S(2)}, u32[]{:S(2)}) collective-permute-start(bf16[192,256]{1,0:T(8,128)(2,1)S(1)} %get-tuple-element.17), channel_id=1, source_target_pairs={{0,4},{4,0},{8,12},{12,8},{1,5},{5,1},{9,13},{13,9},{2,6},{6,2},{1... | collective-permute-start | bytes 294920 | tf_op jit(solution)/shard_map/ppermute | solution.py:181
  39.7 0.0 collective-permute-done.3.end2
  39.7 0.0 collective-permute-done.4.b3
  39.7 1.5 %audio_keys.1 = (bf16[128,768]{1,0:T(8,128)(2,1)S(1)}, bf16[64,768]{1,0:T(8,128)(2,1)S(1)}, bf16[64,768]{1,0:T(8,128)(2,1)S(1)}) custom-call(s32[1]{0:T(128)} %bitcast.role_ref, s32[1,256]{1,0:T(1,128)S(1)} %fusion.gap_ref, bf16[192,768]{1,0:T(8,128)(2,1)S(1)} %constant_dynamic-update-slice_fusion.q_own, bf16[192,768]{1,0:T(8,128)(2,1)S(1)} %collective-permute-done.q_mate, ...), custom_call_target="tpu_custom_call" | custom-call | flops 301989888 | bytes 1179648 | tf_op jit(solution)/shard_map/audio_keys/pallas_call | solution.py:238
  41.2 0.1 collective-permute-start.11
  41.3 1.6 %collective-permute-done.13.refs_5_ = bf16[192,256]{1,0:T(8,128)(2,1)S(1)} collective-permute-done((bf16[192,256]{1,0:T(8,128)(2,1)S(1)}, bf16[192,256]{1,0:T(8,128)(2,1)S(1)}, u32[]{:S(2)}, u32[]{:S(2)}) %collective-permute-start.13) | collective-permute-done | bytes 98336 | tf_op jit(solution)/shard_map/ppermute | solution.py:181
  42.9 3.0 %collective-permute-done.11.refs_3_ = bf16[64,768]{1,0:T(8,128)(2,1)S(1)} collective-permute-done((bf16[64,768]{1,0:T(8,128)(2,1)S(1)}, bf16[64,768]{1,0:T(8,128)(2,1)S(1)}, u32[]{:S(2)}, u32[]{:S(2)}) %collective-permute-start.11) | collective-permute-done | bytes 98336 | tf_op jit(solution)/shard_map/ppermute | solution.py:181
  45.9 0.0 collective-permute-done.12.refs_4_
  45.9 0.8 %place.1 = (bf16[128,768]{1,0:T(8,128)(2,1)}, bf16[128,768]{1,0:T(8,128)(2,1)}, bf16[64,768]{1,0:T(8,128)(2,1)}, bf16[64,768]{1,0:T(8,128)(2,1)}) custom-call(s32[1]{0:T(128)} %bitcast.role_ref, bf16[128,768]{1,0:T(8,128)(2,1)S(1)} %get-tuple-element.11.cross, bf16[64,768]{1,0:T(8,128)(2,1)S(1)} %get-tuple-element.12.refs_0_, ...), custom_call_target="tpu_custom_call" | custom-call | tf_op jit(solution)/shard_map/place/pallas_call | solution.py:249
  (10 shorter events, 0.1 us)
Async XLA Ops:
  0.6 0.9 %copy-start.1 = (bf16[64,768]{1,0:T(8,128)(2,1)S(1)}, bf16[64,768]{1,0:T(8,128)(2,1)}, u32[]{:S(2)}) copy-start(bf16[64,768]{1,0:T(8,128)(2,1)} %param.13) | copy-start | bytes 294916
  1.6 22.1 %collective-permute-start.1 = (bf16[128,768]{1,0:T(8,128)(2,1)S(1)}, bf16[128,768]{1,0:T(8,128)(2,1)S(1)}, u32[]{:S(2)}, u32[]{:S(2)}) collective-permute-start(bf16[128,768]{1,0:T(8,128)(2,1)S(1)} %constant_dynamic-update-slice_fusion.2.b0), channel_id=1, source_target_pairs={{0,4},{4,0},{8,12},{12,8},{1,5},{5,1},{9,13},{13,9},{2,6},{6,2},{1... | collective-permute-start | bytes 589832 | tf_op jit(solution)/shard_map/ppermute | solution.py:181
  4.7 15.8 %collective-permute-start.2 = (bf16[128,768]{1,0:T(8,128)(2,1)S(1)}, bf16[128,768]{1,0:T(8,128)(2,1)S(1)}, u32[]{:S(2)}, u32[]{:S(2)}) collective-permute-start(bf16[128,768]{1,0:T(8,128)(2,1)S(1)} %constant_dynamic-update-slice_fusion.2.b0), channel_id=1, source_target_pairs={{0,1},{1,0},{4,8},{5,9},{8,4},{9,5},{12,13},{13,12},{2,3},{3,2},{6... | collective-permute-start | bytes 589832 | tf_op jit(solution)/shard_map/ppermute | solution.py:184
  4.7 0.9 %slice-start = ((bf16[128,768]{1,0:T(8,128)(2,1)}), bf16[128,512]{1,0:T(8,128)(2,1)S(1)}, s32[]{:S(2)}) async-start(bf16[128,768]{1,0:T(8,128)(2,1)} %param.10), calls=%async_computation | async-start | bytes 262144 | tf_op jit(solution)/shard_map/slice | solution.py:208
  4.7 1.0 %slice-start.2 = ((bf16[128,768]{1,0:T(8,128)(2,1)}), bf16[128,512]{1,0:T(8,128)(2,1)S(1)}, s32[]{:S(2)}) async-start(bf16[128,768]{1,0:T(8,128)(2,1)} %param.9), calls=%async_computation.2 | async-start | bytes 262144 | tf_op jit(solution)/shard_map/slice | solution.py:208
  5.7 14.1 %collective-permute-start.5 = (bf16[256,512]{1,0:T(8,128)(2,1)S(1)}, bf16[256,512]{1,0:T(8,128)(2,1)S(1)}, u32[]{:S(2)}, u32[]{:S(2)}) collective-permute-start(bf16[256,512]{1,0:T(8,128)(2,1)S(1)} %pad_maximum_fusion.b0), channel_id=1, source_target_pairs={{0,4},{4,0},{8,12},{12,8},{1,5},{5,1},{9,13},{13,9},{2,6},{6,2},{1... | collective-permute-start | bytes 786440 | tf_op jit(solution)/shard_map/ppermute | solution.py:181
  8.9 14.9 %collective-permute-start.6 = (bf16[256,512]{1,0:T(8,128)(2,1)S(1)}, bf16[256,512]{1,0:T(8,128)(2,1)S(1)}, u32[]{:S(2)}, u32[]{:S(2)}) collective-permute-start(bf16[256,512]{1,0:T(8,128)(2,1)S(1)} %pad_maximum_fusion.b0), channel_id=1, source_target_pairs={{0,1},{1,0},{4,8},{5,9},{8,4},{9,5},{12,13},{13,12},{2,3},{3,2},{6... | collective-permute-start | bytes 786440 | tf_op jit(solution)/shard_map/ppermute | solution.py:184
  8.9 0.8 %slice-start.1 = ((bf16[128,768]{1,0:T(8,128)(2,1)}), bf16[128,256]{1,0:T(8,128)(2,1)S(1)}, s32[]{:S(2)}) async-start(bf16[128,768]{1,0:T(8,128)(2,1)} %param.10), calls=%async_computation.1 | async-start | bytes 131072 | tf_op jit(solution)/shard_map/slice | solution.py:208
  8.9 0.9 %slice-start.3 = ((bf16[128,768]{1,0:T(8,128)(2,1)}), bf16[128,256]{1,0:T(8,128)(2,1)S(1)}, s32[]{:S(2)}) async-start(bf16[128,768]{1,0:T(8,128)(2,1)} %param.9), calls=%async_computation.3 | async-start | bytes 131072 | tf_op jit(solution)/shard_map/slice | solution.py:208
  8.9 2.2 %copy-start = (bf16[128,768]{1,0:T(8,128)(2,1)S(1)}, bf16[128,768]{1,0:T(8,128)(2,1)}, u32[]{:S(2)}) copy-start(bf16[128,768]{1,0:T(8,128)(2,1)} %param.8) | copy-start | bytes 589828
  9.8 8.2 %collective-permute-start.8 = (bf16[256,256]{1,0:T(8,128)(2,1)S(1)}, bf16[256,256]{1,0:T(8,128)(2,1)S(1)}, u32[]{:S(2)}, u32[]{:S(2)}) collective-permute-start(bf16[256,256]{1,0:T(8,128)(2,1)S(1)} %pad_maximum_fusion.1.b0), channel_id=1, source_target_pairs={{0,4},{4,0},{8,12},{12,8},{1,5},{5,1},{9,13},{13,9},{2,6},{6,2},{1... | collective-permute-start | bytes 393224 | tf_op jit(solution)/shard_map/ppermute | solution.py:181
  10.3 0.7 %copy-start.3 = (s32[256]{0:T(256)S(1)}, s32[256]{0:T(256)}, u32[]{:S(2)}) copy-start(s32[256]{0:T(256)} %param.14) | copy-start | bytes 3076
  11.1 0.7 %copy-start.4 = (s32[4]{0:T(128)S(1)}, s32[4]{0:T(128)}, u32[]{:S(2)}) copy-start(s32[4]{0:T(128)} %param.15) | copy-start | bytes 52
  11.1 6.0 %copy-start.2 = (bf16[64,768]{1,0:T(8,128)(2,1)S(1)}, bf16[64,768]{1,0:T(8,128)(2,1)}, u32[]{:S(2)}) copy-start(bf16[64,768]{1,0:T(8,128)(2,1)} %param.11) | copy-start | bytes 294916
  18.0 9.9 %collective-permute-start = (bf16[192,768]{1,0:T(8,128)(2,1)S(1)}, bf16[192,768]{1,0:T(8,128)(2,1)S(1)}, u32[]{:S(2)}, u32[]{:S(2)}) collective-permute-start(bf16[192,768]{1,0:T(8,128)(2,1)S(1)} %constant_dynamic-update-slice_fusion.q_own), channel_id=1, source_target_pairs={{0,4},{4,0},{8,12},{12,8},{1,5},{5,1},{9,13},{13,9},{2,6},{6,2},{1... | collective-permute-start | bytes 884744 | tf_op jit(solution)/shard_map/ppermute | solution.py:181
  19.8 8.1 %collective-permute-start.7 = (bf16[256,512]{1,0:T(8,128)(2,1)S(1)}, bf16[256,512]{1,0:T(8,128)(2,1)S(1)}, u32[]{:S(2)}, u32[]{:S(2)}) collective-permute-start(bf16[256,512]{1,0:T(8,128)(2,1)S(1)} %collective-permute-done.5.b1), channel_id=1, source_target_pairs={{0,1},{1,0},{4,8},{5,9},{8,4},{9,5},{12,13},{13,12},{2,3},{3,2},{6... | collective-permute-start | bytes 786440 | tf_op jit(solution)/shard_map/ppermute | solution.py:184
  20.5 19.3 %collective-permute-start.3 = (bf16[128,768]{1,0:T(8,128)(2,1)S(1)}, bf16[128,768]{1,0:T(8,128)(2,1)S(1)}, u32[]{:S(2)}, u32[]{:S(2)}) collective-permute-start(bf16[128,768]{1,0:T(8,128)(2,1)S(1)} %collective-permute-done.2.inner2), channel_id=1, source_target_pairs={{0,4},{4,0},{8,12},{12,8},{1,5},{5,1},{9,13},{13,9},{2,6},{6,2},{1... | collective-permute-start | bytes 589832 | tf_op jit(solution)/shard_map/ppermute | solution.py:181
  23.7 16.1 %collective-permute-start.4 = (bf16[128,768]{1,0:T(8,128)(2,1)S(1)}, bf16[128,768]{1,0:T(8,128)(2,1)S(1)}, u32[]{:S(2)}, u32[]{:S(2)}) collective-permute-start(bf16[128,768]{1,0:T(8,128)(2,1)S(1)} %collective-permute-done.1.b1), channel_id=1, source_target_pairs={{0,1},{1,0},{4,8},{5,9},{8,4},{9,5},{12,13},{13,12},{2,3},{3,2},{6... | collective-permute-start | bytes 589832 | tf_op jit(solution)/shard_map/ppermute | solution.py:184
  23.8 10.8 %collective-permute-start.9 = (bf16[256,256]{1,0:T(8,128)(2,1)S(1)}, bf16[256,256]{1,0:T(8,128)(2,1)S(1)}, u32[]{:S(2)}, u32[]{:S(2)}) collective-permute-start(bf16[256,256]{1,0:T(8,128)(2,1)S(1)} %pad_maximum_fusion.1.b0), channel_id=1, source_target_pairs={{0,1},{1,0},{4,8},{5,9},{8,4},{9,5},{12,13},{13,12},{2,3},{3,2},{6... | collective-permute-start | bytes 393224 | tf_op jit(solution)/shard_map/ppermute | solution.py:184
  27.9 6.8 %collective-permute-start.10 = (bf16[256,256]{1,0:T(8,128)(2,1)S(1)}, bf16[256,256]{1,0:T(8,128)(2,1)S(1)}, u32[]{:S(2)}, u32[]{:S(2)}) collective-permute-start(bf16[256,256]{1,0:T(8,128)(2,1)S(1)} %collective-permute-done.8.b1), channel_id=1, source_target_pairs={{0,1},{1,0},{4,8},{5,9},{8,4},{9,5},{12,13},{13,12},{2,3},{3,2},{6... | collective-permute-start | bytes 393224 | tf_op jit(solution)/shard_map/ppermute | solution.py:184
  27.9 18.0 %collective-permute-start.12 = (bf16[192,512]{1,0:T(8,128)(2,1)S(1)}, bf16[192,512]{1,0:T(8,128)(2,1)S(1)}, u32[]{:S(2)}, u32[]{:S(2)}) collective-permute-start(bf16[192,512]{1,0:T(8,128)(2,1)S(1)} %get-tuple-element.16), channel_id=1, source_target_pairs={{0,4},{4,0},{8,12},{12,8},{1,5},{5,1},{9,13},{13,9},{2,6},{6,2},{1... | collective-permute-start | bytes 589832 | tf_op jit(solution)/shard_map/ppermute | solution.py:181
  34.7 8.2 %collective-permute-start.13 = (bf16[192,256]{1,0:T(8,128)(2,1)S(1)}, bf16[192,256]{1,0:T(8,128)(2,1)S(1)}, u32[]{:S(2)}, u32[]{:S(2)}) collective-permute-start(bf16[192,256]{1,0:T(8,128)(2,1)S(1)} %get-tuple-element.17), channel_id=1, source_target_pairs={{0,4},{4,0},{8,12},{12,8},{1,5},{5,1},{9,13},{13,9},{2,6},{6,2},{1... | collective-permute-start | bytes 294920 | tf_op jit(solution)/shard_map/ppermute | solution.py:181
  41.2 4.7 %collective-permute-start.11 = (bf16[64,768]{1,0:T(8,128)(2,1)S(1)}, bf16[64,768]{1,0:T(8,128)(2,1)S(1)}, u32[]{:S(2)}, u32[]{:S(2)}) collective-permute-start(bf16[64,768]{1,0:T(8,128)(2,1)S(1)} %get-tuple-element.15), channel_id=1, source_target_pairs={{0,4},{4,0},{8,12},{12,8},{1,5},{5,1},{9,13},{13,9},{2,6},{6,2},{1... | collective-permute-start | bytes 294920 | tf_op jit(solution)/shard_map/ppermute | solution.py:181

commit v3 on v2

--- a/solution.py
+++ b/solution.py
@@ -73,42 +73,76 @@
     return (mixed * (1.0 / total)).astype(jnp.bfloat16)
 
 
-def audio_kernel(role_ref, gap_ref, q_own, q_mate, b0, b1, inner2, end2, b3, cross_ref, own_ref, mate_ref):
+def frames_of(me, n):
+    mate, other = me ^ 1, jnp.where(me * 2 >= n, 0, n - 2)
+    inner = jnp.where(me * 2 >= n, 1, 0) + other
+    return me, mate, inner, jnp.where(me * 2 >= n, 0, 1) + other
+
+
+def pick(pieces, at):
+    chosen = pieces[0]
+    for i in range(1, len(pieces)):
+        chosen = jnp.where(at == i, pieces[i], chosen)
+    return chosen
+
+
+def offset_rows(offset_ref, audio_rows, frames):
+    n = offset_ref.shape[1] // audio_rows
+    pieces = [offset_ref[:, i * audio_rows : (i + 1) * audio_rows] for i in range(n)]
+    return [pick(pieces, frame) for frame in frames]
+
+
+def audio_kernel(me_ref, offset_ref, q_own, q_mate, b0, b1, inner2, end2, b3, cross_ref, own_ref, mate_ref):
     video_rows = cross_ref.shape[0]
     audio_rows = own_ref.shape[0]
-    reach = jnp.abs(gap_ref[...]) <= SPAN
+    n = offset_ref.shape[1] // audio_rows
+    me = me_ref[0]
+    at_end = (me == 0) | (me == n - 1)
+    key_offsets = offset_rows(offset_ref, audio_rows, frames_of(me, n))
 
     def run(blocks, alone):
+        offsets = jnp.concatenate(key_offsets[: len(blocks)], axis=1)
+        reach = jnp.abs(offsets - me) <= SPAN
         for head in range(q_own.shape[1] // HEAD_DIM):
             cols = slice(head * HEAD_DIM, (head + 1) * HEAD_DIM)
             keys = jnp.concatenate([b[:audio_rows, cols] for b in blocks], axis=0)
             values = jnp.concatenate([b[audio_rows:, cols] for b in blocks], axis=0)
-            span = slice(0, keys.shape[0])
-            cross_ref[:, cols] = blend(q_own[:video_rows, cols], keys, values, reach[:, span])
+            cross_ref[:, cols] = blend(q_own[:video_rows, cols], keys, values, reach)
             if not alone:
                 both = jnp.concatenate([q_own[video_rows:, cols], q_mate[video_rows:, cols]], axis=0)
                 out = blend(both, keys, values, None)
                 own_ref[:, cols] = out[:audio_rows]
                 mate_ref[:, cols] = out[audio_rows:]
 
-    @pl.when(role_ref[0] == 0)
+    @pl.when(jnp.logical_not(at_end))
     def _():
         run((b0, b1, inner2, b3), False)
 
-    @pl.when(role_ref[0] == 1)
+    @pl.when(at_end)
     def _():
         run((b0, b1, end2), True)
 
 
-def video_kernel(first, role_ref, frame_ref, off_ref, q_own, q_mate, b0, b1, b2, b3, own_ref, mate_ref):
+def video_kernel(first, me_ref, count_ref, offset_ref, q_own, q_mate, b0, b1, b2, b3, own_ref, mate_ref):
     video_rows = b0.shape[0] // 2
     audio_rows = q_own.shape[0] - video_rows
-
-    @pl.when(role_ref[0] == 0)
+    n = offset_ref.shape[1] // audio_rows
+    me = me_ref[0]
+
+    @pl.when((me > 0) & (me < n - 1))
     def _():
-        frames = frame_ref[...]
+        order = frames_of(me, n)
+        within = lax.broadcasted_iota(jnp.int32, (1, video_rows), 1)
+        tags = [jnp.where(within < count_ref[frame], frame, DEAD) for frame in order]
+        frames = jnp.concatenate(tags, axis=1)
         live = frames < DEAD
-        reach = jnp.abs(off_ref[...] - frames) <= SPAN
+        asking = jnp.concatenate(offset_rows(offset_ref, audio_rows, order[:2]), axis=1)
+        size = 2 * audio_rows
+        corner = lax.broadcasted_iota(jnp.int32, (size, size), 0) == lax.broadcasted_iota(
+            jnp.int32, (size, size), 1
+        )
+        asking = jnp.sum(jnp.where(corner, asking, 0), axis=1, keepdims=True)
+        reach = jnp.abs(asking - frames) <= SPAN
         for head in range(b0.shape[1] // HEAD_DIM):
             cols = slice(head * HEAD_DIM, (head + 1) * HEAD_DIM)
             q_cols = slice((first + head) * HEAD_DIM, (first + head + 1) * HEAD_DIM)
@@ -122,7 +156,7 @@
             mate_ref[video_rows:, cols] = out[audio_rows:]
 
 
-def place_kernel(video_rows, role_ref, cross, *refs):
+def place_kernel(n_frames, video_rows, me_ref, cross, *refs):
     n = (len(refs) - 5) // 2
     own, back = refs[:n], refs[n : 2 * n]
     video_self, video_cross, audio_self, audio_cross = refs[2 * n : 2 * n + 4]
@@ -138,9 +172,10 @@
             yield part.at[video_rows:], audio_cross.at[:, cols]
             at += part.shape[1]
 
-    for role, parts in ((0, own), (1, back)):
-
-        @pl.when(role_ref[0] == role)
+    at_end = (me_ref[0] == 0) | (me_ref[0] == n_frames - 1)
+    for role, parts in ((jnp.logical_not(at_end), own), (at_end, back)):
+
+        @pl.when(role)
         def _(parts=parts):
             moves = [
                 pltpu.make_async_copy(src, dst, sem.at[i])
@@ -183,23 +218,8 @@
     def cross(rows):
         return lax.ppermute(rows, ("seq", "mp"), cross_pairs)
 
-    role = jnp.where((me == 0) | (me == n - 1), 1, 0).astype(jnp.int32).reshape(1)
-    upper = me * 2 >= n
-
-    def by_block(parts):
-        own = jnp.where(me % 2 == 0, jnp.concatenate(parts[:2]), jnp.concatenate(parts[1::-1]))
-        other = jnp.where(me % 2 == 0, jnp.concatenate(parts[2:]), jnp.concatenate(parts[:1:-1]))
-        low = jnp.concatenate([own] + parts[2:])
-        high = jnp.concatenate([other] + parts[1::-1])
-        return jnp.where(upper, high, low)
-
-    key_offsets = by_block([offsets[i * audio_rows : (i + 1) * audio_rows] for i in range(n)])
-    gap = (key_offsets - me)[None, :]
-    within = jnp.arange(video_rows, dtype=jnp.int32)
-    frames = by_block([jnp.where(within < counts[i], i, DEAD) for i in range(n)])
-    frames = frames.astype(jnp.int32)[None, :]
-    row_offsets = key_offsets[: 2 * audio_rows, None]
-
+    place = me.astype(jnp.int32).reshape(1)
+    offsets = offsets.reshape(1, -1)
     sound = jnp.concatenate([audio_k, audio_v], axis=0)
     asks = jnp.concatenate([video_q, audio_q], axis=0)
     sights, at = [], 0
@@ -225,11 +245,11 @@
         own, theirs = pl.pallas_call(
             functools.partial(video_kernel, at),
             out_shape=(shape, shape),
-            in_specs=[SMEM] + [VMEM] * 8,
+            in_specs=[SMEM, SMEM] + [VMEM] * 7,
             out_specs=(VMEM, VMEM),
             cost_estimate=cost(2 * rows, n * video_rows, size),
             compiler_params=PARAMS,
-        )(role, frames, row_offsets, asks, asks_mate, sights[i], sight_mate[i], sight_across[i], sight_far[i])
+        )(place, counts, offsets, asks, asks_mate, sights[i], sight_mate[i], sight_across[i], sight_far[i])
         mine.append(own)
         back.append(mate(theirs))
         at += size
@@ -243,18 +263,18 @@
         cost_estimate=cost(2 * rows, n * audio_rows, heads),
         compiler_params=PARAMS,
         name="audio_keys",
-    )(role, gap, asks, asks_mate, sound, sound_mate, sound_across, sound_passed, sound_far)
+    )(place, offsets, asks, asks_mate, sound, sound_mate, sound_across, sound_passed, sound_far)
     mine = [own] + mine
     back = [mate(theirs)] + back
     return pl.pallas_call(
-        functools.partial(place_kernel, video_rows),
+        functools.partial(place_kernel, n, video_rows),
         out_shape=(video_shape, video_shape, audio_shape, audio_shape),
         in_specs=[SMEM] + [VMEM] * (1 + 2 * len(mine)),
         out_specs=(ANY,) * 4,
         scratch_shapes=[pltpu.SemaphoreType.DMA((2 * len(mine),))],
         compiler_params=PARAMS,
         name="place",
-    )(role, video_cross, *mine, *back)
+    )(place, video_cross, *mine, *back)
 
 
 def solution(mesh):

time: 47.1 us -> 50 us (1.062)
  waiting for transfers between devices: 9.09 us -> 17.3 us
  other arithmetic: 5.46 us -> 0.03 us
  local copies, waits for them, and re-layouts: 4.91 us -> 3.38 us
  Pallas kernels: 2.33 us -> 3.63 us
  starting transfers between devices: 24.2 us -> 24.7 us
    ppermute x8, waiting for transfers between devices: 9.08 us -> 17.3 us  [mate(): return lax.ppermute(rows, 'seq', mate_pairs)]
    select_n x7 -> x0, other arithmetic: 2.69 us -> none  [the longest x4 2.6 us: lined(): jnp.where(within < counts[i], i, DEAD)]
    concatenate x3 -> x0, other arithmetic: 2.67 us -> none  [the longest x1 1.3 us: by_block(): low = jnp.concatenate([own] + parts[2:])]
    pallas_call x2, Pallas kernels: 0.01 us -> 1.09 us  [lined(): pl.pallas_call(functools.partial(video_kernel, at), out_shape=(shape, sha...]
    unnamed x12 -> x14, local copies, waits for them, and re-layouts: 2.27 us -> 1.54 us
    slice x2 -> x0, local copies, waits for them, and re-layouts: 0.67 us -> none  [the longest x1 0.6 us: lined(): counts[i]]
  transfers between devices with their start and end apart: 14 -> 14, of which waited for: 4 -> 4; matrix products, arithmetic and copies ran while one was open for 13% -> 0% of each run, Pallas kernels for 3% -> 6%
where the time goes in v3:
time: 50 us; the launch traced here: 49.8 us
  starting transfers between devices  24.7 us (49%)
  waiting for transfers between devices  17.3 us (35%)
  Pallas kernels  3.63 us (7%)
  local copies, waits for them, and re-layouts  3.38 us (7%)
  between operations  0.75 us (2%)
    ppermute x8, starting transfers between devices, mate(): return lax.ppermute(rows, 'seq', mate_pairs)  24.1 us
    ppermute x8, waiting for transfers between devices, mate(): return lax.ppermute(rows, 'seq', mate_pairs)  17.3 us
    slice x8, local copies, waits for them, and re-layouts, lined(): sights.append(jnp.concatenate([video_k[:, cols], video_v[:, cols]], axis=0))  1.83 us
    pallas_call x1, Pallas kernels, lined(): pl.pallas_call(audio_kernel, out_shape=(video_shape, audio_shape, audio_s...  1.69 us
    unnamed x14, local copies, waits for them, and re-layouts  1.54 us
    pallas_call x2, Pallas kernels, lined(): pl.pallas_call(functools.partial(video_kernel, at), out_shape=(shape, sha...  1.09 us
  transfers between devices with their start and end apart: 14, of which 4 were waited for; matrix products, arithmetic and copies ran while one was open for 0% of the time, Pallas kernels for 6%

profile of v3, /device:TPU:0, one launch (start us, length us, event | category | flops | bytes accessed | tf_op | source)
XLA Modules:
  0.0 49.8 jit_solution(12170795837907013913)
XLA Ops:
  0.6 0.0 slice-start
  0.6 0.0 slice-start.2
  0.7 0.9 %slice-done = bf16[128,512]{1,0:T(8,128)(2,1)S(1)} async-done(((bf16[128,768]{1,0:T(8,128)(2,1)}), bf16[128,512]{1,0:T(8,128)(2,1)S(1)}, s32[]{:S(2)}) %slice-start) | async-done | bytes 131096 | tf_op jit(solution)/shard_map/slice | solution.py:228
  1.5 0.1 slice-done.2
  1.6 0.0 copy-start.2
  1.6 0.0 copy-start.3
  1.6 3.1 %collective-permute-start.5 = (bf16[256,512]{1,0:T(8,128)(2,1)S(1)}, bf16[256,512]{1,0:T(8,128)(2,1)S(1)}, u32[]{:S(2)}, u32[]{:S(2)}) collective-permute-start(bf16[256,512]{1,0:T(8,128)(2,1)S(1)} %pad_maximum_fusion.b0), channel_id=1, source_target_pairs={{0,4},{4,0},{8,12},{12,8},{1,5},{5,1},{9,13},{13,9},{2,6},{6,2},{1... | collective-permute-start | bytes 786440 | tf_op jit(solution)/shard_map/ppermute | solution.py:216
  4.8 0.0 collective-permute-start.6
  4.8 0.0 copy-done.2
  4.8 0.0 copy-done.3
  4.8 3.2 %collective-permute-start = (bf16[192,768]{1,0:T(8,128)(2,1)S(1)}, bf16[192,768]{1,0:T(8,128)(2,1)S(1)}, u32[]{:S(2)}, u32[]{:S(2)}) collective-permute-start(bf16[192,768]{1,0:T(8,128)(2,1)S(1)} %constant_dynamic-update-slice_fusion.q_own), channel_id=1, source_target_pairs={{0,4},{4,0},{8,12},{12,8},{1,5},{5,1},{9,13},{13,9},{2,6},{6,2},{1... | collective-permute-start | bytes 884744 | tf_op jit(solution)/shard_map/ppermute | solution.py:216
  8.0 0.0 slice-start.1
  8.0 0.0 slice-start.3
  8.0 0.8 %slice-done.1 = bf16[128,256]{1,0:T(8,128)(2,1)S(1)} async-done(((bf16[128,768]{1,0:T(8,128)(2,1)}), bf16[128,256]{1,0:T(8,128)(2,1)S(1)}, s32[]{:S(2)}) %slice-start.1) | async-done | bytes 65560 | tf_op jit(solution)/shard_map/slice | solution.py:228
  8.9 0.0 slice-done.3
  8.9 0.0 copy-start.4
  8.9 0.0 copy-start.5
  8.9 0.1 collective-permute-start.8
  9.0 0.8 %copy-done.4 = bf16[64,768]{1,0:T(8,128)(2,1)S(1)} copy-done((bf16[64,768]{1,0:T(8,128)(2,1)S(1)}, bf16[64,768]{1,0:T(8,128)(2,1)}, u32[]{:S(2)}) %copy-start.4) | copy-done | bytes 98328
  9.8 0.0 copy-done.5
  9.8 0.1 collective-permute-start.2
  9.9 10.3 %collective-permute-done.8.b1 = bf16[256,256]{1,0:T(8,128)(2,1)S(1)} collective-permute-done((bf16[256,256]{1,0:T(8,128)(2,1)S(1)}, bf16[256,256]{1,0:T(8,128)(2,1)S(1)}, u32[]{:S(2)}, u32[]{:S(2)}) %collective-permute-start.8) | collective-permute-done | bytes 131104 | tf_op jit(solution)/shard_map/ppermute | solution.py:216
  20.2 1.7 %collective-permute-start.1 = (bf16[128,768]{1,0:T(8,128)(2,1)S(1)}, bf16[128,768]{1,0:T(8,128)(2,1)S(1)}, u32[]{:S(2)}, u32[]{:S(2)}) collective-permute-start(bf16[128,768]{1,0:T(8,128)(2,1)S(1)} %constant_dynamic-update-slice_fusion.2.b0), channel_id=1, source_target_pairs={{0,4},{4,0},{8,12},{12,8},{1,5},{5,1},{9,13},{13,9},{2,6},{6,2},{1... | collective-permute-start | bytes 589832 | tf_op jit(solution)/shard_map/ppermute | solution.py:216
  21.9 0.0 collective-permute-done.5.b1
  21.9 0.0 collective-permute-start.7
  21.9 0.0 collective-permute-done.2.inner2
  21.9 3.1 %collective-permute-start.3 = (bf16[128,768]{1,0:T(8,128)(2,1)S(1)}, bf16[128,768]{1,0:T(8,128)(2,1)S(1)}, u32[]{:S(2)}, u32[]{:S(2)}) collective-permute-start(bf16[128,768]{1,0:T(8,128)(2,1)S(1)} %collective-permute-done.2.inner2), channel_id=1, source_target_pairs={{0,4},{4,0},{8,12},{12,8},{1,5},{5,1},{9,13},{13,9},{2,6},{6,2},{1... | collective-permute-start | bytes 589832 | tf_op jit(solution)/shard_map/ppermute | solution.py:216
  25.1 2.4 %collective-permute-done.1.b1 = bf16[128,768]{1,0:T(8,128)(2,1)S(1)} collective-permute-done((bf16[128,768]{1,0:T(8,128)(2,1)S(1)}, bf16[128,768]{1,0:T(8,128)(2,1)S(1)}, u32[]{:S(2)}, u32[]{:S(2)}) %collective-permute-start.1) | collective-permute-done | bytes 196640 | tf_op jit(solution)/shard_map/ppermute | solution.py:216
  27.5 0.0 collective-permute-start.4
  27.5 0.0 collective-permute-done.6.b2
  27.5 0.5 %collective-permute-start.9 = (bf16[256,256]{1,0:T(8,128)(2,1)S(1)}, bf16[256,256]{1,0:T(8,128)(2,1)S(1)}, u32[]{:S(2)}, u32[]{:S(2)}) collective-permute-start(bf16[256,256]{1,0:T(8,128)(2,1)S(1)} %pad_maximum_fusion.1.b0), channel_id=1, source_target_pairs={{0,1},{1,0},{4,8},{5,9},{8,4},{9,5},{12,13},{13,12},{2,3},{3,2},{6... | collective-permute-start | bytes 393224 | tf_op jit(solution)/shard_map/ppermute | solution.py:219
  28.0 0.0 collective-permute-done.q_mate
  28.0 0.1 collective-permute-start.10
  28.1 0.0 collective-permute-done.7.b3
  28.1 0.0 copy-start
  28.1 0.0 copy-start.1
  28.1 0.7 %copy-done = s32[256]{0:T(256)S(1)} copy-done((s32[256]{0:T(256)S(1)}, s32[256]{0:T(256)}, u32[]{:S(2)}) %copy-start) | copy-done | bytes 1048
  28.7 0.0 copy-done.1
  28.7 0.5 %shard_map.111 = (bf16[192,512]{1,0:T(8,128)(2,1)S(1)}, bf16[192,512]{1,0:T(8,128)(2,1)S(1)}) custom-call(s32[1]{0:T(128)} %bitcast.me_ref, s32[4]{0:T(128)S(1)} %copy-done.1, s32[1,256]{1,0:T(1,128)S(1)} %bitcast.2, bf16[192,768]{1,0:T(8,128)(2,1)S(1)} %constant_dynamic-update-slice_fusion.q_own, bf16[192,768]{1,0:T(8,128)(2,1)S(1)} %collective-permute-done.q_mate, ...), custom_call_target="tpu_custom_call" | custom-call | flops 402653184 | bytes 786432 | tf_op jit(solution)/shard_map/pallas_call | solution.py:245
  29.3 8.8 %collective-permute-start.12 = (bf16[192,512]{1,0:T(8,128)(2,1)S(1)}, bf16[192,512]{1,0:T(8,128)(2,1)S(1)}, u32[]{:S(2)}, u32[]{:S(2)}) collective-permute-start(bf16[192,512]{1,0:T(8,128)(2,1)S(1)} %get-tuple-element.16), channel_id=1, source_target_pairs={{0,4},{4,0},{8,12},{12,8},{1,5},{5,1},{9,13},{13,9},{2,6},{6,2},{1... | collective-permute-start | bytes 589832 | tf_op jit(solution)/shard_map/ppermute | solution.py:216
  38.1 0.0 collective-permute-done.9.b2
  38.1 0.0 collective-permute-done.10.b3
  38.1 0.5 %shard_map.112 = (bf16[192,256]{1,0:T(8,128)(2,1)S(1)}, bf16[192,256]{1,0:T(8,128)(2,1)S(1)}) custom-call(s32[1]{0:T(128)} %bitcast.me_ref, s32[4]{0:T(128)S(1)} %copy-done.1, s32[1,256]{1,0:T(1,128)S(1)} %bitcast.3, bf16[192,768]{1,0:T(8,128)(2,1)S(1)} %constant_dynamic-update-slice_fusion.q_own, bf16[192,768]{1,0:T(8,128)(2,1)S(1)} %collective-permute-done.q_mate, ...), custom_call_target="tpu_custom_call" | custom-call | flops 201326592 | bytes 393216 | tf_op jit(solution)/shard_map/pallas_call | solution.py:245
  38.6 3.9 %collective-permute-start.13 = (bf16[192,256]{1,0:T(8,128)(2,1)S(1)}, bf16[192,256]{1,0:T(8,128)(2,1)S(1)}, u32[]{:S(2)}, u32[]{:S(2)}) collective-permute-start(bf16[192,256]{1,0:T(8,128)(2,1)S(1)} %get-tuple-element.17), channel_id=1, source_target_pairs={{0,4},{4,0},{8,12},{12,8},{1,5},{5,1},{9,13},{13,9},{2,6},{6,2},{1... | collective-permute-start | bytes 294920 | tf_op jit(solution)/shard_map/ppermute | solution.py:216
  42.6 0.0 collective-permute-done.3.end2
  42.6 0.0 collective-permute-done.4.b3
  42.6 1.7 %audio_keys.1 = (bf16[128,768]{1,0:T(8,128)(2,1)S(1)}, bf16[64,768]{1,0:T(8,128)(2,1)S(1)}, bf16[64,768]{1,0:T(8,128)(2,1)S(1)}) custom-call(s32[1]{0:T(128)} %bitcast.me_ref, s32[1,256]{1,0:T(1,128)S(1)} %bitcast.4, bf16[192,768]{1,0:T(8,128)(2,1)S(1)} %constant_dynamic-update-slice_fusion.q_own, bf16[192,768]{1,0:T(8,128)(2,1)S(1)} %collective-permute-done.q_mate, ...), custom_call_target="tpu_custom_call" | custom-call | flops 301989888 | bytes 1179648 | tf_op jit(solution)/shard_map/audio_keys/pallas_call | solution.py:258
  44.3 0.1 collective-permute-start.11
  44.3 1.8 %collective-permute-done.13.refs_5_ = bf16[192,256]{1,0:T(8,128)(2,1)S(1)} collective-permute-done((bf16[192,256]{1,0:T(8,128)(2,1)S(1)}, bf16[192,256]{1,0:T(8,128)(2,1)S(1)}, u32[]{:S(2)}, u32[]{:S(2)}) %collective-permute-start.13) | collective-permute-done | bytes 98336 | tf_op jit(solution)/shard_map/ppermute | solution.py:216
  46.2 2.8 %collective-permute-done.11.refs_3_ = bf16[64,768]{1,0:T(8,128)(2,1)S(1)} collective-permute-done((bf16[64,768]{1,0:T(8,128)(2,1)S(1)}, bf16[64,768]{1,0:T(8,128)(2,1)S(1)}, u32[]{:S(2)}, u32[]{:S(2)}) %collective-permute-start.11) | collective-permute-done | bytes 98336 | tf_op jit(solution)/shard_map/ppermute | solution.py:216
  49.0 0.0 collective-permute-done.12.refs_4_
  49.0 0.8 %place.1 = (bf16[128,768]{1,0:T(8,128)(2,1)}, bf16[128,768]{1,0:T(8,128)(2,1)}, bf16[64,768]{1,0:T(8,128)(2,1)}, bf16[64,768]{1,0:T(8,128)(2,1)}) custom-call(s32[1]{0:T(128)} %bitcast.me_ref, bf16[128,768]{1,0:T(8,128)(2,1)S(1)} %get-tuple-element.11.cross, bf16[64,768]{1,0:T(8,128)(2,1)S(1)} %get-tuple-element.12.refs_0_, ...), custom_call_target="tpu_custom_call" | custom-call | tf_op jit(solution)/shard_map/place/pallas_call | solution.py:269
  (6 shorter events, 0.1 us)
Async XLA Ops:
  0.6 0.9 %slice-start = ((bf16[128,768]{1,0:T(8,128)(2,1)}), bf16[128,512]{1,0:T(8,128)(2,1)S(1)}, s32[]{:S(2)}) async-start(bf16[128,768]{1,0:T(8,128)(2,1)} %param.9), calls=%async_computation | async-start | bytes 262144 | tf_op jit(solution)/shard_map/slice | solution.py:228
  0.6 1.0 %slice-start.2 = ((bf16[128,768]{1,0:T(8,128)(2,1)}), bf16[128,512]{1,0:T(8,128)(2,1)S(1)}, s32[]{:S(2)}) async-start(bf16[128,768]{1,0:T(8,128)(2,1)} %param.10), calls=%async_computation.2 | async-start | bytes 262144 | tf_op jit(solution)/shard_map/slice | solution.py:228
  1.6 3.2 %copy-start.2 = (bf16[128,768]{1,0:T(8,128)(2,1)S(1)}, bf16[128,768]{1,0:T(8,128)(2,1)}, u32[]{:S(2)}) copy-start(bf16[128,768]{1,0:T(8,128)(2,1)} %param.8) | copy-start | bytes 589828
  1.6 3.2 %copy-start.3 = (bf16[64,768]{1,0:T(8,128)(2,1)S(1)}, bf16[64,768]{1,0:T(8,128)(2,1)}, u32[]{:S(2)}) copy-start(bf16[64,768]{1,0:T(8,128)(2,1)} %param.11) | copy-start | bytes 294916
  1.6 20.3 %collective-permute-start.5 = (bf16[256,512]{1,0:T(8,128)(2,1)S(1)}, bf16[256,512]{1,0:T(8,128)(2,1)S(1)}, u32[]{:S(2)}, u32[]{:S(2)}) collective-permute-start(bf16[256,512]{1,0:T(8,128)(2,1)S(1)} %pad_maximum_fusion.b0), channel_id=1, source_target_pairs={{0,4},{4,0},{8,12},{12,8},{1,5},{5,1},{9,13},{13,9},{2,6},{6,2},{1... | collective-permute-start | bytes 786440 | tf_op jit(solution)/shard_map/ppermute | solution.py:216
  4.8 22.7 %collective-permute-start.6 = (bf16[256,512]{1,0:T(8,128)(2,1)S(1)}, bf16[256,512]{1,0:T(8,128)(2,1)S(1)}, u32[]{:S(2)}, u32[]{:S(2)}) collective-permute-start(bf16[256,512]{1,0:T(8,128)(2,1)S(1)} %pad_maximum_fusion.b0), channel_id=1, source_target_pairs={{0,1},{1,0},{4,8},{5,9},{8,4},{9,5},{12,13},{13,12},{2,3},{3,2},{6... | collective-permute-start | bytes 786440 | tf_op jit(solution)/shard_map/ppermute | solution.py:219
  4.8 23.2 %collective-permute-start = (bf16[192,768]{1,0:T(8,128)(2,1)S(1)}, bf16[192,768]{1,0:T(8,128)(2,1)S(1)}, u32[]{:S(2)}, u32[]{:S(2)}) collective-permute-start(bf16[192,768]{1,0:T(8,128)(2,1)S(1)} %constant_dynamic-update-slice_fusion.q_own), channel_id=1, source_target_pairs={{0,4},{4,0},{8,12},{12,8},{1,5},{5,1},{9,13},{13,9},{2,6},{6,2},{1... | collective-permute-start | bytes 884744 | tf_op jit(solution)/shard_map/ppermute | solution.py:216
  8.0 0.8 %slice-start.1 = ((bf16[128,768]{1,0:T(8,128)(2,1)}), bf16[128,256]{1,0:T(8,128)(2,1)S(1)}, s32[]{:S(2)}) async-start(bf16[128,768]{1,0:T(8,128)(2,1)} %param.9), calls=%async_computation.1 | async-start | bytes 131072 | tf_op jit(solution)/shard_map/slice | solution.py:228
  8.0 0.9 %slice-start.3 = ((bf16[128,768]{1,0:T(8,128)(2,1)}), bf16[128,256]{1,0:T(8,128)(2,1)S(1)}, s32[]{:S(2)}) async-start(bf16[128,768]{1,0:T(8,128)(2,1)} %param.10), calls=%async_computation.3 | async-start | bytes 131072 | tf_op jit(solution)/shard_map/slice | solution.py:228
  8.9 0.9 %copy-start.4 = (bf16[64,768]{1,0:T(8,128)(2,1)S(1)}, bf16[64,768]{1,0:T(8,128)(2,1)}, u32[]{:S(2)}) copy-start(bf16[64,768]{1,0:T(8,128)(2,1)} %param.12) | copy-start | bytes 294916
  8.9 0.9 %copy-start.5 = (bf16[64,768]{1,0:T(8,128)(2,1)S(1)}, bf16[64,768]{1,0:T(8,128)(2,1)}, u32[]{:S(2)}) copy-start(bf16[64,768]{1,0:T(8,128)(2,1)} %param.13) | copy-start | bytes 294916
  8.9 11.3 %collective-permute-start.8 = (bf16[256,256]{1,0:T(8,128)(2,1)S(1)}, bf16[256,256]{1,0:T(8,128)(2,1)S(1)}, u32[]{:S(2)}, u32[]{:S(2)}) collective-permute-start(bf16[256,256]{1,0:T(8,128)(2,1)S(1)} %pad_maximum_fusion.1.b0), channel_id=1, source_target_pairs={{0,4},{4,0},{8,12},{12,8},{1,5},{5,1},{9,13},{13,9},{2,6},{6,2},{1... | collective-permute-start | bytes 393224 | tf_op jit(solution)/shard_map/ppermute | solution.py:216
  9.8 12.1 %collective-permute-start.2 = (bf16[128,768]{1,0:T(8,128)(2,1)S(1)}, bf16[128,768]{1,0:T(8,128)(2,1)S(1)}, u32[]{:S(2)}, u32[]{:S(2)}) collective-permute-start(bf16[128,768]{1,0:T(8,128)(2,1)S(1)} %constant_dynamic-update-slice_fusion.2.b0), channel_id=1, source_target_pairs={{0,1},{1,0},{4,8},{5,9},{8,4},{9,5},{12,13},{13,12},{2,3},{3,2},{6... | collective-permute-start | bytes 589832 | tf_op jit(solution)/shard_map/ppermute | solution.py:219
  20.2 7.3 %collective-permute-start.1 = (bf16[128,768]{1,0:T(8,128)(2,1)S(1)}, bf16[128,768]{1,0:T(8,128)(2,1)S(1)}, u32[]{:S(2)}, u32[]{:S(2)}) collective-permute-start(bf16[128,768]{1,0:T(8,128)(2,1)S(1)} %constant_dynamic-update-slice_fusion.2.b0), channel_id=1, source_target_pairs={{0,4},{4,0},{8,12},{12,8},{1,5},{5,1},{9,13},{13,9},{2,6},{6,2},{1... | collective-permute-start | bytes 589832 | tf_op jit(solution)/shard_map/ppermute | solution.py:216
  21.9 6.1 %collective-permute-start.7 = (bf16[256,512]{1,0:T(8,128)(2,1)S(1)}, bf16[256,512]{1,0:T(8,128)(2,1)S(1)}, u32[]{:S(2)}, u32[]{:S(2)}) collective-permute-start(bf16[256,512]{1,0:T(8,128)(2,1)S(1)} %collective-permute-done.5.b1), channel_id=1, source_target_pairs={{0,1},{1,0},{4,8},{5,9},{8,4},{9,5},{12,13},{13,12},{2,3},{3,2},{6... | collective-permute-start | bytes 786440 | tf_op jit(solution)/shard_map/ppermute | solution.py:219
  21.9 20.6 %collective-permute-start.3 = (bf16[128,768]{1,0:T(8,128)(2,1)S(1)}, bf16[128,768]{1,0:T(8,128)(2,1)S(1)}, u32[]{:S(2)}, u32[]{:S(2)}) collective-permute-start(bf16[128,768]{1,0:T(8,128)(2,1)S(1)} %collective-permute-done.2.inner2), channel_id=1, source_target_pairs={{0,4},{4,0},{8,12},{12,8},{1,5},{5,1},{9,13},{13,9},{2,6},{6,2},{1... | collective-permute-start | bytes 589832 | tf_op jit(solution)/shard_map/ppermute | solution.py:216
  27.5 15.1 %collective-permute-start.4 = (bf16[128,768]{1,0:T(8,128)(2,1)S(1)}, bf16[128,768]{1,0:T(8,128)(2,1)S(1)}, u32[]{:S(2)}, u32[]{:S(2)}) collective-permute-start(bf16[128,768]{1,0:T(8,128)(2,1)S(1)} %collective-permute-done.1.b1), channel_id=1, source_target_pairs={{0,1},{1,0},{4,8},{5,9},{8,4},{9,5},{12,13},{13,12},{2,3},{3,2},{6... | collective-permute-start | bytes 589832 | tf_op jit(solution)/shard_map/ppermute | solution.py:219
  27.5 10.6 %collective-permute-start.9 = (bf16[256,256]{1,0:T(8,128)(2,1)S(1)}, bf16[256,256]{1,0:T(8,128)(2,1)S(1)}, u32[]{:S(2)}, u32[]{:S(2)}) collective-permute-start(bf16[256,256]{1,0:T(8,128)(2,1)S(1)} %pad_maximum_fusion.1.b0), channel_id=1, source_target_pairs={{0,1},{1,0},{4,8},{5,9},{8,4},{9,5},{12,13},{13,12},{2,3},{3,2},{6... | collective-permute-start | bytes 393224 | tf_op jit(solution)/shard_map/ppermute | solution.py:219
  28.0 10.1 %collective-permute-start.10 = (bf16[256,256]{1,0:T(8,128)(2,1)S(1)}, bf16[256,256]{1,0:T(8,128)(2,1)S(1)}, u32[]{:S(2)}, u32[]{:S(2)}) collective-permute-start(bf16[256,256]{1,0:T(8,128)(2,1)S(1)} %collective-permute-done.8.b1), channel_id=1, source_target_pairs={{0,1},{1,0},{4,8},{5,9},{8,4},{9,5},{12,13},{13,12},{2,3},{3,2},{6... | collective-permute-start | bytes 393224 | tf_op jit(solution)/shard_map/ppermute | solution.py:219
  28.1 0.7 %copy-start = (s32[256]{0:T(256)S(1)}, s32[256]{0:T(256)}, u32[]{:S(2)}) copy-start(s32[256]{0:T(256)} %param.14) | copy-start | bytes 3076
  28.1 0.7 %copy-start.1 = (s32[4]{0:T(128)S(1)}, s32[4]{0:T(128)}, u32[]{:S(2)}) copy-start(s32[4]{0:T(128)} %count_ref.3) | copy-start | bytes 52
  29.3 19.7 %collective-permute-start.12 = (bf16[192,512]{1,0:T(8,128)(2,1)S(1)}, bf16[192,512]{1,0:T(8,128)(2,1)S(1)}, u32[]{:S(2)}, u32[]{:S(2)}) collective-permute-start(bf16[192,512]{1,0:T(8,128)(2,1)S(1)} %get-tuple-element.16), channel_id=1, source_target_pairs={{0,4},{4,0},{8,12},{12,8},{1,5},{5,1},{9,13},{13,9},{2,6},{6,2},{1... | collective-permute-start | bytes 589832 | tf_op jit(solution)/shard_map/ppermute | solution.py:216
  38.6 7.6 %collective-permute-start.13 = (bf16[192,256]{1,0:T(8,128)(2,1)S(1)}, bf16[192,256]{1,0:T(8,128)(2,1)S(1)}, u32[]{:S(2)}, u32[]{:S(2)}) collective-permute-start(bf16[192,256]{1,0:T(8,128)(2,1)S(1)} %get-tuple-element.17), channel_id=1, source_target_pairs={{0,4},{4,0},{8,12},{12,8},{1,5},{5,1},{9,13},{13,9},{2,6},{6,2},{1... | collective-permute-start | bytes 294920 | tf_op jit(solution)/shard_map/ppermute | solution.py:216
  44.3 4.7 %collective-permute-start.11 = (bf16[64,768]{1,0:T(8,128)(2,1)S(1)}, bf16[64,768]{1,0:T(8,128)(2,1)S(1)}, u32[]{:S(2)}, u32[]{:S(2)}) collective-permute-start(bf16[64,768]{1,0:T(8,128)(2,1)S(1)} %get-tuple-element.15), channel_id=1, source_target_pairs={{0,4},{4,0},{8,12},{12,8},{1,5},{5,1},{9,13},{13,9},{2,6},{6,2},{1... | collective-permute-start | bytes 294920 | tf_op jit(solution)/shard_map/ppermute | solution.py:216

commit v4 on v3

v4 whole, which is shorter than its diff:
```python
import functools

import jax
import jax.numpy as jnp
from jax import lax
from jax.experimental import pallas as pl
from jax.experimental.pallas import tpu as pltpu
from jax.sharding import PartitionSpec as P


HEAD_DIM = 128
SPAN = 1
MASKED = -1e30
LOG2E = 1.4426950408889634
VMEM = pl.BlockSpec(memory_space=pltpu.VMEM)
SMEM = pl.BlockSpec(memory_space=pltpu.SMEM)
ANY = pl.BlockSpec(memory_space=pl.ANY)
PARAMS = pltpu.CompilerParams(vmem_limit_bytes=16 << 20)


def attend(queries, key_rows, value_rows, allowed):
    scores = jnp.einsum(
        "qhe,khe->hqk", queries, key_rows, preferred_element_type=jnp.float32
    ) * HEAD_DIM ** (-0.5)
    scores = jnp.where(allowed[None], scores, MASKED)
    peak = jnp.max(scores, axis=2)
    weights = jnp.where(allowed[None], jnp.exp(scores - peak[:, :, None]), 0.0)
    total = jnp.sum(weights, axis=2)
    blended = jnp.einsum(
        "hqk,khe->hqe", weights.astype(jnp.bfloat16), value_rows, preferred_element_type=jnp.float32
    )
    blended = blended / total[:, :, None]
    return jnp.transpose(blended, (1, 0, 2)).reshape(blended.shape[1], -1).astype(jnp.bfloat16)


def gathered(video_q, video_k, video_v, audio_q, audio_k, audio_v, offsets, counts):
    my_frame = lax.axis_index("seq")
    video_rows, audio_rows = video_q.shape[0], audio_q.shape[0]

    def heads(rows):
        return rows.reshape(rows.shape[0], -1, HEAD_DIM)

    def everywhere(rows):
        return heads(lax.all_gather(rows, "seq", axis=0, tiled=True))

    my_offsets = lax.dynamic_slice_in_dim(offsets, my_frame * audio_rows, audio_rows)
    keys, values = everywhere(video_k), everywhere(video_v)
    audio_keys, audio_values = everywhere(audio_k), everywhere(audio_v)
    positions = jnp.arange(keys.shape[0], dtype=jnp.int32)
    source = positions // video_rows
    is_live = positions % video_rows < jnp.repeat(counts, video_rows)
    video_self = attend(heads(video_q), keys, values, is_live[None, :])
    in_reach = (jnp.abs(my_offsets[:, None] - source[None, :]) <= SPAN) & is_live[None, :]
    audio_cross = attend(heads(audio_q), keys, values, in_reach)
    every = jnp.ones((1, audio_keys.shape[0]), jnp.bool_)
    audio_self = attend(heads(audio_q), audio_keys, audio_values, every)
    in_reach = jnp.abs(offsets - my_frame) <= SPAN
    video_cross = attend(heads(video_q), audio_keys, audio_values, in_reach[None, :])
    return (video_self, video_cross, audio_self, audio_cross)


def blend(queries, keys, values, bias):
    scores = lax.dot_general(
        queries, keys, (((1,), (1,)), ((), ())), preferred_element_type=jnp.float32
    )
    if bias is not None:
        scores = scores + bias
    peak = jnp.max(scores, axis=1, keepdims=True)
    weights = jnp.exp2((scores - peak) * (HEAD_DIM ** (-0.5) * LOG2E))
    total = jnp.sum(weights, axis=1, keepdims=True)
    mixed = jnp.dot(weights.astype(jnp.bfloat16), values, preferred_element_type=jnp.float32)
    return (mixed * (1.0 / total)).astype(jnp.bfloat16)


def pick(pieces, at):
    chosen = pieces[0]
    for i in range(1, len(pieces)):
        chosen = jnp.where(at == i, pieces[i], chosen)
    return chosen


def table_kernel(n, me_ref, count_ref, offset_ref, live_ref, reach_ref, near_ref):
    me = me_ref[0]
    upper = me * 2 >= n
    inner, end = jnp.where(upper, 1, n - 2), jnp.where(upper, 0, n - 1)
    frames = (me, me ^ 1, inner, end)
    audio_rows = offset_ref.shape[1] // n
    video_rows = live_ref.shape[1] // n
    pieces = [offset_ref[:, i * audio_rows : (i + 1) * audio_rows] for i in range(n)]
    offsets = jnp.concatenate([pick(pieces, frame) for frame in frames], axis=1)
    near_ref[...] = jnp.where(jnp.abs(offsets - me) <= SPAN, 0.0, MASKED)
    size = 2 * audio_rows
    corner = lax.broadcasted_iota(jnp.int32, (size, size), 0) == lax.broadcasted_iota(
        jnp.int32, (size, size), 1
    )
    asking = jnp.sum(jnp.where(corner, offsets[:, :size], 0), axis=1, keepdims=True)
    within = lax.broadcasted_iota(jnp.int32, (1, video_rows), 1)
    for i, frame in enumerate(frames):
        cols = slice(i * video_rows, (i + 1) * video_rows)
        live = jnp.where(within < count_ref[frame], 0.0, MASKED)
        live_ref[:, cols] = live
        reach_ref[:, cols] = jnp.where(jnp.abs(asking - frame) <= SPAN, live, MASKED)


def audio_kernel(n, me_ref, near_ref, *refs):
    parts, (b0, b1, inner2, end2, b3, cross_ref, own_ref, mate_ref) = refs[:-8], refs[-8:]
    audio_rows = own_ref.shape[0]
    video_rows = cross_ref.shape[0]
    me = me_ref[0]
    at_end = (me == 0) | (me == n - 1)

    def run(blocks, alone):
        near = near_ref[:, : audio_rows * len(blocks)]
        at = 0
        for q_own, q_mate in zip(parts[::2], parts[1::2]):
            for first in range(0, q_own.shape[1], HEAD_DIM):
                q_cols = slice(first, first + HEAD_DIM)
                cols = slice(at, at + HEAD_DIM)
                keys = jnp.concatenate([b[:audio_rows, cols] for b in blocks], axis=0)
                values = jnp.concatenate([b[audio_rows:, cols] for b in blocks], axis=0)
                cross_ref[:, cols] = blend(q_own[:video_rows, q_cols], keys, values, near)
                if not alone:
                    both = jnp.concatenate(
                        [q_own[video_rows:, q_cols], q_mate[video_rows:, q_cols]], axis=0
                    )
                    out = blend(both, keys, values, None)
                    own_ref[:, cols] = out[:audio_rows]
                    mate_ref[:, cols] = out[audio_rows:]
                at += HEAD_DIM

    @pl.when(jnp.logical_not(at_end))
    def _():
        run((b0, b1, inner2, b3), False)

    @pl.when(at_end)
    def _():
        run((b0, b1, end2), True)


def video_kernel(n, first, me_ref, live_ref, reach_ref, q_own, q_mate, b0, b1, b2, b3, own_ref, mate_ref):
    video_rows = b0.shape[0] // 2
    audio_rows = q_own.shape[0] - video_rows
    me = me_ref[0]

    @pl.when((me > 0) & (me < n - 1))
    def _():
        for head in range(b0.shape[1] // HEAD_DIM):
            cols = slice(head * HEAD_DIM, (head + 1) * HEAD_DIM)
            q_cols = slice((first + head) * HEAD_DIM, (first + head + 1) * HEAD_DIM)
            keys = jnp.concatenate([b[:video_rows, cols] for b in (b0, b1, b2, b3)], axis=0)
            values = jnp.concatenate([b[video_rows:, cols] for b in (b0, b1, b2, b3)], axis=0)
            for q_ref, o_ref in ((q_own, own_ref), (q_mate, mate_ref)):
                queries = q_ref[:video_rows, q_cols]
                o_ref[:video_rows, cols] = blend(queries, keys, values, live_ref[...])
            both = jnp.concatenate([q_own[video_rows:, q_cols], q_mate[video_rows:, q_cols]], axis=0)
            out = blend(both, keys, values, reach_ref[...])
            own_ref[video_rows:, cols] = out[:audio_rows]
            mate_ref[video_rows:, cols] = out[audio_rows:]


def place_kernel(n_frames, video_rows, me_ref, cross, *refs):
    n = (len(refs) - 5) // 2
    own, back = refs[:n], refs[n : 2 * n]
    video_self, video_cross, audio_self, audio_cross = refs[2 * n : 2 * n + 4]
    sem = refs[-1]

    def copies(parts):
        yield cross, video_cross
        yield parts[0], audio_self
        at = 0
        for part in parts[1:]:
            cols = pl.ds(at, part.shape[1])
            yield part.at[:video_rows], video_self.at[:, cols]
            yield part.at[video_rows:], audio_cross.at[:, cols]
            at += part.shape[1]

    at_end = (me_ref[0] == 0) | (me_ref[0] == n_frames - 1)
    for role, parts in ((jnp.logical_not(at_end), own), (at_end, back)):

        @pl.when(role)
        def _(parts=parts):
            moves = [
                pltpu.make_async_copy(src, dst, sem.at[i])
                for i, (src, dst) in enumerate(copies(parts))
            ]
            for move in moves:
                move.start()
            for move in moves:
                move.wait()


def cost(rows, keys, heads):
    scores = rows * keys * heads
    return pl.CostEstimate(flops=4 * scores * HEAD_DIM, bytes_accessed=rows * heads * 512, transcendentals=scores)


def chunks_of(heads):
    head = (heads + 1) // 2
    return head, (heads - head + 1) // 2, (heads - head) // 2


def lined(video_q, video_k, video_v, audio_q, audio_k, audio_v, offsets, counts):
    n, cores = lax.axis_size("seq"), lax.axis_size("mp")
    me = lax.axis_index("seq")
    video_rows, audio_rows = video_q.shape[0], audio_q.shape[0]
    rows = video_rows + audio_rows
    width = video_q.shape[1]
    heads = width // HEAD_DIM
    chunks = chunks_of(heads)
    mate_pairs = [(i, i ^ 1) for i in range(n)]
    cross_pairs = []
    for i in range(n):
        for core in range(cores):
            inner = 0 < i < n - 1
            to = (n - 1 - i) * cores + core if inner else i * cores + cores - 1 - core
            cross_pairs.append((i * cores + core, to))

    def mate(block):
        return lax.ppermute(block, "seq", mate_pairs)

    def cross(block):
        return lax.ppermute(block, ("seq", "mp"), cross_pairs)

    def call(kernel, outs, spaces, *args, **more):
        return pl.pallas_call(
            kernel,
            out_shape=tuple(jax.ShapeDtypeStruct(shape, dtype) for shape, dtype in outs),
            in_specs=spaces,
            compiler_params=PARAMS,
            **more,
        )(*args)

    place = me.astype(jnp.int32).reshape(1)
    live, reach, near = call(
        functools.partial(table_kernel, n),
        (
            ((1, n * video_rows), jnp.float32),
            ((2 * audio_rows, n * video_rows), jnp.float32),
            ((1, n * audio_rows), jnp.float32),
        ),
        [SMEM, SMEM, VMEM],
        place,
        counts,
        offsets.reshape(1, -1),
    )
    split = chunks[0] * HEAD_DIM
    asks = [
        jnp.concatenate([video_q[:, cols], audio_q[:, cols]], axis=0)
        for cols in (slice(0, split), slice(split, width))
    ]
    sound = jnp.concatenate([audio_k, audio_v], axis=0)
    sights, at = [], 0
    for size in chunks:
        cols = slice(at * HEAD_DIM, (at + size) * HEAD_DIM)
        sights.append(jnp.concatenate([video_k[:, cols], video_v[:, cols]], axis=0))
        at += size

    pieces = range(len(chunks))
    sight_mate = [mate(sights[i]) for i in pieces]
    sight_across = [cross(sights[i]) for i in pieces]
    sight_far = [cross(sight_mate[i]) for i in pieces]
    asks_mate = [mate(asks[i]) for i in range(2)]
    sound_mate = mate(sound)
    sound_across = cross(sound)
    sound_far = cross(sound_mate)
    sound_passed = mate(sound_across)

    mine, back, at = [], [], 0
    for i, size in enumerate(chunks):
        half = min(i, 1)
        own, theirs = call(
            functools.partial(video_kernel, n, at - half * chunks[0]),
            (((rows, size * HEAD_DIM), jnp.bfloat16),) * 2,
            [SMEM] + [VMEM] * 8,
            place,
            live,
            reach,
            asks[half],
            asks_mate[half],
            sights[i],
            sight_mate[i],
            sight_across[i],
            sight_far[i],
            cost_estimate=cost(2 * rows, n * video_rows, size),
        )
        mine.append(own)
        back.append(mate(theirs))
        at += size
    video_cross, own, theirs = call(
        functools.partial(audio_kernel, n),
        (((video_rows, width), jnp.bfloat16),) + (((audio_rows, width), jnp.bfloat16),) * 2,
        [SMEM] + [VMEM] * 10,
        place,
        near,
        asks[0],
        asks_mate[0],
        asks[1],
        asks_mate[1],
        sound,
        sound_mate,
        sound_across,
        sound_passed,
        sound_far,
        cost_estimate=cost(2 * rows, n * audio_rows, heads),
    )
    mine = [own] + mine
    back = [mate(theirs)] + back
    return call(
        functools.partial(place_kernel, n, video_rows),
        (((video_rows, width), jnp.bfloat16),) * 2 + (((audio_rows, width), jnp.bfloat16),) * 2,
        [SMEM] + [VMEM] * (1 + 2 * len(mine)),
        place,
        video_cross,
        *mine,
        *back,
        out_specs=(ANY,) * 4,
        scratch_shapes=[pltpu.SemaphoreType.DMA((2 * len(mine),))],
    )


def solution(mesh):
    split = P(("groups", "seq"), ("tower", "mp"))
    placed = (split,) * 6 + (P("groups"), P("groups"))
    sizes = mesh.shape
    line = sizes["seq"] == 4 and sizes["mp"] == 2

    def whole(*arrays):
        heads = arrays[0].shape[1] // HEAD_DIM // (sizes["tower"] * sizes["mp"])
        body = lined if line and heads > 3 else gathered
        return jax.shard_map(
            body, mesh=mesh, in_specs=placed, out_specs=(split,) * 4, check_vma=False
        )(*arrays)

    return whole
```

time: 50 us -> 48.9 us (0.978)
  waiting for transfers between devices: 17.3 us -> 14 us
  local copies, waits for them, and re-layouts: 3.38 us -> 5.09 us
  starting transfers between devices: 24.7 us -> 25.2 us
    ppermute x14 -> x19, waiting for transfers between devices: 17.3 us -> 14 us  [the longest x11 14 us: mate(): return lax.ppermute(block, 'seq', mate_pairs)]
    unnamed x14 -> x11, local copies, waits for them, and re-layouts: 1.54 us -> 2.47 us
    slice x8 -> x12, local copies, waits for them, and re-layouts: 1.83 us -> 2.57 us  [lined(): sights.append(jnp.concatenate([video_k[:, cols], video_v[:, cols]], axis=0))]
    ppermute x14 -> x19, starting transfers between devices: 24.7 us -> 25.2 us  [the longest x11 23.7 us: mate(): return lax.ppermute(block, 'seq', mate_pairs)]
    pallas_call x4 -> x6, Pallas kernels: 3.63 us -> 3.34 us  [call(): pl.pallas_call(kernel, out_shape=tuple((jax.ShapeDtypeStruct(shape, dtype...]
  transfers between devices with their start and end apart: 14 -> 19, of which waited for: 4 -> 4; matrix products, arithmetic and copies ran while one was open for 0% -> 0% of each run, Pallas kernels for 6% -> 5%
where the time goes in v4:
time: 48.9 us; the launch traced here: 48.5 us
  starting transfers between devices  25.2 us (52%)
  waiting for transfers between devices  14 us (29%)
  local copies, waits for them, and re-layouts  5.09 us (10%)
  Pallas kernels  3.34 us (7%)
  between operations  0.81 us (2%)
    ppermute x11, starting transfers between devices, mate(): return lax.ppermute(block, 'seq', mate_pairs)  23.7 us
    ppermute x11, waiting for transfers between devices, mate(): return lax.ppermute(block, 'seq', mate_pairs)  14 us
    pallas_call x6, Pallas kernels, call(): pl.pallas_call(kernel, out_shape=tuple((jax.ShapeDtypeStruct(shape, dtype...  3.34 us
    slice x12, local copies, waits for them, and re-layouts, lined(): sights.append(jnp.concatenate([video_k[:, cols], video_v[:, cols]], axis=0))  2.57 us
    unnamed x11, local copies, waits for them, and re-layouts  2.47 us
    ppermute x8, starting transfers between devices, cross(): return lax.ppermute(block, ('seq', 'mp'), cross_pairs)  1.58 us
  transfers between devices with their start and end apart: 19, of which 4 were waited for; matrix products, arithmetic and copies ran while one was open for 0% of the time, Pallas kernels for 5%

profile of v4, /device:TPU:0, one launch (start us, length us, event | category | flops | bytes accessed | tf_op | source)
XLA Modules:
  0.0 48.5 jit_solution(6374951929839226141)
XLA Ops:
  0.6 0.0 copy-start.3
  0.6 0.9 %constant_dynamic-update-slice_fusion.1 = bf16[128,768]{1,0:T(8,128)(2,1)S(1)} fusion(bf16[64,768]{1,0:T(8,128)(2,1)} %param.12), kind=kLoop, calls=%fused_computation.6 | loop fusion | bytes 196608
  1.6 0.0 copy-done.3
  1.6 0.6 %collective-permute-start.3 = (bf16[128,768]{1,0:T(8,128)(2,1)S(1)}, bf16[128,768]{1,0:T(8,128)(2,1)S(1)}, u32[]{:S(2)}, u32[]{:S(2)}) collective-permute-start(bf16[128,768]{1,0:T(8,128)(2,1)S(1)} %constant_dynamic-update-slice_fusion.refs_4_), channel_id=1, source_target_pairs={{0,1},{1,0},{4,8},{5,9},{8,4},{9,5},{12,13},{13,12},{2,3},{3,2},{6... | collective-permute-start | bytes 589832 | tf_op jit(solution)/shard_map/ppermute | solution.py:222
  2.2 4.1 %collective-permute-start.2 = (bf16[128,768]{1,0:T(8,128)(2,1)S(1)}, bf16[128,768]{1,0:T(8,128)(2,1)S(1)}, u32[]{:S(2)}, u32[]{:S(2)}) collective-permute-start(bf16[128,768]{1,0:T(8,128)(2,1)S(1)} %constant_dynamic-update-slice_fusion.refs_4_), channel_id=1, source_target_pairs={{0,4},{4,0},{8,12},{12,8},{1,5},{5,1},{9,13},{13,9},{2,6},{6,2},{1... | collective-permute-start | bytes 589832 | tf_op jit(solution)/shard_map/ppermute | solution.py:219
  6.3 0.0 slice-start
  6.3 0.0 slice-start.3
  6.3 0.8 %slice-done = bf16[128,256]{1,0:T(8,128)(2,1)S(1)} async-done(((bf16[128,768]{1,0:T(8,128)(2,1)}), bf16[128,256]{1,0:T(8,128)(2,1)S(1)}, s32[]{:S(2)}) %slice-start) | async-done | bytes 65560 | tf_op jit(solution)/shard_map/slice | solution.py:255
  7.1 0.0 slice-done.3
  7.2 0.1 collective-permute-start.9
  7.3 0.0 slice-start.1
  7.3 0.0 slice-start.4
  7.3 0.7 %slice-done.1 = bf16[128,128]{1,0:T(8,128)(2,1)S(1)} async-done(((bf16[128,768]{1,0:T(8,128)(2,1)}), bf16[128,128]{1,0:T(8,128)(2,1)S(1)}, s32[]{:S(2)}) %slice-start.1) | async-done | bytes 32792 | tf_op jit(solution)/shard_map/slice | solution.py:255
  8.0 0.0 slice-done.4
  8.0 2.1 %collective-permute-start.12 = (bf16[256,128]{1,0:T(8,128)(2,1)S(1)}, bf16[256,128]{1,0:T(8,128)(2,1)S(1)}, u32[]{:S(2)}, u32[]{:S(2)}) collective-permute-start(bf16[256,128]{1,0:T(8,128)(2,1)S(1)} %pad_maximum_fusion.4.b0), channel_id=1, source_target_pairs={{0,4},{4,0},{8,12},{12,8},{1,5},{5,1},{9,13},{13,9},{2,6},{6,2},{1... | collective-permute-start | bytes 196616 | tf_op jit(solution)/shard_map/ppermute | solution.py:219
  10.1 0.0 slice-start.2
  10.1 0.0 slice-start.5
  10.1 0.9 %slice-done.2 = bf16[128,384]{1,0:T(8,128)(2,1)S(1)} async-done(((bf16[128,768]{1,0:T(8,128)(2,1)}), bf16[128,384]{1,0:T(8,128)(2,1)S(1)}, s32[]{:S(2)}) %slice-start.2) | async-done | bytes 98328 | tf_op jit(solution)/shard_map/slice | solution.py:255
  11.0 0.0 slice-done.5
  11.0 0.0 copy-start.2
  11.1 0.0 copy-start.4
  11.1 0.1 collective-permute-start.6
  11.2 0.8 %copy-done.2 = bf16[128,768]{1,0:T(8,128)(2,1)S(1)} copy-done((bf16[128,768]{1,0:T(8,128)(2,1)S(1)}, bf16[128,768]{1,0:T(8,128)(2,1)}, u32[]{:S(2)}) %copy-start.2) | copy-done | bytes 196632
  12.0 0.0 copy-done.4
  12.1 4.2 %collective-permute-done.12.b1 = bf16[256,128]{1,0:T(8,128)(2,1)S(1)} collective-permute-done((bf16[256,128]{1,0:T(8,128)(2,1)S(1)}, bf16[256,128]{1,0:T(8,128)(2,1)S(1)}, u32[]{:S(2)}, u32[]{:S(2)}) %collective-permute-start.12) | collective-permute-done | bytes 65568 | tf_op jit(solution)/shard_map/ppermute | solution.py:219
  16.3 0.0 collective-permute-start.7
  16.3 3.1 %collective-permute-done.6.b1 = bf16[256,384]{1,0:T(8,128)(2,1)S(1)} collective-permute-done((bf16[256,384]{1,0:T(8,128)(2,1)S(1)}, bf16[256,384]{1,0:T(8,128)(2,1)S(1)}, u32[]{:S(2)}, u32[]{:S(2)}) %collective-permute-start.6) | collective-permute-done | bytes 196640 | tf_op jit(solution)/shard_map/ppermute | solution.py:219
  19.3 0.0 collective-permute-start.8
  19.4 0.0 collective-permute-done.9.b1
  19.4 2.6 %collective-permute-start = (bf16[192,384]{1,0:T(8,128)(2,1)S(1)}, bf16[192,384]{1,0:T(8,128)(2,1)S(1)}, u32[]{:S(2)}, u32[]{:S(2)}) collective-permute-start(bf16[192,384]{1,0:T(8,128)(2,1)S(1)} %pad_maximum_fusion.1.refs_0_.q_own), channel_id=1, source_target_pairs={{0,4},{4,0},{8,12},{12,8},{1,5},{5,1},{9,13},{13,9},{2,6},{6,2},{1... | collective-permute-start | bytes 442376 | tf_op jit(solution)/shard_map/ppermute | solution.py:219
  22.0 0.0 collective-permute-done.3.refs_6_
  22.0 0.1 collective-permute-start.4
  22.1 0.0 collective-permute-done.2.refs_5_
  22.1 0.0 collective-permute-start.5
  22.1 4.6 %collective-permute-done.refs_1_.q_mate = bf16[192,384]{1,0:T(8,128)(2,1)S(1)} collective-permute-done((bf16[192,384]{1,0:T(8,128)(2,1)S(1)}, bf16[192,384]{1,0:T(8,128)(2,1)S(1)}, u32[]{:S(2)}, u32[]{:S(2)}) %collective-permute-start) | collective-permute-done | bytes 147488 | tf_op jit(solution)/shard_map/ppermute | solution.py:219
  26.7 2.0 %collective-permute-start.1 = (bf16[192,384]{1,0:T(8,128)(2,1)S(1)}, bf16[192,384]{1,0:T(8,128)(2,1)S(1)}, u32[]{:S(2)}, u32[]{:S(2)}) collective-permute-start(bf16[192,384]{1,0:T(8,128)(2,1)S(1)} %pad_maximum_fusion.2.refs_2_.q_own), channel_id=1, source_target_pairs={{0,4},{4,0},{8,12},{12,8},{1,5},{5,1},{9,13},{13,9},{2,6},{6,2},{1... | collective-permute-start | bytes 442376 | tf_op jit(solution)/shard_map/ppermute | solution.py:219
  28.7 0.0 collective-permute-done.7.b2
  28.7 0.0 collective-permute-start.10
  28.7 0.0 collective-permute-done.8.b3
  28.7 0.5 %collective-permute-start.11 = (bf16[256,256]{1,0:T(8,128)(2,1)S(1)}, bf16[256,256]{1,0:T(8,128)(2,1)S(1)}, u32[]{:S(2)}, u32[]{:S(2)}) collective-permute-start(bf16[256,256]{1,0:T(8,128)(2,1)S(1)} %collective-permute-done.9.b1), channel_id=1, source_target_pairs={{0,1},{1,0},{4,8},{5,9},{8,4},{9,5},{12,13},{13,12},{2,3},{3,2},{6... | collective-permute-start | bytes 393224 | tf_op jit(solution)/shard_map/ppermute | solution.py:222
  29.2 0.0 copy-start
  29.2 0.0 copy-start.1
  29.2 0.7 %copy-done = s32[256]{0:T(256)S(1)} copy-done((s32[256]{0:T(256)S(1)}, s32[256]{0:T(256)}, u32[]{:S(2)}) %copy-start) | copy-done | bytes 1048
  29.9 0.0 copy-done.1
  29.9 1.0 %shard_map.111 = (f32[1,512]{1,0:T(1,128)S(1)}, f32[128,512]{1,0:T(8,128)S(1)}, f32[1,256]{1,0:T(1,128)S(1)}) custom-call(s32[1]{0:T(128)} %bitcast.me_ref, s32[4]{0:T(128)S(1)} %copy-done.1, s32[1,256]{1,0:T(1,128)S(1)} %bitcast.2), custom_call_target="tpu_custom_call" | custom-call | tf_op jit(solution)/shard_map/pallas_call | solution.py:225
  30.9 0.0 collective-permute-done.10.b2
  30.9 5.9 %collective-permute-start.16 = (bf16[192,384]{1,0:T(8,128)(2,1)S(1)}, bf16[192,384]{1,0:T(8,128)(2,1)S(1)}, u32[]{:S(2)}, u32[]{:S(2)}) collective-permute-start(bf16[192,384]{1,0:T(8,128)(2,1)S(1)} %get-tuple-element.25), channel_id=1, source_target_pairs={{0,4},{4,0},{8,12},{12,8},{1,5},{5,1},{9,13},{13,9},{2,6},{6,2},{1... | collective-permute-start | bytes 442376 | tf_op jit(solution)/shard_map/ppermute | solution.py:219
  36.8 0.0 collective-permute-done.1.refs_3_.q_mate
  36.8 0.0 collective-permute-start.13
  36.8 0.0 collective-permute-done.11.b3
  36.8 0.5 %collective-permute-start.14 = (bf16[256,128]{1,0:T(8,128)(2,1)S(1)}, bf16[256,128]{1,0:T(8,128)(2,1)S(1)}, u32[]{:S(2)}, u32[]{:S(2)}) collective-permute-start(bf16[256,128]{1,0:T(8,128)(2,1)S(1)} %collective-permute-done.12.b1), channel_id=1, source_target_pairs={{0,1},{1,0},{4,8},{5,9},{8,4},{9,5},{12,13},{13,12},{2,3},{3,2},{6... | collective-permute-start | bytes 196616 | tf_op jit(solution)/shard_map/ppermute | solution.py:222
  37.3 0.0 collective-permute-done.4.refs_7_
  37.3 3.7 %collective-permute-start.17 = (bf16[192,256]{1,0:T(8,128)(2,1)S(1)}, bf16[192,256]{1,0:T(8,128)(2,1)S(1)}, u32[]{:S(2)}, u32[]{:S(2)}) collective-permute-start(bf16[192,256]{1,0:T(8,128)(2,1)S(1)} %get-tuple-element.26), channel_id=1, source_target_pairs={{0,4},{4,0},{8,12},{12,8},{1,5},{5,1},{9,13},{13,9},{2,6},{6,2},{1... | collective-permute-start | bytes 294920 | tf_op jit(solution)/shard_map/ppermute | solution.py:219
  40.9 0.0 collective-permute-done.5.refs_8_
  40.9 1.5 %shard_map.112 = (bf16[128,768]{1,0:T(8,128)(2,1)S(1)}, bf16[64,768]{1,0:T(8,128)(2,1)S(1)}, bf16[64,768]{1,0:T(8,128)(2,1)S(1)}) custom-call(s32[1]{0:T(128)} %bitcast.me_ref, f32[1,256]{1,0:T(1,128)S(1)} %get-tuple-element.16.near_ref, bf16[192,384]{1,0:T(8,128)(2,1)S(1)} %pad_maximum_fusion.1.refs_0_.q_own, ...), custom_call_target="tpu_custom_call" | custom-call | flops 301989888 | bytes 1179648 | tf_op jit(solution)/shard_map/pallas_call | solution.py:225
  42.4 0.1 collective-permute-start.15
  42.5 0.0 collective-permute-done.13.b2
  42.5 0.0 collective-permute-done.14.b3
  42.6 3.0 %collective-permute-start.18 = (bf16[192,128]{1,0:T(8,128)(2,1)S(1)}, bf16[192,128]{1,0:T(8,128)(2,1)S(1)}, u32[]{:S(2)}, u32[]{:S(2)}) collective-permute-start(bf16[192,128]{1,0:T(8,128)(2,1)S(1)} %get-tuple-element.27), channel_id=1, source_target_pairs={{0,4},{4,0},{8,12},{12,8},{1,5},{5,1},{9,13},{13,9},{2,6},{6,2},{1... | collective-permute-start | bytes 147464 | tf_op jit(solution)/shard_map/ppermute | solution.py:219
  45.6 2.1 %collective-permute-done.18.refs_7_ = bf16[192,128]{1,0:T(8,128)(2,1)S(1)} collective-permute-done((bf16[192,128]{1,0:T(8,128)(2,1)S(1)}, bf16[192,128]{1,0:T(8,128)(2,1)S(1)}, u32[]{:S(2)}, u32[]{:S(2)}) %collective-permute-start.18) | collective-permute-done | bytes 49184 | tf_op jit(solution)/shard_map/ppermute | solution.py:219
  47.6 0.0 collective-permute-done.17.refs_6_
  47.6 0.0 collective-permute-done.15.refs_4_
  47.7 0.0 collective-permute-done.16.refs_5_
  47.7 0.9 %shard_map.116 = (bf16[128,768]{1,0:T(8,128)(2,1)}, bf16[128,768]{1,0:T(8,128)(2,1)}, bf16[64,768]{1,0:T(8,128)(2,1)}, bf16[64,768]{1,0:T(8,128)(2,1)}) custom-call(s32[1]{0:T(128)} %bitcast.me_ref, bf16[128,768]{1,0:T(8,128)(2,1)S(1)} %get-tuple-element.17.cross, bf16[64,768]{1,0:T(8,128)(2,1)S(1)} %get-tuple-element.18.refs_0_, ...), custom_call_target="tpu_custom_call" | custom-call | tf_op jit(solution)/shard_map/pallas_call | solution.py:225
  (11 shorter events, 0.1 us)
Async XLA Ops:
  0.6 0.9 %copy-start.3 = (bf16[64,768]{1,0:T(8,128)(2,1)S(1)}, bf16[64,768]{1,0:T(8,128)(2,1)}, u32[]{:S(2)}) copy-start(bf16[64,768]{1,0:T(8,128)(2,1)} %param.13) | copy-start | bytes 294916
  1.6 20.4 %collective-permute-start.3 = (bf16[128,768]{1,0:T(8,128)(2,1)S(1)}, bf16[128,768]{1,0:T(8,128)(2,1)S(1)}, u32[]{:S(2)}, u32[]{:S(2)}) collective-permute-start(bf16[128,768]{1,0:T(8,128)(2,1)S(1)} %constant_dynamic-update-slice_fusion.refs_4_), channel_id=1, source_target_pairs={{0,1},{1,0},{4,8},{5,9},{8,4},{9,5},{12,13},{13,12},{2,3},{3,2},{6... | collective-permute-start | bytes 589832 | tf_op jit(solution)/shard_map/ppermute | solution.py:222
  2.2 19.9 %collective-permute-start.2 = (bf16[128,768]{1,0:T(8,128)(2,1)S(1)}, bf16[128,768]{1,0:T(8,128)(2,1)S(1)}, u32[]{:S(2)}, u32[]{:S(2)}) collective-permute-start(bf16[128,768]{1,0:T(8,128)(2,1)S(1)} %constant_dynamic-update-slice_fusion.refs_4_), channel_id=1, source_target_pairs={{0,4},{4,0},{8,12},{12,8},{1,5},{5,1},{9,13},{13,9},{2,6},{6,2},{1... | collective-permute-start | bytes 589832 | tf_op jit(solution)/shard_map/ppermute | solution.py:219
  6.3 0.8 %slice-start = ((bf16[128,768]{1,0:T(8,128)(2,1)}), bf16[128,256]{1,0:T(8,128)(2,1)S(1)}, s32[]{:S(2)}) async-start(bf16[128,768]{1,0:T(8,128)(2,1)} %param.9), calls=%async_computation | async-start | bytes 131072 | tf_op jit(solution)/shard_map/slice | solution.py:255
  6.3 0.9 %slice-start.3 = ((bf16[128,768]{1,0:T(8,128)(2,1)}), bf16[128,256]{1,0:T(8,128)(2,1)S(1)}, s32[]{:S(2)}) async-start(bf16[128,768]{1,0:T(8,128)(2,1)} %param.10), calls=%async_computation.3 | async-start | bytes 131072 | tf_op jit(solution)/shard_map/slice | solution.py:255
  7.2 12.2 %collective-permute-start.9 = (bf16[256,256]{1,0:T(8,128)(2,1)S(1)}, bf16[256,256]{1,0:T(8,128)(2,1)S(1)}, u32[]{:S(2)}, u32[]{:S(2)}) collective-permute-start(bf16[256,256]{1,0:T(8,128)(2,1)S(1)} %pad_maximum_fusion.3.b0), channel_id=1, source_target_pairs={{0,4},{4,0},{8,12},{12,8},{1,5},{5,1},{9,13},{13,9},{2,6},{6,2},{1... | collective-permute-start | bytes 393224 | tf_op jit(solution)/shard_map/ppermute | solution.py:219
  7.3 0.8 %slice-start.1 = ((bf16[128,768]{1,0:T(8,128)(2,1)}), bf16[128,128]{1,0:T(8,128)(2,1)S(1)}, s32[]{:S(2)}) async-start(bf16[128,768]{1,0:T(8,128)(2,1)} %param.9), calls=%async_computation.1 | async-start | bytes 65536 | tf_op jit(solution)/shard_map/slice | solution.py:255
  7.3 0.8 %slice-start.4 = ((bf16[128,768]{1,0:T(8,128)(2,1)}), bf16[128,128]{1,0:T(8,128)(2,1)S(1)}, s32[]{:S(2)}) async-start(bf16[128,768]{1,0:T(8,128)(2,1)} %param.10), calls=%async_computation.4 | async-start | bytes 65536 | tf_op jit(solution)/shard_map/slice | solution.py:255
  8.0 8.2 %collective-permute-start.12 = (bf16[256,128]{1,0:T(8,128)(2,1)S(1)}, bf16[256,128]{1,0:T(8,128)(2,1)S(1)}, u32[]{:S(2)}, u32[]{:S(2)}) collective-permute-start(bf16[256,128]{1,0:T(8,128)(2,1)S(1)} %pad_maximum_fusion.4.b0), channel_id=1, source_target_pairs={{0,4},{4,0},{8,12},{12,8},{1,5},{5,1},{9,13},{13,9},{2,6},{6,2},{1... | collective-permute-start | bytes 196616 | tf_op jit(solution)/shard_map/ppermute | solution.py:219
  10.1 0.9 %slice-start.2 = ((bf16[128,768]{1,0:T(8,128)(2,1)}), bf16[128,384]{1,0:T(8,128)(2,1)S(1)}, s32[]{:S(2)}) async-start(bf16[128,768]{1,0:T(8,128)(2,1)} %param.9), calls=%async_computation.2 | async-start | bytes 196608 | tf_op jit(solution)/shard_map/slice | solution.py:255
  10.1 0.9 %slice-start.5 = ((bf16[128,768]{1,0:T(8,128)(2,1)}), bf16[128,384]{1,0:T(8,128)(2,1)S(1)}, s32[]{:S(2)}) async-start(bf16[128,768]{1,0:T(8,128)(2,1)} %param.10), calls=%async_computation.5 | async-start | bytes 196608 | tf_op jit(solution)/shard_map/slice | solution.py:255
  11.0 0.9 %copy-start.2 = (bf16[128,768]{1,0:T(8,128)(2,1)S(1)}, bf16[128,768]{1,0:T(8,128)(2,1)}, u32[]{:S(2)}) copy-start(bf16[128,768]{1,0:T(8,128)(2,1)} %param.8) | copy-start | bytes 589828
  11.1 1.0 %copy-start.4 = (bf16[64,768]{1,0:T(8,128)(2,1)S(1)}, bf16[64,768]{1,0:T(8,128)(2,1)}, u32[]{:S(2)}) copy-start(bf16[64,768]{1,0:T(8,128)(2,1)} %param.11) | copy-start | bytes 294916
  11.1 8.3 %collective-permute-start.6 = (bf16[256,384]{1,0:T(8,128)(2,1)S(1)}, bf16[256,384]{1,0:T(8,128)(2,1)S(1)}, u32[]{:S(2)}, u32[]{:S(2)}) collective-permute-start(bf16[256,384]{1,0:T(8,128)(2,1)S(1)} %pad_maximum_fusion.b0), channel_id=1, source_target_pairs={{0,4},{4,0},{8,12},{12,8},{1,5},{5,1},{9,13},{13,9},{2,6},{6,2},{1... | collective-permute-start | bytes 589832 | tf_op jit(solution)/shard_map/ppermute | solution.py:219
  16.3 12.4 %collective-permute-start.7 = (bf16[256,384]{1,0:T(8,128)(2,1)S(1)}, bf16[256,384]{1,0:T(8,128)(2,1)S(1)}, u32[]{:S(2)}, u32[]{:S(2)}) collective-permute-start(bf16[256,384]{1,0:T(8,128)(2,1)S(1)} %pad_maximum_fusion.b0), channel_id=1, source_target_pairs={{0,1},{1,0},{4,8},{5,9},{8,4},{9,5},{12,13},{13,12},{2,3},{3,2},{6... | collective-permute-start | bytes 589832 | tf_op jit(solution)/shard_map/ppermute | solution.py:222
  19.3 9.4 %collective-permute-start.8 = (bf16[256,384]{1,0:T(8,128)(2,1)S(1)}, bf16[256,384]{1,0:T(8,128)(2,1)S(1)}, u32[]{:S(2)}, u32[]{:S(2)}) collective-permute-start(bf16[256,384]{1,0:T(8,128)(2,1)S(1)} %collective-permute-done.6.b1), channel_id=1, source_target_pairs={{0,1},{1,0},{4,8},{5,9},{8,4},{9,5},{12,13},{13,12},{2,3},{3,2},{6... | collective-permute-start | bytes 589832 | tf_op jit(solution)/shard_map/ppermute | solution.py:222
  19.4 7.3 %collective-permute-start = (bf16[192,384]{1,0:T(8,128)(2,1)S(1)}, bf16[192,384]{1,0:T(8,128)(2,1)S(1)}, u32[]{:S(2)}, u32[]{:S(2)}) collective-permute-start(bf16[192,384]{1,0:T(8,128)(2,1)S(1)} %pad_maximum_fusion.1.refs_0_.q_own), channel_id=1, source_target_pairs={{0,4},{4,0},{8,12},{12,8},{1,5},{5,1},{9,13},{13,9},{2,6},{6,2},{1... | collective-permute-start | bytes 442376 | tf_op jit(solution)/shard_map/ppermute | solution.py:219
  22.0 15.3 %collective-permute-start.4 = (bf16[128,768]{1,0:T(8,128)(2,1)S(1)}, bf16[128,768]{1,0:T(8,128)(2,1)S(1)}, u32[]{:S(2)}, u32[]{:S(2)}) collective-permute-start(bf16[128,768]{1,0:T(8,128)(2,1)S(1)} %collective-permute-done.3.refs_6_), channel_id=1, source_target_pairs={{0,4},{4,0},{8,12},{12,8},{1,5},{5,1},{9,13},{13,9},{2,6},{6,2},{1... | collective-permute-start | bytes 589832 | tf_op jit(solution)/shard_map/ppermute | solution.py:219
  22.1 18.9 %collective-permute-start.5 = (bf16[128,768]{1,0:T(8,128)(2,1)S(1)}, bf16[128,768]{1,0:T(8,128)(2,1)S(1)}, u32[]{:S(2)}, u32[]{:S(2)}) collective-permute-start(bf16[128,768]{1,0:T(8,128)(2,1)S(1)} %collective-permute-done.2.refs_5_), channel_id=1, source_target_pairs={{0,1},{1,0},{4,8},{5,9},{8,4},{9,5},{12,13},{13,12},{2,3},{3,2},{6... | collective-permute-start | bytes 589832 | tf_op jit(solution)/shard_map/ppermute | solution.py:222
  26.7 10.1 %collective-permute-start.1 = (bf16[192,384]{1,0:T(8,128)(2,1)S(1)}, bf16[192,384]{1,0:T(8,128)(2,1)S(1)}, u32[]{:S(2)}, u32[]{:S(2)}) collective-permute-start(bf16[192,384]{1,0:T(8,128)(2,1)S(1)} %pad_maximum_fusion.2.refs_2_.q_own), channel_id=1, source_target_pairs={{0,4},{4,0},{8,12},{12,8},{1,5},{5,1},{9,13},{13,9},{2,6},{6,2},{1... | collective-permute-start | bytes 442376 | tf_op jit(solution)/shard_map/ppermute | solution.py:219
  28.7 2.2 %collective-permute-start.10 = (bf16[256,256]{1,0:T(8,128)(2,1)S(1)}, bf16[256,256]{1,0:T(8,128)(2,1)S(1)}, u32[]{:S(2)}, u32[]{:S(2)}) collective-permute-start(bf16[256,256]{1,0:T(8,128)(2,1)S(1)} %pad_maximum_fusion.3.b0), channel_id=1, source_target_pairs={{0,1},{1,0},{4,8},{5,9},{8,4},{9,5},{12,13},{13,12},{2,3},{3,2},{6... | collective-permute-start | bytes 393224 | tf_op jit(solution)/shard_map/ppermute | solution.py:222
  28.7 8.1 %collective-permute-start.11 = (bf16[256,256]{1,0:T(8,128)(2,1)S(1)}, bf16[256,256]{1,0:T(8,128)(2,1)S(1)}, u32[]{:S(2)}, u32[]{:S(2)}) collective-permute-start(bf16[256,256]{1,0:T(8,128)(2,1)S(1)} %collective-permute-done.9.b1), channel_id=1, source_target_pairs={{0,1},{1,0},{4,8},{5,9},{8,4},{9,5},{12,13},{13,12},{2,3},{3,2},{6... | collective-permute-start | bytes 393224 | tf_op jit(solution)/shard_map/ppermute | solution.py:222
  29.2 0.7 %copy-start = (s32[256]{0:T(256)S(1)}, s32[256]{0:T(256)}, u32[]{:S(2)}) copy-start(s32[256]{0:T(256)} %param.14) | copy-start | bytes 3076
  29.2 0.7 %copy-start.1 = (s32[4]{0:T(128)S(1)}, s32[4]{0:T(128)}, u32[]{:S(2)}) copy-start(s32[4]{0:T(128)} %count_ref.1) | copy-start | bytes 52
  30.9 16.8 %collective-permute-start.16 = (bf16[192,384]{1,0:T(8,128)(2,1)S(1)}, bf16[192,384]{1,0:T(8,128)(2,1)S(1)}, u32[]{:S(2)}, u32[]{:S(2)}) collective-permute-start(bf16[192,384]{1,0:T(8,128)(2,1)S(1)} %get-tuple-element.25), channel_id=1, source_target_pairs={{0,4},{4,0},{8,12},{12,8},{1,5},{5,1},{9,13},{13,9},{2,6},{6,2},{1... | collective-permute-start | bytes 442376 | tf_op jit(solution)/shard_map/ppermute | solution.py:219
  36.8 5.8 %collective-permute-start.13 = (bf16[256,128]{1,0:T(8,128)(2,1)S(1)}, bf16[256,128]{1,0:T(8,128)(2,1)S(1)}, u32[]{:S(2)}, u32[]{:S(2)}) collective-permute-start(bf16[256,128]{1,0:T(8,128)(2,1)S(1)} %pad_maximum_fusion.4.b0), channel_id=1, source_target_pairs={{0,1},{1,0},{4,8},{5,9},{8,4},{9,5},{12,13},{13,12},{2,3},{3,2},{6... | collective-permute-start | bytes 196616 | tf_op jit(solution)/shard_map/ppermute | solution.py:222
  36.8 5.8 %collective-permute-start.14 = (bf16[256,128]{1,0:T(8,128)(2,1)S(1)}, bf16[256,128]{1,0:T(8,128)(2,1)S(1)}, u32[]{:S(2)}, u32[]{:S(2)}) collective-permute-start(bf16[256,128]{1,0:T(8,128)(2,1)S(1)} %collective-permute-done.12.b1), channel_id=1, source_target_pairs={{0,1},{1,0},{4,8},{5,9},{8,4},{9,5},{12,13},{13,12},{2,3},{3,2},{6... | collective-permute-start | bytes 196616 | tf_op jit(solution)/shard_map/ppermute | solution.py:222
  37.3 10.4 %collective-permute-start.17 = (bf16[192,256]{1,0:T(8,128)(2,1)S(1)}, bf16[192,256]{1,0:T(8,128)(2,1)S(1)}, u32[]{:S(2)}, u32[]{:S(2)}) collective-permute-start(bf16[192,256]{1,0:T(8,128)(2,1)S(1)} %get-tuple-element.26), channel_id=1, source_target_pairs={{0,4},{4,0},{8,12},{12,8},{1,5},{5,1},{9,13},{13,9},{2,6},{6,2},{1... | collective-permute-start | bytes 294920 | tf_op jit(solution)/shard_map/ppermute | solution.py:219
  42.4 5.2 %collective-permute-start.15 = (bf16[64,768]{1,0:T(8,128)(2,1)S(1)}, bf16[64,768]{1,0:T(8,128)(2,1)S(1)}, u32[]{:S(2)}, u32[]{:S(2)}) collective-permute-start(bf16[64,768]{1,0:T(8,128)(2,1)S(1)} %get-tuple-element.24), channel_id=1, source_target_pairs={{0,4},{4,0},{8,12},{12,8},{1,5},{5,1},{9,13},{13,9},{2,6},{6,2},{1... | collective-permute-start | bytes 294920 | tf_op jit(solution)/shard_map/ppermute | solution.py:219
  42.6 5.1 %collective-permute-start.18 = (bf16[192,128]{1,0:T(8,128)(2,1)S(1)}, bf16[192,128]{1,0:T(8,128)(2,1)S(1)}, u32[]{:S(2)}, u32[]{:S(2)}) collective-permute-start(bf16[192,128]{1,0:T(8,128)(2,1)S(1)} %get-tuple-element.27), channel_id=1, source_target_pairs={{0,4},{4,0},{8,12},{12,8},{1,5},{5,1},{9,13},{13,9},{2,6},{6,2},{1... | collective-permute-start | bytes 147464 | tf_op jit(solution)/shard_map/ppermute | solution.py:219

commit v5 on v4

--- a/solution.py
+++ b/solution.py
@@ -14,7 +14,7 @@
 LOG2E = 1.4426950408889634
 VMEM = pl.BlockSpec(memory_space=pltpu.VMEM)
 SMEM = pl.BlockSpec(memory_space=pltpu.SMEM)
-ANY = pl.BlockSpec(memory_space=pl.ANY)
+HBM = pl.BlockSpec(memory_space=pltpu.HBM)
 PARAMS = pltpu.CompilerParams(vmem_limit_bytes=16 << 20)
 
 
@@ -79,8 +79,57 @@
     return chosen
 
 
-def table_kernel(n, me_ref, count_ref, offset_ref, live_ref, reach_ref, near_ref):
+def move_all(moves, sem):
+    copies = [pltpu.make_async_copy(src, dst, sem.at[i]) for i, (src, dst) in enumerate(moves)]
+    for copy in copies:
+        copy.start()
+    return copies
+
+
+def sight_moves(video_k, video_v, first, out):
+    rows, cols = video_k.shape[0], pl.ds(first, out.shape[1])
+    return [(video_k.at[:, cols], out.at[:rows]), (video_v.at[:, cols], out.at[rows:])]
+
+
+def sound_moves(audio_k, audio_v, out):
+    rows, width = audio_k.shape[0], out.shape[1]
+    moves = []
+    for src in (audio_k, audio_v):
+        for half in range(2):
+            at = len(moves) * rows
+            moves.append((src.at[:, pl.ds(half * width, width)], out.at[at : at + rows]))
+    return moves
+
+
+def first_pack(n, me_ref, video_k, video_v, audio_k, audio_v, out_ref, over_ref, sem):
     me = me_ref[0]
+    at_end = (me == 0) | (me == n - 1)
+    for role, sight, sound in ((at_end, out_ref, over_ref), (jnp.logical_not(at_end), over_ref, out_ref)):
+
+        @pl.when(role)
+        def _(sight=sight, sound=sound):
+            moves = sight_moves(video_k, video_v, 0, sight) + sound_moves(audio_k, audio_v, sound)
+            for copy in move_all(moves, sem):
+                copy.wait()
+
+
+def second_pack(n, me_ref, count_ref, offset_ref, video_k, video_v, video_q, audio_q, *outs):
+    sight1, sight2, asks0, asks1, live_ref, reach_ref, near_ref, sem = outs
+    rows = video_q.shape[0]
+    moves, at = [], asks0.shape[1]
+    for half, out in enumerate((asks0, asks1)):
+        cols = pl.ds(half * at, at)
+        moves += [(video_q.at[:, cols], out.at[:rows]), (audio_q.at[:, cols], out.at[rows:])]
+    for out in (sight1, sight2):
+        moves += sight_moves(video_k, video_v, at, out)
+        at += out.shape[1]
+    copies = move_all(moves, sem)
+    tables(n, me_ref[0], count_ref, offset_ref, live_ref, reach_ref, near_ref)
+    for copy in copies:
+        copy.wait()
+
+
+def tables(n, me, count_ref, offset_ref, live_ref, reach_ref, near_ref):
     upper = me * 2 >= n
     inner, end = jnp.where(upper, 1, n - 2), jnp.where(upper, 0, n - 1)
     frames = (me, me ^ 1, inner, end)
@@ -103,38 +152,40 @@
 
 
 def audio_kernel(n, me_ref, near_ref, *refs):
-    parts, (b0, b1, inner2, end2, b3, cross_ref, own_ref, mate_ref) = refs[:-8], refs[-8:]
+    asks, (out, over, first, second, across, far, cross_ref, own_ref, mate_ref) = refs[:-9], refs[-9:]
     audio_rows = own_ref.shape[0]
     video_rows = cross_ref.shape[0]
+    width = out.shape[1]
     me = me_ref[0]
     at_end = (me == 0) | (me == n - 1)
 
     def run(blocks, alone):
         near = near_ref[:, : audio_rows * len(blocks)]
-        at = 0
-        for q_own, q_mate in zip(parts[::2], parts[1::2]):
-            for first in range(0, q_own.shape[1], HEAD_DIM):
-                q_cols = slice(first, first + HEAD_DIM)
+        for half in range(2):
+            q_own, q_mate = asks[2 * half], asks[2 * half + 1]
+            key_rows = slice(half * audio_rows, (half + 1) * audio_rows)
+            value_rows = slice((2 + half) * audio_rows, (3 + half) * audio_rows)
+            for at in range(0, width, HEAD_DIM):
                 cols = slice(at, at + HEAD_DIM)
-                keys = jnp.concatenate([b[:audio_rows, cols] for b in blocks], axis=0)
-                values = jnp.concatenate([b[audio_rows:, cols] for b in blocks], axis=0)
-                cross_ref[:, cols] = blend(q_own[:video_rows, q_cols], keys, values, near)
+                to = slice(half * width + at, half * width + at + HEAD_DIM)
+                keys = jnp.concatenate([b[key_rows, cols] for b in blocks], axis=0)
+                values = jnp.concatenate([b[value_rows, cols] for b in blocks], axis=0)
+                cross_ref[:, to] = blend(q_own[:video_rows, cols], keys, values, near)
                 if not alone:
                     both = jnp.concatenate(
-                        [q_own[video_rows:, q_cols], q_mate[video_rows:, q_cols]], axis=0
+                        [q_own[video_rows:, cols], q_mate[video_rows:, cols]], axis=0
                     )
-                    out = blend(both, keys, values, None)
-                    own_ref[:, cols] = out[:audio_rows]
-                    mate_ref[:, cols] = out[audio_rows:]
-                at += HEAD_DIM
+                    mixed = blend(both, keys, values, None)
+                    own_ref[:, to] = mixed[:audio_rows]
+                    mate_ref[:, to] = mixed[audio_rows:]
 
     @pl.when(jnp.logical_not(at_end))
     def _():
-        run((b0, b1, inner2, b3), False)
+        run((out, second, across, far), False)
 
     @pl.when(at_end)
     def _():
-        run((b0, b1, end2), True)
+        run((over, first, second), True)
 
 
 def video_kernel(n, first, me_ref, live_ref, reach_ref, q_own, q_mate, b0, b1, b2, b3, own_ref, mate_ref):
@@ -195,8 +246,8 @@
 
 
 def chunks_of(heads):
-    head = (heads + 1) // 2
-    return head, (heads - head + 1) // 2, (heads - head) // 2
+    head = heads // 2
+    return head, (head + 1) // 2, head // 2
 
 
 def lined(video_q, video_k, video_v, audio_q, audio_k, audio_v, offsets, counts):
@@ -231,39 +282,59 @@
         )(*args)
 
     place = me.astype(jnp.int32).reshape(1)
-    live, reach, near = call(
-        functools.partial(table_kernel, n),
-        (
-            ((1, n * video_rows), jnp.float32),
-            ((2 * audio_rows, n * video_rows), jnp.float32),
-            ((1, n * audio_rows), jnp.float32),
-        ),
-        [SMEM, SMEM, VMEM],
+    video_q, video_k, video_v, audio_q, audio_k, audio_v = (
+        pltpu.with_memory_space_constraint(block, pltpu.HBM)
+        for block in (video_q, video_k, video_v, audio_q, audio_k, audio_v)
+    )
+    at_end = (me == 0) | (me == n - 1)
+    lengths = [size * HEAD_DIM for size in chunks]
+    half = lengths[0]
+    first_out, first_over = call(
+        functools.partial(first_pack, n),
+        (((2 * video_rows, half), jnp.bfloat16),) * 2,
+        [SMEM] + [HBM] * 4,
+        place,
+        video_k,
+        video_v,
+        audio_k,
+        audio_v,
+        out_specs=(VMEM,) * 2,
+        scratch_shapes=[pltpu.SemaphoreType.DMA((6,))],
+    )
+    outs = tuple(((2 * video_rows, length), jnp.bfloat16) for length in lengths[1:])
+    outs += (((rows, half), jnp.bfloat16),) * 2
+    outs += (
+        ((1, n * video_rows), jnp.float32),
+        ((2 * audio_rows, n * video_rows), jnp.float32),
+        ((1, n * audio_rows), jnp.float32),
+    )
+    *sights, asks0, asks1, live, reach, near = call(
+        functools.partial(second_pack, n),
+        outs,
+        [SMEM, SMEM, VMEM] + [HBM] * 4,
         place,
         counts,
         offsets.reshape(1, -1),
-    )
-    split = chunks[0] * HEAD_DIM
-    asks = [
-        jnp.concatenate([video_q[:, cols], audio_q[:, cols]], axis=0)
-        for cols in (slice(0, split), slice(split, width))
-    ]
-    sound = jnp.concatenate([audio_k, audio_v], axis=0)
-    sights, at = [], 0
-    for size in chunks:
-        cols = slice(at * HEAD_DIM, (at + size) * HEAD_DIM)
-        sights.append(jnp.concatenate([video_k[:, cols], video_v[:, cols]], axis=0))
-        at += size
-
-    pieces = range(len(chunks))
-    sight_mate = [mate(sights[i]) for i in pieces]
-    sight_across = [cross(sights[i]) for i in pieces]
-    sight_far = [cross(sight_mate[i]) for i in pieces]
+        video_k,
+        video_v,
+        video_q,
+        audio_q,
+        out_specs=(VMEM,) * len(outs),
+        scratch_shapes=[pltpu.SemaphoreType.DMA((8,))],
+    )
+    asks = [asks0, asks1]
+    sights = [first_over] + sights
+
+    sight_mate = [mate(first_out)]
+    sight_across = [cross(first_over)]
+    sound_across = cross(first_out)
+    second_mate = mate(jnp.where(at_end, first_over, sound_across))
+    sound_far = cross(second_mate)
+    for i in (1, 2):
+        sight_mate.append(mate(sights[i]))
+        sight_across.append(cross(sights[i]))
+    sight_far = [cross(sight_mate[i]) for i in range(3)]
     asks_mate = [mate(asks[i]) for i in range(2)]
-    sound_mate = mate(sound)
-    sound_across = cross(sound)
-    sound_far = cross(sound_mate)
-    sound_passed = mate(sound_across)
 
     mine, back, at = [], [], 0
     for i, size in enumerate(chunks):
@@ -281,6 +352,7 @@
             sight_mate[i],
             sight_across[i],
             sight_far[i],
+            out_specs=(VMEM,) * 2,
             cost_estimate=cost(2 * rows, n * video_rows, size),
         )
         mine.append(own)
@@ -289,18 +361,20 @@
     video_cross, own, theirs = call(
         functools.partial(audio_kernel, n),
         (((video_rows, width), jnp.bfloat16),) + (((audio_rows, width), jnp.bfloat16),) * 2,
-        [SMEM] + [VMEM] * 10,
+        [SMEM] + [VMEM] * 11,
         place,
         near,
         asks[0],
         asks_mate[0],
         asks[1],
         asks_mate[1],
-        sound,
-        sound_mate,
+        first_out,
+        first_over,
+        sight_mate[0],
+        second_mate,
         sound_across,
-        sound_passed,
         sound_far,
+        out_specs=(VMEM,) * 3,
         cost_estimate=cost(2 * rows, n * audio_rows, heads),
     )
     mine = [own] + mine
@@ -313,7 +387,7 @@
         video_cross,
         *mine,
         *back,
-        out_specs=(ANY,) * 4,
+        out_specs=(HBM,) * 4,
         scratch_shapes=[pltpu.SemaphoreType.DMA((2 * len(mine),))],
     )
 
@@ -326,7 +400,8 @@
 
     def whole(*arrays):
         heads = arrays[0].shape[1] // HEAD_DIM // (sizes["tower"] * sizes["mp"])
-        body = lined if line and heads > 3 else gathered
+        paired = heads % 2 == 0 and heads > 3 and arrays[0].shape[0] == 2 * arrays[3].shape[0]
+        body = lined if line and paired else gathered
         return jax.shard_map(
             body, mesh=mesh, in_specs=placed, out_specs=(split,) * 4, check_vma=False
         )(*arrays)

time: 48.9 us -> 43 us (0.88)
  local copies, waits for them, and re-layouts: 5.09 us -> 0.01 us
  waiting for transfers between devices: 14 us -> 11.5 us
  Pallas kernels: 3.34 us -> 5.22 us
    slice x14 -> x0, local copies, waits for them, and re-layouts: 2.61 us -> none  [the longest x12 2.57 us: lined(): sights.append(jnp.concatenate([video_k[:, cols], video_v[:, cols]], axis=0))]
    ppermute x11 -> x10, waiting for transfers between devices: 14 us -> 11.5 us  [mate(): return lax.ppermute(block, 'seq', mate_pairs)]
    unnamed x11 -> x4, local copies, waits for them, and re-layouts: 2.47 us -> 0.01 us
    pallas_call x6 -> x7, Pallas kernels: 3.34 us -> 5.22 us  [call(): pl.pallas_call(kernel, out_shape=tuple((jax.ShapeDtypeStruct(shape, dtype...]
    ppermute x11 -> x10, starting transfers between devices: 23.7 us -> 23.3 us  [mate(): return lax.ppermute(block, 'seq', mate_pairs)]
  transfers between devices with their start and end apart: 19 -> 18, of which waited for: 4 -> 4; matrix products, arithmetic and copies ran while one was open for 0% -> 0% of each run, Pallas kernels for 5% -> 8%
where the time goes in v5:
time: 43 us; the launch traced here: 42.8 us
  starting transfers between devices  25.3 us (59%)
  waiting for transfers between devices  11.5 us (27%)
  Pallas kernels  5.22 us (12%)
  between operations  0.74 us (2%)
    ppermute x10, starting transfers between devices, mate(): return lax.ppermute(block, 'seq', mate_pairs)  23.3 us
    ppermute x10, waiting for transfers between devices, mate(): return lax.ppermute(block, 'seq', mate_pairs)  11.5 us
    pallas_call x7, Pallas kernels, call(): pl.pallas_call(kernel, out_shape=tuple((jax.ShapeDtypeStruct(shape, dtype...  5.22 us
    ppermute x8, starting transfers between devices, cross(): return lax.ppermute(block, ('seq', 'mp'), cross_pairs)  1.99 us
  transfers between devices with their start and end apart: 18, of which 4 were waited for; matrix products, arithmetic and copies ran while one was open for 0% of the time, Pallas kernels for 8%

profile of v5, /device:TPU:0, one launch (start us, length us, event | category | flops | bytes accessed | tf_op | source)
XLA Modules:
  0.0 42.8 jit_solution(17600766859507400442)
XLA Ops:
  0.6 1.0 %shard_map.112 = (bf16[256,384]{1,0:T(8,128)(2,1)S(1)}, bf16[256,384]{1,0:T(8,128)(2,1)S(1)}) custom-call(s32[1]{0:T(128)} %bitcast.me_ref, bf16[128,768]{1,0:T(8,128)(2,1)} %video_k.3, bf16[128,768]{1,0:T(8,128)(2,1)} %video_v.3, bf16[64,768]{1,0:T(8,128)(2,1)} %audio_k.1, bf16[64,768]{1,0:T(8,128)(2,1)} %audio_v.1), custom_call_target="tpu_custom_call" | custom-call | tf_op jit(solution)/shard_map/pallas_call | solution.py:276
  1.7 0.6 %collective-permute-start.3 = (bf16[256,384]{1,0:T(8,128)(2,1)S(1)}, bf16[256,384]{1,0:T(8,128)(2,1)S(1)}, u32[]{:S(2)}, u32[]{:S(2)}) collective-permute-start(bf16[256,384]{1,0:T(8,128)(2,1)S(1)} %get-tuple-element.25.refs_4_), channel_id=1, source_target_pairs={{0,1},{1,0},{4,8},{5,9},{8,4},{9,5},{12,13},{13,12},{2,3},{3,2},{6... | collective-permute-start | bytes 589832 | tf_op jit(solution)/shard_map/ppermute | solution.py:273
  2.2 4.1 %collective-permute-start.2 = (bf16[256,384]{1,0:T(8,128)(2,1)S(1)}, bf16[256,384]{1,0:T(8,128)(2,1)S(1)}, u32[]{:S(2)}, u32[]{:S(2)}) collective-permute-start(bf16[256,384]{1,0:T(8,128)(2,1)S(1)} %get-tuple-element.25.refs_4_), channel_id=1, source_target_pairs={{0,4},{4,0},{8,12},{12,8},{1,5},{5,1},{9,13},{13,9},{2,6},{6,2},{1... | collective-permute-start | bytes 589832 | tf_op jit(solution)/shard_map/ppermute | solution.py:270
  6.4 0.0 collective-permute-done.3.refs_8_
  6.4 0.0 copy-start
  6.4 0.0 copy-start.1
  6.4 5.1 %collective-permute-start.4 = (bf16[256,384]{1,0:T(8,128)(2,1)S(1)}, bf16[256,384]{1,0:T(8,128)(2,1)S(1)}, u32[]{:S(2)}, u32[]{:S(2)}) collective-permute-start(bf16[256,384]{1,0:T(8,128)(2,1)S(1)} %broadcast_select_fusion), channel_id=1, source_target_pairs={{0,4},{4,0},{8,12},{12,8},{1,5},{5,1},{9,13},{13,9},{2,6},{6,2},{1... | collective-permute-start | bytes 589832 | tf_op jit(solution)/shard_map/ppermute | solution.py:270
  11.6 0.0 collective-permute-start.6
  11.6 0.0 copy-done
  11.6 0.0 copy-done.1
  11.6 1.8 %shard_map.111 = (bf16[256,256]{1,0:T(8,128)(2,1)S(1)}, bf16[256,128]{1,0:T(8,128)(2,1)S(1)}, bf16[192,384]{1,0:T(8,128)(2,1)S(1)}, bf16[192,384]{1,0:T(8,128)(2...) custom-call(s32[1]{0:T(128)} %bitcast.me_ref, s32[4]{0:T(128)S(1)} %copy-done.1, ...), custom_call_target="tpu_custom_call" | custom-call | tf_op jit(solution)/shard_map/pallas_call | solution.py:276
  13.4 1.7 %collective-permute-start = (bf16[192,384]{1,0:T(8,128)(2,1)S(1)}, bf16[192,384]{1,0:T(8,128)(2,1)S(1)}, u32[]{:S(2)}, u32[]{:S(2)}) collective-permute-start(bf16[192,384]{1,0:T(8,128)(2,1)S(1)} %get-tuple-element.23.refs_0_.q_own), channel_id=1, source_target_pairs={{0,4},{4,0},{8,12},{12,8},{1,5},{5,1},{9,13},{13,9},{2,6},{6,2},{1... | collective-permute-start | bytes 442376 | tf_op jit(solution)/shard_map/ppermute | solution.py:270
  15.1 0.4 collective-permute-start.8
  15.5 0.0 collective-permute-done.2.refs_6_.b1
  15.5 0.0 collective-permute-start.7
  15.5 0.1 collective-permute-done.4.refs_7_
  15.6 0.4 collective-permute-start.5
  16.0 6.5 %collective-permute-done.8.b1 = bf16[256,256]{1,0:T(8,128)(2,1)S(1)} collective-permute-done((bf16[256,256]{1,0:T(8,128)(2,1)S(1)}, bf16[256,256]{1,0:T(8,128)(2,1)S(1)}, u32[]{:S(2)}, u32[]{:S(2)}) %collective-permute-start.8) | collective-permute-done | bytes 131104 | tf_op jit(solution)/shard_map/ppermute | solution.py:270
  22.5 0.8 %collective-permute-start.1 = (bf16[192,384]{1,0:T(8,128)(2,1)S(1)}, bf16[192,384]{1,0:T(8,128)(2,1)S(1)}, u32[]{:S(2)}, u32[]{:S(2)}) collective-permute-start(bf16[192,384]{1,0:T(8,128)(2,1)S(1)} %get-tuple-element.24.refs_2_.q_own), channel_id=1, source_target_pairs={{0,4},{4,0},{8,12},{12,8},{1,5},{5,1},{9,13},{13,9},{2,6},{6,2},{1... | collective-permute-start | bytes 442376 | tf_op jit(solution)/shard_map/ppermute | solution.py:270
  23.3 0.0 collective-permute-done.refs_1_.q_mate
  23.3 0.0 collective-permute-start.9
  23.3 0.0 collective-permute-done.6.b2
  23.3 0.5 %collective-permute-start.10 = (bf16[256,256]{1,0:T(8,128)(2,1)S(1)}, bf16[256,256]{1,0:T(8,128)(2,1)S(1)}, u32[]{:S(2)}, u32[]{:S(2)}) collective-permute-start(bf16[256,256]{1,0:T(8,128)(2,1)S(1)} %collective-permute-done.8.b1), channel_id=1, source_target_pairs={{0,1},{1,0},{4,8},{5,9},{8,4},{9,5},{12,13},{13,12},{2,3},{3,2},{6... | collective-permute-start | bytes 393224 | tf_op jit(solution)/shard_map/ppermute | solution.py:273
  23.8 0.0 collective-permute-done.7.b3
  23.8 2.8 %collective-permute-start.11 = (bf16[256,128]{1,0:T(8,128)(2,1)S(1)}, bf16[256,128]{1,0:T(8,128)(2,1)S(1)}, u32[]{:S(2)}, u32[]{:S(2)}) collective-permute-start(bf16[256,128]{1,0:T(8,128)(2,1)S(1)} %get-tuple-element.34.b0), channel_id=1, source_target_pairs={{0,4},{4,0},{8,12},{12,8},{1,5},{5,1},{9,13},{13,9},{2,6},{6,2},{1... | collective-permute-start | bytes 196616 | tf_op jit(solution)/shard_map/ppermute | solution.py:270
  26.6 2.7 %collective-permute-done.11.b1 = bf16[256,128]{1,0:T(8,128)(2,1)S(1)} collective-permute-done((bf16[256,128]{1,0:T(8,128)(2,1)S(1)}, bf16[256,128]{1,0:T(8,128)(2,1)S(1)}, u32[]{:S(2)}, u32[]{:S(2)}) %collective-permute-start.11) | collective-permute-done | bytes 65568 | tf_op jit(solution)/shard_map/ppermute | solution.py:270
  29.3 1.5 %collective-permute-start.15 = (bf16[192,384]{1,0:T(8,128)(2,1)S(1)}, bf16[192,384]{1,0:T(8,128)(2,1)S(1)}, u32[]{:S(2)}, u32[]{:S(2)}) collective-permute-start(bf16[192,384]{1,0:T(8,128)(2,1)S(1)} %get-tuple-element.37), channel_id=1, source_target_pairs={{0,4},{4,0},{8,12},{12,8},{1,5},{5,1},{9,13},{13,9},{2,6},{6,2},{1... | collective-permute-start | bytes 442376 | tf_op jit(solution)/shard_map/ppermute | solution.py:270
  30.9 0.0 collective-permute-done.9.b2
  30.9 0.0 collective-permute-start.12
  30.9 0.0 collective-permute-done.1.refs_3_.q_mate
  30.9 0.5 %collective-permute-start.13 = (bf16[256,128]{1,0:T(8,128)(2,1)S(1)}, bf16[256,128]{1,0:T(8,128)(2,1)S(1)}, u32[]{:S(2)}, u32[]{:S(2)}) collective-permute-start(bf16[256,128]{1,0:T(8,128)(2,1)S(1)} %collective-permute-done.11.b1), channel_id=1, source_target_pairs={{0,1},{1,0},{4,8},{5,9},{8,4},{9,5},{12,13},{13,12},{2,3},{3,2},{6... | collective-permute-start | bytes 196616 | tf_op jit(solution)/shard_map/ppermute | solution.py:273
  31.4 0.0 collective-permute-done.10.b3
  31.4 3.8 %collective-permute-start.16 = (bf16[192,256]{1,0:T(8,128)(2,1)S(1)}, bf16[192,256]{1,0:T(8,128)(2,1)S(1)}, u32[]{:S(2)}, u32[]{:S(2)}) collective-permute-start(bf16[192,256]{1,0:T(8,128)(2,1)S(1)} %get-tuple-element.38), channel_id=1, source_target_pairs={{0,4},{4,0},{8,12},{12,8},{1,5},{5,1},{9,13},{13,9},{2,6},{6,2},{1... | collective-permute-start | bytes 294920 | tf_op jit(solution)/shard_map/ppermute | solution.py:270
  35.2 0.0 collective-permute-done.5.refs_9_
  35.2 1.5 %shard_map.113 = (bf16[128,768]{1,0:T(8,128)(2,1)S(1)}, bf16[64,768]{1,0:T(8,128)(2,1)S(1)}, bf16[64,768]{1,0:T(8,128)(2,1)S(1)}) custom-call(s32[1]{0:T(128)} %bitcast.me_ref, f32[1,256]{1,0:T(1,128)S(1)} %get-tuple-element.22.near_ref, bf16[192,384]{1,0:T(8,128)(2,1)S(1)} %get-tuple-element.23.refs_0_.q_own, ...), custom_call_target="tpu_custom_call" | custom-call | flops 301989888 | bytes 1179648 | tf_op jit(solution)/shard_map/pallas_call | solution.py:276
  36.7 0.1 collective-permute-start.14
  36.8 0.0 collective-permute-done.12.b2
  36.8 0.0 collective-permute-done.13.b3
  36.8 3.0 %collective-permute-start.17 = (bf16[192,128]{1,0:T(8,128)(2,1)S(1)}, bf16[192,128]{1,0:T(8,128)(2,1)S(1)}, u32[]{:S(2)}, u32[]{:S(2)}) collective-permute-start(bf16[192,128]{1,0:T(8,128)(2,1)S(1)} %get-tuple-element.39), channel_id=1, source_target_pairs={{0,4},{4,0},{8,12},{12,8},{1,5},{5,1},{9,13},{13,9},{2,6},{6,2},{1... | collective-permute-start | bytes 147464 | tf_op jit(solution)/shard_map/ppermute | solution.py:270
  39.8 2.1 %collective-permute-done.17.refs_7_ = bf16[192,128]{1,0:T(8,128)(2,1)S(1)} collective-permute-done((bf16[192,128]{1,0:T(8,128)(2,1)S(1)}, bf16[192,128]{1,0:T(8,128)(2,1)S(1)}, u32[]{:S(2)}, u32[]{:S(2)}) %collective-permute-start.17) | collective-permute-done | bytes 49184 | tf_op jit(solution)/shard_map/ppermute | solution.py:270
  41.9 0.0 collective-permute-done.16.refs_6_
  41.9 0.0 collective-permute-done.15.refs_5_
  41.9 0.0 collective-permute-done.14.refs_4_
  41.9 0.9 %shard_map.117 = (bf16[128,768]{1,0:T(8,128)(2,1)}, bf16[128,768]{1,0:T(8,128)(2,1)}, bf16[64,768]{1,0:T(8,128)(2,1)}, bf16[64,768]{1,0:T(8,128)(2,1)}) custom-call(s32[1]{0:T(128)} %bitcast.me_ref, bf16[128,768]{1,0:T(8,128)(2,1)S(1)} %get-tuple-element.27.cross, bf16[64,768]{1,0:T(8,128)(2,1)S(1)} %get-tuple-element.28.refs_0_, ...), custom_call_target="tpu_custom_call" | custom-call | tf_op jit(solution)/shard_map/pallas_call | solution.py:276
  (4 shorter events, 0.0 us)
Async XLA Ops:
  1.7 4.7 %collective-permute-start.3 = (bf16[256,384]{1,0:T(8,128)(2,1)S(1)}, bf16[256,384]{1,0:T(8,128)(2,1)S(1)}, u32[]{:S(2)}, u32[]{:S(2)}) collective-permute-start(bf16[256,384]{1,0:T(8,128)(2,1)S(1)} %get-tuple-element.25.refs_4_), channel_id=1, source_target_pairs={{0,1},{1,0},{4,8},{5,9},{8,4},{9,5},{12,13},{13,12},{2,3},{3,2},{6... | collective-permute-start | bytes 589832 | tf_op jit(solution)/shard_map/ppermute | solution.py:273
  2.2 13.3 %collective-permute-start.2 = (bf16[256,384]{1,0:T(8,128)(2,1)S(1)}, bf16[256,384]{1,0:T(8,128)(2,1)S(1)}, u32[]{:S(2)}, u32[]{:S(2)}) collective-permute-start(bf16[256,384]{1,0:T(8,128)(2,1)S(1)} %get-tuple-element.25.refs_4_), channel_id=1, source_target_pairs={{0,4},{4,0},{8,12},{12,8},{1,5},{5,1},{9,13},{13,9},{2,6},{6,2},{1... | collective-permute-start | bytes 589832 | tf_op jit(solution)/shard_map/ppermute | solution.py:270
  6.4 5.2 %copy-start = (s32[256]{0:T(256)S(1)}, s32[256]{0:T(256)}, u32[]{:S(2)}) copy-start(s32[256]{0:T(256)} %param.14) | copy-start | bytes 3076
  6.4 5.1 %copy-start.1 = (s32[4]{0:T(128)S(1)}, s32[4]{0:T(128)}, u32[]{:S(2)}) copy-start(s32[4]{0:T(128)} %count_ref.1) | copy-start | bytes 52
  6.4 9.2 %collective-permute-start.4 = (bf16[256,384]{1,0:T(8,128)(2,1)S(1)}, bf16[256,384]{1,0:T(8,128)(2,1)S(1)}, u32[]{:S(2)}, u32[]{:S(2)}) collective-permute-start(bf16[256,384]{1,0:T(8,128)(2,1)S(1)} %broadcast_select_fusion), channel_id=1, source_target_pairs={{0,4},{4,0},{8,12},{12,8},{1,5},{5,1},{9,13},{13,9},{2,6},{6,2},{1... | collective-permute-start | bytes 589832 | tf_op jit(solution)/shard_map/ppermute | solution.py:270
  11.6 11.8 %collective-permute-start.6 = (bf16[256,384]{1,0:T(8,128)(2,1)S(1)}, bf16[256,384]{1,0:T(8,128)(2,1)S(1)}, u32[]{:S(2)}, u32[]{:S(2)}) collective-permute-start(bf16[256,384]{1,0:T(8,128)(2,1)S(1)} %get-tuple-element.26.refs_5_.b0), channel_id=1, source_target_pairs={{0,1},{1,0},{4,8},{5,9},{8,4},{9,5},{12,13},{13,12},{2,3},{3,2},{6... | collective-permute-start | bytes 589832 | tf_op jit(solution)/shard_map/ppermute | solution.py:273
  13.4 9.9 %collective-permute-start = (bf16[192,384]{1,0:T(8,128)(2,1)S(1)}, bf16[192,384]{1,0:T(8,128)(2,1)S(1)}, u32[]{:S(2)}, u32[]{:S(2)}) collective-permute-start(bf16[192,384]{1,0:T(8,128)(2,1)S(1)} %get-tuple-element.23.refs_0_.q_own), channel_id=1, source_target_pairs={{0,4},{4,0},{8,12},{12,8},{1,5},{5,1},{9,13},{13,9},{2,6},{6,2},{1... | collective-permute-start | bytes 442376 | tf_op jit(solution)/shard_map/ppermute | solution.py:270
  15.1 7.4 %collective-permute-start.8 = (bf16[256,256]{1,0:T(8,128)(2,1)S(1)}, bf16[256,256]{1,0:T(8,128)(2,1)S(1)}, u32[]{:S(2)}, u32[]{:S(2)}) collective-permute-start(bf16[256,256]{1,0:T(8,128)(2,1)S(1)} %get-tuple-element.32.b0), channel_id=1, source_target_pairs={{0,4},{4,0},{8,12},{12,8},{1,5},{5,1},{9,13},{13,9},{2,6},{6,2},{1... | collective-permute-start | bytes 393224 | tf_op jit(solution)/shard_map/ppermute | solution.py:270
  15.5 8.3 %collective-permute-start.7 = (bf16[256,384]{1,0:T(8,128)(2,1)S(1)}, bf16[256,384]{1,0:T(8,128)(2,1)S(1)}, u32[]{:S(2)}, u32[]{:S(2)}) collective-permute-start(bf16[256,384]{1,0:T(8,128)(2,1)S(1)} %collective-permute-done.2.refs_6_.b1), channel_id=1, source_target_pairs={{0,1},{1,0},{4,8},{5,9},{8,4},{9,5},{12,13},{13,12},{2,3},{3,2},{6... | collective-permute-start | bytes 589832 | tf_op jit(solution)/shard_map/ppermute | solution.py:273
  15.6 19.6 %collective-permute-start.5 = (bf16[256,384]{1,0:T(8,128)(2,1)S(1)}, bf16[256,384]{1,0:T(8,128)(2,1)S(1)}, u32[]{:S(2)}, u32[]{:S(2)}) collective-permute-start(bf16[256,384]{1,0:T(8,128)(2,1)S(1)} %collective-permute-done.4.refs_7_), channel_id=1, source_target_pairs={{0,1},{1,0},{4,8},{5,9},{8,4},{9,5},{12,13},{13,12},{2,3},{3,2},{6... | collective-permute-start | bytes 589832 | tf_op jit(solution)/shard_map/ppermute | solution.py:273
  22.5 8.3 %collective-permute-start.1 = (bf16[192,384]{1,0:T(8,128)(2,1)S(1)}, bf16[192,384]{1,0:T(8,128)(2,1)S(1)}, u32[]{:S(2)}, u32[]{:S(2)}) collective-permute-start(bf16[192,384]{1,0:T(8,128)(2,1)S(1)} %get-tuple-element.24.refs_2_.q_own), channel_id=1, source_target_pairs={{0,4},{4,0},{8,12},{12,8},{1,5},{5,1},{9,13},{13,9},{2,6},{6,2},{1... | collective-permute-start | bytes 442376 | tf_op jit(solution)/shard_map/ppermute | solution.py:270
  23.3 7.6 %collective-permute-start.9 = (bf16[256,256]{1,0:T(8,128)(2,1)S(1)}, bf16[256,256]{1,0:T(8,128)(2,1)S(1)}, u32[]{:S(2)}, u32[]{:S(2)}) collective-permute-start(bf16[256,256]{1,0:T(8,128)(2,1)S(1)} %get-tuple-element.32.b0), channel_id=1, source_target_pairs={{0,1},{1,0},{4,8},{5,9},{8,4},{9,5},{12,13},{13,12},{2,3},{3,2},{6... | collective-permute-start | bytes 393224 | tf_op jit(solution)/shard_map/ppermute | solution.py:273
  23.3 8.1 %collective-permute-start.10 = (bf16[256,256]{1,0:T(8,128)(2,1)S(1)}, bf16[256,256]{1,0:T(8,128)(2,1)S(1)}, u32[]{:S(2)}, u32[]{:S(2)}) collective-permute-start(bf16[256,256]{1,0:T(8,128)(2,1)S(1)} %collective-permute-done.8.b1), channel_id=1, source_target_pairs={{0,1},{1,0},{4,8},{5,9},{8,4},{9,5},{12,13},{13,12},{2,3},{3,2},{6... | collective-permute-start | bytes 393224 | tf_op jit(solution)/shard_map/ppermute | solution.py:273
  23.8 5.5 %collective-permute-start.11 = (bf16[256,128]{1,0:T(8,128)(2,1)S(1)}, bf16[256,128]{1,0:T(8,128)(2,1)S(1)}, u32[]{:S(2)}, u32[]{:S(2)}) collective-permute-start(bf16[256,128]{1,0:T(8,128)(2,1)S(1)} %get-tuple-element.34.b0), channel_id=1, source_target_pairs={{0,4},{4,0},{8,12},{12,8},{1,5},{5,1},{9,13},{13,9},{2,6},{6,2},{1... | collective-permute-start | bytes 196616 | tf_op jit(solution)/shard_map/ppermute | solution.py:270
  29.3 12.6 %collective-permute-start.15 = (bf16[192,384]{1,0:T(8,128)(2,1)S(1)}, bf16[192,384]{1,0:T(8,128)(2,1)S(1)}, u32[]{:S(2)}, u32[]{:S(2)}) collective-permute-start(bf16[192,384]{1,0:T(8,128)(2,1)S(1)} %get-tuple-element.37), channel_id=1, source_target_pairs={{0,4},{4,0},{8,12},{12,8},{1,5},{5,1},{9,13},{13,9},{2,6},{6,2},{1... | collective-permute-start | bytes 442376 | tf_op jit(solution)/shard_map/ppermute | solution.py:270
  30.9 5.9 %collective-permute-start.12 = (bf16[256,128]{1,0:T(8,128)(2,1)S(1)}, bf16[256,128]{1,0:T(8,128)(2,1)S(1)}, u32[]{:S(2)}, u32[]{:S(2)}) collective-permute-start(bf16[256,128]{1,0:T(8,128)(2,1)S(1)} %get-tuple-element.34.b0), channel_id=1, source_target_pairs={{0,1},{1,0},{4,8},{5,9},{8,4},{9,5},{12,13},{13,12},{2,3},{3,2},{6... | collective-permute-start | bytes 196616 | tf_op jit(solution)/shard_map/ppermute | solution.py:273
  30.9 5.9 %collective-permute-start.13 = (bf16[256,128]{1,0:T(8,128)(2,1)S(1)}, bf16[256,128]{1,0:T(8,128)(2,1)S(1)}, u32[]{:S(2)}, u32[]{:S(2)}) collective-permute-start(bf16[256,128]{1,0:T(8,128)(2,1)S(1)} %collective-permute-done.11.b1), channel_id=1, source_target_pairs={{0,1},{1,0},{4,8},{5,9},{8,4},{9,5},{12,13},{13,12},{2,3},{3,2},{6... | collective-permute-start | bytes 196616 | tf_op jit(solution)/shard_map/ppermute | solution.py:273
  31.4 10.6 %collective-permute-start.16 = (bf16[192,256]{1,0:T(8,128)(2,1)S(1)}, bf16[192,256]{1,0:T(8,128)(2,1)S(1)}, u32[]{:S(2)}, u32[]{:S(2)}) collective-permute-start(bf16[192,256]{1,0:T(8,128)(2,1)S(1)} %get-tuple-element.38), channel_id=1, source_target_pairs={{0,4},{4,0},{8,12},{12,8},{1,5},{5,1},{9,13},{13,9},{2,6},{6,2},{1... | collective-permute-start | bytes 294920 | tf_op jit(solution)/shard_map/ppermute | solution.py:270
  36.7 5.2 %collective-permute-start.14 = (bf16[64,768]{1,0:T(8,128)(2,1)S(1)}, bf16[64,768]{1,0:T(8,128)(2,1)S(1)}, u32[]{:S(2)}, u32[]{:S(2)}) collective-permute-start(bf16[64,768]{1,0:T(8,128)(2,1)S(1)} %get-tuple-element.36), channel_id=1, source_target_pairs={{0,4},{4,0},{8,12},{12,8},{1,5},{5,1},{9,13},{13,9},{2,6},{6,2},{1... | collective-permute-start | bytes 294920 | tf_op jit(solution)/shard_map/ppermute | solution.py:270
  36.8 5.1 %collective-permute-start.17 = (bf16[192,128]{1,0:T(8,128)(2,1)S(1)}, bf16[192,128]{1,0:T(8,128)(2,1)S(1)}, u32[]{:S(2)}, u32[]{:S(2)}) collective-permute-start(bf16[192,128]{1,0:T(8,128)(2,1)S(1)} %get-tuple-element.39), channel_id=1, source_target_pairs={{0,4},{4,0},{8,12},{12,8},{1,5},{5,1},{9,13},{13,9},{2,6},{6,2},{1... | collective-permute-start | bytes 147464 | tf_op jit(solution)/shard_map/ppermute | solution.py:270

commit v6 on v5

--- a/solution.py
+++ b/solution.py
@@ -151,33 +151,46 @@
         reach_ref[:, cols] = jnp.where(jnp.abs(asking - frame) <= SPAN, live, MASKED)
 
 
-def audio_kernel(n, me_ref, near_ref, *refs):
-    asks, (out, over, first, second, across, far, cross_ref, own_ref, mate_ref) = refs[:-9], refs[-9:]
-    audio_rows = own_ref.shape[0]
-    video_rows = cross_ref.shape[0]
-    width = out.shape[1]
+def sound_blocks(blocks, audio_rows, half, cols):
+    key_rows = slice(half * audio_rows, (half + 1) * audio_rows)
+    value_rows = slice((2 + half) * audio_rows, (3 + half) * audio_rows)
+    keys = jnp.concatenate([b[key_rows, cols] for b in blocks], axis=0)
+    values = jnp.concatenate([b[value_rows, cols] for b in blocks], axis=0)
+    return keys, values
+
+
+def audio_mate_kernel(n, me_ref, asks0, asks1, out, second, across, far, mate_ref):
+    audio_rows, width = mate_ref.shape[0], out.shape[1]
+    video_rows = asks0.shape[0] - audio_rows
     me = me_ref[0]
-    at_end = (me == 0) | (me == n - 1)
-
-    def run(blocks, alone):
-        near = near_ref[:, : audio_rows * len(blocks)]
-        for half in range(2):
-            q_own, q_mate = asks[2 * half], asks[2 * half + 1]
-            key_rows = slice(half * audio_rows, (half + 1) * audio_rows)
-            value_rows = slice((2 + half) * audio_rows, (3 + half) * audio_rows)
+
+    @pl.when((me > 0) & (me < n - 1))
+    def _():
+        for half, asks in enumerate((asks0, asks1)):
             for at in range(0, width, HEAD_DIM):
                 cols = slice(at, at + HEAD_DIM)
                 to = slice(half * width + at, half * width + at + HEAD_DIM)
-                keys = jnp.concatenate([b[key_rows, cols] for b in blocks], axis=0)
-                values = jnp.concatenate([b[value_rows, cols] for b in blocks], axis=0)
-                cross_ref[:, to] = blend(q_own[:video_rows, cols], keys, values, near)
+                keys, values = sound_blocks((out, second, across, far), audio_rows, half, cols)
+                mate_ref[:, to] = blend(asks[video_rows:, cols], keys, values, None)
+
+
+def audio_own_kernel(n, me_ref, near_ref, asks0, asks1, out, over, first, second, across, far, *outs):
+    cross_ref, own_ref = outs
+    audio_rows, width = own_ref.shape[0], out.shape[1]
+    video_rows = cross_ref.shape[0]
+    me = me_ref[0]
+    at_end = (me == 0) | (me == n - 1)
+
+    def run(blocks, alone):
+        near = near_ref[:, : audio_rows * len(blocks)]
+        for half, asks in enumerate((asks0, asks1)):
+            for at in range(0, width, HEAD_DIM):
+                cols = slice(at, at + HEAD_DIM)
+                to = slice(half * width + at, half * width + at + HEAD_DIM)
+                keys, values = sound_blocks(blocks, audio_rows, half, cols)
+                cross_ref[:, to] = blend(asks[:video_rows, cols], keys, values, near)
                 if not alone:
-                    both = jnp.concatenate(
-                        [q_own[video_rows:, cols], q_mate[video_rows:, cols]], axis=0
-                    )
-                    mixed = blend(both, keys, values, None)
-                    own_ref[:, to] = mixed[:audio_rows]
-                    mate_ref[:, to] = mixed[audio_rows:]
+                    own_ref[:, to] = blend(asks[video_rows:, cols], keys, values, None)
 
     @pl.when(jnp.logical_not(at_end))
     def _():
@@ -188,25 +201,27 @@
         run((over, first, second), True)
 
 
-def video_kernel(n, first, me_ref, live_ref, reach_ref, q_own, q_mate, b0, b1, b2, b3, own_ref, mate_ref):
-    video_rows = b0.shape[0] // 2
-    audio_rows = q_own.shape[0] - video_rows
+def video_kernel(n, who, at, shift, me_ref, live_ref, reach_ref, asks, own, mate, keys2, values2, far, out_ref):
+    video_rows = own.shape[0] // 2
+    audio_rows = asks.shape[0] - video_rows
     me = me_ref[0]
 
     @pl.when((me > 0) & (me < n - 1))
     def _():
-        for head in range(b0.shape[1] // HEAD_DIM):
+        for head in range(own.shape[1] // HEAD_DIM):
             cols = slice(head * HEAD_DIM, (head + 1) * HEAD_DIM)
-            q_cols = slice((first + head) * HEAD_DIM, (first + head + 1) * HEAD_DIM)
-            keys = jnp.concatenate([b[:video_rows, cols] for b in (b0, b1, b2, b3)], axis=0)
-            values = jnp.concatenate([b[video_rows:, cols] for b in (b0, b1, b2, b3)], axis=0)
-            for q_ref, o_ref in ((q_own, own_ref), (q_mate, mate_ref)):
-                queries = q_ref[:video_rows, q_cols]
-                o_ref[:video_rows, cols] = blend(queries, keys, values, live_ref[...])
-            both = jnp.concatenate([q_own[video_rows:, q_cols], q_mate[video_rows:, q_cols]], axis=0)
-            out = blend(both, keys, values, reach_ref[...])
-            own_ref[video_rows:, cols] = out[:audio_rows]
-            mate_ref[video_rows:, cols] = out[audio_rows:]
+            all_cols = slice((at + head) * HEAD_DIM, (at + head + 1) * HEAD_DIM)
+            q_cols = slice((at - shift + head) * HEAD_DIM, (at - shift + head + 1) * HEAD_DIM)
+            top, low = slice(0, video_rows), slice(video_rows, 2 * video_rows)
+            keys = jnp.concatenate(
+                [own[top, cols], mate[top, cols], keys2[:, all_cols], far[top, cols]], axis=0
+            )
+            values = jnp.concatenate(
+                [own[low, cols], mate[low, cols], values2[:, all_cols], far[low, cols]], axis=0
+            )
+            reach = reach_ref[who * audio_rows : (who + 1) * audio_rows, :]
+            out_ref[:video_rows, cols] = blend(asks[:video_rows, q_cols], keys, values, live_ref[...])
+            out_ref[video_rows:, cols] = blend(asks[video_rows:, q_cols], keys, values, reach)
 
 
 def place_kernel(n_frames, video_rows, me_ref, cross, *refs):
@@ -282,6 +297,7 @@
         )(*args)
 
     place = me.astype(jnp.int32).reshape(1)
+    raw_keys, raw_values = video_k, video_v
     video_q, video_k, video_v, audio_q, audio_k, audio_v = (
         pltpu.with_memory_space_constraint(block, pltpu.HBM)
         for block in (video_q, video_k, video_v, audio_q, audio_k, audio_v)
@@ -325,57 +341,66 @@
     asks = [asks0, asks1]
     sights = [first_over] + sights
 
+    keys_across = cross(raw_keys)
+    values_across = cross(raw_values)
     sight_mate = [mate(first_out)]
-    sight_across = [cross(first_over)]
     sound_across = cross(first_out)
     second_mate = mate(jnp.where(at_end, first_over, sound_across))
     sound_far = cross(second_mate)
-    for i in (1, 2):
-        sight_mate.append(mate(sights[i]))
-        sight_across.append(cross(sights[i]))
+    sight_mate += [mate(sights[i]) for i in (1, 2)]
     sight_far = [cross(sight_mate[i]) for i in range(3)]
     asks_mate = [mate(asks[i]) for i in range(2)]
 
-    mine, back, at = [], [], 0
-    for i, size in enumerate(chunks):
+    def look(who, i, queries):
+        at, size = sum(chunks[:i]), chunks[i]
         half = min(i, 1)
-        own, theirs = call(
-            functools.partial(video_kernel, n, at - half * chunks[0]),
-            (((rows, size * HEAD_DIM), jnp.bfloat16),) * 2,
+        return call(
+            functools.partial(video_kernel, n, who, at, half * chunks[0]),
+            (((rows, size * HEAD_DIM), jnp.bfloat16),),
             [SMEM] + [VMEM] * 8,
             place,
             live,
             reach,
-            asks[half],
-            asks_mate[half],
+            queries[half],
             sights[i],
             sight_mate[i],
-            sight_across[i],
+            keys_across,
+            values_across,
             sight_far[i],
-            out_specs=(VMEM,) * 2,
-            cost_estimate=cost(2 * rows, n * video_rows, size),
-        )
-        mine.append(own)
-        back.append(mate(theirs))
-        at += size
-    video_cross, own, theirs = call(
-        functools.partial(audio_kernel, n),
-        (((video_rows, width), jnp.bfloat16),) + (((audio_rows, width), jnp.bfloat16),) * 2,
-        [SMEM] + [VMEM] * 11,
+            out_specs=(VMEM,),
+            cost_estimate=cost(rows, n * video_rows, size),
+        )[0]
+
+    back = [mate(look(1, i, asks_mate)) for i in range(3)]
+    mine = [look(0, i, asks) for i in range(3)]
+    theirs = call(
+        functools.partial(audio_mate_kernel, n),
+        (((audio_rows, width), jnp.bfloat16),),
+        [SMEM] + [VMEM] * 6,
+        place,
+        *asks_mate,
+        first_out,
+        second_mate,
+        sound_across,
+        sound_far,
+        out_specs=(VMEM,),
+        cost_estimate=cost(audio_rows, n * audio_rows, heads),
+    )[0]
+    video_cross, own = call(
+        functools.partial(audio_own_kernel, n),
+        (((video_rows, width), jnp.bfloat16), ((audio_rows, width), jnp.bfloat16)),
+        [SMEM] + [VMEM] * 9,
         place,
         near,
-        asks[0],
-        asks_mate[0],
-        asks[1],
-        asks_mate[1],
+        *asks,
         first_out,
         first_over,
         sight_mate[0],
         second_mate,
         sound_across,
         sound_far,
-        out_specs=(VMEM,) * 3,
-        cost_estimate=cost(2 * rows, n * audio_rows, heads),
+        out_specs=(VMEM,) * 2,
+        cost_estimate=cost(rows, n * audio_rows, heads),
     )
     mine = [own] + mine
     back = [mate(theirs)] + back

time: 43 us -> 42.9 us (level); the launches traced: 42.8 us -> 42.2 us
  waiting for transfers between devices: 11.5 us -> 8.24 us
  starting transfers between devices: 25.3 us -> 27.9 us
    ppermute x10, starting transfers between devices: 23.3 us -> 26.8 us  [mate(): return lax.ppermute(block, 'seq', mate_pairs)]
    ppermute x10, waiting for transfers between devices: 11.5 us -> 8.22 us  [mate(): return lax.ppermute(block, 'seq', mate_pairs)]
    ppermute x8 -> x7, starting transfers between devices: 1.99 us -> 1.08 us  [cross(): return lax.ppermute(block, ('seq', 'mp'), cross_pairs)]
    pallas_call x7 -> x11, Pallas kernels: 5.22 us -> 5.21 us  [call(): pl.pallas_call(kernel, out_shape=tuple((jax.ShapeDtypeStruct(shape, dtype...]
  transfers between devices with their start and end apart: 18 -> 17, of which waited for: 4 -> 4; matrix products, arithmetic and copies ran while one was open for 0% -> 0% of each run, Pallas kernels for 8% -> 8%
where the time goes in v6:
time: 42.9 us; the launch traced here: 42.2 us
  starting transfers between devices  27.9 us (65%)
  waiting for transfers between devices  8.24 us (19%)
  Pallas kernels  5.21 us (12%)
  between operations  0.77 us (2%)
    ppermute x10, starting transfers between devices, mate(): return lax.ppermute(block, 'seq', mate_pairs)  26.8 us
    ppermute x10, waiting for transfers between devices, mate(): return lax.ppermute(block, 'seq', mate_pairs)  8.22 us
    pallas_call x11, Pallas kernels, call(): pl.pallas_call(kernel, out_shape=tuple((jax.ShapeDtypeStruct(shape, dtype...  5.21 us
    ppermute x7, starting transfers between devices, cross(): return lax.ppermute(block, ('seq', 'mp'), cross_pairs)  1.08 us
  transfers between devices with their start and end apart: 17, of which 4 were waited for; matrix products, arithmetic and copies ran while one was open for 0% of the time, Pallas kernels for 8%

profile of v6, /device:TPU:0, one launch (start us, length us, event | category | flops | bytes accessed | tf_op | source)
XLA Modules:
  0.0 42.2 jit_solution(13459039183810849004)
XLA Ops:
  0.6 1.0 %shard_map.112 = (bf16[256,384]{1,0:T(8,128)(2,1)S(1)}, bf16[256,384]{1,0:T(8,128)(2,1)S(1)}) custom-call(s32[1]{0:T(128)} %bitcast.me_ref, bf16[128,768]{1,0:T(8,128)(2,1)} %video_k.3, bf16[128,768]{1,0:T(8,128)(2,1)} %video_v.3, bf16[64,768]{1,0:T(8,128)(2,1)} %audio_k.1, bf16[64,768]{1,0:T(8,128)(2,1)} %audio_v.1), custom_call_target="tpu_custom_call" | custom-call | tf_op jit(solution)/shard_map/pallas_call | solution.py:291
  1.7 0.0 copy-start
  1.7 0.0 copy-start.1
  1.7 0.6 %collective-permute-start.1 = (bf16[256,384]{1,0:T(8,128)(2,1)S(1)}, bf16[256,384]{1,0:T(8,128)(2,1)S(1)}, u32[]{:S(2)}, u32[]{:S(2)}) collective-permute-start(bf16[256,384]{1,0:T(8,128)(2,1)S(1)} %get-tuple-element.18.out), channel_id=1, source_target_pairs={{0,1},{1,0},{4,8},{5,9},{8,4},{9,5},{12,13},{13,12},{2,3},{3,2},{6... | collective-permute-start | bytes 589832 | tf_op jit(solution)/shard_map/ppermute | solution.py:288
  2.2 4.1 %collective-permute-start = (bf16[256,384]{1,0:T(8,128)(2,1)S(1)}, bf16[256,384]{1,0:T(8,128)(2,1)S(1)}, u32[]{:S(2)}, u32[]{:S(2)}) collective-permute-start(bf16[256,384]{1,0:T(8,128)(2,1)S(1)} %get-tuple-element.18.out), channel_id=1, source_target_pairs={{0,4},{4,0},{8,12},{12,8},{1,5},{5,1},{9,13},{13,9},{2,6},{6,2},{1... | collective-permute-start | bytes 589832 | tf_op jit(solution)/shard_map/ppermute | solution.py:285
  6.4 0.0 copy-done
  6.4 0.0 copy-done.1
  6.4 1.8 %shard_map.111 = (bf16[256,256]{1,0:T(8,128)(2,1)S(1)}, bf16[256,128]{1,0:T(8,128)(2,1)S(1)}, bf16[192,384]{1,0:T(8,128)(2,1)S(1)}, bf16[192,384]{1,0:T(8,128)(2...) custom-call(s32[1]{0:T(128)} %bitcast.me_ref, s32[4]{0:T(128)S(1)} %copy-done.1, ...), custom_call_target="tpu_custom_call" | custom-call | tf_op jit(solution)/shard_map/pallas_call | solution.py:291
  8.2 0.1 collective-permute-start.7
  8.3 0.0 collective-permute-done.1.across
  8.3 0.0 copy-start.2
  8.3 0.0 copy-start.3
  8.4 3.2 %collective-permute-start.2 = (bf16[256,384]{1,0:T(8,128)(2,1)S(1)}, bf16[256,384]{1,0:T(8,128)(2,1)S(1)}, u32[]{:S(2)}, u32[]{:S(2)}) collective-permute-start(bf16[256,384]{1,0:T(8,128)(2,1)S(1)} %broadcast_select_fusion), channel_id=1, source_target_pairs={{0,4},{4,0},{8,12},{12,8},{1,5},{5,1},{9,13},{13,9},{2,6},{6,2},{1... | collective-permute-start | bytes 589832 | tf_op jit(solution)/shard_map/ppermute | solution.py:285
  11.6 0.0 copy-done.2
  11.6 0.0 collective-permute-start.4
  11.6 2.4 %collective-permute-start.11 = (bf16[192,384]{1,0:T(8,128)(2,1)S(1)}, bf16[192,384]{1,0:T(8,128)(2,1)S(1)}, u32[]{:S(2)}, u32[]{:S(2)}) collective-permute-start(bf16[192,384]{1,0:T(8,128)(2,1)S(1)} %get-tuple-element.16.asks0.asks), channel_id=1, source_target_pairs={{0,4},{4,0},{8,12},{12,8},{1,5},{5,1},{9,13},{13,9},{2,6},{6,2},{1... | collective-permute-start | bytes 442376 | tf_op jit(solution)/shard_map/ppermute | solution.py:285
  14.0 0.7 %collective-permute-done.7.mate = bf16[256,256]{1,0:T(8,128)(2,1)S(1)} collective-permute-done((bf16[256,256]{1,0:T(8,128)(2,1)S(1)}, bf16[256,256]{1,0:T(8,128)(2,1)S(1)}, u32[]{:S(2)}, u32[]{:S(2)}) %collective-permute-start.7) | collective-permute-done | bytes 131104 | tf_op jit(solution)/shard_map/ppermute | solution.py:285
  14.7 0.0 copy-done.3
  14.7 0.0 collective-permute-start.5
  14.7 0.0 collective-permute-done.first.mate
  14.7 0.5 %collective-permute-start.6 = (bf16[256,384]{1,0:T(8,128)(2,1)S(1)}, bf16[256,384]{1,0:T(8,128)(2,1)S(1)}, u32[]{:S(2)}, u32[]{:S(2)}) collective-permute-start(bf16[256,384]{1,0:T(8,128)(2,1)S(1)} %collective-permute-done.first.mate), channel_id=1, source_target_pairs={{0,1},{1,0},{4,8},{5,9},{8,4},{9,5},{12,13},{13,12},{2,3},{3,2},{6... | collective-permute-start | bytes 589832 | tf_op jit(solution)/shard_map/ppermute | solution.py:288
  15.2 3.7 %collective-permute-done.2.second = bf16[256,384]{1,0:T(8,128)(2,1)S(1)} collective-permute-done((bf16[256,384]{1,0:T(8,128)(2,1)S(1)}, bf16[256,384]{1,0:T(8,128)(2,1)S(1)}, u32[]{:S(2)}, u32[]{:S(2)}) %collective-permute-start.2) | collective-permute-done | bytes 196640 | tf_op jit(solution)/shard_map/ppermute | solution.py:285
  18.9 0.0 collective-permute-start.3
  18.9 2.3 %collective-permute-done.11.asks0.asks = bf16[192,384]{1,0:T(8,128)(2,1)S(1)} collective-permute-done((bf16[192,384]{1,0:T(8,128)(2,1)S(1)}, bf16[192,384]{1,0:T(8,128)(2,1)S(1)}, u32[]{:S(2)}, u32[]{:S(2)}) %collective-permute-start.11) | collective-permute-done | bytes 147488 | tf_op jit(solution)/shard_map/ppermute | solution.py:285
  21.2 1.7 %collective-permute-start.12 = (bf16[192,384]{1,0:T(8,128)(2,1)S(1)}, bf16[192,384]{1,0:T(8,128)(2,1)S(1)}, u32[]{:S(2)}, u32[]{:S(2)}) collective-permute-start(bf16[192,384]{1,0:T(8,128)(2,1)S(1)} %get-tuple-element.17.asks1.asks), channel_id=1, source_target_pairs={{0,4},{4,0},{8,12},{12,8},{1,5},{5,1},{9,13},{13,9},{2,6},{6,2},{1... | collective-permute-start | bytes 442376 | tf_op jit(solution)/shard_map/ppermute | solution.py:285
  22.9 0.0 collective-permute-done.4.keys2
  22.9 0.0 collective-permute-start.8
  22.9 0.0 collective-permute-done.5.values2
  22.9 2.5 %collective-permute-start.9 = (bf16[256,128]{1,0:T(8,128)(2,1)S(1)}, bf16[256,128]{1,0:T(8,128)(2,1)S(1)}, u32[]{:S(2)}, u32[]{:S(2)}) collective-permute-start(bf16[256,128]{1,0:T(8,128)(2,1)S(1)} %get-tuple-element.25.own), channel_id=1, source_target_pairs={{0,4},{4,0},{8,12},{12,8},{1,5},{5,1},{9,13},{13,9},{2,6},{6,2},{1... | collective-permute-start | bytes 196616 | tf_op jit(solution)/shard_map/ppermute | solution.py:285
  25.5 0.0 collective-permute-done.6.far
  25.5 5.3 %collective-permute-start.14 = (bf16[192,384]{1,0:T(8,128)(2,1)S(1)}, bf16[192,384]{1,0:T(8,128)(2,1)S(1)}, u32[]{:S(2)}, u32[]{:S(2)}) collective-permute-start(bf16[192,384]{1,0:T(8,128)(2,1)S(1)} %shard_map.118), channel_id=1, source_target_pairs={{0,4},{4,0},{8,12},{12,8},{1,5},{5,1},{9,13},{13,9},{2,6},{6,2},{1... | collective-permute-start | bytes 442376 | tf_op jit(solution)/shard_map/ppermute | solution.py:285
  30.7 0.0 collective-permute-done.9.mate
  30.7 0.0 collective-permute-start.10
  30.7 0.0 collective-permute-done.12.asks1.asks
  30.7 0.0 collective-permute-done.8.far
  30.8 4.8 %collective-permute-start.15 = (bf16[192,256]{1,0:T(8,128)(2,1)S(1)}, bf16[192,256]{1,0:T(8,128)(2,1)S(1)}, u32[]{:S(2)}, u32[]{:S(2)}) collective-permute-start(bf16[192,256]{1,0:T(8,128)(2,1)S(1)} %shard_map.119), channel_id=1, source_target_pairs={{0,4},{4,0},{8,12},{12,8},{1,5},{5,1},{9,13},{13,9},{2,6},{6,2},{1... | collective-permute-start | bytes 294920 | tf_op jit(solution)/shard_map/ppermute | solution.py:285
  35.6 0.0 collective-permute-done.3.far
  35.6 1.6 %collective-permute-start.13 = (bf16[64,768]{1,0:T(8,128)(2,1)S(1)}, bf16[64,768]{1,0:T(8,128)(2,1)S(1)}, u32[]{:S(2)}, u32[]{:S(2)}) collective-permute-start(bf16[64,768]{1,0:T(8,128)(2,1)S(1)} %shard_map.117), channel_id=1, source_target_pairs={{0,4},{4,0},{8,12},{12,8},{1,5},{5,1},{9,13},{13,9},{2,6},{6,2},{1... | collective-permute-start | bytes 294920 | tf_op jit(solution)/shard_map/ppermute | solution.py:285
  37.2 0.0 collective-permute-done.10.far
  37.2 1.1 %collective-permute-start.16 = (bf16[192,128]{1,0:T(8,128)(2,1)S(1)}, bf16[192,128]{1,0:T(8,128)(2,1)S(1)}, u32[]{:S(2)}, u32[]{:S(2)}) collective-permute-start(bf16[192,128]{1,0:T(8,128)(2,1)S(1)} %shard_map.120), channel_id=1, source_target_pairs={{0,4},{4,0},{8,12},{12,8},{1,5},{5,1},{9,13},{13,9},{2,6},{6,2},{1... | collective-permute-start | bytes 147464 | tf_op jit(solution)/shard_map/ppermute | solution.py:285
  38.3 1.5 %shard_map.113 = (bf16[128,768]{1,0:T(8,128)(2,1)S(1)}, bf16[64,768]{1,0:T(8,128)(2,1)S(1)}) custom-call(s32[1]{0:T(128)} %bitcast.me_ref, f32[1,256]{1,0:T(1,128)S(1)} %get-tuple-element.15.near_ref, bf16[192,384]{1,0:T(8,128)(2,1)S(1)} %get-tuple-element.16.asks0.asks, bf16[192,384]{1,0:T(8,128)(2,1)S(1)} %get-tuple-element.17.asks1.asks, ...), custom_call_target="tpu_custom_call" | custom-call | flops 150994944 | bytes 589824 | tf_op jit(solution)/shard_map/pallas_call | solution.py:291
  39.8 1.5 %collective-permute-done.16.refs_7_ = bf16[192,128]{1,0:T(8,128)(2,1)S(1)} collective-permute-done((bf16[192,128]{1,0:T(8,128)(2,1)S(1)}, bf16[192,128]{1,0:T(8,128)(2,1)S(1)}, u32[]{:S(2)}, u32[]{:S(2)}) %collective-permute-start.16) | collective-permute-done | bytes 49184 | tf_op jit(solution)/shard_map/ppermute | solution.py:285
  41.3 0.0 collective-permute-done.15.refs_6_
  41.3 0.0 collective-permute-done.14.refs_5_
  41.3 0.0 collective-permute-done.13.refs_4_
  41.3 0.9 %shard_map.121 = (bf16[128,768]{1,0:T(8,128)(2,1)}, bf16[128,768]{1,0:T(8,128)(2,1)}, bf16[64,768]{1,0:T(8,128)(2,1)}, bf16[64,768]{1,0:T(8,128)(2,1)}) custom-call(s32[1]{0:T(128)} %bitcast.me_ref, bf16[128,768]{1,0:T(8,128)(2,1)S(1)} %get-tuple-element.20.cross, bf16[64,768]{1,0:T(8,128)(2,1)S(1)} %get-tuple-element.21.refs_0_, ...), custom_call_target="tpu_custom_call" | custom-call | tf_op jit(solution)/shard_map/pallas_call | solution.py:291
  (8 shorter events, 0.0 us)
Async XLA Ops:
  1.7 4.7 %copy-start = (s32[256]{0:T(256)S(1)}, s32[256]{0:T(256)}, u32[]{:S(2)}) copy-start(s32[256]{0:T(256)} %param.14) | copy-start | bytes 3076
  1.7 4.7 %copy-start.1 = (s32[4]{0:T(128)S(1)}, s32[4]{0:T(128)}, u32[]{:S(2)}) copy-start(s32[4]{0:T(128)} %count_ref.1) | copy-start | bytes 52
  1.7 6.6 %collective-permute-start.1 = (bf16[256,384]{1,0:T(8,128)(2,1)S(1)}, bf16[256,384]{1,0:T(8,128)(2,1)S(1)}, u32[]{:S(2)}, u32[]{:S(2)}) collective-permute-start(bf16[256,384]{1,0:T(8,128)(2,1)S(1)} %get-tuple-element.18.out), channel_id=1, source_target_pairs={{0,1},{1,0},{4,8},{5,9},{8,4},{9,5},{12,13},{13,12},{2,3},{3,2},{6... | collective-permute-start | bytes 589832 | tf_op jit(solution)/shard_map/ppermute | solution.py:288
  2.2 12.4 %collective-permute-start = (bf16[256,384]{1,0:T(8,128)(2,1)S(1)}, bf16[256,384]{1,0:T(8,128)(2,1)S(1)}, u32[]{:S(2)}, u32[]{:S(2)}) collective-permute-start(bf16[256,384]{1,0:T(8,128)(2,1)S(1)} %get-tuple-element.18.out), channel_id=1, source_target_pairs={{0,4},{4,0},{8,12},{12,8},{1,5},{5,1},{9,13},{13,9},{2,6},{6,2},{1... | collective-permute-start | bytes 589832 | tf_op jit(solution)/shard_map/ppermute | solution.py:285
  8.2 6.4 %collective-permute-start.7 = (bf16[256,256]{1,0:T(8,128)(2,1)S(1)}, bf16[256,256]{1,0:T(8,128)(2,1)S(1)}, u32[]{:S(2)}, u32[]{:S(2)}) collective-permute-start(bf16[256,256]{1,0:T(8,128)(2,1)S(1)} %get-tuple-element.24.own), channel_id=1, source_target_pairs={{0,4},{4,0},{8,12},{12,8},{1,5},{5,1},{9,13},{13,9},{2,6},{6,2},{1... | collective-permute-start | bytes 393224 | tf_op jit(solution)/shard_map/ppermute | solution.py:285
  8.3 3.2 %copy-start.2 = (bf16[128,768]{1,0:T(8,128)(2,1)S(1)}, bf16[128,768]{1,0:T(8,128)(2,1)}, u32[]{:S(2)}) copy-start(bf16[128,768]{1,0:T(8,128)(2,1)} %video_k.3) | copy-start | bytes 589828
  8.3 6.3 %copy-start.3 = (bf16[128,768]{1,0:T(8,128)(2,1)S(1)}, bf16[128,768]{1,0:T(8,128)(2,1)}, u32[]{:S(2)}) copy-start(bf16[128,768]{1,0:T(8,128)(2,1)} %video_v.3) | copy-start | bytes 589828
  8.4 10.5 %collective-permute-start.2 = (bf16[256,384]{1,0:T(8,128)(2,1)S(1)}, bf16[256,384]{1,0:T(8,128)(2,1)S(1)}, u32[]{:S(2)}, u32[]{:S(2)}) collective-permute-start(bf16[256,384]{1,0:T(8,128)(2,1)S(1)} %broadcast_select_fusion), channel_id=1, source_target_pairs={{0,4},{4,0},{8,12},{12,8},{1,5},{5,1},{9,13},{13,9},{2,6},{6,2},{1... | collective-permute-start | bytes 589832 | tf_op jit(solution)/shard_map/ppermute | solution.py:285
  11.6 11.4 %collective-permute-start.4 = (bf16[128,768]{1,0:T(8,128)(2,1)S(1)}, bf16[128,768]{1,0:T(8,128)(2,1)S(1)}, u32[]{:S(2)}, u32[]{:S(2)}) collective-permute-start(bf16[128,768]{1,0:T(8,128)(2,1)S(1)} %copy-done.2), channel_id=1, source_target_pairs={{0,1},{1,0},{4,8},{5,9},{8,4},{9,5},{12,13},{13,12},{2,3},{3,2},{6... | collective-permute-start | bytes 589832 | tf_op jit(solution)/shard_map/ppermute | solution.py:288
  11.6 9.6 %collective-permute-start.11 = (bf16[192,384]{1,0:T(8,128)(2,1)S(1)}, bf16[192,384]{1,0:T(8,128)(2,1)S(1)}, u32[]{:S(2)}, u32[]{:S(2)}) collective-permute-start(bf16[192,384]{1,0:T(8,128)(2,1)S(1)} %get-tuple-element.16.asks0.asks), channel_id=1, source_target_pairs={{0,4},{4,0},{8,12},{12,8},{1,5},{5,1},{9,13},{13,9},{2,6},{6,2},{1... | collective-permute-start | bytes 442376 | tf_op jit(solution)/shard_map/ppermute | solution.py:285
  14.7 8.3 %collective-permute-start.5 = (bf16[128,768]{1,0:T(8,128)(2,1)S(1)}, bf16[128,768]{1,0:T(8,128)(2,1)S(1)}, u32[]{:S(2)}, u32[]{:S(2)}) collective-permute-start(bf16[128,768]{1,0:T(8,128)(2,1)S(1)} %copy-done.3), channel_id=1, source_target_pairs={{0,1},{1,0},{4,8},{5,9},{8,4},{9,5},{12,13},{13,12},{2,3},{3,2},{6... | collective-permute-start | bytes 589832 | tf_op jit(solution)/shard_map/ppermute | solution.py:288
  14.7 10.8 %collective-permute-start.6 = (bf16[256,384]{1,0:T(8,128)(2,1)S(1)}, bf16[256,384]{1,0:T(8,128)(2,1)S(1)}, u32[]{:S(2)}, u32[]{:S(2)}) collective-permute-start(bf16[256,384]{1,0:T(8,128)(2,1)S(1)} %collective-permute-done.first.mate), channel_id=1, source_target_pairs={{0,1},{1,0},{4,8},{5,9},{8,4},{9,5},{12,13},{13,12},{2,3},{3,2},{6... | collective-permute-start | bytes 589832 | tf_op jit(solution)/shard_map/ppermute | solution.py:288
  18.9 16.7 %collective-permute-start.3 = (bf16[256,384]{1,0:T(8,128)(2,1)S(1)}, bf16[256,384]{1,0:T(8,128)(2,1)S(1)}, u32[]{:S(2)}, u32[]{:S(2)}) collective-permute-start(bf16[256,384]{1,0:T(8,128)(2,1)S(1)} %collective-permute-done.2.second), channel_id=1, source_target_pairs={{0,1},{1,0},{4,8},{5,9},{8,4},{9,5},{12,13},{13,12},{2,3},{3,2},{6... | collective-permute-start | bytes 589832 | tf_op jit(solution)/shard_map/ppermute | solution.py:288
  21.2 9.5 %collective-permute-start.12 = (bf16[192,384]{1,0:T(8,128)(2,1)S(1)}, bf16[192,384]{1,0:T(8,128)(2,1)S(1)}, u32[]{:S(2)}, u32[]{:S(2)}) collective-permute-start(bf16[192,384]{1,0:T(8,128)(2,1)S(1)} %get-tuple-element.17.asks1.asks), channel_id=1, source_target_pairs={{0,4},{4,0},{8,12},{12,8},{1,5},{5,1},{9,13},{13,9},{2,6},{6,2},{1... | collective-permute-start | bytes 442376 | tf_op jit(solution)/shard_map/ppermute | solution.py:285
  22.9 7.8 %collective-permute-start.8 = (bf16[256,256]{1,0:T(8,128)(2,1)S(1)}, bf16[256,256]{1,0:T(8,128)(2,1)S(1)}, u32[]{:S(2)}, u32[]{:S(2)}) collective-permute-start(bf16[256,256]{1,0:T(8,128)(2,1)S(1)} %collective-permute-done.7.mate), channel_id=1, source_target_pairs={{0,1},{1,0},{4,8},{5,9},{8,4},{9,5},{12,13},{13,12},{2,3},{3,2},{6... | collective-permute-start | bytes 393224 | tf_op jit(solution)/shard_map/ppermute | solution.py:288
  22.9 7.8 %collective-permute-start.9 = (bf16[256,128]{1,0:T(8,128)(2,1)S(1)}, bf16[256,128]{1,0:T(8,128)(2,1)S(1)}, u32[]{:S(2)}, u32[]{:S(2)}) collective-permute-start(bf16[256,128]{1,0:T(8,128)(2,1)S(1)} %get-tuple-element.25.own), channel_id=1, source_target_pairs={{0,4},{4,0},{8,12},{12,8},{1,5},{5,1},{9,13},{13,9},{2,6},{6,2},{1... | collective-permute-start | bytes 196616 | tf_op jit(solution)/shard_map/ppermute | solution.py:285
  25.5 15.8 %collective-permute-start.14 = (bf16[192,384]{1,0:T(8,128)(2,1)S(1)}, bf16[192,384]{1,0:T(8,128)(2,1)S(1)}, u32[]{:S(2)}, u32[]{:S(2)}) collective-permute-start(bf16[192,384]{1,0:T(8,128)(2,1)S(1)} %shard_map.118), channel_id=1, source_target_pairs={{0,4},{4,0},{8,12},{12,8},{1,5},{5,1},{9,13},{13,9},{2,6},{6,2},{1... | collective-permute-start | bytes 442376 | tf_op jit(solution)/shard_map/ppermute | solution.py:285
  30.7 6.5 %collective-permute-start.10 = (bf16[256,128]{1,0:T(8,128)(2,1)S(1)}, bf16[256,128]{1,0:T(8,128)(2,1)S(1)}, u32[]{:S(2)}, u32[]{:S(2)}) collective-permute-start(bf16[256,128]{1,0:T(8,128)(2,1)S(1)} %collective-permute-done.9.mate), channel_id=1, source_target_pairs={{0,1},{1,0},{4,8},{5,9},{8,4},{9,5},{12,13},{13,12},{2,3},{3,2},{6... | collective-permute-start | bytes 196616 | tf_op jit(solution)/shard_map/ppermute | solution.py:288
  30.8 10.5 %collective-permute-start.15 = (bf16[192,256]{1,0:T(8,128)(2,1)S(1)}, bf16[192,256]{1,0:T(8,128)(2,1)S(1)}, u32[]{:S(2)}, u32[]{:S(2)}) collective-permute-start(bf16[192,256]{1,0:T(8,128)(2,1)S(1)} %shard_map.119), channel_id=1, source_target_pairs={{0,4},{4,0},{8,12},{12,8},{1,5},{5,1},{9,13},{13,9},{2,6},{6,2},{1... | collective-permute-start | bytes 294920 | tf_op jit(solution)/shard_map/ppermute | solution.py:285
  35.6 5.7 %collective-permute-start.13 = (bf16[64,768]{1,0:T(8,128)(2,1)S(1)}, bf16[64,768]{1,0:T(8,128)(2,1)S(1)}, u32[]{:S(2)}, u32[]{:S(2)}) collective-permute-start(bf16[64,768]{1,0:T(8,128)(2,1)S(1)} %shard_map.117), channel_id=1, source_target_pairs={{0,4},{4,0},{8,12},{12,8},{1,5},{5,1},{9,13},{13,9},{2,6},{6,2},{1... | collective-permute-start | bytes 294920 | tf_op jit(solution)/shard_map/ppermute | solution.py:285
  37.2 4.1 %collective-permute-start.16 = (bf16[192,128]{1,0:T(8,128)(2,1)S(1)}, bf16[192,128]{1,0:T(8,128)(2,1)S(1)}, u32[]{:S(2)}, u32[]{:S(2)}) collective-permute-start(bf16[192,128]{1,0:T(8,128)(2,1)S(1)} %shard_map.120), channel_id=1, source_target_pairs={{0,4},{4,0},{8,12},{12,8},{1,5},{5,1},{9,13},{13,9},{2,6},{6,2},{1... | collective-permute-start | bytes 147464 | tf_op jit(solution)/shard_map/ppermute | solution.py:285

commit v7 on v6

--- a/solution.py
+++ b/solution.py
@@ -10,6 +10,7 @@
 
 HEAD_DIM = 128
 SPAN = 1
+STEP = 128
 MASKED = -1e30
 LOG2E = 1.4426950408889634
 VMEM = pl.BlockSpec(memory_space=pltpu.VMEM)
@@ -68,7 +69,12 @@
     peak = jnp.max(scores, axis=1, keepdims=True)
     weights = jnp.exp2((scores - peak) * (HEAD_DIM ** (-0.5) * LOG2E))
     total = jnp.sum(weights, axis=1, keepdims=True)
-    mixed = jnp.dot(weights.astype(jnp.bfloat16), values, preferred_element_type=jnp.float32)
+    weights = weights.astype(jnp.bfloat16)
+    mixed = 0.0
+    for at in range(0, keys.shape[0], STEP):
+        mixed += jnp.dot(
+            weights[:, at : at + STEP], values[at : at + STEP], preferred_element_type=jnp.float32
+        )
     return (mixed * (1.0 / total)).astype(jnp.bfloat16)
 
 
@@ -101,22 +107,25 @@
     return moves
 
 
-def first_pack(n, me_ref, video_k, video_v, audio_k, audio_v, out_ref, over_ref, sem):
+def first_pack(n, me_ref, video_k, video_v, audio_k, audio_v, out_ref, over_ref, values_ref, sem):
     me = me_ref[0]
+    half = values_ref.shape[1]
     at_end = (me == 0) | (me == n - 1)
     for role, sight, sound in ((at_end, out_ref, over_ref), (jnp.logical_not(at_end), over_ref, out_ref)):
 
         @pl.when(role)
         def _(sight=sight, sound=sound):
             moves = sight_moves(video_k, video_v, 0, sight) + sound_moves(audio_k, audio_v, sound)
+            moves.append((video_v.at[:, pl.ds(0, half)], values_ref))
             for copy in move_all(moves, sem):
                 copy.wait()
 
 
 def second_pack(n, me_ref, count_ref, offset_ref, video_k, video_v, video_q, audio_q, *outs):
-    sight1, sight2, asks0, asks1, live_ref, reach_ref, near_ref, sem = outs
+    sight1, sight2, asks0, asks1, values_ref, mask0_ref, mask1_ref, near_ref, sem = outs
     rows = video_q.shape[0]
-    moves, at = [], asks0.shape[1]
+    at = asks0.shape[1]
+    moves = [(video_v.at[:, pl.ds(at, at)], values_ref)]
     for half, out in enumerate((asks0, asks1)):
         cols = pl.ds(half * at, at)
         moves += [(video_q.at[:, cols], out.at[:rows]), (audio_q.at[:, cols], out.at[rows:])]
@@ -124,20 +133,22 @@
         moves += sight_moves(video_k, video_v, at, out)
         at += out.shape[1]
     copies = move_all(moves, sem)
-    tables(n, me_ref[0], count_ref, offset_ref, live_ref, reach_ref, near_ref)
+    tables(n, me_ref[0], count_ref, offset_ref, (mask0_ref, mask1_ref), near_ref)
     for copy in copies:
         copy.wait()
 
 
-def tables(n, me, count_ref, offset_ref, live_ref, reach_ref, near_ref):
+def tables(n, me, count_ref, offset_ref, mask_refs, near_ref):
     upper = me * 2 >= n
     inner, end = jnp.where(upper, 1, n - 2), jnp.where(upper, 0, n - 1)
     frames = (me, me ^ 1, inner, end)
     audio_rows = offset_ref.shape[1] // n
-    video_rows = live_ref.shape[1] // n
+    video_rows = mask_refs[0].shape[1] // n
     pieces = [offset_ref[:, i * audio_rows : (i + 1) * audio_rows] for i in range(n)]
     offsets = jnp.concatenate([pick(pieces, frame) for frame in frames], axis=1)
-    near_ref[...] = jnp.where(jnp.abs(offsets - me) <= SPAN, 0.0, MASKED)
+    near = jnp.where(jnp.abs(offsets - me) <= SPAN, 0.0, MASKED)
+    near_ref[:video_rows, :] = jnp.broadcast_to(near, (video_rows, n * audio_rows))
+    near_ref[video_rows:, :] = jnp.zeros((audio_rows, n * audio_rows), jnp.float32)
     size = 2 * audio_rows
     corner = lax.broadcasted_iota(jnp.int32, (size, size), 0) == lax.broadcasted_iota(
         jnp.int32, (size, size), 1
@@ -147,8 +158,10 @@
     for i, frame in enumerate(frames):
         cols = slice(i * video_rows, (i + 1) * video_rows)
         live = jnp.where(within < count_ref[frame], 0.0, MASKED)
-        live_ref[:, cols] = live
-        reach_ref[:, cols] = jnp.where(jnp.abs(asking - frame) <= SPAN, live, MASKED)
+        reach = jnp.where(jnp.abs(asking - frame) <= SPAN, live, MASKED)
+        for who, mask_ref in enumerate(mask_refs):
+            mask_ref[:video_rows, cols] = jnp.broadcast_to(live, (video_rows, video_rows))
+            mask_ref[video_rows:, cols] = reach[who * audio_rows : (who + 1) * audio_rows]
 
 
 def sound_blocks(blocks, audio_rows, half, cols):
@@ -181,29 +194,27 @@
     me = me_ref[0]
     at_end = (me == 0) | (me == n - 1)
 
-    def run(blocks, alone):
-        near = near_ref[:, : audio_rows * len(blocks)]
+    def run(blocks):
         for half, asks in enumerate((asks0, asks1)):
             for at in range(0, width, HEAD_DIM):
                 cols = slice(at, at + HEAD_DIM)
                 to = slice(half * width + at, half * width + at + HEAD_DIM)
                 keys, values = sound_blocks(blocks, audio_rows, half, cols)
-                cross_ref[:, to] = blend(asks[:video_rows, cols], keys, values, near)
-                if not alone:
-                    own_ref[:, to] = blend(asks[video_rows:, cols], keys, values, None)
+                mixed = blend(asks[:, cols], keys, values, near_ref[...])
+                cross_ref[:, to] = mixed[:video_rows]
+                own_ref[:, to] = mixed[video_rows:]
 
     @pl.when(jnp.logical_not(at_end))
     def _():
-        run((out, second, across, far), False)
+        run((out, second, across, far))
 
     @pl.when(at_end)
     def _():
-        run((over, first, second), True)
-
-
-def video_kernel(n, who, at, shift, me_ref, live_ref, reach_ref, asks, own, mate, keys2, values2, far, out_ref):
+        run((over, first, second, far))
+
+
+def video_kernel(n, at, half, me_ref, mask_ref, asks, own, mate, keys2, values2, far, out_ref):
     video_rows = own.shape[0] // 2
-    audio_rows = asks.shape[0] - video_rows
     me = me_ref[0]
 
     @pl.when((me > 0) & (me < n - 1))
@@ -211,48 +222,52 @@
         for head in range(own.shape[1] // HEAD_DIM):
             cols = slice(head * HEAD_DIM, (head + 1) * HEAD_DIM)
             all_cols = slice((at + head) * HEAD_DIM, (at + head + 1) * HEAD_DIM)
-            q_cols = slice((at - shift + head) * HEAD_DIM, (at - shift + head + 1) * HEAD_DIM)
+            half_cols = slice((at - half + head) * HEAD_DIM, (at - half + head + 1) * HEAD_DIM)
             top, low = slice(0, video_rows), slice(video_rows, 2 * video_rows)
             keys = jnp.concatenate(
                 [own[top, cols], mate[top, cols], keys2[:, all_cols], far[top, cols]], axis=0
             )
             values = jnp.concatenate(
-                [own[low, cols], mate[low, cols], values2[:, all_cols], far[low, cols]], axis=0
+                [own[low, cols], mate[low, cols], values2[:, half_cols], far[low, cols]], axis=0
             )
-            reach = reach_ref[who * audio_rows : (who + 1) * audio_rows, :]
-            out_ref[:video_rows, cols] = blend(asks[:video_rows, q_cols], keys, values, live_ref[...])
-            out_ref[video_rows:, cols] = blend(asks[video_rows:, q_cols], keys, values, reach)
-
-
-def place_kernel(n_frames, video_rows, me_ref, cross, *refs):
-    n = (len(refs) - 5) // 2
-    own, back = refs[:n], refs[n : 2 * n]
-    video_self, video_cross, audio_self, audio_cross = refs[2 * n : 2 * n + 4]
-    sem = refs[-1]
-
-    def copies(parts):
-        yield cross, video_cross
-        yield parts[0], audio_self
-        at = 0
-        for part in parts[1:]:
-            cols = pl.ds(at, part.shape[1])
-            yield part.at[:video_rows], video_self.at[:, cols]
-            yield part.at[video_rows:], audio_cross.at[:, cols]
-            at += part.shape[1]
-
-    at_end = (me_ref[0] == 0) | (me_ref[0] == n_frames - 1)
-    for role, parts in ((jnp.logical_not(at_end), own), (at_end, back)):
+            out_ref[:, cols] = blend(asks[:, half_cols], keys, values, mask_ref[...])
+
+
+def place_pieces(parts, first, video_rows, video_self, audio_cross):
+    moves, at = [], first
+    for part in parts:
+        cols = pl.ds(at, part.shape[1])
+        moves.append((part.at[:video_rows], video_self.at[:, cols]))
+        moves.append((part.at[video_rows:], audio_cross.at[:, cols]))
+        at += part.shape[1]
+    return moves
+
+
+def place_kernel(n, me_ref, cross, own0, own1, own2, back0, back1, back2, *outs):
+    video_self, video_cross, audio_self, audio_cross, sem = outs
+    at_end = (me_ref[0] == 0) | (me_ref[0] == n - 1)
+    for role, sound, parts in (
+        (jnp.logical_not(at_end), own0, (own1, own2)),
+        (at_end, back0, (back1, back2)),
+    ):
 
         @pl.when(role)
-        def _(parts=parts):
-            moves = [
-                pltpu.make_async_copy(src, dst, sem.at[i])
-                for i, (src, dst) in enumerate(copies(parts))
-            ]
-            for move in moves:
-                move.start()
-            for move in moves:
-                move.wait()
+        def _(sound=sound, parts=parts):
+            moves = [(cross, video_cross), (sound, audio_self)]
+            moves += place_pieces(parts, 0, cross.shape[0], video_self, audio_cross)
+            for copy in move_all(moves, sem):
+                copy.wait()
+
+
+def place_last_kernel(n, first, me_ref, own, back, old_self, old_cross, video_self, audio_cross, sem):
+    at_end = (me_ref[0] == 0) | (me_ref[0] == n - 1)
+    for role, part in ((jnp.logical_not(at_end), own), (at_end, back)):
+
+        @pl.when(role)
+        def _(part=part):
+            moves = place_pieces((part,), first, video_self.shape[0], video_self, audio_cross)
+            for copy in move_all(moves, sem):
+                copy.wait()
 
 
 def cost(rows, keys, heads):
@@ -297,7 +312,7 @@
         )(*args)
 
     place = me.astype(jnp.int32).reshape(1)
-    raw_keys, raw_values = video_k, video_v
+    raw_keys = video_k
     video_q, video_k, video_v, audio_q, audio_k, audio_v = (
         pltpu.with_memory_space_constraint(block, pltpu.HBM)
         for block in (video_q, video_k, video_v, audio_q, audio_k, audio_v)
@@ -305,26 +320,23 @@
     at_end = (me == 0) | (me == n - 1)
     lengths = [size * HEAD_DIM for size in chunks]
     half = lengths[0]
-    first_out, first_over = call(
+    first_out, first_over, values0 = call(
         functools.partial(first_pack, n),
-        (((2 * video_rows, half), jnp.bfloat16),) * 2,
+        (((2 * video_rows, half), jnp.bfloat16),) * 2 + (((video_rows, half), jnp.bfloat16),),
         [SMEM] + [HBM] * 4,
         place,
         video_k,
         video_v,
         audio_k,
         audio_v,
-        out_specs=(VMEM,) * 2,
-        scratch_shapes=[pltpu.SemaphoreType.DMA((6,))],
+        out_specs=(VMEM,) * 3,
+        scratch_shapes=[pltpu.SemaphoreType.DMA((7,))],
     )
     outs = tuple(((2 * video_rows, length), jnp.bfloat16) for length in lengths[1:])
     outs += (((rows, half), jnp.bfloat16),) * 2
-    outs += (
-        ((1, n * video_rows), jnp.float32),
-        ((2 * audio_rows, n * video_rows), jnp.float32),
-        ((1, n * audio_rows), jnp.float32),
-    )
-    *sights, asks0, asks1, live, reach, near = call(
+    outs += (((video_rows, half), jnp.bfloat16),)
+    outs += (((rows, n * video_rows), jnp.float32),) * 2 + (((rows, n * audio_rows), jnp.float32),)
+    *sights, asks0, asks1, values1, mask0, mask1, near = call(
         functools.partial(second_pack, n),
         outs,
         [SMEM, SMEM, VMEM] + [HBM] * 4,
@@ -336,13 +348,13 @@
         video_q,
         audio_q,
         out_specs=(VMEM,) * len(outs),
-        scratch_shapes=[pltpu.SemaphoreType.DMA((8,))],
+        scratch_shapes=[pltpu.SemaphoreType.DMA((9,))],
     )
     asks = [asks0, asks1]
     sights = [first_over] + sights
 
     keys_across = cross(raw_keys)
-    values_across = cross(raw_values)
+    values_across = [cross(values0), cross(values1)]
     sight_mate = [mate(first_out)]
     sound_across = cross(first_out)
     second_mate = mate(jnp.where(at_end, first_over, sound_across))
@@ -351,28 +363,27 @@
     sight_far = [cross(sight_mate[i]) for i in range(3)]
     asks_mate = [mate(asks[i]) for i in range(2)]
 
-    def look(who, i, queries):
+    def look(i, queries, mask):
         at, size = sum(chunks[:i]), chunks[i]
         half = min(i, 1)
         return call(
-            functools.partial(video_kernel, n, who, at, half * chunks[0]),
+            functools.partial(video_kernel, n, at, half * chunks[0]),
             (((rows, size * HEAD_DIM), jnp.bfloat16),),
-            [SMEM] + [VMEM] * 8,
+            [SMEM] + [VMEM] * 7,
             place,
-            live,
-            reach,
+            mask,
             queries[half],
             sights[i],
             sight_mate[i],
             keys_across,
-            values_across,
+            values_across[half],
             sight_far[i],
             out_specs=(VMEM,),
             cost_estimate=cost(rows, n * video_rows, size),
         )[0]
 
-    back = [mate(look(1, i, asks_mate)) for i in range(3)]
-    mine = [look(0, i, asks) for i in range(3)]
+    back = [mate(look(i, asks_mate, mask1)) for i in range(3)]
+    mine = [look(i, asks, mask0) for i in range(3)]
     theirs = call(
         functools.partial(audio_mate_kernel, n),
         (((audio_rows, width), jnp.bfloat16),),
@@ -402,19 +413,36 @@
         out_specs=(VMEM,) * 2,
         cost_estimate=cost(rows, n * audio_rows, heads),
     )
-    mine = [own] + mine
-    back = [mate(theirs)] + back
-    return call(
-        functools.partial(place_kernel, n, video_rows),
-        (((video_rows, width), jnp.bfloat16),) * 2 + (((audio_rows, width), jnp.bfloat16),) * 2,
-        [SMEM] + [VMEM] * (1 + 2 * len(mine)),
+    back_sound = mate(theirs)
+    video_shape = ((video_rows, width), jnp.bfloat16)
+    audio_shape = ((audio_rows, width), jnp.bfloat16)
+    video_self, video_cross, audio_self, audio_cross = call(
+        functools.partial(place_kernel, n),
+        (video_shape, video_shape, audio_shape, audio_shape),
+        [SMEM] + [VMEM] * 7,
         place,
         video_cross,
-        *mine,
-        *back,
+        own,
+        *mine[:2],
+        back_sound,
+        *back[:2],
         out_specs=(HBM,) * 4,
-        scratch_shapes=[pltpu.SemaphoreType.DMA((2 * len(mine),))],
-    )
+        scratch_shapes=[pltpu.SemaphoreType.DMA((6,))],
+    )
+    video_self, audio_cross = call(
+        functools.partial(place_last_kernel, n, width - lengths[2]),
+        (video_shape, audio_shape),
+        [SMEM] + [VMEM] * 2 + [HBM] * 2,
+        place,
+        mine[2],
+        back[2],
+        video_self,
+        audio_cross,
+        out_specs=(HBM,) * 2,
+        scratch_shapes=[pltpu.SemaphoreType.DMA((2,))],
+        input_output_aliases={3: 0, 4: 1},
+    )
+    return video_self, video_cross, audio_self, audio_cross
 
 
 def solution(mesh):

time: 42.9 us -> 41.7 us (0.972); the launches traced: 42.2 us -> 41.5 us
  starting transfers between devices: 27.9 us -> 25.7 us
  waiting for transfers between devices: 8.24 us -> 9.54 us
    ppermute x10, starting transfers between devices: 26.8 us -> 24 us  [mate(): return lax.ppermute(block, 'seq', mate_pairs)]
    ppermute x10, waiting for transfers between devices: 8.22 us -> 9.52 us  [mate(): return lax.ppermute(block, 'seq', mate_pairs)]
    ppermute x7 -> x8, starting transfers between devices: 1.08 us -> 1.65 us  [cross(): return lax.ppermute(block, ('seq', 'mp'), cross_pairs)]
    pallas_call x11 -> x12, Pallas kernels: 5.21 us -> 5.45 us  [call(): pl.pallas_call(kernel, out_shape=tuple((jax.ShapeDtypeStruct(shape, dtype...]
  transfers between devices with their start and end apart: 17 -> 18, of which waited for: 4 -> 4; matrix products, arithmetic and copies ran while one was open for 0% -> 0% of each run, Pallas kernels for 8% -> 9%
where the time goes in v7:
time: 41.7 us; the launch traced here: 41.5 us
  starting transfers between devices  25.7 us (62%)
  waiting for transfers between devices  9.54 us (23%)
  Pallas kernels  5.45 us (13%)
  between operations  0.74 us (2%)
    ppermute x10, starting transfers between devices, mate(): return lax.ppermute(block, 'seq', mate_pairs)  24 us
    ppermute x10, waiting for transfers between devices, mate(): return lax.ppermute(block, 'seq', mate_pairs)  9.52 us
    pallas_call x12, Pallas kernels, call(): pl.pallas_call(kernel, out_shape=tuple((jax.ShapeDtypeStruct(shape, dtype...  5.45 us
    ppermute x8, starting transfers between devices, cross(): return lax.ppermute(block, ('seq', 'mp'), cross_pairs)  1.65 us
  transfers between devices with their start and end apart: 18, of which 4 were waited for; matrix products, arithmetic and copies ran while one was open for 0% of the time, Pallas kernels for 9%

profile of v7, /device:TPU:0, one launch (start us, length us, event | category | flops | bytes accessed | tf_op | source)
XLA Modules:
  0.0 41.5 jit_solution(11485133835992917616)
XLA Ops:
  0.6 1.1 %shard_map.114 = (bf16[256,384]{1,0:T(8,128)(2,1)S(1)}, bf16[256,384]{1,0:T(8,128)(2,1)S(1)}, bf16[128,384]{1,0:T(8,128)(2,1)S(1)}) custom-call(s32[1]{0:T(128)} %bitcast.me_ref, bf16[128,768]{1,0:T(8,128)(2,1)} %video_k.3, bf16[128,768]{1,0:T(8,128)(2,1)} %video_v.3, bf16[64,768]{1,0:T(8,128)(2,1)} %audio_k.1, bf16[64,768]{1,0:T(8,128)(2,1)} %audio_v.1), custom_call_target="tpu_custom_call" | custom-call | tf_op jit(solution)/shard_map/pallas_call | solution.py:306
  1.8 0.6 %collective-permute-start.7 = (bf16[256,384]{1,0:T(8,128)(2,1)S(1)}, bf16[256,384]{1,0:T(8,128)(2,1)S(1)}, u32[]{:S(2)}, u32[]{:S(2)}) collective-permute-start(bf16[256,384]{1,0:T(8,128)(2,1)S(1)} %get-tuple-element.30.out), channel_id=1, source_target_pairs={{0,1},{1,0},{4,8},{5,9},{8,4},{9,5},{12,13},{13,12},{2,3},{3,2},{6... | collective-permute-start | bytes 589832 | tf_op jit(solution)/shard_map/ppermute | solution.py:303
  2.3 4.1 %collective-permute-start.6 = (bf16[256,384]{1,0:T(8,128)(2,1)S(1)}, bf16[256,384]{1,0:T(8,128)(2,1)S(1)}, u32[]{:S(2)}, u32[]{:S(2)}) collective-permute-start(bf16[256,384]{1,0:T(8,128)(2,1)S(1)} %get-tuple-element.30.out), channel_id=1, source_target_pairs={{0,4},{4,0},{8,12},{12,8},{1,5},{5,1},{9,13},{13,9},{2,6},{6,2},{1... | collective-permute-start | bytes 589832 | tf_op jit(solution)/shard_map/ppermute | solution.py:300
  6.5 0.0 collective-permute-done.7.across
  6.5 0.0 copy-start.2
  6.5 5.1 %collective-permute-start.8 = (bf16[256,384]{1,0:T(8,128)(2,1)S(1)}, bf16[256,384]{1,0:T(8,128)(2,1)S(1)}, u32[]{:S(2)}, u32[]{:S(2)}) collective-permute-start(bf16[256,384]{1,0:T(8,128)(2,1)S(1)} %broadcast_select_fusion), channel_id=1, source_target_pairs={{0,4},{4,0},{8,12},{12,8},{1,5},{5,1},{9,13},{13,9},{2,6},{6,2},{1... | collective-permute-start | bytes 589832 | tf_op jit(solution)/shard_map/ppermute | solution.py:300
  11.7 0.0 copy-start
  11.7 0.0 copy-start.1
  11.7 0.0 collective-permute-start.10
  11.7 0.0 copy-done.2
  11.7 0.5 %collective-permute-start.1 = (bf16[128,768]{1,0:T(8,128)(2,1)S(1)}, bf16[128,768]{1,0:T(8,128)(2,1)S(1)}, u32[]{:S(2)}, u32[]{:S(2)}) collective-permute-start(bf16[128,768]{1,0:T(8,128)(2,1)S(1)} %copy-done.2), channel_id=1, source_target_pairs={{0,1},{1,0},{4,8},{5,9},{8,4},{9,5},{12,13},{13,12},{2,3},{3,2},{6... | collective-permute-start | bytes 589832 | tf_op jit(solution)/shard_map/ppermute | solution.py:303
  12.2 0.0 collective-permute-done.6.first.mate
  12.2 0.1 collective-permute-start.11
  12.3 0.1 copy-done
  12.3 0.0 copy-done.1
  12.3 1.9 %shard_map.111 = (bf16[256,256]{1,0:T(8,128)(2,1)S(1)}, bf16[256,128]{1,0:T(8,128)(2,1)S(1)}, bf16[192,384]{1,0:T(8,128)(2,1)S(1)}, bf16[192,384]{1,0:T(8,128)(2...) custom-call(s32[1]{0:T(128)} %bitcast.me_ref, ...), custom_call_target="tpu_custom_call" | custom-call | tf_op jit(solution)/shard_map/pallas_call | solution.py:306
  14.2 3.1 %collective-permute-start.12 = (bf16[256,256]{1,0:T(8,128)(2,1)S(1)}, bf16[256,256]{1,0:T(8,128)(2,1)S(1)}, u32[]{:S(2)}, u32[]{:S(2)}) collective-permute-start(bf16[256,256]{1,0:T(8,128)(2,1)S(1)} %get-tuple-element.35.own), channel_id=1, source_target_pairs={{0,4},{4,0},{8,12},{12,8},{1,5},{5,1},{9,13},{13,9},{2,6},{6,2},{1... | collective-permute-start | bytes 393224 | tf_op jit(solution)/shard_map/ppermute | solution.py:300
  17.3 0.0 collective-permute-done.10.values2
  17.3 0.1 collective-permute-start.14
  17.4 0.0 collective-permute-done.8.second
  17.4 0.0 collective-permute-start.9
  17.4 4.3 %collective-permute-done.12.mate = bf16[256,256]{1,0:T(8,128)(2,1)S(1)} collective-permute-done((bf16[256,256]{1,0:T(8,128)(2,1)S(1)}, bf16[256,256]{1,0:T(8,128)(2,1)S(1)}, u32[]{:S(2)}, u32[]{:S(2)}) %collective-permute-start.12) | collective-permute-done | bytes 131104 | tf_op jit(solution)/shard_map/ppermute | solution.py:300
  21.7 1.0 %collective-permute-start.4 = (bf16[192,384]{1,0:T(8,128)(2,1)S(1)}, bf16[192,384]{1,0:T(8,128)(2,1)S(1)}, u32[]{:S(2)}, u32[]{:S(2)}) collective-permute-start(bf16[192,384]{1,0:T(8,128)(2,1)S(1)} %get-tuple-element.24.asks.asks1), channel_id=1, source_target_pairs={{0,4},{4,0},{8,12},{12,8},{1,5},{5,1},{9,13},{13,9},{2,6},{6,2},{1... | collective-permute-start | bytes 442376 | tf_op jit(solution)/shard_map/ppermute | solution.py:300
  22.7 2.1 %collective-permute-done.14.asks0.asks = bf16[192,384]{1,0:T(8,128)(2,1)S(1)} collective-permute-done((bf16[192,384]{1,0:T(8,128)(2,1)S(1)}, bf16[192,384]{1,0:T(8,128)(2,1)S(1)}, u32[]{:S(2)}, u32[]{:S(2)}) %collective-permute-start.14) | collective-permute-done | bytes 147488 | tf_op jit(solution)/shard_map/ppermute | solution.py:300
  24.8 0.0 collective-permute-start.13
  24.8 0.0 collective-permute-done.1.keys2
  24.8 0.5 %collective-permute-start.2 = (bf16[128,384]{1,0:T(8,128)(2,1)S(1)}, bf16[128,384]{1,0:T(8,128)(2,1)S(1)}, u32[]{:S(2)}, u32[]{:S(2)}) collective-permute-start(bf16[128,384]{1,0:T(8,128)(2,1)S(1)} %get-tuple-element.26), channel_id=1, source_target_pairs={{0,1},{1,0},{4,8},{5,9},{8,4},{9,5},{12,13},{13,12},{2,3},{3,2},{6... | collective-permute-start | bytes 294920 | tf_op jit(solution)/shard_map/ppermute | solution.py:303
  25.3 0.0 collective-permute-done.11.far
  25.3 2.3 %collective-permute-start = (bf16[256,128]{1,0:T(8,128)(2,1)S(1)}, bf16[256,128]{1,0:T(8,128)(2,1)S(1)}, u32[]{:S(2)}, u32[]{:S(2)}) collective-permute-start(bf16[256,128]{1,0:T(8,128)(2,1)S(1)} %get-tuple-element.25.own), channel_id=1, source_target_pairs={{0,4},{4,0},{8,12},{12,8},{1,5},{5,1},{9,13},{13,9},{2,6},{6,2},{1... | collective-permute-start | bytes 196616 | tf_op jit(solution)/shard_map/ppermute | solution.py:300
  27.7 2.2 %collective-permute-done.mate = bf16[256,128]{1,0:T(8,128)(2,1)S(1)} collective-permute-done((bf16[256,128]{1,0:T(8,128)(2,1)S(1)}, bf16[256,128]{1,0:T(8,128)(2,1)S(1)}, u32[]{:S(2)}, u32[]{:S(2)}) %collective-permute-start) | collective-permute-done | bytes 65568 | tf_op jit(solution)/shard_map/ppermute | solution.py:300
  29.9 2.3 %collective-permute-start.16 = (bf16[192,384]{1,0:T(8,128)(2,1)S(1)}, bf16[192,384]{1,0:T(8,128)(2,1)S(1)}, u32[]{:S(2)}, u32[]{:S(2)}) collective-permute-start(bf16[192,384]{1,0:T(8,128)(2,1)S(1)} %shard_map.119), channel_id=1, source_target_pairs={{0,4},{4,0},{8,12},{12,8},{1,5},{5,1},{9,13},{13,9},{2,6},{6,2},{1... | collective-permute-start | bytes 442376 | tf_op jit(solution)/shard_map/ppermute | solution.py:300
  32.2 0.0 collective-permute-done.2.values2
  32.2 0.0 collective-permute-start.3
  32.2 0.0 collective-permute-done.4.asks.asks1
  32.2 0.0 collective-permute-done.13.far
  32.2 3.1 %collective-permute-start.17 = (bf16[192,256]{1,0:T(8,128)(2,1)S(1)}, bf16[192,256]{1,0:T(8,128)(2,1)S(1)}, u32[]{:S(2)}, u32[]{:S(2)}) collective-permute-start(bf16[192,256]{1,0:T(8,128)(2,1)S(1)} %shard_map.120), channel_id=1, source_target_pairs={{0,4},{4,0},{8,12},{12,8},{1,5},{5,1},{9,13},{13,9},{2,6},{6,2},{1... | collective-permute-start | bytes 294920 | tf_op jit(solution)/shard_map/ppermute | solution.py:300
  35.3 0.0 collective-permute-done.9.far
  35.3 0.7 %collective-permute-start.15 = (bf16[64,768]{1,0:T(8,128)(2,1)S(1)}, bf16[64,768]{1,0:T(8,128)(2,1)S(1)}, u32[]{:S(2)}, u32[]{:S(2)}) collective-permute-start(bf16[64,768]{1,0:T(8,128)(2,1)S(1)} %shard_map.118), channel_id=1, source_target_pairs={{0,4},{4,0},{8,12},{12,8},{1,5},{5,1},{9,13},{13,9},{2,6},{6,2},{1... | collective-permute-start | bytes 294920 | tf_op jit(solution)/shard_map/ppermute | solution.py:300
  36.0 0.0 collective-permute-done.3.far
  36.0 2.1 %collective-permute-start.5 = (bf16[192,128]{1,0:T(8,128)(2,1)S(1)}, bf16[192,128]{1,0:T(8,128)(2,1)S(1)}, u32[]{:S(2)}, u32[]{:S(2)}) collective-permute-start(bf16[192,128]{1,0:T(8,128)(2,1)S(1)} %shard_map.113), channel_id=1, source_target_pairs={{0,4},{4,0},{8,12},{12,8},{1,5},{5,1},{9,13},{13,9},{2,6},{6,2},{1... | collective-permute-start | bytes 147464 | tf_op jit(solution)/shard_map/ppermute | solution.py:300
  38.1 0.9 %shard_map.115 = (bf16[128,768]{1,0:T(8,128)(2,1)S(1)}, bf16[64,768]{1,0:T(8,128)(2,1)S(1)}) custom-call(s32[1]{0:T(128)} %bitcast.me_ref, f32[192,256]{1,0:T(8,128)S(1)} %get-tuple-element.28.near_ref, bf16[192,384]{1,0:T(8,128)(2,1)S(1)} %get-tuple-element.29.asks0.asks, bf16[192,384]{1,0:T(8,128)(2,1)S(1)} %get-tuple-element.24.asks.asks1, ...), custom_call_target="tpu_custom_call" | custom-call | flops 150994944 | bytes 589824 | tf_op jit(solution)/shard_map/pallas_call | solution.py:306
  39.1 0.0 collective-permute-done.17.back2
  39.1 0.0 collective-permute-done.16.back1
  39.1 0.9 %collective-permute-done.15.back0 = bf16[64,768]{1,0:T(8,128)(2,1)S(1)} collective-permute-done((bf16[64,768]{1,0:T(8,128)(2,1)S(1)}, bf16[64,768]{1,0:T(8,128)(2,1)S(1)}, u32[]{:S(2)}, u32[]{:S(2)}) %collective-permute-start.15) | collective-permute-done | bytes 98336 | tf_op jit(solution)/shard_map/ppermute | solution.py:300
  40.0 0.8 %shard_map.121 = (bf16[128,768]{1,0:T(8,128)(2,1)}, bf16[128,768]{1,0:T(8,128)(2,1)}, bf16[64,768]{1,0:T(8,128)(2,1)}, bf16[64,768]{1,0:T(8,128)(2,1)}) custom-call(s32[1]{0:T(128)} %bitcast.me_ref, bf16[128,768]{1,0:T(8,128)(2,1)S(1)} %get-tuple-element.32.cross, bf16[64,768]{1,0:T(8,128)(2,1)S(1)} %get-tuple-element.33.own0, ...), custom_call_target="tpu_custom_call" | custom-call | tf_op jit(solution)/shard_map/pallas_call | solution.py:306
  40.9 0.0 collective-permute-done.5.back
  40.9 0.6 %shard_map.122 = (bf16[128,768]{1,0:T(8,128)(2,1)}, bf16[64,768]{1,0:T(8,128)(2,1)}) custom-call(s32[1]{0:T(128)} %bitcast.me_ref, bf16[192,128]{1,0:T(8,128)(2,1)S(1)} %shard_map.112.own, bf16[192,128]{1,0:T(8,128)(2,1)S(1)} %collective-permute-done.5.back, ...), custom_call_target="tpu_custom_call", output_to_operand_aliasing={{0}: (3, {}), {1}: (4, {})} | custom-call | tf_op jit(solution)/shard_map/pallas_call | solution.py:306
  (8 shorter events, 0.0 us)
Async XLA Ops:
  1.8 4.7 %collective-permute-start.7 = (bf16[256,384]{1,0:T(8,128)(2,1)S(1)}, bf16[256,384]{1,0:T(8,128)(2,1)S(1)}, u32[]{:S(2)}, u32[]{:S(2)}) collective-permute-start(bf16[256,384]{1,0:T(8,128)(2,1)S(1)} %get-tuple-element.30.out), channel_id=1, source_target_pairs={{0,1},{1,0},{4,8},{5,9},{8,4},{9,5},{12,13},{13,12},{2,3},{3,2},{6... | collective-permute-start | bytes 589832 | tf_op jit(solution)/shard_map/ppermute | solution.py:303
  2.3 9.8 %collective-permute-start.6 = (bf16[256,384]{1,0:T(8,128)(2,1)S(1)}, bf16[256,384]{1,0:T(8,128)(2,1)S(1)}, u32[]{:S(2)}, u32[]{:S(2)}) collective-permute-start(bf16[256,384]{1,0:T(8,128)(2,1)S(1)} %get-tuple-element.30.out), channel_id=1, source_target_pairs={{0,4},{4,0},{8,12},{12,8},{1,5},{5,1},{9,13},{13,9},{2,6},{6,2},{1... | collective-permute-start | bytes 589832 | tf_op jit(solution)/shard_map/ppermute | solution.py:300
  6.5 5.2 %copy-start.2 = (bf16[128,768]{1,0:T(8,128)(2,1)S(1)}, bf16[128,768]{1,0:T(8,128)(2,1)}, u32[]{:S(2)}) copy-start(bf16[128,768]{1,0:T(8,128)(2,1)} %video_k.3) | copy-start | bytes 589828
  6.5 10.9 %collective-permute-start.8 = (bf16[256,384]{1,0:T(8,128)(2,1)S(1)}, bf16[256,384]{1,0:T(8,128)(2,1)S(1)}, u32[]{:S(2)}, u32[]{:S(2)}) collective-permute-start(bf16[256,384]{1,0:T(8,128)(2,1)S(1)} %broadcast_select_fusion), channel_id=1, source_target_pairs={{0,4},{4,0},{8,12},{12,8},{1,5},{5,1},{9,13},{13,9},{2,6},{6,2},{1... | collective-permute-start | bytes 589832 | tf_op jit(solution)/shard_map/ppermute | solution.py:300
  11.7 0.7 %copy-start = (s32[256]{0:T(256)S(1)}, s32[256]{0:T(256)}, u32[]{:S(2)}) copy-start(s32[256]{0:T(256)} %param.14) | copy-start | bytes 3076
  11.7 0.7 %copy-start.1 = (s32[4]{0:T(128)S(1)}, s32[4]{0:T(128)}, u32[]{:S(2)}) copy-start(s32[4]{0:T(128)} %count_ref.1) | copy-start | bytes 52
  11.7 5.7 %collective-permute-start.10 = (bf16[128,384]{1,0:T(8,128)(2,1)S(1)}, bf16[128,384]{1,0:T(8,128)(2,1)S(1)}, u32[]{:S(2)}, u32[]{:S(2)}) collective-permute-start(bf16[128,384]{1,0:T(8,128)(2,1)S(1)} %get-tuple-element.34), channel_id=1, source_target_pairs={{0,1},{1,0},{4,8},{5,9},{8,4},{9,5},{12,13},{13,12},{2,3},{3,2},{6... | collective-permute-start | bytes 294920 | tf_op jit(solution)/shard_map/ppermute | solution.py:303
  11.7 13.1 %collective-permute-start.1 = (bf16[128,768]{1,0:T(8,128)(2,1)S(1)}, bf16[128,768]{1,0:T(8,128)(2,1)S(1)}, u32[]{:S(2)}, u32[]{:S(2)}) collective-permute-start(bf16[128,768]{1,0:T(8,128)(2,1)S(1)} %copy-done.2), channel_id=1, source_target_pairs={{0,1},{1,0},{4,8},{5,9},{8,4},{9,5},{12,13},{13,12},{2,3},{3,2},{6... | collective-permute-start | bytes 589832 | tf_op jit(solution)/shard_map/ppermute | solution.py:303
  12.2 13.1 %collective-permute-start.11 = (bf16[256,384]{1,0:T(8,128)(2,1)S(1)}, bf16[256,384]{1,0:T(8,128)(2,1)S(1)}, u32[]{:S(2)}, u32[]{:S(2)}) collective-permute-start(bf16[256,384]{1,0:T(8,128)(2,1)S(1)} %collective-permute-done.6.first.mate), channel_id=1, source_target_pairs={{0,1},{1,0},{4,8},{5,9},{8,4},{9,5},{12,13},{13,12},{2,3},{3,2},{6... | collective-permute-start | bytes 589832 | tf_op jit(solution)/shard_map/ppermute | solution.py:303
  14.2 7.5 %collective-permute-start.12 = (bf16[256,256]{1,0:T(8,128)(2,1)S(1)}, bf16[256,256]{1,0:T(8,128)(2,1)S(1)}, u32[]{:S(2)}, u32[]{:S(2)}) collective-permute-start(bf16[256,256]{1,0:T(8,128)(2,1)S(1)} %get-tuple-element.35.own), channel_id=1, source_target_pairs={{0,4},{4,0},{8,12},{12,8},{1,5},{5,1},{9,13},{13,9},{2,6},{6,2},{1... | collective-permute-start | bytes 393224 | tf_op jit(solution)/shard_map/ppermute | solution.py:300
  17.3 7.5 %collective-permute-start.14 = (bf16[192,384]{1,0:T(8,128)(2,1)S(1)}, bf16[192,384]{1,0:T(8,128)(2,1)S(1)}, u32[]{:S(2)}, u32[]{:S(2)}) collective-permute-start(bf16[192,384]{1,0:T(8,128)(2,1)S(1)} %get-tuple-element.29.asks0.asks), channel_id=1, source_target_pairs={{0,4},{4,0},{8,12},{12,8},{1,5},{5,1},{9,13},{13,9},{2,6},{6,2},{1... | collective-permute-start | bytes 442376 | tf_op jit(solution)/shard_map/ppermute | solution.py:300
  17.4 17.9 %collective-permute-start.9 = (bf16[256,384]{1,0:T(8,128)(2,1)S(1)}, bf16[256,384]{1,0:T(8,128)(2,1)S(1)}, u32[]{:S(2)}, u32[]{:S(2)}) collective-permute-start(bf16[256,384]{1,0:T(8,128)(2,1)S(1)} %collective-permute-done.8.second), channel_id=1, source_target_pairs={{0,1},{1,0},{4,8},{5,9},{8,4},{9,5},{12,13},{13,12},{2,3},{3,2},{6... | collective-permute-start | bytes 589832 | tf_op jit(solution)/shard_map/ppermute | solution.py:303
  21.7 10.5 %collective-permute-start.4 = (bf16[192,384]{1,0:T(8,128)(2,1)S(1)}, bf16[192,384]{1,0:T(8,128)(2,1)S(1)}, u32[]{:S(2)}, u32[]{:S(2)}) collective-permute-start(bf16[192,384]{1,0:T(8,128)(2,1)S(1)} %get-tuple-element.24.asks.asks1), channel_id=1, source_target_pairs={{0,4},{4,0},{8,12},{12,8},{1,5},{5,1},{9,13},{13,9},{2,6},{6,2},{1... | collective-permute-start | bytes 442376 | tf_op jit(solution)/shard_map/ppermute | solution.py:300
  24.8 7.4 %collective-permute-start.13 = (bf16[256,256]{1,0:T(8,128)(2,1)S(1)}, bf16[256,256]{1,0:T(8,128)(2,1)S(1)}, u32[]{:S(2)}, u32[]{:S(2)}) collective-permute-start(bf16[256,256]{1,0:T(8,128)(2,1)S(1)} %collective-permute-done.12.mate), channel_id=1, source_target_pairs={{0,1},{1,0},{4,8},{5,9},{8,4},{9,5},{12,13},{13,12},{2,3},{3,2},{6... | collective-permute-start | bytes 393224 | tf_op jit(solution)/shard_map/ppermute | solution.py:303
  24.8 7.4 %collective-permute-start.2 = (bf16[128,384]{1,0:T(8,128)(2,1)S(1)}, bf16[128,384]{1,0:T(8,128)(2,1)S(1)}, u32[]{:S(2)}, u32[]{:S(2)}) collective-permute-start(bf16[128,384]{1,0:T(8,128)(2,1)S(1)} %get-tuple-element.26), channel_id=1, source_target_pairs={{0,1},{1,0},{4,8},{5,9},{8,4},{9,5},{12,13},{13,12},{2,3},{3,2},{6... | collective-permute-start | bytes 294920 | tf_op jit(solution)/shard_map/ppermute | solution.py:303
  25.3 4.6 %collective-permute-start = (bf16[256,128]{1,0:T(8,128)(2,1)S(1)}, bf16[256,128]{1,0:T(8,128)(2,1)S(1)}, u32[]{:S(2)}, u32[]{:S(2)}) collective-permute-start(bf16[256,128]{1,0:T(8,128)(2,1)S(1)} %get-tuple-element.25.own), channel_id=1, source_target_pairs={{0,4},{4,0},{8,12},{12,8},{1,5},{5,1},{9,13},{13,9},{2,6},{6,2},{1... | collective-permute-start | bytes 196616 | tf_op jit(solution)/shard_map/ppermute | solution.py:300
  29.9 9.2 %collective-permute-start.16 = (bf16[192,384]{1,0:T(8,128)(2,1)S(1)}, bf16[192,384]{1,0:T(8,128)(2,1)S(1)}, u32[]{:S(2)}, u32[]{:S(2)}) collective-permute-start(bf16[192,384]{1,0:T(8,128)(2,1)S(1)} %shard_map.119), channel_id=1, source_target_pairs={{0,4},{4,0},{8,12},{12,8},{1,5},{5,1},{9,13},{13,9},{2,6},{6,2},{1... | collective-permute-start | bytes 442376 | tf_op jit(solution)/shard_map/ppermute | solution.py:300
  32.2 3.8 %collective-permute-start.3 = (bf16[256,128]{1,0:T(8,128)(2,1)S(1)}, bf16[256,128]{1,0:T(8,128)(2,1)S(1)}, u32[]{:S(2)}, u32[]{:S(2)}) collective-permute-start(bf16[256,128]{1,0:T(8,128)(2,1)S(1)} %collective-permute-done.mate), channel_id=1, source_target_pairs={{0,1},{1,0},{4,8},{5,9},{8,4},{9,5},{12,13},{13,12},{2,3},{3,2},{6... | collective-permute-start | bytes 196616 | tf_op jit(solution)/shard_map/ppermute | solution.py:303
  32.2 6.9 %collective-permute-start.17 = (bf16[192,256]{1,0:T(8,128)(2,1)S(1)}, bf16[192,256]{1,0:T(8,128)(2,1)S(1)}, u32[]{:S(2)}, u32[]{:S(2)}) collective-permute-start(bf16[192,256]{1,0:T(8,128)(2,1)S(1)} %shard_map.120), channel_id=1, source_target_pairs={{0,4},{4,0},{8,12},{12,8},{1,5},{5,1},{9,13},{13,9},{2,6},{6,2},{1... | collective-permute-start | bytes 294920 | tf_op jit(solution)/shard_map/ppermute | solution.py:300
  35.3 4.7 %collective-permute-start.15 = (bf16[64,768]{1,0:T(8,128)(2,1)S(1)}, bf16[64,768]{1,0:T(8,128)(2,1)S(1)}, u32[]{:S(2)}, u32[]{:S(2)}) collective-permute-start(bf16[64,768]{1,0:T(8,128)(2,1)S(1)} %shard_map.118), channel_id=1, source_target_pairs={{0,4},{4,0},{8,12},{12,8},{1,5},{5,1},{9,13},{13,9},{2,6},{6,2},{1... | collective-permute-start | bytes 294920 | tf_op jit(solution)/shard_map/ppermute | solution.py:300
  36.0 4.9 %collective-permute-start.5 = (bf16[192,128]{1,0:T(8,128)(2,1)S(1)}, bf16[192,128]{1,0:T(8,128)(2,1)S(1)}, u32[]{:S(2)}, u32[]{:S(2)}) collective-permute-start(bf16[192,128]{1,0:T(8,128)(2,1)S(1)} %shard_map.113), channel_id=1, source_target_pairs={{0,4},{4,0},{8,12},{12,8},{1,5},{5,1},{9,13},{13,9},{2,6},{6,2},{1... | collective-permute-start | bytes 147464 | tf_op jit(solution)/shard_map/ppermute | solution.py:300

commit v8 on v7

--- a/solution.py
+++ b/solution.py
@@ -122,16 +122,13 @@
 
 
 def second_pack(n, me_ref, count_ref, offset_ref, video_k, video_v, video_q, audio_q, *outs):
-    sight1, sight2, asks0, asks1, values_ref, mask0_ref, mask1_ref, near_ref, sem = outs
-    rows = video_q.shape[0]
-    at = asks0.shape[1]
-    moves = [(video_v.at[:, pl.ds(at, at)], values_ref)]
-    for half, out in enumerate((asks0, asks1)):
-        cols = pl.ds(half * at, at)
+    sight, asks0, asks1, values_ref, mask0_ref, mask1_ref, near_ref, sem = outs
+    rows, half = video_q.shape[0], sight.shape[1]
+    moves = sight_moves(video_k, video_v, half, sight)
+    moves.append((video_v.at[:, pl.ds(half, half)], values_ref))
+    for side, out in enumerate((asks0, asks1)):
+        cols = pl.ds(side * half, half)
         moves += [(video_q.at[:, cols], out.at[:rows]), (audio_q.at[:, cols], out.at[rows:])]
-    for out in (sight1, sight2):
-        moves += sight_moves(video_k, video_v, at, out)
-        at += out.shape[1]
     copies = move_all(moves, sem)
     tables(n, me_ref[0], count_ref, offset_ref, (mask0_ref, mask1_ref), near_ref)
     for copy in copies:
@@ -172,22 +169,20 @@
     return keys, values
 
 
-def audio_mate_kernel(n, me_ref, asks0, asks1, out, second, across, far, mate_ref):
-    audio_rows, width = mate_ref.shape[0], out.shape[1]
-    video_rows = asks0.shape[0] - audio_rows
+def audio_mate_kernel(n, half, me_ref, asks, out, second, across, far, mate_ref):
+    audio_rows, width = mate_ref.shape
+    video_rows = asks.shape[0] - audio_rows
     me = me_ref[0]
 
     @pl.when((me > 0) & (me < n - 1))
     def _():
-        for half, asks in enumerate((asks0, asks1)):
-            for at in range(0, width, HEAD_DIM):
-                cols = slice(at, at + HEAD_DIM)
-                to = slice(half * width + at, half * width + at + HEAD_DIM)
-                keys, values = sound_blocks((out, second, across, far), audio_rows, half, cols)
-                mate_ref[:, to] = blend(asks[video_rows:, cols], keys, values, None)
-
-
-def audio_own_kernel(n, me_ref, near_ref, asks0, asks1, out, over, first, second, across, far, *outs):
+        for at in range(0, width, HEAD_DIM):
+            cols = slice(at, at + HEAD_DIM)
+            keys, values = sound_blocks((out, second, across, far), audio_rows, half, cols)
+            mate_ref[:, cols] = blend(asks[video_rows:, cols], keys, values, None)
+
+
+def audio_own_kernel(n, me_ref, near_ref, asks0, asks1, out, over, first, second, third, across, far, *outs):
     cross_ref, own_ref = outs
     audio_rows, width = own_ref.shape[0], out.shape[1]
     video_rows = cross_ref.shape[0]
@@ -210,7 +205,7 @@
 
     @pl.when(at_end)
     def _():
-        run((over, first, second, far))
+        run((over, first, third, far))
 
 
 def video_kernel(n, at, half, me_ref, mask_ref, asks, own, mate, keys2, values2, far, out_ref):
@@ -219,16 +214,17 @@
 
     @pl.when((me > 0) & (me < n - 1))
     def _():
-        for head in range(own.shape[1] // HEAD_DIM):
+        for head in range(far.shape[1] // HEAD_DIM):
             cols = slice(head * HEAD_DIM, (head + 1) * HEAD_DIM)
             all_cols = slice((at + head) * HEAD_DIM, (at + head + 1) * HEAD_DIM)
             half_cols = slice((at - half + head) * HEAD_DIM, (at - half + head + 1) * HEAD_DIM)
             top, low = slice(0, video_rows), slice(video_rows, 2 * video_rows)
             keys = jnp.concatenate(
-                [own[top, cols], mate[top, cols], keys2[:, all_cols], far[top, cols]], axis=0
+                [own[top, half_cols], mate[top, half_cols], keys2[:, all_cols], far[top, cols]], axis=0
             )
             values = jnp.concatenate(
-                [own[low, cols], mate[low, cols], values2[:, half_cols], far[low, cols]], axis=0
+                [own[low, half_cols], mate[low, half_cols], values2[:, half_cols], far[low, cols]],
+                axis=0,
             )
             out_ref[:, cols] = blend(asks[:, half_cols], keys, values, mask_ref[...])
 
@@ -243,17 +239,22 @@
     return moves
 
 
-def place_kernel(n, me_ref, cross, own0, own1, own2, back0, back1, back2, *outs):
-    video_self, video_cross, audio_self, audio_cross, sem = outs
+def place_kernel(n, me_ref, cross, own_sound, back_sound0, back_sound1, *refs):
+    count = (len(refs) - 5) // 2
+    own, back = refs[:count], refs[count : 2 * count]
+    video_self, video_cross, audio_self, audio_cross, sem = refs[2 * count :]
     at_end = (me_ref[0] == 0) | (me_ref[0] == n - 1)
-    for role, sound, parts in (
-        (jnp.logical_not(at_end), own0, (own1, own2)),
-        (at_end, back0, (back1, back2)),
+    for role, sounds, parts in (
+        (jnp.logical_not(at_end), (own_sound,), own),
+        (at_end, (back_sound0, back_sound1), back),
     ):
 
         @pl.when(role)
-        def _(sound=sound, parts=parts):
-            moves = [(cross, video_cross), (sound, audio_self)]
+        def _(sounds=sounds, parts=parts):
+            moves = [(cross, video_cross)]
+            for i, sound in enumerate(sounds):
+                length = sound.shape[1]
+                moves.append((sound, audio_self.at[:, pl.ds(i * length, length)]))
             moves += place_pieces(parts, 0, cross.shape[0], video_self, audio_cross)
             for copy in move_all(moves, sem):
                 copy.wait()
@@ -273,11 +274,6 @@
 def cost(rows, keys, heads):
     scores = rows * keys * heads
     return pl.CostEstimate(flops=4 * scores * HEAD_DIM, bytes_accessed=rows * heads * 512, transcendentals=scores)
-
-
-def chunks_of(heads):
-    head = heads // 2
-    return head, (head + 1) // 2, head // 2
 
 
 def lined(video_q, video_k, video_v, audio_q, audio_k, audio_v, offsets, counts):
@@ -287,7 +283,8 @@
     rows = video_rows + audio_rows
     width = video_q.shape[1]
     heads = width // HEAD_DIM
-    chunks = chunks_of(heads)
+    chunks = (heads // 2,) + (1,) * (heads // 2)
+    last = len(chunks) - 1
     mate_pairs = [(i, i ^ 1) for i in range(n)]
     cross_pairs = []
     for i in range(n):
@@ -318,8 +315,7 @@
         for block in (video_q, video_k, video_v, audio_q, audio_k, audio_v)
     )
     at_end = (me == 0) | (me == n - 1)
-    lengths = [size * HEAD_DIM for size in chunks]
-    half = lengths[0]
+    half = width // 2
     first_out, first_over, values0 = call(
         functools.partial(first_pack, n),
         (((2 * video_rows, half), jnp.bfloat16),) * 2 + (((video_rows, half), jnp.bfloat16),),
@@ -332,11 +328,10 @@
         out_specs=(VMEM,) * 3,
         scratch_shapes=[pltpu.SemaphoreType.DMA((7,))],
     )
-    outs = tuple(((2 * video_rows, length), jnp.bfloat16) for length in lengths[1:])
-    outs += (((rows, half), jnp.bfloat16),) * 2
-    outs += (((video_rows, half), jnp.bfloat16),)
+    outs = (((2 * video_rows, half), jnp.bfloat16),)
+    outs += (((rows, half), jnp.bfloat16),) * 2 + (((video_rows, half), jnp.bfloat16),)
     outs += (((rows, n * video_rows), jnp.float32),) * 2 + (((rows, n * audio_rows), jnp.float32),)
-    *sights, asks0, asks1, values1, mask0, mask1, near = call(
+    sight, asks0, asks1, values1, mask0, mask1, near = call(
         functools.partial(second_pack, n),
         outs,
         [SMEM, SMEM, VMEM] + [HBM] * 4,
@@ -348,19 +343,23 @@
         video_q,
         audio_q,
         out_specs=(VMEM,) * len(outs),
-        scratch_shapes=[pltpu.SemaphoreType.DMA((9,))],
+        scratch_shapes=[pltpu.SemaphoreType.DMA((7,))],
     )
     asks = [asks0, asks1]
-    sights = [first_over] + sights
+    sights = [first_over, sight]
 
     keys_across = cross(raw_keys)
     values_across = [cross(values0), cross(values1)]
-    sight_mate = [mate(first_out)]
+    first_mate = mate(first_out)
     sound_across = cross(first_out)
-    second_mate = mate(jnp.where(at_end, first_over, sound_across))
+    second_mate = mate(first_over)
     sound_far = cross(second_mate)
-    sight_mate += [mate(sights[i]) for i in (1, 2)]
-    sight_far = [cross(sight_mate[i]) for i in range(3)]
+    third_mate = mate(jnp.where(at_end, sight, sound_across))
+    sight_mate = [first_mate, third_mate]
+    sight_far = [cross(first_mate)]
+    for i in range(1, last + 1):
+        piece = third_mate[:, (i - 1) * HEAD_DIM : i * HEAD_DIM]
+        sight_far.append(cross(piece))
     asks_mate = [mate(asks[i]) for i in range(2)]
 
     def look(i, queries, mask):
@@ -373,8 +372,8 @@
             place,
             mask,
             queries[half],
-            sights[i],
-            sight_mate[i],
+            sights[half],
+            sight_mate[half],
             keys_across,
             values_across[half],
             sight_far[i],
@@ -382,60 +381,63 @@
             cost_estimate=cost(rows, n * video_rows, size),
         )[0]
 
-    back = [mate(look(i, asks_mate, mask1)) for i in range(3)]
-    mine = [look(i, asks, mask0) for i in range(3)]
-    theirs = call(
-        functools.partial(audio_mate_kernel, n),
-        (((audio_rows, width), jnp.bfloat16),),
-        [SMEM] + [VMEM] * 6,
-        place,
-        *asks_mate,
-        first_out,
-        second_mate,
-        sound_across,
-        sound_far,
-        out_specs=(VMEM,),
-        cost_estimate=cost(audio_rows, n * audio_rows, heads),
-    )[0]
+    back = [mate(look(i, asks_mate, mask1)) for i in range(last + 1)]
+    mine = [look(i, asks, mask0) for i in range(last + 1)]
+    back_sound = []
+    for i in range(2):
+        theirs = call(
+            functools.partial(audio_mate_kernel, n, i),
+            (((audio_rows, half), jnp.bfloat16),),
+            [SMEM] + [VMEM] * 5,
+            place,
+            asks_mate[i],
+            first_out,
+            second_mate,
+            sound_across,
+            sound_far,
+            out_specs=(VMEM,),
+            cost_estimate=cost(audio_rows, n * audio_rows, heads // 2),
+        )[0]
+        back_sound.append(mate(theirs))
     video_cross, own = call(
         functools.partial(audio_own_kernel, n),
         (((video_rows, width), jnp.bfloat16), ((audio_rows, width), jnp.bfloat16)),
-        [SMEM] + [VMEM] * 9,
+        [SMEM] + [VMEM] * 10,
         place,
         near,
         *asks,
         first_out,
         first_over,
-        sight_mate[0],
+        first_mate,
         second_mate,
+        third_mate,
         sound_across,
         sound_far,
         out_specs=(VMEM,) * 2,
         cost_estimate=cost(rows, n * audio_rows, heads),
     )
-    back_sound = mate(theirs)
     video_shape = ((video_rows, width), jnp.bfloat16)
     audio_shape = ((audio_rows, width), jnp.bfloat16)
     video_self, video_cross, audio_self, audio_cross = call(
         functools.partial(place_kernel, n),
         (video_shape, video_shape, audio_shape, audio_shape),
-        [SMEM] + [VMEM] * 7,
+        [SMEM] + [VMEM] * (4 + 2 * last),
         place,
         video_cross,
         own,
-        *mine[:2],
-        back_sound,
-        *back[:2],
+        *back_sound,
+        *mine[:last],
+        *back[:last],
         out_specs=(HBM,) * 4,
-        scratch_shapes=[pltpu.SemaphoreType.DMA((6,))],
+        scratch_shapes=[pltpu.SemaphoreType.DMA((3 + 2 * last,))],
     )
     video_self, audio_cross = call(
-        functools.partial(place_last_kernel, n, width - lengths[2]),
+        functools.partial(place_last_kernel, n, width - HEAD_DIM),
         (video_shape, audio_shape),
         [SMEM] + [VMEM] * 2 + [HBM] * 2,
         place,
-        mine[2],
-        back[2],
+        mine[last],
+        back[last],
         video_self,
         audio_cross,
         out_specs=(HBM,) * 2,

time: 41.7 us -> 46.2 us (1.11)
  starting transfers between devices: 25.7 us -> 32.8 us
  waiting for transfers between devices: 9.54 us -> 5.99 us
  local copies, waits for them, and re-layouts: 0.1 us -> 0.72 us
    ppermute x10 -> x11, starting transfers between devices: 24 us -> 31.1 us  [mate(): return lax.ppermute(block, 'seq', mate_pairs)]
    ppermute x10 -> x11, waiting for transfers between devices: 9.52 us -> 5.97 us  [mate(): return lax.ppermute(block, 'seq', mate_pairs)]
    unnamed x6, local copies, waits for them, and re-layouts: 0.1 us -> 0.69 us
    pallas_call x12 -> x15, Pallas kernels: 5.45 us -> 5.67 us  [call(): pl.pallas_call(kernel, out_shape=tuple((jax.ShapeDtypeStruct(shape, dtype...]
    ppermute x8 -> x9, starting transfers between devices: 1.65 us -> 1.74 us  [cross(): return lax.ppermute(block, ('seq', 'mp'), cross_pairs)]
  transfers between devices with their start and end apart: 18 -> 20, of which waited for: 4 -> 3; matrix products, arithmetic and copies ran while one was open for 0% -> 0% of each run, Pallas kernels for 9% -> 8%
where the time goes in v8:
time: 46.2 us; the launch traced here: 46 us
  starting transfers between devices  32.8 us (71%)
  waiting for transfers between devices  5.99 us (13%)
  Pallas kernels  5.67 us (12%)
  between operations  0.8 us (2%)
  local copies, waits for them, and re-layouts  0.72 us (2%)
    ppermute x11, starting transfers between devices, mate(): return lax.ppermute(block, 'seq', mate_pairs)  31.1 us
    ppermute x11, waiting for transfers between devices, mate(): return lax.ppermute(block, 'seq', mate_pairs)  5.97 us
    pallas_call x15, Pallas kernels, call(): pl.pallas_call(kernel, out_shape=tuple((jax.ShapeDtypeStruct(shape, dtype...  5.67 us
    ppermute x9, starting transfers between devices, cross(): return lax.ppermute(block, ('seq', 'mp'), cross_pairs)  1.74 us
  transfers between devices with their start and end apart: 20, of which 3 were waited for; matrix products, arithmetic and copies ran while one was open for 0% of the time, Pallas kernels for 8%

profile of v8, /device:TPU:0, one launch (start us, length us, event | category | flops | bytes accessed | tf_op | source)
XLA Modules:
  0.0 46.0 jit_solution(14840757436088432770)
XLA Ops:
  0.6 0.0 copy-start.2
  0.6 1.2 %shard_map.112 = (bf16[256,384]{1,0:T(8,128)(2,1)S(1)}, bf16[256,384]{1,0:T(8,128)(2,1)S(1)}, bf16[128,384]{1,0:T(8,128)(2,1)S(1)}) custom-call(s32[1]{0:T(128)} %bitcast.me_ref, bf16[128,768]{1,0:T(8,128)(2,1)} %video_k.3, bf16[128,768]{1,0:T(8,128)(2,1)} %video_v.3, bf16[64,768]{1,0:T(8,128)(2,1)} %audio_k.1, bf16[64,768]{1,0:T(8,128)(2,1)} %audio_v.1), custom_call_target="tpu_custom_call" | custom-call | tf_op jit(solution)/shard_map/pallas_call | solution.py:303
  1.8 3.1 %collective-permute-start.7 = (bf16[256,384]{1,0:T(8,128)(2,1)S(1)}, bf16[256,384]{1,0:T(8,128)(2,1)S(1)}, u32[]{:S(2)}, u32[]{:S(2)}) collective-permute-start(bf16[256,384]{1,0:T(8,128)(2,1)S(1)} %get-tuple-element.25.out), channel_id=1, source_target_pairs={{0,4},{4,0},{8,12},{12,8},{1,5},{5,1},{9,13},{13,9},{2,6},{6,2},{1... | collective-permute-start | bytes 589832 | tf_op jit(solution)/shard_map/ppermute | solution.py:297
  5.0 0.0 collective-permute-start
  5.0 0.0 copy-done.2
  5.0 0.5 %collective-permute-start.2 = (bf16[128,768]{1,0:T(8,128)(2,1)S(1)}, bf16[128,768]{1,0:T(8,128)(2,1)S(1)}, u32[]{:S(2)}, u32[]{:S(2)}) collective-permute-start(bf16[128,768]{1,0:T(8,128)(2,1)S(1)} %copy-done.2), channel_id=1, source_target_pairs={{0,1},{1,0},{4,8},{5,9},{8,4},{9,5},{12,13},{13,12},{2,3},{3,2},{6... | collective-permute-start | bytes 589832 | tf_op jit(solution)/shard_map/ppermute | solution.py:300
  5.5 2.6 %collective-permute-start.8 = (bf16[256,384]{1,0:T(8,128)(2,1)S(1)}, bf16[256,384]{1,0:T(8,128)(2,1)S(1)}, u32[]{:S(2)}, u32[]{:S(2)}) collective-permute-start(bf16[256,384]{1,0:T(8,128)(2,1)S(1)} %get-tuple-element.30.over.own), channel_id=1, source_target_pairs={{0,4},{4,0},{8,12},{12,8},{1,5},{5,1},{9,13},{13,9},{2,6},{6,2},{1... | collective-permute-start | bytes 589832 | tf_op jit(solution)/shard_map/ppermute | solution.py:297
  8.1 0.0 collective-permute-start.13
  8.1 0.0 copy-start
  8.1 0.0 copy-start.1
  8.1 0.7 %copy-done = s32[256]{0:T(256)S(1)} copy-done((s32[256]{0:T(256)S(1)}, s32[256]{0:T(256)}, u32[]{:S(2)}) %copy-start) | copy-done | bytes 1048
  8.8 0.0 copy-done.1
  8.8 2.0 %shard_map.111 = (bf16[256,384]{1,0:T(8,128)(2,1)S(1)}, bf16[192,384]{1,0:T(8,128)(2,1)S(1)}, bf16[192,384]{1,0:T(8,128)(2,1)S(1)}, bf16[128,384]{1,0:T(8,128)(2...) custom-call(s32[1]{0:T(128)} %bitcast.me_ref, s32[4]{0:T(128)S(1)} %copy-done.1, ...), custom_call_target="tpu_custom_call" | custom-call | tf_op jit(solution)/shard_map/pallas_call | solution.py:303
  10.8 0.0 collective-permute-done.7.first.mate
  10.8 0.6 %collective-permute-start.14 = (bf16[256,384]{1,0:T(8,128)(2,1)S(1)}, bf16[256,384]{1,0:T(8,128)(2,1)S(1)}, u32[]{:S(2)}, u32[]{:S(2)}) collective-permute-start(bf16[256,384]{1,0:T(8,128)(2,1)S(1)} %collective-permute-done.7.first.mate), channel_id=1, source_target_pairs={{0,1},{1,0},{4,8},{5,9},{8,4},{9,5},{12,13},{13,12},{2,3},{3,2},{6... | collective-permute-start | bytes 589832 | tf_op jit(solution)/shard_map/ppermute | solution.py:300
  11.4 0.0 collective-permute-done.across
  11.5 3.0 %collective-permute-start.1 = (bf16[256,384]{1,0:T(8,128)(2,1)S(1)}, bf16[256,384]{1,0:T(8,128)(2,1)S(1)}, u32[]{:S(2)}, u32[]{:S(2)}) collective-permute-start(bf16[256,384]{1,0:T(8,128)(2,1)S(1)} %broadcast_select_fusion), channel_id=1, source_target_pairs={{0,4},{4,0},{8,12},{12,8},{1,5},{5,1},{9,13},{13,9},{2,6},{6,2},{1... | collective-permute-start | bytes 589832 | tf_op jit(solution)/shard_map/ppermute | solution.py:297
  14.4 0.0 collective-permute-done.13.values2
  14.4 5.7 %collective-permute-start.10 = (bf16[192,384]{1,0:T(8,128)(2,1)S(1)}, bf16[192,384]{1,0:T(8,128)(2,1)S(1)}, u32[]{:S(2)}, u32[]{:S(2)}) collective-permute-start(bf16[192,384]{1,0:T(8,128)(2,1)S(1)} %get-tuple-element.29.asks0.asks), channel_id=1, source_target_pairs={{0,4},{4,0},{8,12},{12,8},{1,5},{5,1},{9,13},{13,9},{2,6},{6,2},{1... | collective-permute-start | bytes 442376 | tf_op jit(solution)/shard_map/ppermute | solution.py:297
  20.2 3.1 %collective-permute-done.10.asks = bf16[192,384]{1,0:T(8,128)(2,1)S(1)} collective-permute-done((bf16[192,384]{1,0:T(8,128)(2,1)S(1)}, bf16[192,384]{1,0:T(8,128)(2,1)S(1)}, u32[]{:S(2)}, u32[]{:S(2)}) %collective-permute-start.10) | collective-permute-done | bytes 147488 | tf_op jit(solution)/shard_map/ppermute | solution.py:297
  23.3 0.0 collective-permute-start.3
  23.3 0.0 collective-permute-done.2.keys2
  23.3 4.0 %collective-permute-start.5 = (bf16[192,384]{1,0:T(8,128)(2,1)S(1)}, bf16[192,384]{1,0:T(8,128)(2,1)S(1)}, u32[]{:S(2)}, u32[]{:S(2)}) collective-permute-start(bf16[192,384]{1,0:T(8,128)(2,1)S(1)} %get-tuple-element.23.asks.asks1), channel_id=1, source_target_pairs={{0,4},{4,0},{8,12},{12,8},{1,5},{5,1},{9,13},{13,9},{2,6},{6,2},{1... | collective-permute-start | bytes 442376 | tf_op jit(solution)/shard_map/ppermute | solution.py:297
  27.4 0.0 collective-permute-done.8.second
  27.4 0.0 collective-permute-start.9
  27.4 0.0 collective-permute-done.14.far
  27.4 0.9 %collective-permute-start.17 = (bf16[192,384]{1,0:T(8,128)(2,1)S(1)}, bf16[192,384]{1,0:T(8,128)(2,1)S(1)}, u32[]{:S(2)}, u32[]{:S(2)}) collective-permute-start(bf16[192,384]{1,0:T(8,128)(2,1)S(1)} %shard_map.121), channel_id=1, source_target_pairs={{0,4},{4,0},{8,12},{12,8},{1,5},{5,1},{9,13},{13,9},{2,6},{6,2},{1... | collective-permute-start | bytes 442376 | tf_op jit(solution)/shard_map/ppermute | solution.py:297
  28.3 0.0 collective-permute-done.1.mate.third
  28.4 0.1 collective-permute-start.15
  28.4 0.0 collective-permute-done.3.values2
  28.4 0.5 %collective-permute-start.16 = (bf16[256,128]{1,0:T(8,128)(2,1)S(1)}, bf16[256,128]{1,0:T(8,128)(2,1)S(1)}, u32[]{:S(2)}, u32[]{:S(2)}) collective-permute-start(bf16[256,128]{1,0:T(8,128)(2,1)S(1)} %get-tuple-element.40), channel_id=1, source_target_pairs={{0,1},{1,0},{4,8},{5,9},{8,4},{9,5},{12,13},{13,12},{2,3},{3,2},{6... | collective-permute-start | bytes 196616 | tf_op jit(solution)/shard_map/ppermute | solution.py:300
  28.9 0.0 collective-permute-done.9.far
  28.9 0.1 collective-permute-start.4
  29.0 2.4 %collective-permute-done.5.asks = bf16[192,384]{1,0:T(8,128)(2,1)S(1)} collective-permute-done((bf16[192,384]{1,0:T(8,128)(2,1)S(1)}, bf16[192,384]{1,0:T(8,128)(2,1)S(1)}, u32[]{:S(2)}, u32[]{:S(2)}) %collective-permute-start.5) | collective-permute-done | bytes 147488 | tf_op jit(solution)/shard_map/ppermute | solution.py:297
  31.4 6.3 %collective-permute-start.11 = (bf16[64,384]{1,0:T(8,128)(2,1)S(1)}, bf16[64,384]{1,0:T(8,128)(2,1)S(1)}, u32[]{:S(2)}, u32[]{:S(2)}) collective-permute-start(bf16[64,384]{1,0:T(8,128)(2,1)S(1)} %shard_map.116), channel_id=1, source_target_pairs={{0,4},{4,0},{8,12},{12,8},{1,5},{5,1},{9,13},{13,9},{2,6},{6,2},{1... | collective-permute-start | bytes 147464 | tf_op jit(solution)/shard_map/ppermute | solution.py:297
  37.8 0.0 collective-permute-done.15.far
  37.8 0.5 %collective-permute-start.12 = (bf16[64,384]{1,0:T(8,128)(2,1)S(1)}, bf16[64,384]{1,0:T(8,128)(2,1)S(1)}, u32[]{:S(2)}, u32[]{:S(2)}) collective-permute-start(bf16[64,384]{1,0:T(8,128)(2,1)S(1)} %shard_map.117), channel_id=1, source_target_pairs={{0,4},{4,0},{8,12},{12,8},{1,5},{5,1},{9,13},{13,9},{2,6},{6,2},{1... | collective-permute-start | bytes 147464 | tf_op jit(solution)/shard_map/ppermute | solution.py:297
  38.3 0.0 collective-permute-done.16.far
  38.3 2.1 %collective-permute-start.18 = (bf16[192,128]{1,0:T(8,128)(2,1)S(1)}, bf16[192,128]{1,0:T(8,128)(2,1)S(1)}, u32[]{:S(2)}, u32[]{:S(2)}) collective-permute-start(bf16[192,128]{1,0:T(8,128)(2,1)S(1)} %shard_map.122), channel_id=1, source_target_pairs={{0,4},{4,0},{8,12},{12,8},{1,5},{5,1},{9,13},{13,9},{2,6},{6,2},{1... | collective-permute-start | bytes 147464 | tf_op jit(solution)/shard_map/ppermute | solution.py:297
  40.4 0.0 collective-permute-done.4.far
  40.4 0.6 %collective-permute-start.19 = (bf16[192,128]{1,0:T(8,128)(2,1)S(1)}, bf16[192,128]{1,0:T(8,128)(2,1)S(1)}, u32[]{:S(2)}, u32[]{:S(2)}) collective-permute-start(bf16[192,128]{1,0:T(8,128)(2,1)S(1)} %shard_map.123), channel_id=1, source_target_pairs={{0,4},{4,0},{8,12},{12,8},{1,5},{5,1},{9,13},{13,9},{2,6},{6,2},{1... | collective-permute-start | bytes 147464 | tf_op jit(solution)/shard_map/ppermute | solution.py:297
  41.0 0.0 collective-permute-done.11.back_sound0
  41.0 2.0 %collective-permute-start.6 = (bf16[192,128]{1,0:T(8,128)(2,1)S(1)}, bf16[192,128]{1,0:T(8,128)(2,1)S(1)}, u32[]{:S(2)}, u32[]{:S(2)}) collective-permute-start(bf16[192,128]{1,0:T(8,128)(2,1)S(1)} %shard_map.114), channel_id=1, source_target_pairs={{0,4},{4,0},{8,12},{12,8},{1,5},{5,1},{9,13},{13,9},{2,6},{6,2},{1... | collective-permute-start | bytes 147464 | tf_op jit(solution)/shard_map/ppermute | solution.py:297
  43.0 0.9 %shard_map.115 = (bf16[128,768]{1,0:T(8,128)(2,1)S(1)}, bf16[64,768]{1,0:T(8,128)(2,1)S(1)}) custom-call(s32[1]{0:T(128)} %bitcast.me_ref, f32[192,256]{1,0:T(8,128)S(1)} %get-tuple-element.28.near_ref, bf16[192,384]{1,0:T(8,128)(2,1)S(1)} %get-tuple-element.29.asks0.asks, bf16[192,384]{1,0:T(8,128)(2,1)S(1)} %get-tuple-element.23.asks.asks1, ...), custom_call_target="tpu_custom_call" | custom-call | flops 150994944 | bytes 589824 | tf_op jit(solution)/shard_map/pallas_call | solution.py:303
  44.1 0.0 collective-permute-done.12.back_sound1
  44.1 0.0 collective-permute-done.18.refs_4_
  44.1 0.4 collective-permute-done.19.refs_5_
  44.5 0.0 collective-permute-done.17.refs_3_
  44.5 0.9 %shard_map.124 = (bf16[128,768]{1,0:T(8,128)(2,1)}, bf16[128,768]{1,0:T(8,128)(2,1)}, bf16[64,768]{1,0:T(8,128)(2,1)}, bf16[64,768]{1,0:T(8,128)(2,1)}) custom-call(s32[1]{0:T(128)} %bitcast.me_ref, bf16[128,768]{1,0:T(8,128)(2,1)S(1)} %get-tuple-element.31.cross, bf16[64,768]{1,0:T(8,128)(2,1)S(1)} %get-tuple-element.32.own_sound, ...), custom_call_target="tpu_custom_call" | custom-call | tf_op jit(solution)/shard_map/pallas_call | solution.py:303
  45.4 0.0 collective-permute-done.6.back
  45.4 0.6 %shard_map.125 = (bf16[128,768]{1,0:T(8,128)(2,1)}, bf16[64,768]{1,0:T(8,128)(2,1)}) custom-call(s32[1]{0:T(128)} %bitcast.me_ref, bf16[192,128]{1,0:T(8,128)(2,1)S(1)} %shard_map.113.own, bf16[192,128]{1,0:T(8,128)(2,1)S(1)} %collective-permute-done.6.back, ...), custom_call_target="tpu_custom_call", output_to_operand_aliasing={{0}: (3, {}), {1}: (4, {})} | custom-call | tf_op jit(solution)/shard_map/pallas_call | solution.py:303
  (12 shorter events, 0.1 us)
Async XLA Ops:
  0.6 4.4 %copy-start.2 = (bf16[128,768]{1,0:T(8,128)(2,1)S(1)}, bf16[128,768]{1,0:T(8,128)(2,1)}, u32[]{:S(2)}) copy-start(bf16[128,768]{1,0:T(8,128)(2,1)} %video_k.3) | copy-start | bytes 589828
  1.8 9.0 %collective-permute-start.7 = (bf16[256,384]{1,0:T(8,128)(2,1)S(1)}, bf16[256,384]{1,0:T(8,128)(2,1)S(1)}, u32[]{:S(2)}, u32[]{:S(2)}) collective-permute-start(bf16[256,384]{1,0:T(8,128)(2,1)S(1)} %get-tuple-element.25.out), channel_id=1, source_target_pairs={{0,4},{4,0},{8,12},{12,8},{1,5},{5,1},{9,13},{13,9},{2,6},{6,2},{1... | collective-permute-start | bytes 589832 | tf_op jit(solution)/shard_map/ppermute | solution.py:297
  5.0 6.4 %collective-permute-start = (bf16[256,384]{1,0:T(8,128)(2,1)S(1)}, bf16[256,384]{1,0:T(8,128)(2,1)S(1)}, u32[]{:S(2)}, u32[]{:S(2)}) collective-permute-start(bf16[256,384]{1,0:T(8,128)(2,1)S(1)} %get-tuple-element.25.out), channel_id=1, source_target_pairs={{0,1},{1,0},{4,8},{5,9},{8,4},{9,5},{12,13},{13,12},{2,3},{3,2},{6... | collective-permute-start | bytes 589832 | tf_op jit(solution)/shard_map/ppermute | solution.py:300
  5.0 18.3 %collective-permute-start.2 = (bf16[128,768]{1,0:T(8,128)(2,1)S(1)}, bf16[128,768]{1,0:T(8,128)(2,1)S(1)}, u32[]{:S(2)}, u32[]{:S(2)}) collective-permute-start(bf16[128,768]{1,0:T(8,128)(2,1)S(1)} %copy-done.2), channel_id=1, source_target_pairs={{0,1},{1,0},{4,8},{5,9},{8,4},{9,5},{12,13},{13,12},{2,3},{3,2},{6... | collective-permute-start | bytes 589832 | tf_op jit(solution)/shard_map/ppermute | solution.py:300
  5.5 21.9 %collective-permute-start.8 = (bf16[256,384]{1,0:T(8,128)(2,1)S(1)}, bf16[256,384]{1,0:T(8,128)(2,1)S(1)}, u32[]{:S(2)}, u32[]{:S(2)}) collective-permute-start(bf16[256,384]{1,0:T(8,128)(2,1)S(1)} %get-tuple-element.30.over.own), channel_id=1, source_target_pairs={{0,4},{4,0},{8,12},{12,8},{1,5},{5,1},{9,13},{13,9},{2,6},{6,2},{1... | collective-permute-start | bytes 589832 | tf_op jit(solution)/shard_map/ppermute | solution.py:297
  8.1 6.3 %collective-permute-start.13 = (bf16[128,384]{1,0:T(8,128)(2,1)S(1)}, bf16[128,384]{1,0:T(8,128)(2,1)S(1)}, u32[]{:S(2)}, u32[]{:S(2)}) collective-permute-start(bf16[128,384]{1,0:T(8,128)(2,1)S(1)} %get-tuple-element.33), channel_id=1, source_target_pairs={{0,1},{1,0},{4,8},{5,9},{8,4},{9,5},{12,13},{13,12},{2,3},{3,2},{6... | collective-permute-start | bytes 294920 | tf_op jit(solution)/shard_map/ppermute | solution.py:300
  8.1 0.7 %copy-start = (s32[256]{0:T(256)S(1)}, s32[256]{0:T(256)}, u32[]{:S(2)}) copy-start(s32[256]{0:T(256)} %param.14) | copy-start | bytes 3076
  8.1 0.7 %copy-start.1 = (s32[4]{0:T(128)S(1)}, s32[4]{0:T(128)}, u32[]{:S(2)}) copy-start(s32[4]{0:T(128)} %count_ref.1) | copy-start | bytes 52
  10.8 16.5 %collective-permute-start.14 = (bf16[256,384]{1,0:T(8,128)(2,1)S(1)}, bf16[256,384]{1,0:T(8,128)(2,1)S(1)}, u32[]{:S(2)}, u32[]{:S(2)}) collective-permute-start(bf16[256,384]{1,0:T(8,128)(2,1)S(1)} %collective-permute-done.7.first.mate), channel_id=1, source_target_pairs={{0,1},{1,0},{4,8},{5,9},{8,4},{9,5},{12,13},{13,12},{2,3},{3,2},{6... | collective-permute-start | bytes 589832 | tf_op jit(solution)/shard_map/ppermute | solution.py:300
  11.5 16.9 %collective-permute-start.1 = (bf16[256,384]{1,0:T(8,128)(2,1)S(1)}, bf16[256,384]{1,0:T(8,128)(2,1)S(1)}, u32[]{:S(2)}, u32[]{:S(2)}) collective-permute-start(bf16[256,384]{1,0:T(8,128)(2,1)S(1)} %broadcast_select_fusion), channel_id=1, source_target_pairs={{0,4},{4,0},{8,12},{12,8},{1,5},{5,1},{9,13},{13,9},{2,6},{6,2},{1... | collective-permute-start | bytes 589832 | tf_op jit(solution)/shard_map/ppermute | solution.py:297
  14.4 8.9 %collective-permute-start.10 = (bf16[192,384]{1,0:T(8,128)(2,1)S(1)}, bf16[192,384]{1,0:T(8,128)(2,1)S(1)}, u32[]{:S(2)}, u32[]{:S(2)}) collective-permute-start(bf16[192,384]{1,0:T(8,128)(2,1)S(1)} %get-tuple-element.29.asks0.asks), channel_id=1, source_target_pairs={{0,4},{4,0},{8,12},{12,8},{1,5},{5,1},{9,13},{13,9},{2,6},{6,2},{1... | collective-permute-start | bytes 442376 | tf_op jit(solution)/shard_map/ppermute | solution.py:297
  23.3 5.1 %collective-permute-start.3 = (bf16[128,384]{1,0:T(8,128)(2,1)S(1)}, bf16[128,384]{1,0:T(8,128)(2,1)S(1)}, u32[]{:S(2)}, u32[]{:S(2)}) collective-permute-start(bf16[128,384]{1,0:T(8,128)(2,1)S(1)} %get-tuple-element.26), channel_id=1, source_target_pairs={{0,1},{1,0},{4,8},{5,9},{8,4},{9,5},{12,13},{13,12},{2,3},{3,2},{6... | collective-permute-start | bytes 294920 | tf_op jit(solution)/shard_map/ppermute | solution.py:300
  23.3 8.1 %collective-permute-start.5 = (bf16[192,384]{1,0:T(8,128)(2,1)S(1)}, bf16[192,384]{1,0:T(8,128)(2,1)S(1)}, u32[]{:S(2)}, u32[]{:S(2)}) collective-permute-start(bf16[192,384]{1,0:T(8,128)(2,1)S(1)} %get-tuple-element.23.asks.asks1), channel_id=1, source_target_pairs={{0,4},{4,0},{8,12},{12,8},{1,5},{5,1},{9,13},{13,9},{2,6},{6,2},{1... | collective-permute-start | bytes 442376 | tf_op jit(solution)/shard_map/ppermute | solution.py:297
  27.4 1.6 %collective-permute-start.9 = (bf16[256,384]{1,0:T(8,128)(2,1)S(1)}, bf16[256,384]{1,0:T(8,128)(2,1)S(1)}, u32[]{:S(2)}, u32[]{:S(2)}) collective-permute-start(bf16[256,384]{1,0:T(8,128)(2,1)S(1)} %collective-permute-done.8.second), channel_id=1, source_target_pairs={{0,1},{1,0},{4,8},{5,9},{8,4},{9,5},{12,13},{13,12},{2,3},{3,2},{6... | collective-permute-start | bytes 589832 | tf_op jit(solution)/shard_map/ppermute | solution.py:300
  27.4 17.1 %collective-permute-start.17 = (bf16[192,384]{1,0:T(8,128)(2,1)S(1)}, bf16[192,384]{1,0:T(8,128)(2,1)S(1)}, u32[]{:S(2)}, u32[]{:S(2)}) collective-permute-start(bf16[192,384]{1,0:T(8,128)(2,1)S(1)} %shard_map.121), channel_id=1, source_target_pairs={{0,4},{4,0},{8,12},{12,8},{1,5},{5,1},{9,13},{13,9},{2,6},{6,2},{1... | collective-permute-start | bytes 442376 | tf_op jit(solution)/shard_map/ppermute | solution.py:297
  28.4 9.4 %collective-permute-start.15 = (bf16[256,128]{1,0:T(8,128)(2,1)S(1)}, bf16[256,128]{1,0:T(8,128)(2,1)S(1)}, u32[]{:S(2)}, u32[]{:S(2)}) collective-permute-start(bf16[256,128]{1,0:T(8,128)(2,1)S(1)} %get-tuple-element.41), channel_id=1, source_target_pairs={{0,1},{1,0},{4,8},{5,9},{8,4},{9,5},{12,13},{13,12},{2,3},{3,2},{6... | collective-permute-start | bytes 196616 | tf_op jit(solution)/shard_map/ppermute | solution.py:300
  28.4 9.9 %collective-permute-start.16 = (bf16[256,128]{1,0:T(8,128)(2,1)S(1)}, bf16[256,128]{1,0:T(8,128)(2,1)S(1)}, u32[]{:S(2)}, u32[]{:S(2)}) collective-permute-start(bf16[256,128]{1,0:T(8,128)(2,1)S(1)} %get-tuple-element.40), channel_id=1, source_target_pairs={{0,1},{1,0},{4,8},{5,9},{8,4},{9,5},{12,13},{13,12},{2,3},{3,2},{6... | collective-permute-start | bytes 196616 | tf_op jit(solution)/shard_map/ppermute | solution.py:300
  28.9 11.5 %collective-permute-start.4 = (bf16[256,128]{1,0:T(8,128)(2,1)S(1)}, bf16[256,128]{1,0:T(8,128)(2,1)S(1)}, u32[]{:S(2)}, u32[]{:S(2)}) collective-permute-start(bf16[256,128]{1,0:T(8,128)(2,1)S(1)} %get-tuple-element.42), channel_id=1, source_target_pairs={{0,1},{1,0},{4,8},{5,9},{8,4},{9,5},{12,13},{13,12},{2,3},{3,2},{6... | collective-permute-start | bytes 196616 | tf_op jit(solution)/shard_map/ppermute | solution.py:300
  31.4 9.6 %collective-permute-start.11 = (bf16[64,384]{1,0:T(8,128)(2,1)S(1)}, bf16[64,384]{1,0:T(8,128)(2,1)S(1)}, u32[]{:S(2)}, u32[]{:S(2)}) collective-permute-start(bf16[64,384]{1,0:T(8,128)(2,1)S(1)} %shard_map.116), channel_id=1, source_target_pairs={{0,4},{4,0},{8,12},{12,8},{1,5},{5,1},{9,13},{13,9},{2,6},{6,2},{1... | collective-permute-start | bytes 147464 | tf_op jit(solution)/shard_map/ppermute | solution.py:297
  37.8 6.3 %collective-permute-start.12 = (bf16[64,384]{1,0:T(8,128)(2,1)S(1)}, bf16[64,384]{1,0:T(8,128)(2,1)S(1)}, u32[]{:S(2)}, u32[]{:S(2)}) collective-permute-start(bf16[64,384]{1,0:T(8,128)(2,1)S(1)} %shard_map.117), channel_id=1, source_target_pairs={{0,4},{4,0},{8,12},{12,8},{1,5},{5,1},{9,13},{13,9},{2,6},{6,2},{1... | collective-permute-start | bytes 147464 | tf_op jit(solution)/shard_map/ppermute | solution.py:297
  38.3 5.8 %collective-permute-start.18 = (bf16[192,128]{1,0:T(8,128)(2,1)S(1)}, bf16[192,128]{1,0:T(8,128)(2,1)S(1)}, u32[]{:S(2)}, u32[]{:S(2)}) collective-permute-start(bf16[192,128]{1,0:T(8,128)(2,1)S(1)} %shard_map.122), channel_id=1, source_target_pairs={{0,4},{4,0},{8,12},{12,8},{1,5},{5,1},{9,13},{13,9},{2,6},{6,2},{1... | collective-permute-start | bytes 147464 | tf_op jit(solution)/shard_map/ppermute | solution.py:297
  40.4 4.1 %collective-permute-start.19 = (bf16[192,128]{1,0:T(8,128)(2,1)S(1)}, bf16[192,128]{1,0:T(8,128)(2,1)S(1)}, u32[]{:S(2)}, u32[]{:S(2)}) collective-permute-start(bf16[192,128]{1,0:T(8,128)(2,1)S(1)} %shard_map.123), channel_id=1, source_target_pairs={{0,4},{4,0},{8,12},{12,8},{1,5},{5,1},{9,13},{13,9},{2,6},{6,2},{1... | collective-permute-start | bytes 147464 | tf_op jit(solution)/shard_map/ppermute | solution.py:297
  41.0 4.3 %collective-permute-start.6 = (bf16[192,128]{1,0:T(8,128)(2,1)S(1)}, bf16[192,128]{1,0:T(8,128)(2,1)S(1)}, u32[]{:S(2)}, u32[]{:S(2)}) collective-permute-start(bf16[192,128]{1,0:T(8,128)(2,1)S(1)} %shard_map.114), channel_id=1, source_target_pairs={{0,4},{4,0},{8,12},{12,8},{1,5},{5,1},{9,13},{13,9},{2,6},{6,2},{1... | collective-permute-start | bytes 147464 | tf_op jit(solution)/shard_map/ppermute | solution.py:297

commit v9 on v7

--- a/solution.py
+++ b/solution.py
@@ -187,48 +187,60 @@
                 mate_ref[:, to] = blend(asks[video_rows:, cols], keys, values, None)
 
 
-def audio_own_kernel(n, me_ref, near_ref, asks0, asks1, out, over, first, second, across, far, *outs):
-    cross_ref, own_ref = outs
+def audio_own_kernel(n, me_ref, near_ref, asks0, asks1, out, second, across, far, cross_ref, own_ref):
     audio_rows, width = own_ref.shape[0], out.shape[1]
     video_rows = cross_ref.shape[0]
     me = me_ref[0]
-    at_end = (me == 0) | (me == n - 1)
-
-    def run(blocks):
+
+    @pl.when((me > 0) & (me < n - 1))
+    def _():
         for half, asks in enumerate((asks0, asks1)):
             for at in range(0, width, HEAD_DIM):
                 cols = slice(at, at + HEAD_DIM)
                 to = slice(half * width + at, half * width + at + HEAD_DIM)
-                keys, values = sound_blocks(blocks, audio_rows, half, cols)
+                keys, values = sound_blocks((out, second, across, far), audio_rows, half, cols)
                 mixed = blend(asks[:, cols], keys, values, near_ref[...])
                 cross_ref[:, to] = mixed[:video_rows]
                 own_ref[:, to] = mixed[video_rows:]
 
-    @pl.when(jnp.logical_not(at_end))
+
+def audio_end_kernel(n, me_ref, near_ref, asks0, asks1, over, first, part1, part2, far, cross_ref):
+    video_rows, width = cross_ref.shape[0], over.shape[1]
+    audio_rows = over.shape[0] // 4
+    me = me_ref[0]
+
+    @pl.when((me == 0) | (me == n - 1))
     def _():
-        run((out, second, across, far))
-
-    @pl.when(at_end)
-    def _():
-        run((over, first, second, far))
-
-
-def video_kernel(n, at, half, me_ref, mask_ref, asks, own, mate, keys2, values2, far, out_ref):
+        for half, asks in enumerate((asks0, asks1)):
+            for at in range(0, width, HEAD_DIM):
+                cols = slice(at, at + HEAD_DIM)
+                to = slice(half * width + at, half * width + at + HEAD_DIM)
+                shift = 0 if at < part1.shape[1] else part1.shape[1]
+                part = (part2 if shift else part1).at[:, at - shift : at - shift + HEAD_DIM]
+                blocks = [b.at[:, cols] for b in (over, first)] + [part, far.at[:, cols]]
+                every = slice(0, HEAD_DIM)
+                keys, values = sound_blocks(blocks, audio_rows, half, every)
+                cross_ref[:, to] = blend(asks[:video_rows, cols], keys, values, near_ref[:video_rows])
+
+
+def video_kernel(n, at, half, offset, me_ref, mask_ref, asks, own, mate, keys2, values2, far, out_ref):
     video_rows = own.shape[0] // 2
     me = me_ref[0]
 
     @pl.when((me > 0) & (me < n - 1))
     def _():
-        for head in range(own.shape[1] // HEAD_DIM):
+        for head in range(far.shape[1] // HEAD_DIM):
             cols = slice(head * HEAD_DIM, (head + 1) * HEAD_DIM)
+            near_cols = slice((offset + head) * HEAD_DIM, (offset + head + 1) * HEAD_DIM)
             all_cols = slice((at + head) * HEAD_DIM, (at + head + 1) * HEAD_DIM)
             half_cols = slice((at - half + head) * HEAD_DIM, (at - half + head + 1) * HEAD_DIM)
             top, low = slice(0, video_rows), slice(video_rows, 2 * video_rows)
             keys = jnp.concatenate(
-                [own[top, cols], mate[top, cols], keys2[:, all_cols], far[top, cols]], axis=0
+                [own[top, near_cols], mate[top, near_cols], keys2[:, all_cols], far[top, cols]], axis=0
             )
             values = jnp.concatenate(
-                [own[low, cols], mate[low, cols], values2[:, half_cols], far[low, cols]], axis=0
+                [own[low, near_cols], mate[low, near_cols], values2[:, half_cols], far[low, cols]],
+                axis=0,
             )
             out_ref[:, cols] = blend(asks[:, half_cols], keys, values, mask_ref[...])
 
@@ -243,18 +255,20 @@
     return moves
 
 
-def place_kernel(n, me_ref, cross, own0, own1, own2, back0, back1, back2, *outs):
-    video_self, video_cross, audio_self, audio_cross, sem = outs
+def place_kernel(n, me_ref, own_cross, end_cross, *refs):
+    count = (len(refs) - 5) // 2
+    own, back = refs[:count], refs[count : 2 * count]
+    video_self, video_cross, audio_self, audio_cross, sem = refs[2 * count :]
     at_end = (me_ref[0] == 0) | (me_ref[0] == n - 1)
-    for role, sound, parts in (
-        (jnp.logical_not(at_end), own0, (own1, own2)),
-        (at_end, back0, (back1, back2)),
+    for role, cross, parts in (
+        (jnp.logical_not(at_end), own_cross, own),
+        (at_end, end_cross, back),
     ):
 
         @pl.when(role)
-        def _(sound=sound, parts=parts):
-            moves = [(cross, video_cross), (sound, audio_self)]
-            moves += place_pieces(parts, 0, cross.shape[0], video_self, audio_cross)
+        def _(cross=cross, parts=parts):
+            moves = [(cross, video_cross), (parts[0], audio_self)]
+            moves += place_pieces(parts[1:], 0, cross.shape[0], video_self, audio_cross)
             for copy in move_all(moves, sem):
                 copy.wait()
 
@@ -357,24 +371,37 @@
     values_across = [cross(values0), cross(values1)]
     sight_mate = [mate(first_out)]
     sound_across = cross(first_out)
-    second_mate = mate(jnp.where(at_end, first_over, sound_across))
+    second_mate = mate(first_over)
     sound_far = cross(second_mate)
-    sight_mate += [mate(sights[i]) for i in (1, 2)]
-    sight_far = [cross(sight_mate[i]) for i in range(3)]
+    at = 0
+    for i in (1, 2):
+        part = sound_across[:, at : at + lengths[i]]
+        sight_mate.append(mate(jnp.where(at_end, sights[i], part)))
+        at += lengths[i]
+    pieces = [(0, chunks[0], 0, 0)]
+    sight_far = [cross(sight_mate[0])]
+    for source in (1, 2):
+        for i in range(chunks[source]):
+            pieces.append((sum(chunks[:source]) + i, 1, source, i))
+            part = sight_mate[source]
+            if chunks[source] > 1:
+                part = part[:, i * HEAD_DIM : (i + 1) * HEAD_DIM]
+            sight_far.append(cross(part))
+    last = len(pieces) - 1
     asks_mate = [mate(asks[i]) for i in range(2)]
 
     def look(i, queries, mask):
-        at, size = sum(chunks[:i]), chunks[i]
-        half = min(i, 1)
+        at, size, source, offset = pieces[i]
+        half = min(source, 1)
         return call(
-            functools.partial(video_kernel, n, at, half * chunks[0]),
+            functools.partial(video_kernel, n, at, half * chunks[0], offset),
             (((rows, size * HEAD_DIM), jnp.bfloat16),),
             [SMEM] + [VMEM] * 7,
             place,
             mask,
             queries[half],
-            sights[i],
-            sight_mate[i],
+            sights[source],
+            sight_mate[source],
             keys_across,
             values_across[half],
             sight_far[i],
@@ -382,8 +409,8 @@
             cost_estimate=cost(rows, n * video_rows, size),
         )[0]
 
-    back = [mate(look(i, asks_mate, mask1)) for i in range(3)]
-    mine = [look(i, asks, mask0) for i in range(3)]
+    back = [mate(look(i, asks_mate, mask1)) for i in range(last + 1)]
+    mine = [look(i, asks, mask0) for i in range(last + 1)]
     theirs = call(
         functools.partial(audio_mate_kernel, n),
         (((audio_rows, width), jnp.bfloat16),),
@@ -397,45 +424,59 @@
         out_specs=(VMEM,),
         cost_estimate=cost(audio_rows, n * audio_rows, heads),
     )[0]
-    video_cross, own = call(
+    own_cross, own = call(
         functools.partial(audio_own_kernel, n),
         (((video_rows, width), jnp.bfloat16), ((audio_rows, width), jnp.bfloat16)),
-        [SMEM] + [VMEM] * 9,
+        [SMEM] + [VMEM] * 7,
         place,
         near,
         *asks,
         first_out,
-        first_over,
-        sight_mate[0],
         second_mate,
         sound_across,
         sound_far,
         out_specs=(VMEM,) * 2,
         cost_estimate=cost(rows, n * audio_rows, heads),
     )
+    end_cross = call(
+        functools.partial(audio_end_kernel, n),
+        (((video_rows, width), jnp.bfloat16),),
+        [SMEM] + [VMEM] * 8,
+        place,
+        near,
+        *asks,
+        first_over,
+        sight_mate[0],
+        sight_mate[1],
+        sight_mate[2],
+        sound_far,
+        out_specs=(VMEM,),
+        cost_estimate=cost(rows, n * audio_rows, heads),
+    )[0]
     back_sound = mate(theirs)
     video_shape = ((video_rows, width), jnp.bfloat16)
     audio_shape = ((audio_rows, width), jnp.bfloat16)
     video_self, video_cross, audio_self, audio_cross = call(
         functools.partial(place_kernel, n),
         (video_shape, video_shape, audio_shape, audio_shape),
-        [SMEM] + [VMEM] * 7,
-        place,
-        video_cross,
+        [SMEM] + [VMEM] * (4 + 2 * last),
+        place,
+        own_cross,
+        end_cross,
         own,
-        *mine[:2],
+        *mine[:last],
         back_sound,
-        *back[:2],
+        *back[:last],
         out_specs=(HBM,) * 4,
-        scratch_shapes=[pltpu.SemaphoreType.DMA((6,))],
+        scratch_shapes=[pltpu.SemaphoreType.DMA((2 + 2 * last,))],
     )
     video_self, audio_cross = call(
-        functools.partial(place_last_kernel, n, width - lengths[2]),
+        functools.partial(place_last_kernel, n, width - HEAD_DIM),
         (video_shape, audio_shape),
         [SMEM] + [VMEM] * 2 + [HBM] * 2,
         place,
-        mine[2],
-        back[2],
+        mine[last],
+        back[last],
         video_self,
         audio_cross,
         out_specs=(HBM,) * 2,

time: 41.7 us -> 44.7 us (1.072)
  starting transfers between devices: 25.7 us -> 33.1 us
  waiting for transfers between devices: 9.54 us -> 4.74 us
  local copies, waits for them, and re-layouts: 0.1 us -> 0.7 us
    ppermute x10 -> x11, starting transfers between devices: 24 us -> 31.4 us  [mate(): return lax.ppermute(block, 'seq', mate_pairs)]
    ppermute x10 -> x11, waiting for transfers between devices: 9.52 us -> 4.72 us  [mate(): return lax.ppermute(block, 'seq', mate_pairs)]
    unnamed x6, local copies, waits for them, and re-layouts: 0.1 us -> 0.69 us
    pallas_call x12 -> x15, Pallas kernels: 5.45 us -> 5.15 us  [call(): pl.pallas_call(kernel, out_shape=tuple((jax.ShapeDtypeStruct(shape, dtype...]
    ppermute x8 -> x9, starting transfers between devices: 1.65 us -> 1.72 us  [cross(): return lax.ppermute(block, ('seq', 'mp'), cross_pairs)]
  transfers between devices with their start and end apart: 18 -> 20, of which waited for: 4 -> 4; matrix products, arithmetic and copies ran while one was open for 0% -> 0% of each run, Pallas kernels for 9% -> 7%
where the time goes in v9:
time: 44.7 us; the launch traced here: 44.5 us
  starting transfers between devices  33.1 us (74%)
  Pallas kernels  5.15 us (12%)
  waiting for transfers between devices  4.74 us (11%)
  between operations  0.76 us (2%)
  local copies, waits for them, and re-layouts  0.7 us (2%)
    ppermute x11, starting transfers between devices, mate(): return lax.ppermute(block, 'seq', mate_pairs)  31.4 us
    pallas_call x15, Pallas kernels, call(): pl.pallas_call(kernel, out_shape=tuple((jax.ShapeDtypeStruct(shape, dtype...  5.15 us
    ppermute x11, waiting for transfers between devices, mate(): return lax.ppermute(block, 'seq', mate_pairs)  4.72 us
    ppermute x9, starting transfers between devices, cross(): return lax.ppermute(block, ('seq', 'mp'), cross_pairs)  1.72 us
  transfers between devices with their start and end apart: 20, of which 4 were waited for; matrix products, arithmetic and copies ran while one was open for 0% of the time, Pallas kernels for 7%

profile of v9, /device:TPU:0, one launch (start us, length us, event | category | flops | bytes accessed | tf_op | source)
XLA Modules:
  0.0 44.5 jit_solution(6028152307652078379)
XLA Ops:
  0.6 0.0 copy-start.2
  0.6 1.2 %shard_map.112 = (bf16[256,384]{1,0:T(8,128)(2,1)S(1)}, bf16[256,384]{1,0:T(8,128)(2,1)S(1)}, bf16[128,384]{1,0:T(8,128)(2,1)S(1)}) custom-call(s32[1]{0:T(128)} %bitcast.me_ref, bf16[128,768]{1,0:T(8,128)(2,1)} %video_k.3, bf16[128,768]{1,0:T(8,128)(2,1)} %video_v.3, bf16[64,768]{1,0:T(8,128)(2,1)} %audio_k.1, bf16[64,768]{1,0:T(8,128)(2,1)} %audio_v.1), custom_call_target="tpu_custom_call" | custom-call | tf_op jit(solution)/shard_map/pallas_call | solution.py:320
  1.8 0.6 %collective-permute-start = (bf16[256,384]{1,0:T(8,128)(2,1)S(1)}, bf16[256,384]{1,0:T(8,128)(2,1)S(1)}, u32[]{:S(2)}, u32[]{:S(2)}) collective-permute-start(bf16[256,384]{1,0:T(8,128)(2,1)S(1)} %get-tuple-element.26.out), channel_id=1, source_target_pairs={{0,1},{1,0},{4,8},{5,9},{8,4},{9,5},{12,13},{13,12},{2,3},{3,2},{6... | collective-permute-start | bytes 589832 | tf_op jit(solution)/shard_map/ppermute | solution.py:317
  2.4 0.0 copy-done.2
  2.4 0.1 collective-permute-start.2
  2.5 4.5 %collective-permute-start.9 = (bf16[256,384]{1,0:T(8,128)(2,1)S(1)}, bf16[256,384]{1,0:T(8,128)(2,1)S(1)}, u32[]{:S(2)}, u32[]{:S(2)}) collective-permute-start(bf16[256,384]{1,0:T(8,128)(2,1)S(1)} %get-tuple-element.26.out), channel_id=1, source_target_pairs={{0,4},{4,0},{8,12},{12,8},{1,5},{5,1},{9,13},{13,9},{2,6},{6,2},{1... | collective-permute-start | bytes 589832 | tf_op jit(solution)/shard_map/ppermute | solution.py:314
  7.0 0.0 collective-permute-start.11
  7.0 1.6 %collective-permute-start.7 = (bf16[256,384]{1,0:T(8,128)(2,1)S(1)}, bf16[256,384]{1,0:T(8,128)(2,1)S(1)}, u32[]{:S(2)}, u32[]{:S(2)}) collective-permute-start(bf16[256,384]{1,0:T(8,128)(2,1)S(1)} %get-tuple-element.31.over.own), channel_id=1, source_target_pairs={{0,4},{4,0},{8,12},{12,8},{1,5},{5,1},{9,13},{13,9},{2,6},{6,2},{1... | collective-permute-start | bytes 589832 | tf_op jit(solution)/shard_map/ppermute | solution.py:314
  8.6 0.0 copy-start
  8.6 0.0 copy-start.1
  8.6 0.7 %copy-done = s32[256]{0:T(256)S(1)} copy-done((s32[256]{0:T(256)S(1)}, s32[256]{0:T(256)}, u32[]{:S(2)}) %copy-start) | copy-done | bytes 1048
  9.3 0.0 copy-done.1
  9.3 1.9 %shard_map.111 = (bf16[256,256]{1,0:T(8,128)(2,1)S(1)}, bf16[256,128]{1,0:T(8,128)(2,1)S(1)}, bf16[192,384]{1,0:T(8,128)(2,1)S(1)}, bf16[192,384]{1,0:T(8,128)(2...) custom-call(s32[1]{0:T(128)} %bitcast.me_ref, ...), custom_call_target="tpu_custom_call" | custom-call | tf_op jit(solution)/shard_map/pallas_call | solution.py:320
  11.2 0.0 collective-permute-done.across
  11.2 1.5 %collective-permute-start.15 = (bf16[192,384]{1,0:T(8,128)(2,1)S(1)}, bf16[192,384]{1,0:T(8,128)(2,1)S(1)}, u32[]{:S(2)}, u32[]{:S(2)}) collective-permute-start(bf16[192,384]{1,0:T(8,128)(2,1)S(1)} %get-tuple-element.30.asks0.asks), channel_id=1, source_target_pairs={{0,4},{4,0},{8,12},{12,8},{1,5},{5,1},{9,13},{13,9},{2,6},{6,2},{1... | collective-permute-start | bytes 442376 | tf_op jit(solution)/shard_map/ppermute | solution.py:314
  12.8 0.0 collective-permute-done.11.values2
  12.8 5.2 %collective-permute-start.10 = (bf16[256,256]{1,0:T(8,128)(2,1)S(1)}, bf16[256,256]{1,0:T(8,128)(2,1)S(1)}, u32[]{:S(2)}, u32[]{:S(2)}) collective-permute-start(bf16[256,256]{1,0:T(8,128)(2,1)S(1)} %slice_select_fusion), channel_id=1, source_target_pairs={{0,4},{4,0},{8,12},{12,8},{1,5},{5,1},{9,13},{13,9},{2,6},{6,2},{1... | collective-permute-start | bytes 393224 | tf_op jit(solution)/shard_map/ppermute | solution.py:314
  17.9 0.0 collective-permute-done.9.first.mate
  17.9 0.0 collective-permute-start.12
  18.0 1.7 %collective-permute-done.15.asks0.asks = bf16[192,384]{1,0:T(8,128)(2,1)S(1)} collective-permute-done((bf16[192,384]{1,0:T(8,128)(2,1)S(1)}, bf16[192,384]{1,0:T(8,128)(2,1)S(1)}, u32[]{:S(2)}, u32[]{:S(2)}) %collective-permute-start.15) | collective-permute-done | bytes 147488 | tf_op jit(solution)/shard_map/ppermute | solution.py:314
  19.7 1.7 %collective-permute-start.1 = (bf16[256,128]{1,0:T(8,128)(2,1)S(1)}, bf16[256,128]{1,0:T(8,128)(2,1)S(1)}, u32[]{:S(2)}, u32[]{:S(2)}) collective-permute-start(bf16[256,128]{1,0:T(8,128)(2,1)S(1)} %slice_select_fusion.1), channel_id=1, source_target_pairs={{0,4},{4,0},{8,12},{12,8},{1,5},{5,1},{9,13},{13,9},{2,6},{6,2},{1... | collective-permute-start | bytes 196616 | tf_op jit(solution)/shard_map/ppermute | solution.py:314
  21.4 0.0 collective-permute-done.2.keys2
  21.4 0.0 collective-permute-start.3
  21.4 0.0 collective-permute-done.7.second
  21.4 2.4 %collective-permute-start.5 = (bf16[192,384]{1,0:T(8,128)(2,1)S(1)}, bf16[192,384]{1,0:T(8,128)(2,1)S(1)}, u32[]{:S(2)}, u32[]{:S(2)}) collective-permute-start(bf16[192,384]{1,0:T(8,128)(2,1)S(1)} %get-tuple-element.24.asks.asks1), channel_id=1, source_target_pairs={{0,4},{4,0},{8,12},{12,8},{1,5},{5,1},{9,13},{13,9},{2,6},{6,2},{1... | collective-permute-start | bytes 442376 | tf_op jit(solution)/shard_map/ppermute | solution.py:314
  23.8 0.1 collective-permute-done.1.mate.part2
  23.9 0.0 collective-permute-start.8
  23.9 0.0 collective-permute-done.12.far
  23.9 0.5 %collective-permute-start.4 = (bf16[256,128]{1,0:T(8,128)(2,1)S(1)}, bf16[256,128]{1,0:T(8,128)(2,1)S(1)}, u32[]{:S(2)}, u32[]{:S(2)}) collective-permute-start(bf16[256,128]{1,0:T(8,128)(2,1)S(1)} %collective-permute-done.1.mate.part2), channel_id=1, source_target_pairs={{0,1},{1,0},{4,8},{5,9},{8,4},{9,5},{12,13},{13,12},{2,3},{3,2},{6... | collective-permute-start | bytes 196616 | tf_op jit(solution)/shard_map/ppermute | solution.py:317
  24.4 0.0 collective-permute-done.10.part1.mate
  24.5 4.8 %collective-permute-start.17 = (bf16[192,384]{1,0:T(8,128)(2,1)S(1)}, bf16[192,384]{1,0:T(8,128)(2,1)S(1)}, u32[]{:S(2)}, u32[]{:S(2)}) collective-permute-start(bf16[192,384]{1,0:T(8,128)(2,1)S(1)} %shard_map.121), channel_id=1, source_target_pairs={{0,4},{4,0},{8,12},{12,8},{1,5},{5,1},{9,13},{13,9},{2,6},{6,2},{1... | collective-permute-start | bytes 442376 | tf_op jit(solution)/shard_map/ppermute | solution.py:314
  29.3 0.0 collective-permute-done.5.asks.asks1
  29.3 0.1 collective-permute-start.13
  29.4 0.0 collective-permute-done.8.far
  29.4 0.5 %collective-permute-start.14 = (bf16[256,128]{1,0:T(8,128)(2,1)S(1)}, bf16[256,128]{1,0:T(8,128)(2,1)S(1)}, u32[]{:S(2)}, u32[]{:S(2)}) collective-permute-start(bf16[256,128]{1,0:T(8,128)(2,1)S(1)} %get-tuple-element.42), channel_id=1, source_target_pairs={{0,1},{1,0},{4,8},{5,9},{8,4},{9,5},{12,13},{13,12},{2,3},{3,2},{6... | collective-permute-start | bytes 196616 | tf_op jit(solution)/shard_map/ppermute | solution.py:317
  29.9 0.0 collective-permute-done.3.values2
  29.9 5.8 %collective-permute-start.16 = (bf16[64,768]{1,0:T(8,128)(2,1)S(1)}, bf16[64,768]{1,0:T(8,128)(2,1)S(1)}, u32[]{:S(2)}, u32[]{:S(2)}) collective-permute-start(bf16[64,768]{1,0:T(8,128)(2,1)S(1)} %shard_map.120), channel_id=1, source_target_pairs={{0,4},{4,0},{8,12},{12,8},{1,5},{5,1},{9,13},{13,9},{2,6},{6,2},{1... | collective-permute-start | bytes 294920 | tf_op jit(solution)/shard_map/ppermute | solution.py:314
  35.7 0.0 collective-permute-done.4.far
  35.7 0.6 %collective-permute-start.6 = (bf16[192,128]{1,0:T(8,128)(2,1)S(1)}, bf16[192,128]{1,0:T(8,128)(2,1)S(1)}, u32[]{:S(2)}, u32[]{:S(2)}) collective-permute-start(bf16[192,128]{1,0:T(8,128)(2,1)S(1)} %shard_map.114), channel_id=1, source_target_pairs={{0,4},{4,0},{8,12},{12,8},{1,5},{5,1},{9,13},{13,9},{2,6},{6,2},{1... | collective-permute-start | bytes 147464 | tf_op jit(solution)/shard_map/ppermute | solution.py:314
  36.3 0.0 collective-permute-done.13.far
  36.3 2.5 %collective-permute-start.18 = (bf16[192,128]{1,0:T(8,128)(2,1)S(1)}, bf16[192,128]{1,0:T(8,128)(2,1)S(1)}, u32[]{:S(2)}, u32[]{:S(2)}) collective-permute-start(bf16[192,128]{1,0:T(8,128)(2,1)S(1)} %shard_map.122), channel_id=1, source_target_pairs={{0,4},{4,0},{8,12},{12,8},{1,5},{5,1},{9,13},{13,9},{2,6},{6,2},{1... | collective-permute-start | bytes 147464 | tf_op jit(solution)/shard_map/ppermute | solution.py:314
  38.9 0.0 collective-permute-done.14.far
  38.9 0.6 %collective-permute-start.19 = (bf16[192,128]{1,0:T(8,128)(2,1)S(1)}, bf16[192,128]{1,0:T(8,128)(2,1)S(1)}, u32[]{:S(2)}, u32[]{:S(2)}) collective-permute-start(bf16[192,128]{1,0:T(8,128)(2,1)S(1)} %shard_map.123), channel_id=1, source_target_pairs={{0,4},{4,0},{8,12},{12,8},{1,5},{5,1},{9,13},{13,9},{2,6},{6,2},{1... | collective-permute-start | bytes 147464 | tf_op jit(solution)/shard_map/ppermute | solution.py:314
  39.5 0.6 %shard_map.116.end_cross = bf16[128,768]{1,0:T(8,128)(2,1)S(1)} custom-call(s32[1]{0:T(128)} %bitcast.me_ref, f32[192,256]{1,0:T(8,128)S(1)} %get-tuple-element.29.near_ref, bf16[192,384]{1,0:T(8,128)(2,1)S(1)} %get-tuple-element.30.asks0.asks, bf16[192,384]{1,0:T(8,128)(2,1)S(1)} %get-tuple-element.24.asks.asks1, ...), custom_call_target="tpu_custom_call" | custom-call | flops 150994944 | bytes 589824 | tf_op jit(solution)/shard_map/pallas_call | solution.py:320
  40.1 0.8 %collective-permute-done.18.refs_6_ = bf16[192,128]{1,0:T(8,128)(2,1)S(1)} collective-permute-done((bf16[192,128]{1,0:T(8,128)(2,1)S(1)}, bf16[192,128]{1,0:T(8,128)(2,1)S(1)}, u32[]{:S(2)}, u32[]{:S(2)}) %collective-permute-start.18) | collective-permute-done | bytes 49184 | tf_op jit(solution)/shard_map/ppermute | solution.py:314
  40.9 2.0 %collective-permute-done.19.refs_7_ = bf16[192,128]{1,0:T(8,128)(2,1)S(1)} collective-permute-done((bf16[192,128]{1,0:T(8,128)(2,1)S(1)}, bf16[192,128]{1,0:T(8,128)(2,1)S(1)}, u32[]{:S(2)}, u32[]{:S(2)}) %collective-permute-start.19) | collective-permute-done | bytes 49184 | tf_op jit(solution)/shard_map/ppermute | solution.py:314
  43.0 0.0 collective-permute-done.16.refs_4_
  43.0 0.0 collective-permute-done.17.refs_5_
  43.0 0.8 %shard_map.124 = (bf16[128,768]{1,0:T(8,128)(2,1)}, bf16[128,768]{1,0:T(8,128)(2,1)}, bf16[64,768]{1,0:T(8,128)(2,1)}, bf16[64,768]{1,0:T(8,128)(2,1)}) custom-call(s32[1]{0:T(128)} %bitcast.me_ref, bf16[128,768]{1,0:T(8,128)(2,1)S(1)} %get-tuple-element.32.own_cross, bf16[128,768]{1,0:T(8,128)(2,1)S(1)} %shard_map.116.end_cross, ...), custom_call_target="tpu_custom_call" | custom-call | tf_op jit(solution)/shard_map/pallas_call | solution.py:320
  43.8 0.0 collective-permute-done.6.back
  43.8 0.6 %shard_map.125 = (bf16[128,768]{1,0:T(8,128)(2,1)}, bf16[64,768]{1,0:T(8,128)(2,1)}) custom-call(s32[1]{0:T(128)} %bitcast.me_ref, bf16[192,128]{1,0:T(8,128)(2,1)S(1)} %shard_map.113.own, bf16[192,128]{1,0:T(8,128)(2,1)S(1)} %collective-permute-done.6.back, ...), custom_call_target="tpu_custom_call", output_to_operand_aliasing={{0}: (3, {}), {1}: (4, {})} | custom-call | tf_op jit(solution)/shard_map/pallas_call | solution.py:320
  (13 shorter events, 0.1 us)
Async XLA Ops:
  0.6 1.8 %copy-start.2 = (bf16[128,768]{1,0:T(8,128)(2,1)S(1)}, bf16[128,768]{1,0:T(8,128)(2,1)}, u32[]{:S(2)}) copy-start(bf16[128,768]{1,0:T(8,128)(2,1)} %video_k.3) | copy-start | bytes 589828
  1.8 9.4 %collective-permute-start = (bf16[256,384]{1,0:T(8,128)(2,1)S(1)}, bf16[256,384]{1,0:T(8,128)(2,1)S(1)}, u32[]{:S(2)}, u32[]{:S(2)}) collective-permute-start(bf16[256,384]{1,0:T(8,128)(2,1)S(1)} %get-tuple-element.26.out), channel_id=1, source_target_pairs={{0,1},{1,0},{4,8},{5,9},{8,4},{9,5},{12,13},{13,12},{2,3},{3,2},{6... | collective-permute-start | bytes 589832 | tf_op jit(solution)/shard_map/ppermute | solution.py:317
  2.4 19.0 %collective-permute-start.2 = (bf16[128,768]{1,0:T(8,128)(2,1)S(1)}, bf16[128,768]{1,0:T(8,128)(2,1)S(1)}, u32[]{:S(2)}, u32[]{:S(2)}) collective-permute-start(bf16[128,768]{1,0:T(8,128)(2,1)S(1)} %copy-done.2), channel_id=1, source_target_pairs={{0,1},{1,0},{4,8},{5,9},{8,4},{9,5},{12,13},{13,12},{2,3},{3,2},{6... | collective-permute-start | bytes 589832 | tf_op jit(solution)/shard_map/ppermute | solution.py:317
  2.5 15.5 %collective-permute-start.9 = (bf16[256,384]{1,0:T(8,128)(2,1)S(1)}, bf16[256,384]{1,0:T(8,128)(2,1)S(1)}, u32[]{:S(2)}, u32[]{:S(2)}) collective-permute-start(bf16[256,384]{1,0:T(8,128)(2,1)S(1)} %get-tuple-element.26.out), channel_id=1, source_target_pairs={{0,4},{4,0},{8,12},{12,8},{1,5},{5,1},{9,13},{13,9},{2,6},{6,2},{1... | collective-permute-start | bytes 589832 | tf_op jit(solution)/shard_map/ppermute | solution.py:314
  7.0 5.8 %collective-permute-start.11 = (bf16[128,384]{1,0:T(8,128)(2,1)S(1)}, bf16[128,384]{1,0:T(8,128)(2,1)S(1)}, u32[]{:S(2)}, u32[]{:S(2)}) collective-permute-start(bf16[128,384]{1,0:T(8,128)(2,1)S(1)} %get-tuple-element.35), channel_id=1, source_target_pairs={{0,1},{1,0},{4,8},{5,9},{8,4},{9,5},{12,13},{13,12},{2,3},{3,2},{6... | collective-permute-start | bytes 294920 | tf_op jit(solution)/shard_map/ppermute | solution.py:317
  7.0 14.4 %collective-permute-start.7 = (bf16[256,384]{1,0:T(8,128)(2,1)S(1)}, bf16[256,384]{1,0:T(8,128)(2,1)S(1)}, u32[]{:S(2)}, u32[]{:S(2)}) collective-permute-start(bf16[256,384]{1,0:T(8,128)(2,1)S(1)} %get-tuple-element.31.over.own), channel_id=1, source_target_pairs={{0,4},{4,0},{8,12},{12,8},{1,5},{5,1},{9,13},{13,9},{2,6},{6,2},{1... | collective-permute-start | bytes 589832 | tf_op jit(solution)/shard_map/ppermute | solution.py:314
  8.6 0.7 %copy-start = (s32[256]{0:T(256)S(1)}, s32[256]{0:T(256)}, u32[]{:S(2)}) copy-start(s32[256]{0:T(256)} %param.14) | copy-start | bytes 3076
  8.6 0.7 %copy-start.1 = (s32[4]{0:T(128)S(1)}, s32[4]{0:T(128)}, u32[]{:S(2)}) copy-start(s32[4]{0:T(128)} %count_ref.1) | copy-start | bytes 52
  11.2 8.5 %collective-permute-start.15 = (bf16[192,384]{1,0:T(8,128)(2,1)S(1)}, bf16[192,384]{1,0:T(8,128)(2,1)S(1)}, u32[]{:S(2)}, u32[]{:S(2)}) collective-permute-start(bf16[192,384]{1,0:T(8,128)(2,1)S(1)} %get-tuple-element.30.asks0.asks), channel_id=1, source_target_pairs={{0,4},{4,0},{8,12},{12,8},{1,5},{5,1},{9,13},{13,9},{2,6},{6,2},{1... | collective-permute-start | bytes 442376 | tf_op jit(solution)/shard_map/ppermute | solution.py:314
  12.8 11.7 %collective-permute-start.10 = (bf16[256,256]{1,0:T(8,128)(2,1)S(1)}, bf16[256,256]{1,0:T(8,128)(2,1)S(1)}, u32[]{:S(2)}, u32[]{:S(2)}) collective-permute-start(bf16[256,256]{1,0:T(8,128)(2,1)S(1)} %slice_select_fusion), channel_id=1, source_target_pairs={{0,4},{4,0},{8,12},{12,8},{1,5},{5,1},{9,13},{13,9},{2,6},{6,2},{1... | collective-permute-start | bytes 393224 | tf_op jit(solution)/shard_map/ppermute | solution.py:314
  17.9 6.0 %collective-permute-start.12 = (bf16[256,384]{1,0:T(8,128)(2,1)S(1)}, bf16[256,384]{1,0:T(8,128)(2,1)S(1)}, u32[]{:S(2)}, u32[]{:S(2)}) collective-permute-start(bf16[256,384]{1,0:T(8,128)(2,1)S(1)} %collective-permute-done.9.first.mate), channel_id=1, source_target_pairs={{0,1},{1,0},{4,8},{5,9},{8,4},{9,5},{12,13},{13,12},{2,3},{3,2},{6... | collective-permute-start | bytes 589832 | tf_op jit(solution)/shard_map/ppermute | solution.py:317
  19.7 4.3 %collective-permute-start.1 = (bf16[256,128]{1,0:T(8,128)(2,1)S(1)}, bf16[256,128]{1,0:T(8,128)(2,1)S(1)}, u32[]{:S(2)}, u32[]{:S(2)}) collective-permute-start(bf16[256,128]{1,0:T(8,128)(2,1)S(1)} %slice_select_fusion.1), channel_id=1, source_target_pairs={{0,4},{4,0},{8,12},{12,8},{1,5},{5,1},{9,13},{13,9},{2,6},{6,2},{1... | collective-permute-start | bytes 196616 | tf_op jit(solution)/shard_map/ppermute | solution.py:314
  21.4 8.5 %collective-permute-start.3 = (bf16[128,384]{1,0:T(8,128)(2,1)S(1)}, bf16[128,384]{1,0:T(8,128)(2,1)S(1)}, u32[]{:S(2)}, u32[]{:S(2)}) collective-permute-start(bf16[128,384]{1,0:T(8,128)(2,1)S(1)} %get-tuple-element.27), channel_id=1, source_target_pairs={{0,1},{1,0},{4,8},{5,9},{8,4},{9,5},{12,13},{13,12},{2,3},{3,2},{6... | collective-permute-start | bytes 294920 | tf_op jit(solution)/shard_map/ppermute | solution.py:317
  21.4 7.9 %collective-permute-start.5 = (bf16[192,384]{1,0:T(8,128)(2,1)S(1)}, bf16[192,384]{1,0:T(8,128)(2,1)S(1)}, u32[]{:S(2)}, u32[]{:S(2)}) collective-permute-start(bf16[192,384]{1,0:T(8,128)(2,1)S(1)} %get-tuple-element.24.asks.asks1), channel_id=1, source_target_pairs={{0,4},{4,0},{8,12},{12,8},{1,5},{5,1},{9,13},{13,9},{2,6},{6,2},{1... | collective-permute-start | bytes 442376 | tf_op jit(solution)/shard_map/ppermute | solution.py:314
  23.9 5.5 %collective-permute-start.8 = (bf16[256,384]{1,0:T(8,128)(2,1)S(1)}, bf16[256,384]{1,0:T(8,128)(2,1)S(1)}, u32[]{:S(2)}, u32[]{:S(2)}) collective-permute-start(bf16[256,384]{1,0:T(8,128)(2,1)S(1)} %collective-permute-done.7.second), channel_id=1, source_target_pairs={{0,1},{1,0},{4,8},{5,9},{8,4},{9,5},{12,13},{13,12},{2,3},{3,2},{6... | collective-permute-start | bytes 589832 | tf_op jit(solution)/shard_map/ppermute | solution.py:317
  23.9 11.7 %collective-permute-start.4 = (bf16[256,128]{1,0:T(8,128)(2,1)S(1)}, bf16[256,128]{1,0:T(8,128)(2,1)S(1)}, u32[]{:S(2)}, u32[]{:S(2)}) collective-permute-start(bf16[256,128]{1,0:T(8,128)(2,1)S(1)} %collective-permute-done.1.mate.part2), channel_id=1, source_target_pairs={{0,1},{1,0},{4,8},{5,9},{8,4},{9,5},{12,13},{13,12},{2,3},{3,2},{6... | collective-permute-start | bytes 196616 | tf_op jit(solution)/shard_map/ppermute | solution.py:317
  24.5 18.5 %collective-permute-start.17 = (bf16[192,384]{1,0:T(8,128)(2,1)S(1)}, bf16[192,384]{1,0:T(8,128)(2,1)S(1)}, u32[]{:S(2)}, u32[]{:S(2)}) collective-permute-start(bf16[192,384]{1,0:T(8,128)(2,1)S(1)} %shard_map.121), channel_id=1, source_target_pairs={{0,4},{4,0},{8,12},{12,8},{1,5},{5,1},{9,13},{13,9},{2,6},{6,2},{1... | collective-permute-start | bytes 442376 | tf_op jit(solution)/shard_map/ppermute | solution.py:314
  29.3 7.0 %collective-permute-start.13 = (bf16[256,128]{1,0:T(8,128)(2,1)S(1)}, bf16[256,128]{1,0:T(8,128)(2,1)S(1)}, u32[]{:S(2)}, u32[]{:S(2)}) collective-permute-start(bf16[256,128]{1,0:T(8,128)(2,1)S(1)} %get-tuple-element.43), channel_id=1, source_target_pairs={{0,1},{1,0},{4,8},{5,9},{8,4},{9,5},{12,13},{13,12},{2,3},{3,2},{6... | collective-permute-start | bytes 196616 | tf_op jit(solution)/shard_map/ppermute | solution.py:317
  29.4 9.5 %collective-permute-start.14 = (bf16[256,128]{1,0:T(8,128)(2,1)S(1)}, bf16[256,128]{1,0:T(8,128)(2,1)S(1)}, u32[]{:S(2)}, u32[]{:S(2)}) collective-permute-start(bf16[256,128]{1,0:T(8,128)(2,1)S(1)} %get-tuple-element.42), channel_id=1, source_target_pairs={{0,1},{1,0},{4,8},{5,9},{8,4},{9,5},{12,13},{13,12},{2,3},{3,2},{6... | collective-permute-start | bytes 196616 | tf_op jit(solution)/shard_map/ppermute | solution.py:317
  29.9 13.1 %collective-permute-start.16 = (bf16[64,768]{1,0:T(8,128)(2,1)S(1)}, bf16[64,768]{1,0:T(8,128)(2,1)S(1)}, u32[]{:S(2)}, u32[]{:S(2)}) collective-permute-start(bf16[64,768]{1,0:T(8,128)(2,1)S(1)} %shard_map.120), channel_id=1, source_target_pairs={{0,4},{4,0},{8,12},{12,8},{1,5},{5,1},{9,13},{13,9},{2,6},{6,2},{1... | collective-permute-start | bytes 294920 | tf_op jit(solution)/shard_map/ppermute | solution.py:314
  35.7 8.1 %collective-permute-start.6 = (bf16[192,128]{1,0:T(8,128)(2,1)S(1)}, bf16[192,128]{1,0:T(8,128)(2,1)S(1)}, u32[]{:S(2)}, u32[]{:S(2)}) collective-permute-start(bf16[192,128]{1,0:T(8,128)(2,1)S(1)} %shard_map.114), channel_id=1, source_target_pairs={{0,4},{4,0},{8,12},{12,8},{1,5},{5,1},{9,13},{13,9},{2,6},{6,2},{1... | collective-permute-start | bytes 147464 | tf_op jit(solution)/shard_map/ppermute | solution.py:314
  36.3 4.6 %collective-permute-start.18 = (bf16[192,128]{1,0:T(8,128)(2,1)S(1)}, bf16[192,128]{1,0:T(8,128)(2,1)S(1)}, u32[]{:S(2)}, u32[]{:S(2)}) collective-permute-start(bf16[192,128]{1,0:T(8,128)(2,1)S(1)} %shard_map.122), channel_id=1, source_target_pairs={{0,4},{4,0},{8,12},{12,8},{1,5},{5,1},{9,13},{13,9},{2,6},{6,2},{1... | collective-permute-start | bytes 147464 | tf_op jit(solution)/shard_map/ppermute | solution.py:314
  38.9 4.1 %collective-permute-start.19 = (bf16[192,128]{1,0:T(8,128)(2,1)S(1)}, bf16[192,128]{1,0:T(8,128)(2,1)S(1)}, u32[]{:S(2)}, u32[]{:S(2)}) collective-permute-start(bf16[192,128]{1,0:T(8,128)(2,1)S(1)} %shard_map.123), channel_id=1, source_target_pairs={{0,4},{4,0},{8,12},{12,8},{1,5},{5,1},{9,13},{13,9},{2,6},{6,2},{1... | collective-permute-start | bytes 147464 | tf_op jit(solution)/shard_map/ppermute | solution.py:314

commit v10 on v9

--- a/solution.py
+++ b/solution.py
@@ -123,12 +123,17 @@
 
 def second_pack(n, me_ref, count_ref, offset_ref, video_k, video_v, video_q, audio_q, *outs):
     sight1, sight2, asks0, asks1, values_ref, mask0_ref, mask1_ref, near_ref, sem = outs
-    rows = video_q.shape[0]
-    at = asks0.shape[1]
-    moves = [(video_v.at[:, pl.ds(at, at)], values_ref)]
-    for half, out in enumerate((asks0, asks1)):
-        cols = pl.ds(half * at, at)
-        moves += [(video_q.at[:, cols], out.at[:rows]), (audio_q.at[:, cols], out.at[rows:])]
+    half = asks0.shape[1]
+    low, high = pl.ds(0, half), pl.ds(half, half)
+    rows, more = video_q.shape[0], audio_q.shape[0]
+    moves = [
+        (video_q.at[:, low], asks0.at[:rows]),
+        (audio_q.at[:, low], asks0.at[rows : rows + more]),
+        (audio_q.at[:, high], asks0.at[rows + more :]),
+        (video_q.at[:, high], asks1),
+        (video_v.at[:, high], values_ref),
+    ]
+    at = half
     for out in (sight1, sight2):
         moves += sight_moves(video_k, video_v, at, out)
         at += out.shape[1]
@@ -172,19 +177,26 @@
     return keys, values
 
 
-def audio_mate_kernel(n, me_ref, asks0, asks1, out, second, across, far, mate_ref):
+def queries_of(half, asks0, asks1, video_rows, audio_rows, cols):
+    rows = video_rows + audio_rows
+    if half == 0:
+        return asks0[:rows, cols]
+    return jnp.concatenate([asks1[:, cols], asks0[rows:, cols]], axis=0)
+
+
+def audio_mate_kernel(n, me_ref, asks0, out, second, across, far, mate_ref):
     audio_rows, width = mate_ref.shape[0], out.shape[1]
-    video_rows = asks0.shape[0] - audio_rows
     me = me_ref[0]
 
     @pl.when((me > 0) & (me < n - 1))
     def _():
-        for half, asks in enumerate((asks0, asks1)):
+        for half in range(2):
+            first = asks0.shape[0] - (2 - half) * audio_rows
             for at in range(0, width, HEAD_DIM):
                 cols = slice(at, at + HEAD_DIM)
                 to = slice(half * width + at, half * width + at + HEAD_DIM)
                 keys, values = sound_blocks((out, second, across, far), audio_rows, half, cols)
-                mate_ref[:, to] = blend(asks[video_rows:, cols], keys, values, None)
+                mate_ref[:, to] = blend(asks0[first : first + audio_rows, cols], keys, values, None)
 
 
 def audio_own_kernel(n, me_ref, near_ref, asks0, asks1, out, second, across, far, cross_ref, own_ref):
@@ -194,12 +206,13 @@
 
     @pl.when((me > 0) & (me < n - 1))
     def _():
-        for half, asks in enumerate((asks0, asks1)):
+        for half in range(2):
             for at in range(0, width, HEAD_DIM):
                 cols = slice(at, at + HEAD_DIM)
                 to = slice(half * width + at, half * width + at + HEAD_DIM)
                 keys, values = sound_blocks((out, second, across, far), audio_rows, half, cols)
-                mixed = blend(asks[:, cols], keys, values, near_ref[...])
+                queries = queries_of(half, asks0, asks1, video_rows, audio_rows, cols)
+                mixed = blend(queries, keys, values, near_ref[...])
                 cross_ref[:, to] = mixed[:video_rows]
                 own_ref[:, to] = mixed[video_rows:]
 
@@ -223,8 +236,10 @@
                 cross_ref[:, to] = blend(asks[:video_rows, cols], keys, values, near_ref[:video_rows])
 
 
-def video_kernel(n, at, half, offset, me_ref, mask_ref, asks, own, mate, keys2, values2, far, out_ref):
+def video_kernel(n, at, half, offset, me_ref, mask_ref, *refs):
+    *asks, own, mate, keys2, values2, far, out_ref = refs
     video_rows = own.shape[0] // 2
+    audio_rows = out_ref.shape[0] - video_rows
     me = me_ref[0]
 
     @pl.when((me > 0) & (me < n - 1))
@@ -242,7 +257,8 @@
                 [own[low, near_cols], mate[low, near_cols], values2[:, half_cols], far[low, cols]],
                 axis=0,
             )
-            out_ref[:, cols] = blend(asks[:, half_cols], keys, values, mask_ref[...])
+            queries = queries_of(len(asks) - 1, asks[0], asks[-1], video_rows, audio_rows, half_cols)
+            out_ref[:, cols] = blend(queries, keys, values, mask_ref[...])
 
 
 def place_pieces(parts, first, video_rows, video_self, audio_cross):
@@ -347,7 +363,7 @@
         scratch_shapes=[pltpu.SemaphoreType.DMA((7,))],
     )
     outs = tuple(((2 * video_rows, length), jnp.bfloat16) for length in lengths[1:])
-    outs += (((rows, half), jnp.bfloat16),) * 2
+    outs += (((rows + audio_rows, half), jnp.bfloat16), ((video_rows, half), jnp.bfloat16))
     outs += (((video_rows, half), jnp.bfloat16),)
     outs += (((rows, n * video_rows), jnp.float32),) * 2 + (((rows, n * audio_rows), jnp.float32),)
     *sights, asks0, asks1, values1, mask0, mask1, near = call(
@@ -396,10 +412,10 @@
         return call(
             functools.partial(video_kernel, n, at, half * chunks[0], offset),
             (((rows, size * HEAD_DIM), jnp.bfloat16),),
-            [SMEM] + [VMEM] * 7,
+            [SMEM] + [VMEM] * (7 + half),
             place,
             mask,
-            queries[half],
+            *queries[: 1 + half],
             sights[source],
             sight_mate[source],
             keys_across,
@@ -414,9 +430,9 @@
     theirs = call(
         functools.partial(audio_mate_kernel, n),
         (((audio_rows, width), jnp.bfloat16),),
-        [SMEM] + [VMEM] * 6,
-        place,
-        *asks_mate,
+        [SMEM] + [VMEM] * 5,
+        place,
+        asks_mate[0],
         first_out,
         second_mate,
         sound_across,

time: 44.7 us -> 45.3 us (1.013)
  waiting for transfers between devices: 4.74 us -> 7.86 us
  starting transfers between devices: 33.1 us -> 31.2 us
  local copies, waits for them, and re-layouts: 0.7 us -> 0.03 us
    ppermute x11, waiting for transfers between devices: 4.72 us -> 7.84 us  [mate(): return lax.ppermute(block, 'seq', mate_pairs)]
    ppermute x11, starting transfers between devices: 31.4 us -> 29.4 us  [mate(): return lax.ppermute(block, 'seq', mate_pairs)]
    unnamed x6, local copies, waits for them, and re-layouts: 0.69 us -> 0.02 us
where the time goes in v10:
time: 45.3 us; the launch traced here: 45.1 us
  starting transfers between devices  31.2 us (69%)
  waiting for transfers between devices  7.86 us (17%)
  Pallas kernels  5.18 us (11%)
  between operations  0.81 us (2%)
    ppermute x11, starting transfers between devices, mate(): return lax.ppermute(block, 'seq', mate_pairs)  29.4 us
    ppermute x11, waiting for transfers between devices, mate(): return lax.ppermute(block, 'seq', mate_pairs)  7.84 us
    pallas_call x15, Pallas kernels, call(): pl.pallas_call(kernel, out_shape=tuple((jax.ShapeDtypeStruct(shape, dtype...  5.18 us
    ppermute x9, starting transfers between devices, cross(): return lax.ppermute(block, ('seq', 'mp'), cross_pairs)  1.79 us
  transfers between devices with their start and end apart: 20, of which 4 were waited for; matrix products, arithmetic and copies ran while one was open for 0% of the time, Pallas kernels for 7%

profile of v10, /device:TPU:0, one launch (start us, length us, event | category | flops | bytes accessed | tf_op | source)
XLA Modules:
  0.0 45.1 jit_solution(2057946795044942616)
XLA Ops:
  0.6 0.0 copy-start.2
  0.6 1.2 %shard_map.112 = (bf16[256,384]{1,0:T(8,128)(2,1)S(1)}, bf16[256,384]{1,0:T(8,128)(2,1)S(1)}, bf16[128,384]{1,0:T(8,128)(2,1)S(1)}) custom-call(s32[1]{0:T(128)} %bitcast.me_ref, bf16[128,768]{1,0:T(8,128)(2,1)} %video_k.3, bf16[128,768]{1,0:T(8,128)(2,1)} %video_v.3, bf16[64,768]{1,0:T(8,128)(2,1)} %audio_k.1, bf16[64,768]{1,0:T(8,128)(2,1)} %audio_v.1), custom_call_target="tpu_custom_call" | custom-call | tf_op jit(solution)/shard_map/pallas_call | solution.py:336
  1.8 0.0 copy-start
  1.9 0.0 copy-start.1
  1.9 0.6 %collective-permute-start = (bf16[256,384]{1,0:T(8,128)(2,1)S(1)}, bf16[256,384]{1,0:T(8,128)(2,1)S(1)}, u32[]{:S(2)}, u32[]{:S(2)}) collective-permute-start(bf16[256,384]{1,0:T(8,128)(2,1)S(1)} %get-tuple-element.27.out), channel_id=1, source_target_pairs={{0,1},{1,0},{4,8},{5,9},{8,4},{9,5},{12,13},{13,12},{2,3},{3,2},{6... | collective-permute-start | bytes 589832 | tf_op jit(solution)/shard_map/ppermute | solution.py:333
  2.4 0.0 copy-done.2
  2.4 0.1 collective-permute-start.2
  2.5 4.5 %collective-permute-start.10 = (bf16[256,384]{1,0:T(8,128)(2,1)S(1)}, bf16[256,384]{1,0:T(8,128)(2,1)S(1)}, u32[]{:S(2)}, u32[]{:S(2)}) collective-permute-start(bf16[256,384]{1,0:T(8,128)(2,1)S(1)} %get-tuple-element.27.out), channel_id=1, source_target_pairs={{0,4},{4,0},{8,12},{12,8},{1,5},{5,1},{9,13},{13,9},{2,6},{6,2},{1... | collective-permute-start | bytes 589832 | tf_op jit(solution)/shard_map/ppermute | solution.py:330
  7.0 0.0 copy-done
  7.0 0.0 copy-done.1
  7.0 1.9 %shard_map.111 = (bf16[256,256]{1,0:T(8,128)(2,1)S(1)}, bf16[256,128]{1,0:T(8,128)(2,1)S(1)}, bf16[256,384]{1,0:T(8,128)(2,1)S(1)}, bf16[128,384]{1,0:T(8,128)(2...) custom-call(s32[1]{0:T(128)} %bitcast.me_ref, ...), custom_call_target="tpu_custom_call" | custom-call | tf_op jit(solution)/shard_map/pallas_call | solution.py:336
  9.0 0.1 collective-permute-start.5
  9.0 0.1 collective-permute-start.12
  9.1 0.0 collective-permute-done.across
  9.1 3.6 %collective-permute-start.8 = (bf16[256,384]{1,0:T(8,128)(2,1)S(1)}, bf16[256,384]{1,0:T(8,128)(2,1)S(1)}, u32[]{:S(2)}, u32[]{:S(2)}) collective-permute-start(bf16[256,384]{1,0:T(8,128)(2,1)S(1)} %get-tuple-element.31.over.refs_1_), channel_id=1, source_target_pairs={{0,4},{4,0},{8,12},{12,8},{1,5},{5,1},{9,13},{13,9},{2,6},{6,2},{1... | collective-permute-start | bytes 589832 | tf_op jit(solution)/shard_map/ppermute | solution.py:330
  12.8 0.0 collective-permute-done.12.refs_4_
  12.8 5.2 %collective-permute-start.11 = (bf16[256,256]{1,0:T(8,128)(2,1)S(1)}, bf16[256,256]{1,0:T(8,128)(2,1)S(1)}, u32[]{:S(2)}, u32[]{:S(2)}) collective-permute-start(bf16[256,256]{1,0:T(8,128)(2,1)S(1)} %slice_select_fusion), channel_id=1, source_target_pairs={{0,4},{4,0},{8,12},{12,8},{1,5},{5,1},{9,13},{13,9},{2,6},{6,2},{1... | collective-permute-start | bytes 393224 | tf_op jit(solution)/shard_map/ppermute | solution.py:330
  18.0 0.0 collective-permute-done.10.first.refs_2_
  18.0 0.0 collective-permute-start.13
  18.0 0.0 collective-permute-done.5.refs_0_.asks0
  18.0 1.6 %collective-permute-start.1 = (bf16[256,128]{1,0:T(8,128)(2,1)S(1)}, bf16[256,128]{1,0:T(8,128)(2,1)S(1)}, u32[]{:S(2)}, u32[]{:S(2)}) collective-permute-start(bf16[256,128]{1,0:T(8,128)(2,1)S(1)} %slice_select_fusion.1), channel_id=1, source_target_pairs={{0,4},{4,0},{8,12},{12,8},{1,5},{5,1},{9,13},{13,9},{2,6},{6,2},{1... | collective-permute-start | bytes 196616 | tf_op jit(solution)/shard_map/ppermute | solution.py:330
  19.6 0.0 collective-permute-done.2.refs_4_.refs_3_
  19.6 0.5 collective-permute-start.6
  20.1 0.9 %collective-permute-done.8.second = bf16[256,384]{1,0:T(8,128)(2,1)S(1)} collective-permute-done((bf16[256,384]{1,0:T(8,128)(2,1)S(1)}, bf16[256,384]{1,0:T(8,128)(2,1)S(1)}, u32[]{:S(2)}, u32[]{:S(2)}) %collective-permute-start.8) | collective-permute-done | bytes 196640 | tf_op jit(solution)/shard_map/ppermute | solution.py:330
  21.0 0.0 collective-permute-start.3
  21.0 4.0 %collective-permute-done.1.refs_3_.part2 = bf16[256,128]{1,0:T(8,128)(2,1)S(1)} collective-permute-done((bf16[256,128]{1,0:T(8,128)(2,1)S(1)}, bf16[256,128]{1,0:T(8,128)(2,1)S(1)}, u32[]{:S(2)}, u32[]{:S(2)}) %collective-permute-start.1) | collective-permute-done | bytes 65568 | tf_op jit(solution)/shard_map/ppermute | solution.py:330
  25.1 0.0 collective-permute-start.9
  25.1 0.0 collective-permute-done.13.refs_5_
  25.1 0.5 %collective-permute-start.4 = (bf16[256,128]{1,0:T(8,128)(2,1)S(1)}, bf16[256,128]{1,0:T(8,128)(2,1)S(1)}, u32[]{:S(2)}, u32[]{:S(2)}) collective-permute-start(bf16[256,128]{1,0:T(8,128)(2,1)S(1)} %collective-permute-done.1.refs_3_.part2), channel_id=1, source_target_pairs={{0,1},{1,0},{4,8},{5,9},{8,4},{9,5},{12,13},{13,12},{2,3},{3,2},{6... | collective-permute-start | bytes 196616 | tf_op jit(solution)/shard_map/ppermute | solution.py:333
  25.6 0.0 collective-permute-done.11.part1.refs_3_
  25.6 4.1 %collective-permute-start.17 = (bf16[192,384]{1,0:T(8,128)(2,1)S(1)}, bf16[192,384]{1,0:T(8,128)(2,1)S(1)}, u32[]{:S(2)}, u32[]{:S(2)}) collective-permute-start(bf16[192,384]{1,0:T(8,128)(2,1)S(1)} %shard_map.121), channel_id=1, source_target_pairs={{0,4},{4,0},{8,12},{12,8},{1,5},{5,1},{9,13},{13,9},{2,6},{6,2},{1... | collective-permute-start | bytes 442376 | tf_op jit(solution)/shard_map/ppermute | solution.py:330
  29.7 0.0 collective-permute-done.6.refs_1_
  29.7 0.1 collective-permute-start.15
  29.8 0.0 collective-permute-done.9.far
  29.8 0.5 %collective-permute-start.14 = (bf16[256,128]{1,0:T(8,128)(2,1)S(1)}, bf16[256,128]{1,0:T(8,128)(2,1)S(1)}, u32[]{:S(2)}, u32[]{:S(2)}) collective-permute-start(bf16[256,128]{1,0:T(8,128)(2,1)S(1)} %get-tuple-element.43), channel_id=1, source_target_pairs={{0,1},{1,0},{4,8},{5,9},{8,4},{9,5},{12,13},{13,12},{2,3},{3,2},{6... | collective-permute-start | bytes 196616 | tf_op jit(solution)/shard_map/ppermute | solution.py:333
  30.3 0.0 collective-permute-done.3.refs_5_
  30.3 6.1 %collective-permute-start.16 = (bf16[64,768]{1,0:T(8,128)(2,1)S(1)}, bf16[64,768]{1,0:T(8,128)(2,1)S(1)}, u32[]{:S(2)}, u32[]{:S(2)}) collective-permute-start(bf16[64,768]{1,0:T(8,128)(2,1)S(1)} %shard_map.120), channel_id=1, source_target_pairs={{0,4},{4,0},{8,12},{12,8},{1,5},{5,1},{9,13},{13,9},{2,6},{6,2},{1... | collective-permute-start | bytes 294920 | tf_op jit(solution)/shard_map/ppermute | solution.py:330
  36.3 0.0 collective-permute-done.4.refs_6_
  36.3 0.6 %collective-permute-start.7 = (bf16[192,128]{1,0:T(8,128)(2,1)S(1)}, bf16[192,128]{1,0:T(8,128)(2,1)S(1)}, u32[]{:S(2)}, u32[]{:S(2)}) collective-permute-start(bf16[192,128]{1,0:T(8,128)(2,1)S(1)} %shard_map.114), channel_id=1, source_target_pairs={{0,4},{4,0},{8,12},{12,8},{1,5},{5,1},{9,13},{13,9},{2,6},{6,2},{1... | collective-permute-start | bytes 147464 | tf_op jit(solution)/shard_map/ppermute | solution.py:330
  37.0 0.0 collective-permute-done.15.refs_6_
  37.0 2.6 %collective-permute-start.19 = (bf16[192,128]{1,0:T(8,128)(2,1)S(1)}, bf16[192,128]{1,0:T(8,128)(2,1)S(1)}, u32[]{:S(2)}, u32[]{:S(2)}) collective-permute-start(bf16[192,128]{1,0:T(8,128)(2,1)S(1)} %shard_map.123), channel_id=1, source_target_pairs={{0,4},{4,0},{8,12},{12,8},{1,5},{5,1},{9,13},{13,9},{2,6},{6,2},{1... | collective-permute-start | bytes 147464 | tf_op jit(solution)/shard_map/ppermute | solution.py:330
  39.5 0.0 collective-permute-done.14.refs_6_
  39.5 0.6 %collective-permute-start.18 = (bf16[192,128]{1,0:T(8,128)(2,1)S(1)}, bf16[192,128]{1,0:T(8,128)(2,1)S(1)}, u32[]{:S(2)}, u32[]{:S(2)}) collective-permute-start(bf16[192,128]{1,0:T(8,128)(2,1)S(1)} %shard_map.122), channel_id=1, source_target_pairs={{0,4},{4,0},{8,12},{12,8},{1,5},{5,1},{9,13},{13,9},{2,6},{6,2},{1... | collective-permute-start | bytes 147464 | tf_op jit(solution)/shard_map/ppermute | solution.py:330
  40.2 0.6 %shard_map.116.end_cross = bf16[128,768]{1,0:T(8,128)(2,1)S(1)} custom-call(s32[1]{0:T(128)} %bitcast.me_ref, f32[192,256]{1,0:T(8,128)S(1)} %get-tuple-element.30.near_ref, bf16[256,384]{1,0:T(8,128)(2,1)S(1)} %get-tuple-element.24.refs_0_.asks0, bf16[128,384]{1,0:T(8,128)(2,1)S(1)} %get-tuple-element.25.refs_1_.asks1, ...), custom_call_target="tpu_custom_call" | custom-call | flops 150994944 | bytes 589824 | tf_op jit(solution)/shard_map/pallas_call | solution.py:336
  40.8 0.8 %collective-permute-done.19.refs_7_ = bf16[192,128]{1,0:T(8,128)(2,1)S(1)} collective-permute-done((bf16[192,128]{1,0:T(8,128)(2,1)S(1)}, bf16[192,128]{1,0:T(8,128)(2,1)S(1)}, u32[]{:S(2)}, u32[]{:S(2)}) %collective-permute-start.19) | collective-permute-done | bytes 49184 | tf_op jit(solution)/shard_map/ppermute | solution.py:330
  41.6 2.0 %collective-permute-done.18.refs_6_ = bf16[192,128]{1,0:T(8,128)(2,1)S(1)} collective-permute-done((bf16[192,128]{1,0:T(8,128)(2,1)S(1)}, bf16[192,128]{1,0:T(8,128)(2,1)S(1)}, u32[]{:S(2)}, u32[]{:S(2)}) %collective-permute-start.18) | collective-permute-done | bytes 49184 | tf_op jit(solution)/shard_map/ppermute | solution.py:330
  43.6 0.0 collective-permute-done.16.refs_4_
  43.6 0.0 collective-permute-done.17.refs_5_
  43.6 0.8 %shard_map.124 = (bf16[128,768]{1,0:T(8,128)(2,1)}, bf16[128,768]{1,0:T(8,128)(2,1)}, bf16[64,768]{1,0:T(8,128)(2,1)}, bf16[64,768]{1,0:T(8,128)(2,1)}) custom-call(s32[1]{0:T(128)} %bitcast.me_ref, bf16[128,768]{1,0:T(8,128)(2,1)S(1)} %get-tuple-element.32.own_cross, bf16[128,768]{1,0:T(8,128)(2,1)S(1)} %shard_map.116.end_cross, ...), custom_call_target="tpu_custom_call" | custom-call | tf_op jit(solution)/shard_map/pallas_call | solution.py:336
  44.5 0.0 collective-permute-done.7.back
  44.5 0.6 %shard_map.125 = (bf16[128,768]{1,0:T(8,128)(2,1)}, bf16[64,768]{1,0:T(8,128)(2,1)}) custom-call(s32[1]{0:T(128)} %bitcast.me_ref, bf16[192,128]{1,0:T(8,128)(2,1)S(1)} %shard_map.113.own, bf16[192,128]{1,0:T(8,128)(2,1)S(1)} %collective-permute-done.7.back, ...), custom_call_target="tpu_custom_call", output_to_operand_aliasing={{0}: (3, {}), {1}: (4, {})} | custom-call | tf_op jit(solution)/shard_map/pallas_call | solution.py:336
  (13 shorter events, 0.1 us)
Async XLA Ops:
  0.6 1.8 %copy-start.2 = (bf16[128,768]{1,0:T(8,128)(2,1)S(1)}, bf16[128,768]{1,0:T(8,128)(2,1)}, u32[]{:S(2)}) copy-start(bf16[128,768]{1,0:T(8,128)(2,1)} %video_k.3) | copy-start | bytes 589828
  1.8 5.2 %copy-start = (s32[256]{0:T(256)S(1)}, s32[256]{0:T(256)}, u32[]{:S(2)}) copy-start(s32[256]{0:T(256)} %param.14) | copy-start | bytes 3076
  1.9 5.2 %copy-start.1 = (s32[4]{0:T(128)S(1)}, s32[4]{0:T(128)}, u32[]{:S(2)}) copy-start(s32[4]{0:T(128)} %count_ref.1) | copy-start | bytes 52
  1.9 7.3 %collective-permute-start = (bf16[256,384]{1,0:T(8,128)(2,1)S(1)}, bf16[256,384]{1,0:T(8,128)(2,1)S(1)}, u32[]{:S(2)}, u32[]{:S(2)}) collective-permute-start(bf16[256,384]{1,0:T(8,128)(2,1)S(1)} %get-tuple-element.27.out), channel_id=1, source_target_pairs={{0,1},{1,0},{4,8},{5,9},{8,4},{9,5},{12,13},{13,12},{2,3},{3,2},{6... | collective-permute-start | bytes 589832 | tf_op jit(solution)/shard_map/ppermute | solution.py:333
  2.4 17.2 %collective-permute-start.2 = (bf16[128,768]{1,0:T(8,128)(2,1)S(1)}, bf16[128,768]{1,0:T(8,128)(2,1)S(1)}, u32[]{:S(2)}, u32[]{:S(2)}) collective-permute-start(bf16[128,768]{1,0:T(8,128)(2,1)S(1)} %copy-done.2), channel_id=1, source_target_pairs={{0,1},{1,0},{4,8},{5,9},{8,4},{9,5},{12,13},{13,12},{2,3},{3,2},{6... | collective-permute-start | bytes 589832 | tf_op jit(solution)/shard_map/ppermute | solution.py:333
  2.5 15.5 %collective-permute-start.10 = (bf16[256,384]{1,0:T(8,128)(2,1)S(1)}, bf16[256,384]{1,0:T(8,128)(2,1)S(1)}, u32[]{:S(2)}, u32[]{:S(2)}) collective-permute-start(bf16[256,384]{1,0:T(8,128)(2,1)S(1)} %get-tuple-element.27.out), channel_id=1, source_target_pairs={{0,4},{4,0},{8,12},{12,8},{1,5},{5,1},{9,13},{13,9},{2,6},{6,2},{1... | collective-permute-start | bytes 589832 | tf_op jit(solution)/shard_map/ppermute | solution.py:330
  9.0 9.0 %collective-permute-start.5 = (bf16[256,384]{1,0:T(8,128)(2,1)S(1)}, bf16[256,384]{1,0:T(8,128)(2,1)S(1)}, u32[]{:S(2)}, u32[]{:S(2)}) collective-permute-start(bf16[256,384]{1,0:T(8,128)(2,1)S(1)} %get-tuple-element.24.refs_0_.asks0), channel_id=1, source_target_pairs={{0,4},{4,0},{8,12},{12,8},{1,5},{5,1},{9,13},{13,9},{2,6},{6,2},{1... | collective-permute-start | bytes 589832 | tf_op jit(solution)/shard_map/ppermute | solution.py:330
  9.0 3.8 %collective-permute-start.12 = (bf16[128,384]{1,0:T(8,128)(2,1)S(1)}, bf16[128,384]{1,0:T(8,128)(2,1)S(1)}, u32[]{:S(2)}, u32[]{:S(2)}) collective-permute-start(bf16[128,384]{1,0:T(8,128)(2,1)S(1)} %get-tuple-element.35), channel_id=1, source_target_pairs={{0,1},{1,0},{4,8},{5,9},{8,4},{9,5},{12,13},{13,12},{2,3},{3,2},{6... | collective-permute-start | bytes 294920 | tf_op jit(solution)/shard_map/ppermute | solution.py:333
  9.1 11.9 %collective-permute-start.8 = (bf16[256,384]{1,0:T(8,128)(2,1)S(1)}, bf16[256,384]{1,0:T(8,128)(2,1)S(1)}, u32[]{:S(2)}, u32[]{:S(2)}) collective-permute-start(bf16[256,384]{1,0:T(8,128)(2,1)S(1)} %get-tuple-element.31.over.refs_1_), channel_id=1, source_target_pairs={{0,4},{4,0},{8,12},{12,8},{1,5},{5,1},{9,13},{13,9},{2,6},{6,2},{1... | collective-permute-start | bytes 589832 | tf_op jit(solution)/shard_map/ppermute | solution.py:330
  12.8 12.8 %collective-permute-start.11 = (bf16[256,256]{1,0:T(8,128)(2,1)S(1)}, bf16[256,256]{1,0:T(8,128)(2,1)S(1)}, u32[]{:S(2)}, u32[]{:S(2)}) collective-permute-start(bf16[256,256]{1,0:T(8,128)(2,1)S(1)} %slice_select_fusion), channel_id=1, source_target_pairs={{0,4},{4,0},{8,12},{12,8},{1,5},{5,1},{9,13},{13,9},{2,6},{6,2},{1... | collective-permute-start | bytes 393224 | tf_op jit(solution)/shard_map/ppermute | solution.py:330
  18.0 7.1 %collective-permute-start.13 = (bf16[256,384]{1,0:T(8,128)(2,1)S(1)}, bf16[256,384]{1,0:T(8,128)(2,1)S(1)}, u32[]{:S(2)}, u32[]{:S(2)}) collective-permute-start(bf16[256,384]{1,0:T(8,128)(2,1)S(1)} %collective-permute-done.10.first.refs_2_), channel_id=1, source_target_pairs={{0,1},{1,0},{4,8},{5,9},{8,4},{9,5},{12,13},{13,12},{2,3},{3,2},{6... | collective-permute-start | bytes 589832 | tf_op jit(solution)/shard_map/ppermute | solution.py:333
  18.0 7.1 %collective-permute-start.1 = (bf16[256,128]{1,0:T(8,128)(2,1)S(1)}, bf16[256,128]{1,0:T(8,128)(2,1)S(1)}, u32[]{:S(2)}, u32[]{:S(2)}) collective-permute-start(bf16[256,128]{1,0:T(8,128)(2,1)S(1)} %slice_select_fusion.1), channel_id=1, source_target_pairs={{0,4},{4,0},{8,12},{12,8},{1,5},{5,1},{9,13},{13,9},{2,6},{6,2},{1... | collective-permute-start | bytes 196616 | tf_op jit(solution)/shard_map/ppermute | solution.py:330
  19.6 10.1 %collective-permute-start.6 = (bf16[128,384]{1,0:T(8,128)(2,1)S(1)}, bf16[128,384]{1,0:T(8,128)(2,1)S(1)}, u32[]{:S(2)}, u32[]{:S(2)}) collective-permute-start(bf16[128,384]{1,0:T(8,128)(2,1)S(1)} %get-tuple-element.25.refs_1_.asks1), channel_id=1, source_target_pairs={{0,4},{4,0},{8,12},{12,8},{1,5},{5,1},{9,13},{13,9},{2,6},{6,2},{1... | collective-permute-start | bytes 294920 | tf_op jit(solution)/shard_map/ppermute | solution.py:330
  21.0 9.3 %collective-permute-start.3 = (bf16[128,384]{1,0:T(8,128)(2,1)S(1)}, bf16[128,384]{1,0:T(8,128)(2,1)S(1)}, u32[]{:S(2)}, u32[]{:S(2)}) collective-permute-start(bf16[128,384]{1,0:T(8,128)(2,1)S(1)} %get-tuple-element.28), channel_id=1, source_target_pairs={{0,1},{1,0},{4,8},{5,9},{8,4},{9,5},{12,13},{13,12},{2,3},{3,2},{6... | collective-permute-start | bytes 294920 | tf_op jit(solution)/shard_map/ppermute | solution.py:333
  25.1 4.7 %collective-permute-start.9 = (bf16[256,384]{1,0:T(8,128)(2,1)S(1)}, bf16[256,384]{1,0:T(8,128)(2,1)S(1)}, u32[]{:S(2)}, u32[]{:S(2)}) collective-permute-start(bf16[256,384]{1,0:T(8,128)(2,1)S(1)} %collective-permute-done.8.second), channel_id=1, source_target_pairs={{0,1},{1,0},{4,8},{5,9},{8,4},{9,5},{12,13},{13,12},{2,3},{3,2},{6... | collective-permute-start | bytes 589832 | tf_op jit(solution)/shard_map/ppermute | solution.py:333
  25.1 11.3 %collective-permute-start.4 = (bf16[256,128]{1,0:T(8,128)(2,1)S(1)}, bf16[256,128]{1,0:T(8,128)(2,1)S(1)}, u32[]{:S(2)}, u32[]{:S(2)}) collective-permute-start(bf16[256,128]{1,0:T(8,128)(2,1)S(1)} %collective-permute-done.1.refs_3_.part2), channel_id=1, source_target_pairs={{0,1},{1,0},{4,8},{5,9},{8,4},{9,5},{12,13},{13,12},{2,3},{3,2},{6... | collective-permute-start | bytes 196616 | tf_op jit(solution)/shard_map/ppermute | solution.py:333
  25.6 18.0 %collective-permute-start.17 = (bf16[192,384]{1,0:T(8,128)(2,1)S(1)}, bf16[192,384]{1,0:T(8,128)(2,1)S(1)}, u32[]{:S(2)}, u32[]{:S(2)}) collective-permute-start(bf16[192,384]{1,0:T(8,128)(2,1)S(1)} %shard_map.121), channel_id=1, source_target_pairs={{0,4},{4,0},{8,12},{12,8},{1,5},{5,1},{9,13},{13,9},{2,6},{6,2},{1... | collective-permute-start | bytes 442376 | tf_op jit(solution)/shard_map/ppermute | solution.py:330
  29.7 7.3 %collective-permute-start.15 = (bf16[256,128]{1,0:T(8,128)(2,1)S(1)}, bf16[256,128]{1,0:T(8,128)(2,1)S(1)}, u32[]{:S(2)}, u32[]{:S(2)}) collective-permute-start(bf16[256,128]{1,0:T(8,128)(2,1)S(1)} %get-tuple-element.42), channel_id=1, source_target_pairs={{0,1},{1,0},{4,8},{5,9},{8,4},{9,5},{12,13},{13,12},{2,3},{3,2},{6... | collective-permute-start | bytes 196616 | tf_op jit(solution)/shard_map/ppermute | solution.py:333
  29.8 9.7 %collective-permute-start.14 = (bf16[256,128]{1,0:T(8,128)(2,1)S(1)}, bf16[256,128]{1,0:T(8,128)(2,1)S(1)}, u32[]{:S(2)}, u32[]{:S(2)}) collective-permute-start(bf16[256,128]{1,0:T(8,128)(2,1)S(1)} %get-tuple-element.43), channel_id=1, source_target_pairs={{0,1},{1,0},{4,8},{5,9},{8,4},{9,5},{12,13},{13,12},{2,3},{3,2},{6... | collective-permute-start | bytes 196616 | tf_op jit(solution)/shard_map/ppermute | solution.py:333
  30.3 13.3 %collective-permute-start.16 = (bf16[64,768]{1,0:T(8,128)(2,1)S(1)}, bf16[64,768]{1,0:T(8,128)(2,1)S(1)}, u32[]{:S(2)}, u32[]{:S(2)}) collective-permute-start(bf16[64,768]{1,0:T(8,128)(2,1)S(1)} %shard_map.120), channel_id=1, source_target_pairs={{0,4},{4,0},{8,12},{12,8},{1,5},{5,1},{9,13},{13,9},{2,6},{6,2},{1... | collective-permute-start | bytes 294920 | tf_op jit(solution)/shard_map/ppermute | solution.py:330
  36.3 8.1 %collective-permute-start.7 = (bf16[192,128]{1,0:T(8,128)(2,1)S(1)}, bf16[192,128]{1,0:T(8,128)(2,1)S(1)}, u32[]{:S(2)}, u32[]{:S(2)}) collective-permute-start(bf16[192,128]{1,0:T(8,128)(2,1)S(1)} %shard_map.114), channel_id=1, source_target_pairs={{0,4},{4,0},{8,12},{12,8},{1,5},{5,1},{9,13},{13,9},{2,6},{6,2},{1... | collective-permute-start | bytes 147464 | tf_op jit(solution)/shard_map/ppermute | solution.py:330
  37.0 4.6 %collective-permute-start.19 = (bf16[192,128]{1,0:T(8,128)(2,1)S(1)}, bf16[192,128]{1,0:T(8,128)(2,1)S(1)}, u32[]{:S(2)}, u32[]{:S(2)}) collective-permute-start(bf16[192,128]{1,0:T(8,128)(2,1)S(1)} %shard_map.123), channel_id=1, source_target_pairs={{0,4},{4,0},{8,12},{12,8},{1,5},{5,1},{9,13},{13,9},{2,6},{6,2},{1... | collective-permute-start | bytes 147464 | tf_op jit(solution)/shard_map/ppermute | solution.py:330
  39.5 4.1 %collective-permute-start.18 = (bf16[192,128]{1,0:T(8,128)(2,1)S(1)}, bf16[192,128]{1,0:T(8,128)(2,1)S(1)}, u32[]{:S(2)}, u32[]{:S(2)}) collective-permute-start(bf16[192,128]{1,0:T(8,128)(2,1)S(1)} %shard_map.122), channel_id=1, source_target_pairs={{0,4},{4,0},{8,12},{12,8},{1,5},{5,1},{9,13},{13,9},{2,6},{6,2},{1... | collective-permute-start | bytes 147464 | tf_op jit(solution)/shard_map/ppermute | solution.py:330

commit v11 on v9

--- a/solution.py
+++ b/solution.py
@@ -223,24 +223,22 @@
                 cross_ref[:, to] = blend(asks[:video_rows, cols], keys, values, near_ref[:video_rows])
 
 
-def video_kernel(n, at, half, offset, me_ref, mask_ref, asks, own, mate, keys2, values2, far, out_ref):
+def video_kernel(n, at, half, me_ref, mask_ref, asks, own, mate, keys2, values2, far, out_ref):
     video_rows = own.shape[0] // 2
     me = me_ref[0]
 
     @pl.when((me > 0) & (me < n - 1))
     def _():
-        for head in range(far.shape[1] // HEAD_DIM):
+        for head in range(own.shape[1] // HEAD_DIM):
             cols = slice(head * HEAD_DIM, (head + 1) * HEAD_DIM)
-            near_cols = slice((offset + head) * HEAD_DIM, (offset + head + 1) * HEAD_DIM)
             all_cols = slice((at + head) * HEAD_DIM, (at + head + 1) * HEAD_DIM)
             half_cols = slice((at - half + head) * HEAD_DIM, (at - half + head + 1) * HEAD_DIM)
             top, low = slice(0, video_rows), slice(video_rows, 2 * video_rows)
             keys = jnp.concatenate(
-                [own[top, near_cols], mate[top, near_cols], keys2[:, all_cols], far[top, cols]], axis=0
+                [own[top, cols], mate[top, cols], keys2[:, all_cols], far[top, cols]], axis=0
             )
             values = jnp.concatenate(
-                [own[low, near_cols], mate[low, near_cols], values2[:, half_cols], far[low, cols]],
-                axis=0,
+                [own[low, cols], mate[low, cols], values2[:, half_cols], far[low, cols]], axis=0
             )
             out_ref[:, cols] = blend(asks[:, half_cols], keys, values, mask_ref[...])
 
@@ -255,20 +253,18 @@
     return moves
 
 
-def place_kernel(n, me_ref, own_cross, end_cross, *refs):
-    count = (len(refs) - 5) // 2
-    own, back = refs[:count], refs[count : 2 * count]
-    video_self, video_cross, audio_self, audio_cross, sem = refs[2 * count :]
+def place_kernel(n, me_ref, own_cross, end_cross, own0, own1, own2, back0, back1, back2, *outs):
+    video_self, video_cross, audio_self, audio_cross, sem = outs
     at_end = (me_ref[0] == 0) | (me_ref[0] == n - 1)
-    for role, cross, parts in (
-        (jnp.logical_not(at_end), own_cross, own),
-        (at_end, end_cross, back),
+    for role, cross, sound, parts in (
+        (jnp.logical_not(at_end), own_cross, own0, (own1, own2)),
+        (at_end, end_cross, back0, (back1, back2)),
     ):
 
         @pl.when(role)
-        def _(cross=cross, parts=parts):
-            moves = [(cross, video_cross), (parts[0], audio_self)]
-            moves += place_pieces(parts[1:], 0, cross.shape[0], video_self, audio_cross)
+        def _(cross=cross, sound=sound, parts=parts):
+            moves = [(cross, video_cross), (sound, audio_self)]
+            moves += place_pieces(parts, 0, cross.shape[0], video_self, audio_cross)
             for copy in move_all(moves, sem):
                 copy.wait()
 
@@ -378,30 +374,21 @@
         part = sound_across[:, at : at + lengths[i]]
         sight_mate.append(mate(jnp.where(at_end, sights[i], part)))
         at += lengths[i]
-    pieces = [(0, chunks[0], 0, 0)]
-    sight_far = [cross(sight_mate[0])]
-    for source in (1, 2):
-        for i in range(chunks[source]):
-            pieces.append((sum(chunks[:source]) + i, 1, source, i))
-            part = sight_mate[source]
-            if chunks[source] > 1:
-                part = part[:, i * HEAD_DIM : (i + 1) * HEAD_DIM]
-            sight_far.append(cross(part))
-    last = len(pieces) - 1
+    sight_far = [cross(sight_mate[i]) for i in range(3)]
     asks_mate = [mate(asks[i]) for i in range(2)]
 
     def look(i, queries, mask):
-        at, size, source, offset = pieces[i]
-        half = min(source, 1)
+        at, size = sum(chunks[:i]), chunks[i]
+        half = min(i, 1)
         return call(
-            functools.partial(video_kernel, n, at, half * chunks[0], offset),
+            functools.partial(video_kernel, n, at, half * chunks[0]),
             (((rows, size * HEAD_DIM), jnp.bfloat16),),
             [SMEM] + [VMEM] * 7,
             place,
             mask,
             queries[half],
-            sights[source],
-            sight_mate[source],
+            sights[i],
+            sight_mate[i],
             keys_across,
             values_across[half],
             sight_far[i],
@@ -409,8 +396,8 @@
             cost_estimate=cost(rows, n * video_rows, size),
         )[0]
 
-    back = [mate(look(i, asks_mate, mask1)) for i in range(last + 1)]
-    mine = [look(i, asks, mask0) for i in range(last + 1)]
+    back = [mate(look(i, asks_mate, mask1)) for i in range(3)]
+    mine = [look(i, asks, mask0) for i in range(3)]
     theirs = call(
         functools.partial(audio_mate_kernel, n),
         (((audio_rows, width), jnp.bfloat16),),
@@ -459,24 +446,24 @@
     video_self, video_cross, audio_self, audio_cross = call(
         functools.partial(place_kernel, n),
         (video_shape, video_shape, audio_shape, audio_shape),
-        [SMEM] + [VMEM] * (4 + 2 * last),
+        [SMEM] + [VMEM] * 8,
         place,
         own_cross,
         end_cross,
         own,
-        *mine[:last],
+        *mine[:2],
         back_sound,
-        *back[:last],
+        *back[:2],
         out_specs=(HBM,) * 4,
-        scratch_shapes=[pltpu.SemaphoreType.DMA((2 + 2 * last,))],
+        scratch_shapes=[pltpu.SemaphoreType.DMA((6,))],
     )
     video_self, audio_cross = call(
-        functools.partial(place_last_kernel, n, width - HEAD_DIM),
+        functools.partial(place_last_kernel, n, width - lengths[2]),
         (video_shape, audio_shape),
         [SMEM] + [VMEM] * 2 + [HBM] * 2,
         place,
-        mine[last],
-        back[last],
+        mine[2],
+        back[2],
         video_self,
         audio_cross,
         out_specs=(HBM,) * 2,

time: 44.7 us -> 44 us (0.984)
  starting transfers between devices: 33.1 us -> 31.8 us
  waiting for transfers between devices: 4.74 us -> 5.37 us
    ppermute x9 -> x8, waiting for transfers between devices: 0.02 us -> 0.86 us  [cross(): return lax.ppermute(block, ('seq', 'mp'), cross_pairs)]
    ppermute x11 -> x10, starting transfers between devices: 31.4 us -> 30.6 us  [mate(): return lax.ppermute(block, 'seq', mate_pairs)]
    ppermute x9 -> x8, starting transfers between devices: 1.72 us -> 1.23 us  [cross(): return lax.ppermute(block, ('seq', 'mp'), cross_pairs)]
    ppermute x11 -> x10, waiting for transfers between devices: 4.72 us -> 4.51 us  [mate(): return lax.ppermute(block, 'seq', mate_pairs)]
    pallas_call x15 -> x13, Pallas kernels: 5.15 us -> 5.15 us  [call(): pl.pallas_call(kernel, out_shape=tuple((jax.ShapeDtypeStruct(shape, dtype...]
  transfers between devices with their start and end apart: 20 -> 18, of which waited for: 4 -> 4; matrix products, arithmetic and copies ran while one was open for 0% -> 0% of each run, Pallas kernels for 7% -> 8%
where the time goes in v11:
time: 44 us; the launch traced here: 43.8 us
  starting transfers between devices  31.8 us (72%)
  waiting for transfers between devices  5.37 us (12%)
  Pallas kernels  5.15 us (12%)
  between operations  0.76 us (2%)
  local copies, waits for them, and re-layouts  0.69 us (2%)
    ppermute x10, starting transfers between devices, mate(): return lax.ppermute(block, 'seq', mate_pairs)  30.6 us
    pallas_call x13, Pallas kernels, call(): pl.pallas_call(kernel, out_shape=tuple((jax.ShapeDtypeStruct(shape, dtype...  5.15 us
    ppermute x10, waiting for transfers between devices, mate(): return lax.ppermute(block, 'seq', mate_pairs)  4.51 us
    ppermute x8, starting transfers between devices, cross(): return lax.ppermute(block, ('seq', 'mp'), cross_pairs)  1.23 us
  transfers between devices with their start and end apart: 18, of which 4 were waited for; matrix products, arithmetic and copies ran while one was open for 0% of the time, Pallas kernels for 8%

profile of v11, /device:TPU:0, one launch (start us, length us, event | category | flops | bytes accessed | tf_op | source)
XLA Modules:
  0.0 43.8 jit_solution(9010065388439928969)
XLA Ops:
  0.6 0.0 copy-start.2
  0.6 1.2 %shard_map.112 = (bf16[256,384]{1,0:T(8,128)(2,1)S(1)}, bf16[256,384]{1,0:T(8,128)(2,1)S(1)}, bf16[128,384]{1,0:T(8,128)(2,1)S(1)}) custom-call(s32[1]{0:T(128)} %bitcast.me_ref, bf16[128,768]{1,0:T(8,128)(2,1)} %video_k.3, bf16[128,768]{1,0:T(8,128)(2,1)} %video_v.3, bf16[64,768]{1,0:T(8,128)(2,1)} %audio_k.1, bf16[64,768]{1,0:T(8,128)(2,1)} %audio_v.1), custom_call_target="tpu_custom_call" | custom-call | tf_op jit(solution)/shard_map/pallas_call | solution.py:316
  1.8 0.6 %collective-permute-start = (bf16[256,384]{1,0:T(8,128)(2,1)S(1)}, bf16[256,384]{1,0:T(8,128)(2,1)S(1)}, u32[]{:S(2)}, u32[]{:S(2)}) collective-permute-start(bf16[256,384]{1,0:T(8,128)(2,1)S(1)} %get-tuple-element.26.out), channel_id=1, source_target_pairs={{0,1},{1,0},{4,8},{5,9},{8,4},{9,5},{12,13},{13,12},{2,3},{3,2},{6... | collective-permute-start | bytes 589832 | tf_op jit(solution)/shard_map/ppermute | solution.py:313
  2.4 0.0 copy-done.2
  2.4 0.1 collective-permute-start.2
  2.5 4.5 %collective-permute-start.9 = (bf16[256,384]{1,0:T(8,128)(2,1)S(1)}, bf16[256,384]{1,0:T(8,128)(2,1)S(1)}, u32[]{:S(2)}, u32[]{:S(2)}) collective-permute-start(bf16[256,384]{1,0:T(8,128)(2,1)S(1)} %get-tuple-element.26.out), channel_id=1, source_target_pairs={{0,4},{4,0},{8,12},{12,8},{1,5},{5,1},{9,13},{13,9},{2,6},{6,2},{1... | collective-permute-start | bytes 589832 | tf_op jit(solution)/shard_map/ppermute | solution.py:310
  7.0 0.0 collective-permute-start.11
  7.0 1.6 %collective-permute-start.7 = (bf16[256,384]{1,0:T(8,128)(2,1)S(1)}, bf16[256,384]{1,0:T(8,128)(2,1)S(1)}, u32[]{:S(2)}, u32[]{:S(2)}) collective-permute-start(bf16[256,384]{1,0:T(8,128)(2,1)S(1)} %get-tuple-element.31.over.own), channel_id=1, source_target_pairs={{0,4},{4,0},{8,12},{12,8},{1,5},{5,1},{9,13},{13,9},{2,6},{6,2},{1... | collective-permute-start | bytes 589832 | tf_op jit(solution)/shard_map/ppermute | solution.py:310
  8.6 0.0 copy-start
  8.6 0.0 copy-start.1
  8.6 0.7 %copy-done = s32[256]{0:T(256)S(1)} copy-done((s32[256]{0:T(256)S(1)}, s32[256]{0:T(256)}, u32[]{:S(2)}) %copy-start) | copy-done | bytes 1048
  9.3 0.0 copy-done.1
  9.3 1.9 %shard_map.111 = (bf16[256,256]{1,0:T(8,128)(2,1)S(1)}, bf16[256,128]{1,0:T(8,128)(2,1)S(1)}, bf16[192,384]{1,0:T(8,128)(2,1)S(1)}, bf16[192,384]{1,0:T(8,128)(2...) custom-call(s32[1]{0:T(128)} %bitcast.me_ref, ...), custom_call_target="tpu_custom_call" | custom-call | tf_op jit(solution)/shard_map/pallas_call | solution.py:316
  11.2 0.0 collective-permute-done.across
  11.2 1.5 %collective-permute-start.14 = (bf16[192,384]{1,0:T(8,128)(2,1)S(1)}, bf16[192,384]{1,0:T(8,128)(2,1)S(1)}, u32[]{:S(2)}, u32[]{:S(2)}) collective-permute-start(bf16[192,384]{1,0:T(8,128)(2,1)S(1)} %get-tuple-element.30.asks0.asks), channel_id=1, source_target_pairs={{0,4},{4,0},{8,12},{12,8},{1,5},{5,1},{9,13},{13,9},{2,6},{6,2},{1... | collective-permute-start | bytes 442376 | tf_op jit(solution)/shard_map/ppermute | solution.py:310
  12.8 0.0 collective-permute-done.11.values2
  12.8 5.2 %collective-permute-start.10 = (bf16[256,256]{1,0:T(8,128)(2,1)S(1)}, bf16[256,256]{1,0:T(8,128)(2,1)S(1)}, u32[]{:S(2)}, u32[]{:S(2)}) collective-permute-start(bf16[256,256]{1,0:T(8,128)(2,1)S(1)} %slice_select_fusion), channel_id=1, source_target_pairs={{0,4},{4,0},{8,12},{12,8},{1,5},{5,1},{9,13},{13,9},{2,6},{6,2},{1... | collective-permute-start | bytes 393224 | tf_op jit(solution)/shard_map/ppermute | solution.py:310
  17.9 1.7 %collective-permute-done.14.asks0.asks = bf16[192,384]{1,0:T(8,128)(2,1)S(1)} collective-permute-done((bf16[192,384]{1,0:T(8,128)(2,1)S(1)}, bf16[192,384]{1,0:T(8,128)(2,1)S(1)}, u32[]{:S(2)}, u32[]{:S(2)}) %collective-permute-start.14) | collective-permute-done | bytes 147488 | tf_op jit(solution)/shard_map/ppermute | solution.py:310
  19.7 0.0 collective-permute-start.3
  19.7 0.0 collective-permute-done.2.keys2
  19.7 3.3 %collective-permute-start.5 = (bf16[192,384]{1,0:T(8,128)(2,1)S(1)}, bf16[192,384]{1,0:T(8,128)(2,1)S(1)}, u32[]{:S(2)}, u32[]{:S(2)}) collective-permute-start(bf16[192,384]{1,0:T(8,128)(2,1)S(1)} %get-tuple-element.24.asks.asks1), channel_id=1, source_target_pairs={{0,4},{4,0},{8,12},{12,8},{1,5},{5,1},{9,13},{13,9},{2,6},{6,2},{1... | collective-permute-start | bytes 442376 | tf_op jit(solution)/shard_map/ppermute | solution.py:310
  23.0 0.0 collective-permute-done.9.first.mate
  23.0 0.0 collective-permute-start.12
  23.0 0.0 collective-permute-done.7.second
  23.0 0.5 %collective-permute-start.8 = (bf16[256,384]{1,0:T(8,128)(2,1)S(1)}, bf16[256,384]{1,0:T(8,128)(2,1)S(1)}, u32[]{:S(2)}, u32[]{:S(2)}) collective-permute-start(bf16[256,384]{1,0:T(8,128)(2,1)S(1)} %collective-permute-done.7.second), channel_id=1, source_target_pairs={{0,1},{1,0},{4,8},{5,9},{8,4},{9,5},{12,13},{13,12},{2,3},{3,2},{6... | collective-permute-start | bytes 589832 | tf_op jit(solution)/shard_map/ppermute | solution.py:313
  23.5 0.0 collective-permute-done.10.part1.mate
  23.5 0.1 collective-permute-start.13
  23.6 0.8 %collective-permute-done.12.far = bf16[256,384]{1,0:T(8,128)(2,1)S(1)} collective-permute-done((bf16[256,384]{1,0:T(8,128)(2,1)S(1)}, bf16[256,384]{1,0:T(8,128)(2,1)S(1)}, u32[]{:S(2)}, u32[]{:S(2)}) %collective-permute-start.12) | collective-permute-done | bytes 196640 | tf_op jit(solution)/shard_map/ppermute | solution.py:313
  24.4 6.9 %collective-permute-start.1 = (bf16[256,128]{1,0:T(8,128)(2,1)S(1)}, bf16[256,128]{1,0:T(8,128)(2,1)S(1)}, u32[]{:S(2)}, u32[]{:S(2)}) collective-permute-start(bf16[256,128]{1,0:T(8,128)(2,1)S(1)} %slice_select_fusion.1), channel_id=1, source_target_pairs={{0,4},{4,0},{8,12},{12,8},{1,5},{5,1},{9,13},{13,9},{2,6},{6,2},{1... | collective-permute-start | bytes 196616 | tf_op jit(solution)/shard_map/ppermute | solution.py:310
  31.3 0.0 collective-permute-done.5.asks.asks1
  31.3 0.9 %collective-permute-start.16 = (bf16[192,384]{1,0:T(8,128)(2,1)S(1)}, bf16[192,384]{1,0:T(8,128)(2,1)S(1)}, u32[]{:S(2)}, u32[]{:S(2)}) collective-permute-start(bf16[192,384]{1,0:T(8,128)(2,1)S(1)} %shard_map.120), channel_id=1, source_target_pairs={{0,4},{4,0},{8,12},{12,8},{1,5},{5,1},{9,13},{13,9},{2,6},{6,2},{1... | collective-permute-start | bytes 442376 | tf_op jit(solution)/shard_map/ppermute | solution.py:310
  32.2 1.5 %collective-permute-done.1.mate.part2 = bf16[256,128]{1,0:T(8,128)(2,1)S(1)} collective-permute-done((bf16[256,128]{1,0:T(8,128)(2,1)S(1)}, bf16[256,128]{1,0:T(8,128)(2,1)S(1)}, u32[]{:S(2)}, u32[]{:S(2)}) %collective-permute-start.1) | collective-permute-done | bytes 65568 | tf_op jit(solution)/shard_map/ppermute | solution.py:310
  33.7 0.0 collective-permute-start.4
  33.7 0.0 collective-permute-done.8.far
  33.7 4.0 %collective-permute-start.15 = (bf16[64,768]{1,0:T(8,128)(2,1)S(1)}, bf16[64,768]{1,0:T(8,128)(2,1)S(1)}, u32[]{:S(2)}, u32[]{:S(2)}) collective-permute-start(bf16[64,768]{1,0:T(8,128)(2,1)S(1)} %shard_map.119), channel_id=1, source_target_pairs={{0,4},{4,0},{8,12},{12,8},{1,5},{5,1},{9,13},{13,9},{2,6},{6,2},{1... | collective-permute-start | bytes 294920 | tf_op jit(solution)/shard_map/ppermute | solution.py:310
  37.7 0.0 collective-permute-done.3.values2
  37.7 0.0 collective-permute-done.13.far
  37.7 0.9 %collective-permute-start.17 = (bf16[192,256]{1,0:T(8,128)(2,1)S(1)}, bf16[192,256]{1,0:T(8,128)(2,1)S(1)}, u32[]{:S(2)}, u32[]{:S(2)}) collective-permute-start(bf16[192,256]{1,0:T(8,128)(2,1)S(1)} %shard_map.121), channel_id=1, source_target_pairs={{0,4},{4,0},{8,12},{12,8},{1,5},{5,1},{9,13},{13,9},{2,6},{6,2},{1... | collective-permute-start | bytes 294920 | tf_op jit(solution)/shard_map/ppermute | solution.py:310
  38.6 0.0 collective-permute-done.4.far
  38.6 1.8 %collective-permute-start.6 = (bf16[192,128]{1,0:T(8,128)(2,1)S(1)}, bf16[192,128]{1,0:T(8,128)(2,1)S(1)}, u32[]{:S(2)}, u32[]{:S(2)}) collective-permute-start(bf16[192,128]{1,0:T(8,128)(2,1)S(1)} %shard_map.114), channel_id=1, source_target_pairs={{0,4},{4,0},{8,12},{12,8},{1,5},{5,1},{9,13},{13,9},{2,6},{6,2},{1... | collective-permute-start | bytes 147464 | tf_op jit(solution)/shard_map/ppermute | solution.py:310
  40.4 0.6 %shard_map.116.end_cross = bf16[128,768]{1,0:T(8,128)(2,1)S(1)} custom-call(s32[1]{0:T(128)} %bitcast.me_ref, f32[192,256]{1,0:T(8,128)S(1)} %get-tuple-element.29.near_ref, bf16[192,384]{1,0:T(8,128)(2,1)S(1)} %get-tuple-element.30.asks0.asks, bf16[192,384]{1,0:T(8,128)(2,1)S(1)} %get-tuple-element.24.asks.asks1, ...), custom_call_target="tpu_custom_call" | custom-call | flops 150994944 | bytes 589824 | tf_op jit(solution)/shard_map/pallas_call | solution.py:316
  41.1 0.0 collective-permute-done.15.back0
  41.1 0.0 collective-permute-done.16.back1
  41.1 1.3 %collective-permute-done.17.back2 = bf16[192,256]{1,0:T(8,128)(2,1)S(1)} collective-permute-done((bf16[192,256]{1,0:T(8,128)(2,1)S(1)}, bf16[192,256]{1,0:T(8,128)(2,1)S(1)}, u32[]{:S(2)}, u32[]{:S(2)}) %collective-permute-start.17) | collective-permute-done | bytes 98336 | tf_op jit(solution)/shard_map/ppermute | solution.py:310
  42.3 0.8 %shard_map.122 = (bf16[128,768]{1,0:T(8,128)(2,1)}, bf16[128,768]{1,0:T(8,128)(2,1)}, bf16[64,768]{1,0:T(8,128)(2,1)}, bf16[64,768]{1,0:T(8,128)(2,1)}) custom-call(s32[1]{0:T(128)} %bitcast.me_ref, bf16[128,768]{1,0:T(8,128)(2,1)S(1)} %get-tuple-element.32.own_cross, bf16[128,768]{1,0:T(8,128)(2,1)S(1)} %shard_map.116.end_cross, ...), custom_call_target="tpu_custom_call" | custom-call | tf_op jit(solution)/shard_map/pallas_call | solution.py:316
  43.2 0.0 collective-permute-done.6.back
  43.2 0.6 %shard_map.123 = (bf16[128,768]{1,0:T(8,128)(2,1)}, bf16[64,768]{1,0:T(8,128)(2,1)}) custom-call(s32[1]{0:T(128)} %bitcast.me_ref, bf16[192,128]{1,0:T(8,128)(2,1)S(1)} %shard_map.113.own, bf16[192,128]{1,0:T(8,128)(2,1)S(1)} %collective-permute-done.6.back, ...), custom_call_target="tpu_custom_call", output_to_operand_aliasing={{0}: (3, {}), {1}: (4, {})} | custom-call | tf_op jit(solution)/shard_map/pallas_call | solution.py:316
  (10 shorter events, 0.1 us)
Async XLA Ops:
  0.6 1.8 %copy-start.2 = (bf16[128,768]{1,0:T(8,128)(2,1)S(1)}, bf16[128,768]{1,0:T(8,128)(2,1)}, u32[]{:S(2)}) copy-start(bf16[128,768]{1,0:T(8,128)(2,1)} %video_k.3) | copy-start | bytes 589828
  1.8 9.4 %collective-permute-start = (bf16[256,384]{1,0:T(8,128)(2,1)S(1)}, bf16[256,384]{1,0:T(8,128)(2,1)S(1)}, u32[]{:S(2)}, u32[]{:S(2)}) collective-permute-start(bf16[256,384]{1,0:T(8,128)(2,1)S(1)} %get-tuple-element.26.out), channel_id=1, source_target_pairs={{0,1},{1,0},{4,8},{5,9},{8,4},{9,5},{12,13},{13,12},{2,3},{3,2},{6... | collective-permute-start | bytes 589832 | tf_op jit(solution)/shard_map/ppermute | solution.py:313
  2.4 17.3 %collective-permute-start.2 = (bf16[128,768]{1,0:T(8,128)(2,1)S(1)}, bf16[128,768]{1,0:T(8,128)(2,1)S(1)}, u32[]{:S(2)}, u32[]{:S(2)}) collective-permute-start(bf16[128,768]{1,0:T(8,128)(2,1)S(1)} %copy-done.2), channel_id=1, source_target_pairs={{0,1},{1,0},{4,8},{5,9},{8,4},{9,5},{12,13},{13,12},{2,3},{3,2},{6... | collective-permute-start | bytes 589832 | tf_op jit(solution)/shard_map/ppermute | solution.py:313
  2.5 20.5 %collective-permute-start.9 = (bf16[256,384]{1,0:T(8,128)(2,1)S(1)}, bf16[256,384]{1,0:T(8,128)(2,1)S(1)}, u32[]{:S(2)}, u32[]{:S(2)}) collective-permute-start(bf16[256,384]{1,0:T(8,128)(2,1)S(1)} %get-tuple-element.26.out), channel_id=1, source_target_pairs={{0,4},{4,0},{8,12},{12,8},{1,5},{5,1},{9,13},{13,9},{2,6},{6,2},{1... | collective-permute-start | bytes 589832 | tf_op jit(solution)/shard_map/ppermute | solution.py:310
  7.0 5.8 %collective-permute-start.11 = (bf16[128,384]{1,0:T(8,128)(2,1)S(1)}, bf16[128,384]{1,0:T(8,128)(2,1)S(1)}, u32[]{:S(2)}, u32[]{:S(2)}) collective-permute-start(bf16[128,384]{1,0:T(8,128)(2,1)S(1)} %get-tuple-element.35), channel_id=1, source_target_pairs={{0,1},{1,0},{4,8},{5,9},{8,4},{9,5},{12,13},{13,12},{2,3},{3,2},{6... | collective-permute-start | bytes 294920 | tf_op jit(solution)/shard_map/ppermute | solution.py:313
  7.0 16.0 %collective-permute-start.7 = (bf16[256,384]{1,0:T(8,128)(2,1)S(1)}, bf16[256,384]{1,0:T(8,128)(2,1)S(1)}, u32[]{:S(2)}, u32[]{:S(2)}) collective-permute-start(bf16[256,384]{1,0:T(8,128)(2,1)S(1)} %get-tuple-element.31.over.own), channel_id=1, source_target_pairs={{0,4},{4,0},{8,12},{12,8},{1,5},{5,1},{9,13},{13,9},{2,6},{6,2},{1... | collective-permute-start | bytes 589832 | tf_op jit(solution)/shard_map/ppermute | solution.py:310
  8.6 0.7 %copy-start = (s32[256]{0:T(256)S(1)}, s32[256]{0:T(256)}, u32[]{:S(2)}) copy-start(s32[256]{0:T(256)} %param.14) | copy-start | bytes 3076
  8.6 0.7 %copy-start.1 = (s32[4]{0:T(128)S(1)}, s32[4]{0:T(128)}, u32[]{:S(2)}) copy-start(s32[4]{0:T(128)} %count_ref.1) | copy-start | bytes 52
  11.2 8.5 %collective-permute-start.14 = (bf16[192,384]{1,0:T(8,128)(2,1)S(1)}, bf16[192,384]{1,0:T(8,128)(2,1)S(1)}, u32[]{:S(2)}, u32[]{:S(2)}) collective-permute-start(bf16[192,384]{1,0:T(8,128)(2,1)S(1)} %get-tuple-element.30.asks0.asks), channel_id=1, source_target_pairs={{0,4},{4,0},{8,12},{12,8},{1,5},{5,1},{9,13},{13,9},{2,6},{6,2},{1... | collective-permute-start | bytes 442376 | tf_op jit(solution)/shard_map/ppermute | solution.py:310
  12.8 10.7 %collective-permute-start.10 = (bf16[256,256]{1,0:T(8,128)(2,1)S(1)}, bf16[256,256]{1,0:T(8,128)(2,1)S(1)}, u32[]{:S(2)}, u32[]{:S(2)}) collective-permute-start(bf16[256,256]{1,0:T(8,128)(2,1)S(1)} %slice_select_fusion), channel_id=1, source_target_pairs={{0,4},{4,0},{8,12},{12,8},{1,5},{5,1},{9,13},{13,9},{2,6},{6,2},{1... | collective-permute-start | bytes 393224 | tf_op jit(solution)/shard_map/ppermute | solution.py:310
  19.7 18.0 %collective-permute-start.3 = (bf16[128,384]{1,0:T(8,128)(2,1)S(1)}, bf16[128,384]{1,0:T(8,128)(2,1)S(1)}, u32[]{:S(2)}, u32[]{:S(2)}) collective-permute-start(bf16[128,384]{1,0:T(8,128)(2,1)S(1)} %get-tuple-element.27), channel_id=1, source_target_pairs={{0,1},{1,0},{4,8},{5,9},{8,4},{9,5},{12,13},{13,12},{2,3},{3,2},{6... | collective-permute-start | bytes 294920 | tf_op jit(solution)/shard_map/ppermute | solution.py:313
  19.7 11.6 %collective-permute-start.5 = (bf16[192,384]{1,0:T(8,128)(2,1)S(1)}, bf16[192,384]{1,0:T(8,128)(2,1)S(1)}, u32[]{:S(2)}, u32[]{:S(2)}) collective-permute-start(bf16[192,384]{1,0:T(8,128)(2,1)S(1)} %get-tuple-element.24.asks.asks1), channel_id=1, source_target_pairs={{0,4},{4,0},{8,12},{12,8},{1,5},{5,1},{9,13},{13,9},{2,6},{6,2},{1... | collective-permute-start | bytes 442376 | tf_op jit(solution)/shard_map/ppermute | solution.py:310
  23.0 1.4 %collective-permute-start.12 = (bf16[256,384]{1,0:T(8,128)(2,1)S(1)}, bf16[256,384]{1,0:T(8,128)(2,1)S(1)}, u32[]{:S(2)}, u32[]{:S(2)}) collective-permute-start(bf16[256,384]{1,0:T(8,128)(2,1)S(1)} %collective-permute-done.9.first.mate), channel_id=1, source_target_pairs={{0,1},{1,0},{4,8},{5,9},{8,4},{9,5},{12,13},{13,12},{2,3},{3,2},{6... | collective-permute-start | bytes 589832 | tf_op jit(solution)/shard_map/ppermute | solution.py:313
  23.0 10.7 %collective-permute-start.8 = (bf16[256,384]{1,0:T(8,128)(2,1)S(1)}, bf16[256,384]{1,0:T(8,128)(2,1)S(1)}, u32[]{:S(2)}, u32[]{:S(2)}) collective-permute-start(bf16[256,384]{1,0:T(8,128)(2,1)S(1)} %collective-permute-done.7.second), channel_id=1, source_target_pairs={{0,1},{1,0},{4,8},{5,9},{8,4},{9,5},{12,13},{13,12},{2,3},{3,2},{6... | collective-permute-start | bytes 589832 | tf_op jit(solution)/shard_map/ppermute | solution.py:313
  23.5 14.2 %collective-permute-start.13 = (bf16[256,256]{1,0:T(8,128)(2,1)S(1)}, bf16[256,256]{1,0:T(8,128)(2,1)S(1)}, u32[]{:S(2)}, u32[]{:S(2)}) collective-permute-start(bf16[256,256]{1,0:T(8,128)(2,1)S(1)} %collective-permute-done.10.part1.mate), channel_id=1, source_target_pairs={{0,1},{1,0},{4,8},{5,9},{8,4},{9,5},{12,13},{13,12},{2,3},{3,2},{6... | collective-permute-start | bytes 393224 | tf_op jit(solution)/shard_map/ppermute | solution.py:313
  24.4 9.2 %collective-permute-start.1 = (bf16[256,128]{1,0:T(8,128)(2,1)S(1)}, bf16[256,128]{1,0:T(8,128)(2,1)S(1)}, u32[]{:S(2)}, u32[]{:S(2)}) collective-permute-start(bf16[256,128]{1,0:T(8,128)(2,1)S(1)} %slice_select_fusion.1), channel_id=1, source_target_pairs={{0,4},{4,0},{8,12},{12,8},{1,5},{5,1},{9,13},{13,9},{2,6},{6,2},{1... | collective-permute-start | bytes 196616 | tf_op jit(solution)/shard_map/ppermute | solution.py:310
  31.3 9.8 %collective-permute-start.16 = (bf16[192,384]{1,0:T(8,128)(2,1)S(1)}, bf16[192,384]{1,0:T(8,128)(2,1)S(1)}, u32[]{:S(2)}, u32[]{:S(2)}) collective-permute-start(bf16[192,384]{1,0:T(8,128)(2,1)S(1)} %shard_map.120), channel_id=1, source_target_pairs={{0,4},{4,0},{8,12},{12,8},{1,5},{5,1},{9,13},{13,9},{2,6},{6,2},{1... | collective-permute-start | bytes 442376 | tf_op jit(solution)/shard_map/ppermute | solution.py:310
  33.7 4.9 %collective-permute-start.4 = (bf16[256,128]{1,0:T(8,128)(2,1)S(1)}, bf16[256,128]{1,0:T(8,128)(2,1)S(1)}, u32[]{:S(2)}, u32[]{:S(2)}) collective-permute-start(bf16[256,128]{1,0:T(8,128)(2,1)S(1)} %collective-permute-done.1.mate.part2), channel_id=1, source_target_pairs={{0,1},{1,0},{4,8},{5,9},{8,4},{9,5},{12,13},{13,12},{2,3},{3,2},{6... | collective-permute-start | bytes 196616 | tf_op jit(solution)/shard_map/ppermute | solution.py:313
  33.7 7.4 %collective-permute-start.15 = (bf16[64,768]{1,0:T(8,128)(2,1)S(1)}, bf16[64,768]{1,0:T(8,128)(2,1)S(1)}, u32[]{:S(2)}, u32[]{:S(2)}) collective-permute-start(bf16[64,768]{1,0:T(8,128)(2,1)S(1)} %shard_map.119), channel_id=1, source_target_pairs={{0,4},{4,0},{8,12},{12,8},{1,5},{5,1},{9,13},{13,9},{2,6},{6,2},{1... | collective-permute-start | bytes 294920 | tf_op jit(solution)/shard_map/ppermute | solution.py:310
  37.7 4.6 %collective-permute-start.17 = (bf16[192,256]{1,0:T(8,128)(2,1)S(1)}, bf16[192,256]{1,0:T(8,128)(2,1)S(1)}, u32[]{:S(2)}, u32[]{:S(2)}) collective-permute-start(bf16[192,256]{1,0:T(8,128)(2,1)S(1)} %shard_map.121), channel_id=1, source_target_pairs={{0,4},{4,0},{8,12},{12,8},{1,5},{5,1},{9,13},{13,9},{2,6},{6,2},{1... | collective-permute-start | bytes 294920 | tf_op jit(solution)/shard_map/ppermute | solution.py:310
  38.6 4.6 %collective-permute-start.6 = (bf16[192,128]{1,0:T(8,128)(2,1)S(1)}, bf16[192,128]{1,0:T(8,128)(2,1)S(1)}, u32[]{:S(2)}, u32[]{:S(2)}) collective-permute-start(bf16[192,128]{1,0:T(8,128)(2,1)S(1)} %shard_map.114), channel_id=1, source_target_pairs={{0,4},{4,0},{8,12},{12,8},{1,5},{5,1},{9,13},{13,9},{2,6},{6,2},{1... | collective-permute-start | bytes 147464 | tf_op jit(solution)/shard_map/ppermute | solution.py:310

commit v12 on v10

--- a/solution.py
+++ b/solution.py
@@ -60,7 +60,7 @@
     return (video_self, video_cross, audio_self, audio_cross)
 
 
-def blend(queries, keys, values, bias):
+def gather_up(queries, keys, values, bias):
     scores = lax.dot_general(
         queries, keys, (((1,), (1,)), ((), ())), preferred_element_type=jnp.float32
     )
@@ -75,6 +75,11 @@
         mixed += jnp.dot(
             weights[:, at : at + STEP], values[at : at + STEP], preferred_element_type=jnp.float32
         )
+    return peak, total, mixed
+
+
+def blend(queries, keys, values, bias):
+    _, total, mixed = gather_up(queries, keys, values, bias)
     return (mixed * (1.0 / total)).astype(jnp.bfloat16)
 
 
@@ -261,6 +266,59 @@
             out_ref[:, cols] = blend(queries, keys, values, mask_ref[...])
 
 
+def early_kernel(n, at, half, me_ref, mask_ref, asks0, asks1, own, mate, keys2, values2, *outs):
+    peak_ref, total_ref, mixed_ref = outs
+    video_rows = own.shape[0] // 2
+    audio_rows = peak_ref.shape[0] - video_rows
+    me = me_ref[0]
+
+    @pl.when((me > 0) & (me < n - 1))
+    def _():
+        for head in range(own.shape[1] // HEAD_DIM):
+            cols = slice(head * HEAD_DIM, (head + 1) * HEAD_DIM)
+            all_cols = slice((at + head) * HEAD_DIM, (at + head + 1) * HEAD_DIM)
+            half_cols = slice((at - half + head) * HEAD_DIM, (at - half + head + 1) * HEAD_DIM)
+            top, low = slice(0, video_rows), slice(video_rows, 2 * video_rows)
+            keys = jnp.concatenate([own[top, cols], mate[top, cols], keys2[:, all_cols]], axis=0)
+            values = jnp.concatenate([own[low, cols], mate[low, cols], values2[:, half_cols]], axis=0)
+            queries = queries_of(1, asks0, asks1, video_rows, audio_rows, half_cols)
+            peak, total, mixed = gather_up(queries, keys, values, mask_ref[:, : keys.shape[0]])
+            peak_ref[:, cols] = jnp.broadcast_to(peak, mixed.shape)
+            total_ref[:, cols] = jnp.broadcast_to(total, mixed.shape)
+            mixed_ref[:, cols] = mixed
+
+
+def late_kernel(n, at, half, me_ref, mask_ref, asks0, asks1, far, peak_ref, total_ref, mixed_ref, out_ref):
+    video_rows = far.shape[0] // 2
+    audio_rows = out_ref.shape[0] - video_rows
+    me = me_ref[0]
+
+    @pl.when((me > 0) & (me < n - 1))
+    def _():
+        for head in range(far.shape[1] // HEAD_DIM):
+            cols = slice(head * HEAD_DIM, (head + 1) * HEAD_DIM)
+            half_cols = slice((at - half + head) * HEAD_DIM, (at - half + head + 1) * HEAD_DIM)
+            queries = queries_of(1, asks0, asks1, video_rows, audio_rows, half_cols)
+            scores = lax.dot_general(
+                queries,
+                far[:video_rows, cols],
+                (((1,), (1,)), ((), ())),
+                preferred_element_type=jnp.float32,
+            )
+            scores = scores + mask_ref[:, mask_ref.shape[1] - video_rows :]
+            before = peak_ref[:, cols]
+            peak = jnp.maximum(before, jnp.max(scores, axis=1, keepdims=True))
+            kept = jnp.exp2((before - peak) * (HEAD_DIM ** (-0.5) * LOG2E))
+            weights = jnp.exp2((scores - peak[:, :1]) * (HEAD_DIM ** (-0.5) * LOG2E))
+            total = total_ref[:, cols] * kept + jnp.sum(weights, axis=1, keepdims=True)
+            mixed = jnp.dot(
+                weights.astype(jnp.bfloat16),
+                far[video_rows:, cols],
+                preferred_element_type=jnp.float32,
+            )
+            out_ref[:, cols] = ((mixed_ref[:, cols] * kept + mixed) / total).astype(jnp.bfloat16)
+
+
 def place_pieces(parts, first, video_rows, video_self, audio_cross):
     moves, at = [], first
     for part in parts:
@@ -397,12 +455,8 @@
     pieces = [(0, chunks[0], 0, 0)]
     sight_far = [cross(sight_mate[0])]
     for source in (1, 2):
-        for i in range(chunks[source]):
-            pieces.append((sum(chunks[:source]) + i, 1, source, i))
-            part = sight_mate[source]
-            if chunks[source] > 1:
-                part = part[:, i * HEAD_DIM : (i + 1) * HEAD_DIM]
-            sight_far.append(cross(part))
+        pieces.append((sum(chunks[:source]), chunks[source], source, 0))
+        sight_far.append(cross(sight_mate[source]))
     last = len(pieces) - 1
     asks_mate = [mate(asks[i]) for i in range(2)]
 
@@ -425,7 +479,35 @@
             cost_estimate=cost(rows, n * video_rows, size),
         )[0]
 
-    back = [mate(look(i, asks_mate, mask1)) for i in range(last + 1)]
+    at, size, source, _ = pieces[1]
+    early = call(
+        functools.partial(early_kernel, n, at, chunks[0]),
+        (((rows, size * HEAD_DIM), jnp.float32),) * 3,
+        [SMEM] + [VMEM] * 7,
+        place,
+        mask1,
+        *asks_mate,
+        sights[source],
+        sight_mate[source],
+        keys_across,
+        values_across[1],
+        out_specs=(VMEM,) * 3,
+        cost_estimate=cost(rows, (n - 1) * video_rows, size),
+    )
+    late = call(
+        functools.partial(late_kernel, n, at, chunks[0]),
+        (((rows, size * HEAD_DIM), jnp.bfloat16),),
+        [SMEM] + [VMEM] * 7,
+        place,
+        mask1,
+        *asks_mate,
+        sight_far[1],
+        *early,
+        out_specs=(VMEM,),
+        cost_estimate=cost(rows, video_rows, size),
+    )[0]
+    results = [look(0, asks_mate, mask1), late, look(2, asks_mate, mask1)]
+    back = [mate(result) for result in results]
     mine = [look(i, asks, mask0) for i in range(last + 1)]
     theirs = call(
         functools.partial(audio_mate_kernel, n),
@@ -487,7 +569,7 @@
         scratch_shapes=[pltpu.SemaphoreType.DMA((2 + 2 * last,))],
     )
     video_self, audio_cross = call(
-        functools.partial(place_last_kernel, n, width - HEAD_DIM),
+        functools.partial(place_last_kernel, n, width - chunks[2] * HEAD_DIM),
         (video_shape, audio_shape),
         [SMEM] + [VMEM] * 2 + [HBM] * 2,
         place,

time: 45.3 us -> 43.2 us (0.954)
  starting transfers between devices: 31.2 us -> 30.1 us
  waiting for transfers between devices: 7.86 us -> 6.89 us
    ppermute x11 -> x10, waiting for transfers between devices: 7.84 us -> 6.87 us  [mate(): return lax.ppermute(block, 'seq', mate_pairs)]
    ppermute x11 -> x10, starting transfers between devices: 29.4 us -> 28.8 us  [mate(): return lax.ppermute(block, 'seq', mate_pairs)]
    ppermute x9 -> x8, starting transfers between devices: 1.79 us -> 1.23 us  [cross(): return lax.ppermute(block, ('seq', 'mp'), cross_pairs)]
    pallas_call x15 -> x14, Pallas kernels: 5.18 us -> 5.19 us  [call(): pl.pallas_call(kernel, out_shape=tuple((jax.ShapeDtypeStruct(shape, dtype...]
  transfers between devices with their start and end apart: 20 -> 18, of which waited for: 4 -> 4; matrix products, arithmetic and copies ran while one was open for 0% -> 0% of each run, Pallas kernels for 7% -> 8%
where the time goes in v12:
time: 43.2 us; the launch traced here: 43 us
  starting transfers between devices  30.1 us (70%)
  waiting for transfers between devices  6.89 us (16%)
  Pallas kernels  5.19 us (12%)
  between operations  0.81 us (2%)
    ppermute x10, starting transfers between devices, mate(): return lax.ppermute(block, 'seq', mate_pairs)  28.8 us
    ppermute x10, waiting for transfers between devices, mate(): return lax.ppermute(block, 'seq', mate_pairs)  6.87 us
    pallas_call x14, Pallas kernels, call(): pl.pallas_call(kernel, out_shape=tuple((jax.ShapeDtypeStruct(shape, dtype...  5.19 us
    ppermute x8, starting transfers between devices, cross(): return lax.ppermute(block, ('seq', 'mp'), cross_pairs)  1.23 us
  transfers between devices with their start and end apart: 18, of which 4 were waited for; matrix products, arithmetic and copies ran while one was open for 0% of the time, Pallas kernels for 8%

profile of v12, /device:TPU:0, one launch (start us, length us, event | category | flops | bytes accessed | tf_op | source)
XLA Modules:
  0.0 43.0 jit_solution(8454618179215201717)
XLA Ops:
  0.6 0.0 copy-start.2
  0.6 1.2 %shard_map.112 = (bf16[256,384]{1,0:T(8,128)(2,1)S(1)}, bf16[256,384]{1,0:T(8,128)(2,1)S(1)}, bf16[128,384]{1,0:T(8,128)(2,1)S(1)}) custom-call(s32[1]{0:T(128)} %bitcast.me_ref, bf16[128,768]{1,0:T(8,128)(2,1)} %video_k.3, bf16[128,768]{1,0:T(8,128)(2,1)} %video_v.3, bf16[64,768]{1,0:T(8,128)(2,1)} %audio_k.1, bf16[64,768]{1,0:T(8,128)(2,1)} %audio_v.1), custom_call_target="tpu_custom_call" | custom-call | tf_op jit(solution)/shard_map/pallas_call | solution.py:394
  1.8 0.0 copy-start
  1.9 0.0 copy-start.1
  1.9 0.6 %collective-permute-start = (bf16[256,384]{1,0:T(8,128)(2,1)S(1)}, bf16[256,384]{1,0:T(8,128)(2,1)S(1)}, u32[]{:S(2)}, u32[]{:S(2)}) collective-permute-start(bf16[256,384]{1,0:T(8,128)(2,1)S(1)} %get-tuple-element.30.out), channel_id=1, source_target_pairs={{0,1},{1,0},{4,8},{5,9},{8,4},{9,5},{12,13},{13,12},{2,3},{3,2},{6... | collective-permute-start | bytes 589832 | tf_op jit(solution)/shard_map/ppermute | solution.py:391
  2.4 0.0 copy-done.2
  2.4 0.1 collective-permute-start.2
  2.5 4.5 %collective-permute-start.10 = (bf16[256,384]{1,0:T(8,128)(2,1)S(1)}, bf16[256,384]{1,0:T(8,128)(2,1)S(1)}, u32[]{:S(2)}, u32[]{:S(2)}) collective-permute-start(bf16[256,384]{1,0:T(8,128)(2,1)S(1)} %get-tuple-element.30.out), channel_id=1, source_target_pairs={{0,4},{4,0},{8,12},{12,8},{1,5},{5,1},{9,13},{13,9},{2,6},{6,2},{1... | collective-permute-start | bytes 589832 | tf_op jit(solution)/shard_map/ppermute | solution.py:388
  7.0 0.0 copy-done
  7.0 0.0 copy-done.1
  7.0 1.9 %shard_map.111 = (bf16[256,256]{1,0:T(8,128)(2,1)S(1)}, bf16[256,128]{1,0:T(8,128)(2,1)S(1)}, bf16[256,384]{1,0:T(8,128)(2,1)S(1)}, bf16[128,384]{1,0:T(8,128)(2...) custom-call(s32[1]{0:T(128)} %bitcast.me_ref, ...), custom_call_target="tpu_custom_call" | custom-call | tf_op jit(solution)/shard_map/pallas_call | solution.py:394
  9.0 0.1 collective-permute-start.5
  9.0 0.1 collective-permute-start.12
  9.1 0.0 collective-permute-done.across
  9.1 3.6 %collective-permute-start.8 = (bf16[256,384]{1,0:T(8,128)(2,1)S(1)}, bf16[256,384]{1,0:T(8,128)(2,1)S(1)}, u32[]{:S(2)}, u32[]{:S(2)}) collective-permute-start(bf16[256,384]{1,0:T(8,128)(2,1)S(1)} %get-tuple-element.34.over.refs_1_), channel_id=1, source_target_pairs={{0,4},{4,0},{8,12},{12,8},{1,5},{5,1},{9,13},{13,9},{2,6},{6,2},{1... | collective-permute-start | bytes 589832 | tf_op jit(solution)/shard_map/ppermute | solution.py:388
  12.8 0.0 collective-permute-done.12.refs_4_
  12.8 5.2 %collective-permute-start.11 = (bf16[256,256]{1,0:T(8,128)(2,1)S(1)}, bf16[256,256]{1,0:T(8,128)(2,1)S(1)}, u32[]{:S(2)}, u32[]{:S(2)}) collective-permute-start(bf16[256,256]{1,0:T(8,128)(2,1)S(1)} %slice_select_fusion), channel_id=1, source_target_pairs={{0,4},{4,0},{8,12},{12,8},{1,5},{5,1},{9,13},{13,9},{2,6},{6,2},{1... | collective-permute-start | bytes 393224 | tf_op jit(solution)/shard_map/ppermute | solution.py:388
  18.0 0.0 collective-permute-done.5.refs_0_.asks0
  18.0 1.1 %collective-permute-start.6 = (bf16[128,384]{1,0:T(8,128)(2,1)S(1)}, bf16[128,384]{1,0:T(8,128)(2,1)S(1)}, u32[]{:S(2)}, u32[]{:S(2)}) collective-permute-start(bf16[128,384]{1,0:T(8,128)(2,1)S(1)} %get-tuple-element.28.refs_1_.asks1), channel_id=1, source_target_pairs={{0,4},{4,0},{8,12},{12,8},{1,5},{5,1},{9,13},{13,9},{2,6},{6,2},{1... | collective-permute-start | bytes 294920 | tf_op jit(solution)/shard_map/ppermute | solution.py:388
  19.0 0.0 collective-permute-done.2.refs_4_.refs_3_.keys2
  19.0 0.0 collective-permute-start.3
  19.0 0.0 collective-permute-done.10.first.refs_2_
  19.0 0.5 %collective-permute-start.13 = (bf16[256,384]{1,0:T(8,128)(2,1)S(1)}, bf16[256,384]{1,0:T(8,128)(2,1)S(1)}, u32[]{:S(2)}, u32[]{:S(2)}) collective-permute-start(bf16[256,384]{1,0:T(8,128)(2,1)S(1)} %collective-permute-done.10.first.refs_2_), channel_id=1, source_target_pairs={{0,1},{1,0},{4,8},{5,9},{8,4},{9,5},{12,13},{13,12},{2,3},{3,2},{6... | collective-permute-start | bytes 589832 | tf_op jit(solution)/shard_map/ppermute | solution.py:391
  19.5 1.5 %collective-permute-done.8.second = bf16[256,384]{1,0:T(8,128)(2,1)S(1)} collective-permute-done((bf16[256,384]{1,0:T(8,128)(2,1)S(1)}, bf16[256,384]{1,0:T(8,128)(2,1)S(1)}, u32[]{:S(2)}, u32[]{:S(2)}) %collective-permute-start.8) | collective-permute-done | bytes 196640 | tf_op jit(solution)/shard_map/ppermute | solution.py:388
  21.0 0.0 collective-permute-start.9
  21.0 2.6 %collective-permute-done.11.part1.refs_3_.mate = bf16[256,256]{1,0:T(8,128)(2,1)S(1)} collective-permute-done((bf16[256,256]{1,0:T(8,128)(2,1)S(1)}, bf16[256,256]{1,0:T(8,128)(2,1)S(1)}, u32[]{:S(2)}, u32[]{:S(2)}) %collective-permute-start.11) | collective-permute-done | bytes 131104 | tf_op jit(solution)/shard_map/ppermute | solution.py:388
  23.7 0.0 collective-permute-start.14
  23.7 0.0 collective-permute-done.13.refs_5_
  23.7 6.2 %collective-permute-start.1 = (bf16[256,128]{1,0:T(8,128)(2,1)S(1)}, bf16[256,128]{1,0:T(8,128)(2,1)S(1)}, u32[]{:S(2)}, u32[]{:S(2)}) collective-permute-start(bf16[256,128]{1,0:T(8,128)(2,1)S(1)} %slice_select_fusion.1), channel_id=1, source_target_pairs={{0,4},{4,0},{8,12},{12,8},{1,5},{5,1},{9,13},{13,9},{2,6},{6,2},{1... | collective-permute-start | bytes 196616 | tf_op jit(solution)/shard_map/ppermute | solution.py:388
  29.9 0.0 collective-permute-done.6.refs_1_.asks1
  29.9 0.8 %collective-permute-start.16 = (bf16[192,384]{1,0:T(8,128)(2,1)S(1)}, bf16[192,384]{1,0:T(8,128)(2,1)S(1)}, u32[]{:S(2)}, u32[]{:S(2)}) collective-permute-start(bf16[192,384]{1,0:T(8,128)(2,1)S(1)} %shard_map.120), channel_id=1, source_target_pairs={{0,4},{4,0},{8,12},{12,8},{1,5},{5,1},{9,13},{13,9},{2,6},{6,2},{1... | collective-permute-start | bytes 442376 | tf_op jit(solution)/shard_map/ppermute | solution.py:388
  30.7 1.4 %collective-permute-done.1.refs_3_.part2 = bf16[256,128]{1,0:T(8,128)(2,1)S(1)} collective-permute-done((bf16[256,128]{1,0:T(8,128)(2,1)S(1)}, bf16[256,128]{1,0:T(8,128)(2,1)S(1)}, u32[]{:S(2)}, u32[]{:S(2)}) %collective-permute-start.1) | collective-permute-done | bytes 65568 | tf_op jit(solution)/shard_map/ppermute | solution.py:388
  32.1 0.0 collective-permute-start.4
  32.1 0.0 collective-permute-done.3.refs_5_.values2
  32.1 0.0 collective-permute-done.9.far
  32.2 4.7 %collective-permute-start.15 = (bf16[64,768]{1,0:T(8,128)(2,1)S(1)}, bf16[64,768]{1,0:T(8,128)(2,1)S(1)}, u32[]{:S(2)}, u32[]{:S(2)}) collective-permute-start(bf16[64,768]{1,0:T(8,128)(2,1)S(1)} %shard_map.119), channel_id=1, source_target_pairs={{0,4},{4,0},{8,12},{12,8},{1,5},{5,1},{9,13},{13,9},{2,6},{6,2},{1... | collective-permute-start | bytes 294920 | tf_op jit(solution)/shard_map/ppermute | solution.py:388
  36.9 0.0 collective-permute-done.14.refs_6_.far
  36.9 0.9 %collective-permute-start.17 = (bf16[192,256]{1,0:T(8,128)(2,1)S(1)}, bf16[192,256]{1,0:T(8,128)(2,1)S(1)}, u32[]{:S(2)}, u32[]{:S(2)}) collective-permute-start(bf16[192,256]{1,0:T(8,128)(2,1)S(1)} %shard_map.122), channel_id=1, source_target_pairs={{0,4},{4,0},{8,12},{12,8},{1,5},{5,1},{9,13},{13,9},{2,6},{6,2},{1... | collective-permute-start | bytes 294920 | tf_op jit(solution)/shard_map/ppermute | solution.py:388
  37.8 0.0 collective-permute-done.4.refs_6_
  37.8 1.8 %collective-permute-start.7 = (bf16[192,128]{1,0:T(8,128)(2,1)S(1)}, bf16[192,128]{1,0:T(8,128)(2,1)S(1)}, u32[]{:S(2)}, u32[]{:S(2)}) collective-permute-start(bf16[192,128]{1,0:T(8,128)(2,1)S(1)} %shard_map.114), channel_id=1, source_target_pairs={{0,4},{4,0},{8,12},{12,8},{1,5},{5,1},{9,13},{13,9},{2,6},{6,2},{1... | collective-permute-start | bytes 147464 | tf_op jit(solution)/shard_map/ppermute | solution.py:388
  39.5 0.6 %shard_map.116.end_cross = bf16[128,768]{1,0:T(8,128)(2,1)S(1)} custom-call(s32[1]{0:T(128)} %bitcast.me_ref, f32[192,256]{1,0:T(8,128)S(1)} %get-tuple-element.33.near_ref, bf16[256,384]{1,0:T(8,128)(2,1)S(1)} %get-tuple-element.27.refs_0_.asks0, bf16[128,384]{1,0:T(8,128)(2,1)S(1)} %get-tuple-element.28.refs_1_.asks1, ...), custom_call_target="tpu_custom_call" | custom-call | flops 150994944 | bytes 589824 | tf_op jit(solution)/shard_map/pallas_call | solution.py:394
  40.2 0.0 collective-permute-done.15.refs_3_
  40.2 0.0 collective-permute-done.16.refs_4_
  40.2 1.3 %collective-permute-done.17.refs_5_ = bf16[192,256]{1,0:T(8,128)(2,1)S(1)} collective-permute-done((bf16[192,256]{1,0:T(8,128)(2,1)S(1)}, bf16[192,256]{1,0:T(8,128)(2,1)S(1)}, u32[]{:S(2)}, u32[]{:S(2)}) %collective-permute-start.17) | collective-permute-done | bytes 98336 | tf_op jit(solution)/shard_map/ppermute | solution.py:388
  41.5 0.8 %shard_map.123 = (bf16[128,768]{1,0:T(8,128)(2,1)}, bf16[128,768]{1,0:T(8,128)(2,1)}, bf16[64,768]{1,0:T(8,128)(2,1)}, bf16[64,768]{1,0:T(8,128)(2,1)}) custom-call(s32[1]{0:T(128)} %bitcast.me_ref, bf16[128,768]{1,0:T(8,128)(2,1)S(1)} %get-tuple-element.35.own_cross, bf16[128,768]{1,0:T(8,128)(2,1)S(1)} %shard_map.116.end_cross, ...), custom_call_target="tpu_custom_call" | custom-call | tf_op jit(solution)/shard_map/pallas_call | solution.py:394
  42.4 0.0 collective-permute-done.7.back
  42.4 0.6 %shard_map.124 = (bf16[128,768]{1,0:T(8,128)(2,1)}, bf16[64,768]{1,0:T(8,128)(2,1)}) custom-call(s32[1]{0:T(128)} %bitcast.me_ref, bf16[192,128]{1,0:T(8,128)(2,1)S(1)} %shard_map.113.own, bf16[192,128]{1,0:T(8,128)(2,1)S(1)} %collective-permute-done.7.back, ...), custom_call_target="tpu_custom_call", output_to_operand_aliasing={{0}: (3, {}), {1}: (4, {})} | custom-call | tf_op jit(solution)/shard_map/pallas_call | solution.py:394
  (11 shorter events, 0.1 us)
Async XLA Ops:
  0.6 1.8 %copy-start.2 = (bf16[128,768]{1,0:T(8,128)(2,1)S(1)}, bf16[128,768]{1,0:T(8,128)(2,1)}, u32[]{:S(2)}) copy-start(bf16[128,768]{1,0:T(8,128)(2,1)} %video_k.3) | copy-start | bytes 589828
  1.8 5.2 %copy-start = (s32[256]{0:T(256)S(1)}, s32[256]{0:T(256)}, u32[]{:S(2)}) copy-start(s32[256]{0:T(256)} %param.14) | copy-start | bytes 3076
  1.9 5.2 %copy-start.1 = (s32[4]{0:T(128)S(1)}, s32[4]{0:T(128)}, u32[]{:S(2)}) copy-start(s32[4]{0:T(128)} %count_ref.1) | copy-start | bytes 52
  1.9 7.3 %collective-permute-start = (bf16[256,384]{1,0:T(8,128)(2,1)S(1)}, bf16[256,384]{1,0:T(8,128)(2,1)S(1)}, u32[]{:S(2)}, u32[]{:S(2)}) collective-permute-start(bf16[256,384]{1,0:T(8,128)(2,1)S(1)} %get-tuple-element.30.out), channel_id=1, source_target_pairs={{0,1},{1,0},{4,8},{5,9},{8,4},{9,5},{12,13},{13,12},{2,3},{3,2},{6... | collective-permute-start | bytes 589832 | tf_op jit(solution)/shard_map/ppermute | solution.py:391
  2.4 16.6 %collective-permute-start.2 = (bf16[128,768]{1,0:T(8,128)(2,1)S(1)}, bf16[128,768]{1,0:T(8,128)(2,1)S(1)}, u32[]{:S(2)}, u32[]{:S(2)}) collective-permute-start(bf16[128,768]{1,0:T(8,128)(2,1)S(1)} %copy-done.2), channel_id=1, source_target_pairs={{0,1},{1,0},{4,8},{5,9},{8,4},{9,5},{12,13},{13,12},{2,3},{3,2},{6... | collective-permute-start | bytes 589832 | tf_op jit(solution)/shard_map/ppermute | solution.py:391
  2.5 16.5 %collective-permute-start.10 = (bf16[256,384]{1,0:T(8,128)(2,1)S(1)}, bf16[256,384]{1,0:T(8,128)(2,1)S(1)}, u32[]{:S(2)}, u32[]{:S(2)}) collective-permute-start(bf16[256,384]{1,0:T(8,128)(2,1)S(1)} %get-tuple-element.30.out), channel_id=1, source_target_pairs={{0,4},{4,0},{8,12},{12,8},{1,5},{5,1},{9,13},{13,9},{2,6},{6,2},{1... | collective-permute-start | bytes 589832 | tf_op jit(solution)/shard_map/ppermute | solution.py:388
  9.0 9.0 %collective-permute-start.5 = (bf16[256,384]{1,0:T(8,128)(2,1)S(1)}, bf16[256,384]{1,0:T(8,128)(2,1)S(1)}, u32[]{:S(2)}, u32[]{:S(2)}) collective-permute-start(bf16[256,384]{1,0:T(8,128)(2,1)S(1)} %get-tuple-element.27.refs_0_.asks0), channel_id=1, source_target_pairs={{0,4},{4,0},{8,12},{12,8},{1,5},{5,1},{9,13},{13,9},{2,6},{6,2},{1... | collective-permute-start | bytes 589832 | tf_op jit(solution)/shard_map/ppermute | solution.py:388
  9.0 3.8 %collective-permute-start.12 = (bf16[128,384]{1,0:T(8,128)(2,1)S(1)}, bf16[128,384]{1,0:T(8,128)(2,1)S(1)}, u32[]{:S(2)}, u32[]{:S(2)}) collective-permute-start(bf16[128,384]{1,0:T(8,128)(2,1)S(1)} %get-tuple-element.38), channel_id=1, source_target_pairs={{0,1},{1,0},{4,8},{5,9},{8,4},{9,5},{12,13},{13,12},{2,3},{3,2},{6... | collective-permute-start | bytes 294920 | tf_op jit(solution)/shard_map/ppermute | solution.py:391
  9.1 11.9 %collective-permute-start.8 = (bf16[256,384]{1,0:T(8,128)(2,1)S(1)}, bf16[256,384]{1,0:T(8,128)(2,1)S(1)}, u32[]{:S(2)}, u32[]{:S(2)}) collective-permute-start(bf16[256,384]{1,0:T(8,128)(2,1)S(1)} %get-tuple-element.34.over.refs_1_), channel_id=1, source_target_pairs={{0,4},{4,0},{8,12},{12,8},{1,5},{5,1},{9,13},{13,9},{2,6},{6,2},{1... | collective-permute-start | bytes 589832 | tf_op jit(solution)/shard_map/ppermute | solution.py:388
  12.8 10.9 %collective-permute-start.11 = (bf16[256,256]{1,0:T(8,128)(2,1)S(1)}, bf16[256,256]{1,0:T(8,128)(2,1)S(1)}, u32[]{:S(2)}, u32[]{:S(2)}) collective-permute-start(bf16[256,256]{1,0:T(8,128)(2,1)S(1)} %slice_select_fusion), channel_id=1, source_target_pairs={{0,4},{4,0},{8,12},{12,8},{1,5},{5,1},{9,13},{13,9},{2,6},{6,2},{1... | collective-permute-start | bytes 393224 | tf_op jit(solution)/shard_map/ppermute | solution.py:388
  18.0 11.9 %collective-permute-start.6 = (bf16[128,384]{1,0:T(8,128)(2,1)S(1)}, bf16[128,384]{1,0:T(8,128)(2,1)S(1)}, u32[]{:S(2)}, u32[]{:S(2)}) collective-permute-start(bf16[128,384]{1,0:T(8,128)(2,1)S(1)} %get-tuple-element.28.refs_1_.asks1), channel_id=1, source_target_pairs={{0,4},{4,0},{8,12},{12,8},{1,5},{5,1},{9,13},{13,9},{2,6},{6,2},{1... | collective-permute-start | bytes 294920 | tf_op jit(solution)/shard_map/ppermute | solution.py:388
  19.0 13.1 %collective-permute-start.3 = (bf16[128,384]{1,0:T(8,128)(2,1)S(1)}, bf16[128,384]{1,0:T(8,128)(2,1)S(1)}, u32[]{:S(2)}, u32[]{:S(2)}) collective-permute-start(bf16[128,384]{1,0:T(8,128)(2,1)S(1)} %get-tuple-element.31), channel_id=1, source_target_pairs={{0,1},{1,0},{4,8},{5,9},{8,4},{9,5},{12,13},{13,12},{2,3},{3,2},{6... | collective-permute-start | bytes 294920 | tf_op jit(solution)/shard_map/ppermute | solution.py:391
  19.0 4.6 %collective-permute-start.13 = (bf16[256,384]{1,0:T(8,128)(2,1)S(1)}, bf16[256,384]{1,0:T(8,128)(2,1)S(1)}, u32[]{:S(2)}, u32[]{:S(2)}) collective-permute-start(bf16[256,384]{1,0:T(8,128)(2,1)S(1)} %collective-permute-done.10.first.refs_2_), channel_id=1, source_target_pairs={{0,1},{1,0},{4,8},{5,9},{8,4},{9,5},{12,13},{13,12},{2,3},{3,2},{6... | collective-permute-start | bytes 589832 | tf_op jit(solution)/shard_map/ppermute | solution.py:391
  21.0 11.1 %collective-permute-start.9 = (bf16[256,384]{1,0:T(8,128)(2,1)S(1)}, bf16[256,384]{1,0:T(8,128)(2,1)S(1)}, u32[]{:S(2)}, u32[]{:S(2)}) collective-permute-start(bf16[256,384]{1,0:T(8,128)(2,1)S(1)} %collective-permute-done.8.second), channel_id=1, source_target_pairs={{0,1},{1,0},{4,8},{5,9},{8,4},{9,5},{12,13},{13,12},{2,3},{3,2},{6... | collective-permute-start | bytes 589832 | tf_op jit(solution)/shard_map/ppermute | solution.py:391
  23.7 13.2 %collective-permute-start.14 = (bf16[256,256]{1,0:T(8,128)(2,1)S(1)}, bf16[256,256]{1,0:T(8,128)(2,1)S(1)}, u32[]{:S(2)}, u32[]{:S(2)}) collective-permute-start(bf16[256,256]{1,0:T(8,128)(2,1)S(1)} %collective-permute-done.11.part1.refs_3_.mate), channel_id=1, source_target_pairs={{0,1},{1,0},{4,8},{5,9},{8,4},{9,5},{12,13},{13,12},{2,3},{3,2},{6... | collective-permute-start | bytes 393224 | tf_op jit(solution)/shard_map/ppermute | solution.py:391
  23.7 8.4 %collective-permute-start.1 = (bf16[256,128]{1,0:T(8,128)(2,1)S(1)}, bf16[256,128]{1,0:T(8,128)(2,1)S(1)}, u32[]{:S(2)}, u32[]{:S(2)}) collective-permute-start(bf16[256,128]{1,0:T(8,128)(2,1)S(1)} %slice_select_fusion.1), channel_id=1, source_target_pairs={{0,4},{4,0},{8,12},{12,8},{1,5},{5,1},{9,13},{13,9},{2,6},{6,2},{1... | collective-permute-start | bytes 196616 | tf_op jit(solution)/shard_map/ppermute | solution.py:388
  29.9 10.3 %collective-permute-start.16 = (bf16[192,384]{1,0:T(8,128)(2,1)S(1)}, bf16[192,384]{1,0:T(8,128)(2,1)S(1)}, u32[]{:S(2)}, u32[]{:S(2)}) collective-permute-start(bf16[192,384]{1,0:T(8,128)(2,1)S(1)} %shard_map.120), channel_id=1, source_target_pairs={{0,4},{4,0},{8,12},{12,8},{1,5},{5,1},{9,13},{13,9},{2,6},{6,2},{1... | collective-permute-start | bytes 442376 | tf_op jit(solution)/shard_map/ppermute | solution.py:388
  32.1 5.6 %collective-permute-start.4 = (bf16[256,128]{1,0:T(8,128)(2,1)S(1)}, bf16[256,128]{1,0:T(8,128)(2,1)S(1)}, u32[]{:S(2)}, u32[]{:S(2)}) collective-permute-start(bf16[256,128]{1,0:T(8,128)(2,1)S(1)} %collective-permute-done.1.refs_3_.part2), channel_id=1, source_target_pairs={{0,1},{1,0},{4,8},{5,9},{8,4},{9,5},{12,13},{13,12},{2,3},{3,2},{6... | collective-permute-start | bytes 196616 | tf_op jit(solution)/shard_map/ppermute | solution.py:391
  32.2 8.0 %collective-permute-start.15 = (bf16[64,768]{1,0:T(8,128)(2,1)S(1)}, bf16[64,768]{1,0:T(8,128)(2,1)S(1)}, u32[]{:S(2)}, u32[]{:S(2)}) collective-permute-start(bf16[64,768]{1,0:T(8,128)(2,1)S(1)} %shard_map.119), channel_id=1, source_target_pairs={{0,4},{4,0},{8,12},{12,8},{1,5},{5,1},{9,13},{13,9},{2,6},{6,2},{1... | collective-permute-start | bytes 294920 | tf_op jit(solution)/shard_map/ppermute | solution.py:388
  36.9 4.6 %collective-permute-start.17 = (bf16[192,256]{1,0:T(8,128)(2,1)S(1)}, bf16[192,256]{1,0:T(8,128)(2,1)S(1)}, u32[]{:S(2)}, u32[]{:S(2)}) collective-permute-start(bf16[192,256]{1,0:T(8,128)(2,1)S(1)} %shard_map.122), channel_id=1, source_target_pairs={{0,4},{4,0},{8,12},{12,8},{1,5},{5,1},{9,13},{13,9},{2,6},{6,2},{1... | collective-permute-start | bytes 294920 | tf_op jit(solution)/shard_map/ppermute | solution.py:388
  37.8 4.6 %collective-permute-start.7 = (bf16[192,128]{1,0:T(8,128)(2,1)S(1)}, bf16[192,128]{1,0:T(8,128)(2,1)S(1)}, u32[]{:S(2)}, u32[]{:S(2)}) collective-permute-start(bf16[192,128]{1,0:T(8,128)(2,1)S(1)} %shard_map.114), channel_id=1, source_target_pairs={{0,4},{4,0},{8,12},{12,8},{1,5},{5,1},{9,13},{13,9},{2,6},{6,2},{1... | collective-permute-start | bytes 147464 | tf_op jit(solution)/shard_map/ppermute | solution.py:388

commit v13 on v10

--- a/solution.py
+++ b/solution.py
@@ -271,22 +271,33 @@
     return moves
 
 
-def place_kernel(n, me_ref, own_cross, end_cross, *refs):
-    count = (len(refs) - 5) // 2
-    own, back = refs[:count], refs[count : 2 * count]
-    video_self, video_cross, audio_self, audio_cross, sem = refs[2 * count :]
+def place_end_kernel(n, me_ref, cross, back0, video_self, video_cross, audio_self, audio_cross, sem):
+    @pl.when((me_ref[0] == 0) | (me_ref[0] == n - 1))
+    def _():
+        moves = [(cross, video_cross)]
+        moves += place_pieces((back0,), 0, cross.shape[0], video_self, audio_cross)
+        for copy in move_all(moves, sem):
+            copy.wait()
+
+
+def place_kernel(n, me_ref, own_cross, own_sound, own0, own1, back_sound, back1, *refs):
+    video_self, video_cross, audio_self, audio_cross, sem = refs[4:]
+    video_rows, first = own_cross.shape[0], own0.shape[1]
     at_end = (me_ref[0] == 0) | (me_ref[0] == n - 1)
-    for role, cross, parts in (
-        (jnp.logical_not(at_end), own_cross, own),
-        (at_end, end_cross, back),
-    ):
-
-        @pl.when(role)
-        def _(cross=cross, parts=parts):
-            moves = [(cross, video_cross), (parts[0], audio_self)]
-            moves += place_pieces(parts[1:], 0, cross.shape[0], video_self, audio_cross)
-            for copy in move_all(moves, sem):
-                copy.wait()
+
+    @pl.when(jnp.logical_not(at_end))
+    def _():
+        moves = [(own_cross, video_cross), (own_sound, audio_self)]
+        moves += place_pieces((own0, own1), 0, video_rows, video_self, audio_cross)
+        for copy in move_all(moves, sem):
+            copy.wait()
+
+    @pl.when(at_end)
+    def _():
+        moves = [(back_sound, audio_self)]
+        moves += place_pieces((back1,), first, video_rows, video_self, audio_cross)
+        for copy in move_all(moves, sem):
+            copy.wait()
 
 
 def place_last_kernel(n, first, me_ref, own, back, old_self, old_cross, video_self, audio_cross, sem):
@@ -397,12 +408,8 @@
     pieces = [(0, chunks[0], 0, 0)]
     sight_far = [cross(sight_mate[0])]
     for source in (1, 2):
-        for i in range(chunks[source]):
-            pieces.append((sum(chunks[:source]) + i, 1, source, i))
-            part = sight_mate[source]
-            if chunks[source] > 1:
-                part = part[:, i * HEAD_DIM : (i + 1) * HEAD_DIM]
-            sight_far.append(cross(part))
+        pieces.append((sum(chunks[:source]), chunks[source], source, 0))
+        sight_far.append(cross(sight_mate[source]))
     last = len(pieces) - 1
     asks_mate = [mate(asks[i]) for i in range(2)]
 
@@ -425,7 +432,8 @@
             cost_estimate=cost(rows, n * video_rows, size),
         )[0]
 
-    back = [mate(look(i, asks_mate, mask1)) for i in range(last + 1)]
+    results = [look(i, asks_mate, mask1) for i in range(last + 1)]
+    back = [mate(result) for result in results]
     mine = [look(i, asks, mask0) for i in range(last + 1)]
     theirs = call(
         functools.partial(audio_mate_kernel, n),
@@ -472,22 +480,34 @@
     back_sound = mate(theirs)
     video_shape = ((video_rows, width), jnp.bfloat16)
     audio_shape = ((audio_rows, width), jnp.bfloat16)
+    shapes = (video_shape, video_shape, audio_shape, audio_shape)
+    begun = call(
+        functools.partial(place_end_kernel, n),
+        shapes,
+        [SMEM] + [VMEM] * 2,
+        place,
+        end_cross,
+        back[0],
+        out_specs=(HBM,) * 4,
+        scratch_shapes=[pltpu.SemaphoreType.DMA((3,))],
+    )
     video_self, video_cross, audio_self, audio_cross = call(
         functools.partial(place_kernel, n),
-        (video_shape, video_shape, audio_shape, audio_shape),
-        [SMEM] + [VMEM] * (4 + 2 * last),
+        shapes,
+        [SMEM] + [VMEM] * 6 + [HBM] * 4,
         place,
         own_cross,
-        end_cross,
         own,
-        *mine[:last],
+        *mine[:2],
         back_sound,
-        *back[:last],
+        back[1],
+        *begun,
         out_specs=(HBM,) * 4,
-        scratch_shapes=[pltpu.SemaphoreType.DMA((2 + 2 * last,))],
+        scratch_shapes=[pltpu.SemaphoreType.DMA((6,))],
+        input_output_aliases={7: 0, 8: 1, 9: 2, 10: 3},
     )
     video_self, audio_cross = call(
-        functools.partial(place_last_kernel, n, width - HEAD_DIM),
+        functools.partial(place_last_kernel, n, width - chunks[2] * HEAD_DIM),
         (video_shape, audio_shape),
         [SMEM] + [VMEM] * 2 + [HBM] * 2,
         place,

time: 45.3 us -> 40.3 us (0.89)
  waiting for transfers between devices: 7.86 us -> 3.28 us
  starting transfers between devices: 31.2 us -> 29.6 us
  local copies, waits for them, and re-layouts: 0.03 us -> 0.69 us
  Pallas kernels: 5.18 us -> 5.78 us
    ppermute x11 -> x10, waiting for transfers between devices: 7.84 us -> 2.47 us  [mate(): return lax.ppermute(block, 'seq', mate_pairs)]
    ppermute x11 -> x10, starting transfers between devices: 29.4 us -> 28 us  [mate(): return lax.ppermute(block, 'seq', mate_pairs)]
    ppermute x9 -> x8, waiting for transfers between devices: 0.02 us -> 0.81 us  [cross(): return lax.ppermute(block, ('seq', 'mp'), cross_pairs)]
    unnamed x6, local copies, waits for them, and re-layouts: 0.02 us -> 0.69 us
    pallas_call x15 -> x14, Pallas kernels: 5.18 us -> 5.78 us  [call(): pl.pallas_call(kernel, out_shape=tuple((jax.ShapeDtypeStruct(shape, dtype...]
    ppermute x9 -> x8, starting transfers between devices: 1.79 us -> 1.58 us  [cross(): return lax.ppermute(block, ('seq', 'mp'), cross_pairs)]
  transfers between devices with their start and end apart: 20 -> 18, of which waited for: 4 -> 4; matrix products, arithmetic and copies ran while one was open for 0% -> 0% of each run, Pallas kernels for 7% -> 10%
where the time goes in v13:
time: 40.3 us; the launch traced here: 40.1 us
  starting transfers between devices  29.6 us (73%)
  Pallas kernels  5.78 us (14%)
  waiting for transfers between devices  3.28 us (8%)
  between operations  0.77 us (2%)
  local copies, waits for them, and re-layouts  0.69 us (2%)
    ppermute x10, starting transfers between devices, mate(): return lax.ppermute(block, 'seq', mate_pairs)  28 us
    pallas_call x14, Pallas kernels, call(): pl.pallas_call(kernel, out_shape=tuple((jax.ShapeDtypeStruct(shape, dtype...  5.78 us
    ppermute x10, waiting for transfers between devices, mate(): return lax.ppermute(block, 'seq', mate_pairs)  2.47 us
    ppermute x8, starting transfers between devices, cross(): return lax.ppermute(block, ('seq', 'mp'), cross_pairs)  1.58 us
    ppermute x8, waiting for transfers between devices, cross(): return lax.ppermute(block, ('seq', 'mp'), cross_pairs)  0.81 us
  transfers between devices with their start and end apart: 18, of which 4 were waited for; matrix products, arithmetic and copies ran while one was open for 0% of the time, Pallas kernels for 10%

profile of v13, /device:TPU:0, one launch (start us, length us, event | category | flops | bytes accessed | tf_op | source)
XLA Modules:
  0.0 40.1 jit_solution(8697124899210408504)
XLA Ops:
  0.6 1.1 %shard_map.112 = (bf16[256,384]{1,0:T(8,128)(2,1)S(1)}, bf16[256,384]{1,0:T(8,128)(2,1)S(1)}, bf16[128,384]{1,0:T(8,128)(2,1)S(1)}) custom-call(s32[1]{0:T(128)} %bitcast.me_ref, bf16[128,768]{1,0:T(8,128)(2,1)} %video_k.3, bf16[128,768]{1,0:T(8,128)(2,1)} %video_v.3, bf16[64,768]{1,0:T(8,128)(2,1)} %audio_k.1, bf16[64,768]{1,0:T(8,128)(2,1)} %audio_v.1), custom_call_target="tpu_custom_call" | custom-call | tf_op jit(solution)/shard_map/pallas_call | solution.py:347
  1.8 0.6 %collective-permute-start = (bf16[256,384]{1,0:T(8,128)(2,1)S(1)}, bf16[256,384]{1,0:T(8,128)(2,1)S(1)}, u32[]{:S(2)}, u32[]{:S(2)}) collective-permute-start(bf16[256,384]{1,0:T(8,128)(2,1)S(1)} %get-tuple-element.31.out), channel_id=1, source_target_pairs={{0,1},{1,0},{4,8},{5,9},{8,4},{9,5},{12,13},{13,12},{2,3},{3,2},{6... | collective-permute-start | bytes 589832 | tf_op jit(solution)/shard_map/ppermute | solution.py:344
  2.3 4.1 %collective-permute-start.10 = (bf16[256,384]{1,0:T(8,128)(2,1)S(1)}, bf16[256,384]{1,0:T(8,128)(2,1)S(1)}, u32[]{:S(2)}, u32[]{:S(2)}) collective-permute-start(bf16[256,384]{1,0:T(8,128)(2,1)S(1)} %get-tuple-element.31.out), channel_id=1, source_target_pairs={{0,4},{4,0},{8,12},{12,8},{1,5},{5,1},{9,13},{13,9},{2,6},{6,2},{1... | collective-permute-start | bytes 589832 | tf_op jit(solution)/shard_map/ppermute | solution.py:341
  6.5 0.0 collective-permute-start.8
  6.5 0.0 copy-start
  6.5 0.0 copy-start.1
  6.5 0.7 %copy-done = s32[256]{0:T(256)S(1)} copy-done((s32[256]{0:T(256)S(1)}, s32[256]{0:T(256)}, u32[]{:S(2)}) %copy-start) | copy-done | bytes 1048
  7.2 0.0 copy-done.1
  7.2 1.9 %shard_map.111 = (bf16[256,256]{1,0:T(8,128)(2,1)S(1)}, bf16[256,128]{1,0:T(8,128)(2,1)S(1)}, bf16[256,384]{1,0:T(8,128)(2,1)S(1)}, bf16[128,384]{1,0:T(8,128)(2...) custom-call(s32[1]{0:T(128)} %bitcast.me_ref, ...), custom_call_target="tpu_custom_call" | custom-call | tf_op jit(solution)/shard_map/pallas_call | solution.py:347
  9.1 0.0 collective-permute-done.across
  9.1 0.0 copy-start.2
  9.2 2.5 %collective-permute-start.13 = (bf16[256,256]{1,0:T(8,128)(2,1)S(1)}, bf16[256,256]{1,0:T(8,128)(2,1)S(1)}, u32[]{:S(2)}, u32[]{:S(2)}) collective-permute-start(bf16[256,256]{1,0:T(8,128)(2,1)S(1)} %slice_select_fusion), channel_id=1, source_target_pairs={{0,4},{4,0},{8,12},{12,8},{1,5},{5,1},{9,13},{13,9},{2,6},{6,2},{1... | collective-permute-start | bytes 393224 | tf_op jit(solution)/shard_map/ppermute | solution.py:341
  11.7 0.0 collective-permute-start.11
  11.7 0.0 copy-done.2
  11.7 0.5 %collective-permute-start.2 = (bf16[128,768]{1,0:T(8,128)(2,1)S(1)}, bf16[128,768]{1,0:T(8,128)(2,1)S(1)}, u32[]{:S(2)}, u32[]{:S(2)}) collective-permute-start(bf16[128,768]{1,0:T(8,128)(2,1)S(1)} %copy-done.2), channel_id=1, source_target_pairs={{0,1},{1,0},{4,8},{5,9},{8,4},{9,5},{12,13},{13,12},{2,3},{3,2},{6... | collective-permute-start | bytes 589832 | tf_op jit(solution)/shard_map/ppermute | solution.py:344
  12.2 0.8 %collective-permute-done.11.refs_4_ = bf16[128,384]{1,0:T(8,128)(2,1)S(1)} collective-permute-done((bf16[128,384]{1,0:T(8,128)(2,1)S(1)}, bf16[128,384]{1,0:T(8,128)(2,1)S(1)}, u32[]{:S(2)}, u32[]{:S(2)}) %collective-permute-start.11) | collective-permute-done | bytes 98336 | tf_op jit(solution)/shard_map/ppermute | solution.py:344
  13.0 4.4 %collective-permute-start.5 = (bf16[256,384]{1,0:T(8,128)(2,1)S(1)}, bf16[256,384]{1,0:T(8,128)(2,1)S(1)}, u32[]{:S(2)}, u32[]{:S(2)}) collective-permute-start(bf16[256,384]{1,0:T(8,128)(2,1)S(1)} %get-tuple-element.28.refs_0_.asks0), channel_id=1, source_target_pairs={{0,4},{4,0},{8,12},{12,8},{1,5},{5,1},{9,13},{13,9},{2,6},{6,2},{1... | collective-permute-start | bytes 589832 | tf_op jit(solution)/shard_map/ppermute | solution.py:341
  17.4 0.0 collective-permute-done.10.refs_2_.first
  17.4 0.0 collective-permute-start.12
  17.4 0.0 collective-permute-done.8.second
  17.4 0.5 %collective-permute-start.9 = (bf16[256,384]{1,0:T(8,128)(2,1)S(1)}, bf16[256,384]{1,0:T(8,128)(2,1)S(1)}, u32[]{:S(2)}, u32[]{:S(2)}) collective-permute-start(bf16[256,384]{1,0:T(8,128)(2,1)S(1)} %collective-permute-done.8.second), channel_id=1, source_target_pairs={{0,1},{1,0},{4,8},{5,9},{8,4},{9,5},{12,13},{13,12},{2,3},{3,2},{6... | collective-permute-start | bytes 589832 | tf_op jit(solution)/shard_map/ppermute | solution.py:344
  17.9 1.4 %collective-permute-done.13.refs_3_.part1 = bf16[256,256]{1,0:T(8,128)(2,1)S(1)} collective-permute-done((bf16[256,256]{1,0:T(8,128)(2,1)S(1)}, bf16[256,256]{1,0:T(8,128)(2,1)S(1)}, u32[]{:S(2)}, u32[]{:S(2)}) %collective-permute-start.13) | collective-permute-done | bytes 131104 | tf_op jit(solution)/shard_map/ppermute | solution.py:341
  19.3 0.0 collective-permute-start.14
  19.3 0.0 collective-permute-done.2.refs_4_.refs_3_
  19.3 2.5 %collective-permute-start.1 = (bf16[256,128]{1,0:T(8,128)(2,1)S(1)}, bf16[256,128]{1,0:T(8,128)(2,1)S(1)}, u32[]{:S(2)}, u32[]{:S(2)}) collective-permute-start(bf16[256,128]{1,0:T(8,128)(2,1)S(1)} %slice_select_fusion.1), channel_id=1, source_target_pairs={{0,4},{4,0},{8,12},{12,8},{1,5},{5,1},{9,13},{13,9},{2,6},{6,2},{1... | collective-permute-start | bytes 196616 | tf_op jit(solution)/shard_map/ppermute | solution.py:341
  21.8 0.5 %collective-permute-done.5.refs_0_.asks0 = bf16[256,384]{1,0:T(8,128)(2,1)S(1)} collective-permute-done((bf16[256,384]{1,0:T(8,128)(2,1)S(1)}, bf16[256,384]{1,0:T(8,128)(2,1)S(1)}, u32[]{:S(2)}, u32[]{:S(2)}) %collective-permute-start.5) | collective-permute-done | bytes 196640 | tf_op jit(solution)/shard_map/ppermute | solution.py:341
  22.4 0.0 collective-permute-start.3
  22.4 0.0 collective-permute-done.12.refs_5_
  22.4 3.5 %collective-permute-start.6 = (bf16[128,384]{1,0:T(8,128)(2,1)S(1)}, bf16[128,384]{1,0:T(8,128)(2,1)S(1)}, u32[]{:S(2)}, u32[]{:S(2)}) collective-permute-start(bf16[128,384]{1,0:T(8,128)(2,1)S(1)} %get-tuple-element.29.refs_1_.asks1), channel_id=1, source_target_pairs={{0,4},{4,0},{8,12},{12,8},{1,5},{5,1},{9,13},{13,9},{2,6},{6,2},{1... | collective-permute-start | bytes 294920 | tf_op jit(solution)/shard_map/ppermute | solution.py:341
  25.8 0.0 collective-permute-done.1.refs_3_.part2
  25.8 0.9 %collective-permute-start.17 = (bf16[192,384]{1,0:T(8,128)(2,1)S(1)}, bf16[192,384]{1,0:T(8,128)(2,1)S(1)}, u32[]{:S(2)}, u32[]{:S(2)}) collective-permute-start(bf16[192,384]{1,0:T(8,128)(2,1)S(1)} %shard_map.121), channel_id=1, source_target_pairs={{0,4},{4,0},{8,12},{12,8},{1,5},{5,1},{9,13},{13,9},{2,6},{6,2},{1... | collective-permute-start | bytes 442376 | tf_op jit(solution)/shard_map/ppermute | solution.py:341
  26.7 0.0 collective-permute-done.9.far
  26.7 0.0 collective-permute-start.4
  26.7 0.0 collective-permute-done.3.refs_5_
  26.7 7.4 %collective-permute-start.15 = (bf16[64,768]{1,0:T(8,128)(2,1)S(1)}, bf16[64,768]{1,0:T(8,128)(2,1)S(1)}, u32[]{:S(2)}, u32[]{:S(2)}) collective-permute-start(bf16[64,768]{1,0:T(8,128)(2,1)S(1)} %shard_map.118), channel_id=1, source_target_pairs={{0,4},{4,0},{8,12},{12,8},{1,5},{5,1},{9,13},{13,9},{2,6},{6,2},{1... | collective-permute-start | bytes 294920 | tf_op jit(solution)/shard_map/ppermute | solution.py:341
  34.1 0.0 collective-permute-done.6.refs_1_
  34.1 0.0 collective-permute-done.14.refs_6_
  34.1 0.7 %collective-permute-start.16 = (bf16[192,256]{1,0:T(8,128)(2,1)S(1)}, bf16[192,256]{1,0:T(8,128)(2,1)S(1)}, u32[]{:S(2)}, u32[]{:S(2)}) collective-permute-start(bf16[192,256]{1,0:T(8,128)(2,1)S(1)} %shard_map.119), channel_id=1, source_target_pairs={{0,4},{4,0},{8,12},{12,8},{1,5},{5,1},{9,13},{13,9},{2,6},{6,2},{1... | collective-permute-start | bytes 294920 | tf_op jit(solution)/shard_map/ppermute | solution.py:341
  34.9 0.0 collective-permute-done.4.refs_6_
  34.9 1.9 %collective-permute-start.7 = (bf16[192,128]{1,0:T(8,128)(2,1)S(1)}, bf16[192,128]{1,0:T(8,128)(2,1)S(1)}, u32[]{:S(2)}, u32[]{:S(2)}) collective-permute-start(bf16[192,128]{1,0:T(8,128)(2,1)S(1)} %shard_map.114), channel_id=1, source_target_pairs={{0,4},{4,0},{8,12},{12,8},{1,5},{5,1},{9,13},{13,9},{2,6},{6,2},{1... | collective-permute-start | bytes 147464 | tf_op jit(solution)/shard_map/ppermute | solution.py:341
  36.7 0.6 %shard_map.120.cross = bf16[128,768]{1,0:T(8,128)(2,1)S(1)} custom-call(s32[1]{0:T(128)} %bitcast.me_ref, f32[192,256]{1,0:T(8,128)S(1)} %get-tuple-element.34.near_ref, bf16[256,384]{1,0:T(8,128)(2,1)S(1)} %get-tuple-element.28.refs_0_.asks0, bf16[128,384]{1,0:T(8,128)(2,1)S(1)} %get-tuple-element.29.refs_1_.asks1, ...), custom_call_target="tpu_custom_call" | custom-call | flops 150994944 | bytes 589824 | tf_op jit(solution)/shard_map/pallas_call | solution.py:347
  37.4 0.0 collective-permute-done.17.back0
  37.4 0.7 %shard_map.122 = (bf16[128,768]{1,0:T(8,128)(2,1)}, bf16[128,768]{1,0:T(8,128)(2,1)}, bf16[64,768]{1,0:T(8,128)(2,1)}, bf16[64,768]{1,0:T(8,128)(2,1)}) custom-call(s32[1]{0:T(128)} %bitcast.me_ref, bf16[128,768]{1,0:T(8,128)(2,1)S(1)} %shard_map.120.cross, bf16[192,384]{1,0:T(8,128)(2,1)S(1)} %collective-permute-done.17.back0), custom_call_target="tpu_custom_call" | custom-call | tf_op jit(solution)/shard_map/pallas_call | solution.py:347
  38.1 0.0 collective-permute-done.15.back_sound
  38.2 0.6 %collective-permute-done.16.back1 = bf16[192,256]{1,0:T(8,128)(2,1)S(1)} collective-permute-done((bf16[192,256]{1,0:T(8,128)(2,1)S(1)}, bf16[192,256]{1,0:T(8,128)(2,1)S(1)}, u32[]{:S(2)}, u32[]{:S(2)}) %collective-permute-start.16) | collective-permute-done | bytes 98336 | tf_op jit(solution)/shard_map/ppermute | solution.py:341
  38.7 0.7 %shard_map.123 = (bf16[128,768]{1,0:T(8,128)(2,1)}, bf16[128,768]{1,0:T(8,128)(2,1)}, bf16[64,768]{1,0:T(8,128)(2,1)}, bf16[64,768]{1,0:T(8,128)(2,1)}) custom-call(s32[1]{0:T(128)} %bitcast.me_ref, bf16[128,768]{1,0:T(8,128)(2,1)S(1)} %get-tuple-element.36.own_cross, ...), custom_call_target="tpu_custom_call", output_to_operand_aliasing={{0}: (7, {}), {1}: (8, {}), {2}: (9, {}), {3}: (10, {})} | custom-call | tf_op jit(solution)/shard_map/pallas_call | solution.py:347
  39.5 0.0 collective-permute-done.7.back
  39.5 0.6 %shard_map.124 = (bf16[128,768]{1,0:T(8,128)(2,1)}, bf16[64,768]{1,0:T(8,128)(2,1)}) custom-call(s32[1]{0:T(128)} %bitcast.me_ref, bf16[192,128]{1,0:T(8,128)(2,1)S(1)} %shard_map.113.own, bf16[192,128]{1,0:T(8,128)(2,1)S(1)} %collective-permute-done.7.back, ...), custom_call_target="tpu_custom_call", output_to_operand_aliasing={{0}: (3, {}), {1}: (4, {})} | custom-call | tf_op jit(solution)/shard_map/pallas_call | solution.py:347
  (10 shorter events, 0.1 us)
Async XLA Ops:
  1.8 7.3 %collective-permute-start = (bf16[256,384]{1,0:T(8,128)(2,1)S(1)}, bf16[256,384]{1,0:T(8,128)(2,1)S(1)}, u32[]{:S(2)}, u32[]{:S(2)}) collective-permute-start(bf16[256,384]{1,0:T(8,128)(2,1)S(1)} %get-tuple-element.31.out), channel_id=1, source_target_pairs={{0,1},{1,0},{4,8},{5,9},{8,4},{9,5},{12,13},{13,12},{2,3},{3,2},{6... | collective-permute-start | bytes 589832 | tf_op jit(solution)/shard_map/ppermute | solution.py:344
  2.3 15.1 %collective-permute-start.10 = (bf16[256,384]{1,0:T(8,128)(2,1)S(1)}, bf16[256,384]{1,0:T(8,128)(2,1)S(1)}, u32[]{:S(2)}, u32[]{:S(2)}) collective-permute-start(bf16[256,384]{1,0:T(8,128)(2,1)S(1)} %get-tuple-element.31.out), channel_id=1, source_target_pairs={{0,4},{4,0},{8,12},{12,8},{1,5},{5,1},{9,13},{13,9},{2,6},{6,2},{1... | collective-permute-start | bytes 589832 | tf_op jit(solution)/shard_map/ppermute | solution.py:341
  6.5 10.9 %collective-permute-start.8 = (bf16[256,384]{1,0:T(8,128)(2,1)S(1)}, bf16[256,384]{1,0:T(8,128)(2,1)S(1)}, u32[]{:S(2)}, u32[]{:S(2)}) collective-permute-start(bf16[256,384]{1,0:T(8,128)(2,1)S(1)} %get-tuple-element.35.refs_1_.over), channel_id=1, source_target_pairs={{0,4},{4,0},{8,12},{12,8},{1,5},{5,1},{9,13},{13,9},{2,6},{6,2},{1... | collective-permute-start | bytes 589832 | tf_op jit(solution)/shard_map/ppermute | solution.py:341
  6.5 0.7 %copy-start = (s32[256]{0:T(256)S(1)}, s32[256]{0:T(256)}, u32[]{:S(2)}) copy-start(s32[256]{0:T(256)} %param.14) | copy-start | bytes 3076
  6.5 0.7 %copy-start.1 = (s32[4]{0:T(128)S(1)}, s32[4]{0:T(128)}, u32[]{:S(2)}) copy-start(s32[4]{0:T(128)} %count_ref.1) | copy-start | bytes 52
  9.1 2.5 %copy-start.2 = (bf16[128,768]{1,0:T(8,128)(2,1)S(1)}, bf16[128,768]{1,0:T(8,128)(2,1)}, u32[]{:S(2)}) copy-start(bf16[128,768]{1,0:T(8,128)(2,1)} %video_k.3) | copy-start | bytes 589828
  9.2 10.1 %collective-permute-start.13 = (bf16[256,256]{1,0:T(8,128)(2,1)S(1)}, bf16[256,256]{1,0:T(8,128)(2,1)S(1)}, u32[]{:S(2)}, u32[]{:S(2)}) collective-permute-start(bf16[256,256]{1,0:T(8,128)(2,1)S(1)} %slice_select_fusion), channel_id=1, source_target_pairs={{0,4},{4,0},{8,12},{12,8},{1,5},{5,1},{9,13},{13,9},{2,6},{6,2},{1... | collective-permute-start | bytes 393224 | tf_op jit(solution)/shard_map/ppermute | solution.py:341
  11.7 1.3 %collective-permute-start.11 = (bf16[128,384]{1,0:T(8,128)(2,1)S(1)}, bf16[128,384]{1,0:T(8,128)(2,1)S(1)}, u32[]{:S(2)}, u32[]{:S(2)}) collective-permute-start(bf16[128,384]{1,0:T(8,128)(2,1)S(1)} %get-tuple-element.38), channel_id=1, source_target_pairs={{0,1},{1,0},{4,8},{5,9},{8,4},{9,5},{12,13},{13,12},{2,3},{3,2},{6... | collective-permute-start | bytes 294920 | tf_op jit(solution)/shard_map/ppermute | solution.py:344
  11.7 7.6 %collective-permute-start.2 = (bf16[128,768]{1,0:T(8,128)(2,1)S(1)}, bf16[128,768]{1,0:T(8,128)(2,1)S(1)}, u32[]{:S(2)}, u32[]{:S(2)}) collective-permute-start(bf16[128,768]{1,0:T(8,128)(2,1)S(1)} %copy-done.2), channel_id=1, source_target_pairs={{0,1},{1,0},{4,8},{5,9},{8,4},{9,5},{12,13},{13,12},{2,3},{3,2},{6... | collective-permute-start | bytes 589832 | tf_op jit(solution)/shard_map/ppermute | solution.py:344
  13.0 9.4 %collective-permute-start.5 = (bf16[256,384]{1,0:T(8,128)(2,1)S(1)}, bf16[256,384]{1,0:T(8,128)(2,1)S(1)}, u32[]{:S(2)}, u32[]{:S(2)}) collective-permute-start(bf16[256,384]{1,0:T(8,128)(2,1)S(1)} %get-tuple-element.28.refs_0_.asks0), channel_id=1, source_target_pairs={{0,4},{4,0},{8,12},{12,8},{1,5},{5,1},{9,13},{13,9},{2,6},{6,2},{1... | collective-permute-start | bytes 589832 | tf_op jit(solution)/shard_map/ppermute | solution.py:341
  17.4 5.0 %collective-permute-start.12 = (bf16[256,384]{1,0:T(8,128)(2,1)S(1)}, bf16[256,384]{1,0:T(8,128)(2,1)S(1)}, u32[]{:S(2)}, u32[]{:S(2)}) collective-permute-start(bf16[256,384]{1,0:T(8,128)(2,1)S(1)} %collective-permute-done.10.refs_2_.first), channel_id=1, source_target_pairs={{0,1},{1,0},{4,8},{5,9},{8,4},{9,5},{12,13},{13,12},{2,3},{3,2},{6... | collective-permute-start | bytes 589832 | tf_op jit(solution)/shard_map/ppermute | solution.py:344
  17.4 9.3 %collective-permute-start.9 = (bf16[256,384]{1,0:T(8,128)(2,1)S(1)}, bf16[256,384]{1,0:T(8,128)(2,1)S(1)}, u32[]{:S(2)}, u32[]{:S(2)}) collective-permute-start(bf16[256,384]{1,0:T(8,128)(2,1)S(1)} %collective-permute-done.8.second), channel_id=1, source_target_pairs={{0,1},{1,0},{4,8},{5,9},{8,4},{9,5},{12,13},{13,12},{2,3},{3,2},{6... | collective-permute-start | bytes 589832 | tf_op jit(solution)/shard_map/ppermute | solution.py:344
  19.3 14.8 %collective-permute-start.14 = (bf16[256,256]{1,0:T(8,128)(2,1)S(1)}, bf16[256,256]{1,0:T(8,128)(2,1)S(1)}, u32[]{:S(2)}, u32[]{:S(2)}) collective-permute-start(bf16[256,256]{1,0:T(8,128)(2,1)S(1)} %collective-permute-done.13.refs_3_.part1), channel_id=1, source_target_pairs={{0,1},{1,0},{4,8},{5,9},{8,4},{9,5},{12,13},{13,12},{2,3},{3,2},{6... | collective-permute-start | bytes 393224 | tf_op jit(solution)/shard_map/ppermute | solution.py:344
  19.3 6.5 %collective-permute-start.1 = (bf16[256,128]{1,0:T(8,128)(2,1)S(1)}, bf16[256,128]{1,0:T(8,128)(2,1)S(1)}, u32[]{:S(2)}, u32[]{:S(2)}) collective-permute-start(bf16[256,128]{1,0:T(8,128)(2,1)S(1)} %slice_select_fusion.1), channel_id=1, source_target_pairs={{0,4},{4,0},{8,12},{12,8},{1,5},{5,1},{9,13},{13,9},{2,6},{6,2},{1... | collective-permute-start | bytes 196616 | tf_op jit(solution)/shard_map/ppermute | solution.py:341
  22.4 4.4 %collective-permute-start.3 = (bf16[128,384]{1,0:T(8,128)(2,1)S(1)}, bf16[128,384]{1,0:T(8,128)(2,1)S(1)}, u32[]{:S(2)}, u32[]{:S(2)}) collective-permute-start(bf16[128,384]{1,0:T(8,128)(2,1)S(1)} %get-tuple-element.32), channel_id=1, source_target_pairs={{0,1},{1,0},{4,8},{5,9},{8,4},{9,5},{12,13},{13,12},{2,3},{3,2},{6... | collective-permute-start | bytes 294920 | tf_op jit(solution)/shard_map/ppermute | solution.py:344
  22.4 11.8 %collective-permute-start.6 = (bf16[128,384]{1,0:T(8,128)(2,1)S(1)}, bf16[128,384]{1,0:T(8,128)(2,1)S(1)}, u32[]{:S(2)}, u32[]{:S(2)}) collective-permute-start(bf16[128,384]{1,0:T(8,128)(2,1)S(1)} %get-tuple-element.29.refs_1_.asks1), channel_id=1, source_target_pairs={{0,4},{4,0},{8,12},{12,8},{1,5},{5,1},{9,13},{13,9},{2,6},{6,2},{1... | collective-permute-start | bytes 294920 | tf_op jit(solution)/shard_map/ppermute | solution.py:341
  25.8 11.5 %collective-permute-start.17 = (bf16[192,384]{1,0:T(8,128)(2,1)S(1)}, bf16[192,384]{1,0:T(8,128)(2,1)S(1)}, u32[]{:S(2)}, u32[]{:S(2)}) collective-permute-start(bf16[192,384]{1,0:T(8,128)(2,1)S(1)} %shard_map.121), channel_id=1, source_target_pairs={{0,4},{4,0},{8,12},{12,8},{1,5},{5,1},{9,13},{13,9},{2,6},{6,2},{1... | collective-permute-start | bytes 442376 | tf_op jit(solution)/shard_map/ppermute | solution.py:341
  26.7 8.2 %collective-permute-start.4 = (bf16[256,128]{1,0:T(8,128)(2,1)S(1)}, bf16[256,128]{1,0:T(8,128)(2,1)S(1)}, u32[]{:S(2)}, u32[]{:S(2)}) collective-permute-start(bf16[256,128]{1,0:T(8,128)(2,1)S(1)} %collective-permute-done.1.refs_3_.part2), channel_id=1, source_target_pairs={{0,1},{1,0},{4,8},{5,9},{8,4},{9,5},{12,13},{13,12},{2,3},{3,2},{6... | collective-permute-start | bytes 196616 | tf_op jit(solution)/shard_map/ppermute | solution.py:344
  26.7 11.4 %collective-permute-start.15 = (bf16[64,768]{1,0:T(8,128)(2,1)S(1)}, bf16[64,768]{1,0:T(8,128)(2,1)S(1)}, u32[]{:S(2)}, u32[]{:S(2)}) collective-permute-start(bf16[64,768]{1,0:T(8,128)(2,1)S(1)} %shard_map.118), channel_id=1, source_target_pairs={{0,4},{4,0},{8,12},{12,8},{1,5},{5,1},{9,13},{13,9},{2,6},{6,2},{1... | collective-permute-start | bytes 294920 | tf_op jit(solution)/shard_map/ppermute | solution.py:341
  34.1 4.6 %collective-permute-start.16 = (bf16[192,256]{1,0:T(8,128)(2,1)S(1)}, bf16[192,256]{1,0:T(8,128)(2,1)S(1)}, u32[]{:S(2)}, u32[]{:S(2)}) collective-permute-start(bf16[192,256]{1,0:T(8,128)(2,1)S(1)} %shard_map.119), channel_id=1, source_target_pairs={{0,4},{4,0},{8,12},{12,8},{1,5},{5,1},{9,13},{13,9},{2,6},{6,2},{1... | collective-permute-start | bytes 294920 | tf_op jit(solution)/shard_map/ppermute | solution.py:341
  34.9 4.6 %collective-permute-start.7 = (bf16[192,128]{1,0:T(8,128)(2,1)S(1)}, bf16[192,128]{1,0:T(8,128)(2,1)S(1)}, u32[]{:S(2)}, u32[]{:S(2)}) collective-permute-start(bf16[192,128]{1,0:T(8,128)(2,1)S(1)} %shard_map.114), channel_id=1, source_target_pairs={{0,4},{4,0},{8,12},{12,8},{1,5},{5,1},{9,13},{13,9},{2,6},{6,2},{1... | collective-permute-start | bytes 147464 | tf_op jit(solution)/shard_map/ppermute | solution.py:341

commit v14 on v13

--- a/solution.py
+++ b/solution.py
@@ -271,18 +271,16 @@
     return moves
 
 
-def place_end_kernel(n, me_ref, cross, back0, video_self, video_cross, audio_self, audio_cross, sem):
+def place_end_kernel(n, me_ref, cross, video_self, video_cross, audio_self, audio_cross, sem):
     @pl.when((me_ref[0] == 0) | (me_ref[0] == n - 1))
     def _():
-        moves = [(cross, video_cross)]
-        moves += place_pieces((back0,), 0, cross.shape[0], video_self, audio_cross)
-        for copy in move_all(moves, sem):
+        for copy in move_all([(cross, video_cross)], sem):
             copy.wait()
 
 
-def place_kernel(n, me_ref, own_cross, own_sound, own0, own1, back_sound, back1, *refs):
+def place_kernel(n, me_ref, own_cross, own_sound, own0, own1, back_sound, back0, back1, *refs):
     video_self, video_cross, audio_self, audio_cross, sem = refs[4:]
-    video_rows, first = own_cross.shape[0], own0.shape[1]
+    video_rows = own_cross.shape[0]
     at_end = (me_ref[0] == 0) | (me_ref[0] == n - 1)
 
     @pl.when(jnp.logical_not(at_end))
@@ -295,7 +293,7 @@
     @pl.when(at_end)
     def _():
         moves = [(back_sound, audio_self)]
-        moves += place_pieces((back1,), first, video_rows, video_self, audio_cross)
+        moves += place_pieces((back0, back1), 0, video_rows, video_self, audio_cross)
         for copy in move_all(moves, sem):
             copy.wait()
 
@@ -484,27 +482,26 @@
     begun = call(
         functools.partial(place_end_kernel, n),
         shapes,
-        [SMEM] + [VMEM] * 2,
+        [SMEM, VMEM],
         place,
         end_cross,
-        back[0],
         out_specs=(HBM,) * 4,
-        scratch_shapes=[pltpu.SemaphoreType.DMA((3,))],
+        scratch_shapes=[pltpu.SemaphoreType.DMA((1,))],
     )
     video_self, video_cross, audio_self, audio_cross = call(
         functools.partial(place_kernel, n),
         shapes,
-        [SMEM] + [VMEM] * 6 + [HBM] * 4,
+        [SMEM] + [VMEM] * 7 + [HBM] * 4,
         place,
         own_cross,
         own,
         *mine[:2],
         back_sound,
-        back[1],
+        *back[:2],
         *begun,
         out_specs=(HBM,) * 4,
         scratch_shapes=[pltpu.SemaphoreType.DMA((6,))],
-        input_output_aliases={7: 0, 8: 1, 9: 2, 10: 3},
+        input_output_aliases={8: 0, 9: 1, 10: 2, 11: 3},
     )
     video_self, audio_cross = call(
         functools.partial(place_last_kernel, n, width - chunks[2] * HEAD_DIM),

time: 40.3 us -> 40.4 us (level)
  no operation moved by 1% of the time
where the time goes in v14:
time: 40.4 us; the launch traced here: 40.2 us
  starting transfers between devices  29.6 us (73%)
  Pallas kernels  5.78 us (14%)
  waiting for transfers between devices  3.32 us (8%)
  between operations  0.78 us (2%)
  local copies, waits for them, and re-layouts  0.69 us (2%)
    ppermute x10, starting transfers between devices, mate(): return lax.ppermute(block, 'seq', mate_pairs)  28 us
    pallas_call x14, Pallas kernels, call(): pl.pallas_call(kernel, out_shape=tuple((jax.ShapeDtypeStruct(shape, dtype...  5.78 us
    ppermute x10, waiting for transfers between devices, mate(): return lax.ppermute(block, 'seq', mate_pairs)  2.51 us
    ppermute x8, starting transfers between devices, cross(): return lax.ppermute(block, ('seq', 'mp'), cross_pairs)  1.58 us
  transfers between devices with their start and end apart: 18, of which 4 were waited for; matrix products, arithmetic and copies ran while one was open for 0% of the time, Pallas kernels for 10%

profile of v14, /device:TPU:0, one launch (start us, length us, event | category | flops | bytes accessed | tf_op | source)
XLA Modules:
  0.0 40.2 jit_solution(2092294665512946531)
XLA Ops:
  0.6 1.1 %shard_map.112 = (bf16[256,384]{1,0:T(8,128)(2,1)S(1)}, bf16[256,384]{1,0:T(8,128)(2,1)S(1)}, bf16[128,384]{1,0:T(8,128)(2,1)S(1)}) custom-call(s32[1]{0:T(128)} %bitcast.me_ref, bf16[128,768]{1,0:T(8,128)(2,1)} %video_k.3, bf16[128,768]{1,0:T(8,128)(2,1)} %video_v.3, bf16[64,768]{1,0:T(8,128)(2,1)} %audio_k.1, bf16[64,768]{1,0:T(8,128)(2,1)} %audio_v.1), custom_call_target="tpu_custom_call" | custom-call | tf_op jit(solution)/shard_map/pallas_call | solution.py:345
  1.8 0.6 %collective-permute-start = (bf16[256,384]{1,0:T(8,128)(2,1)S(1)}, bf16[256,384]{1,0:T(8,128)(2,1)S(1)}, u32[]{:S(2)}, u32[]{:S(2)}) collective-permute-start(bf16[256,384]{1,0:T(8,128)(2,1)S(1)} %get-tuple-element.31.out), channel_id=1, source_target_pairs={{0,1},{1,0},{4,8},{5,9},{8,4},{9,5},{12,13},{13,12},{2,3},{3,2},{6... | collective-permute-start | bytes 589832 | tf_op jit(solution)/shard_map/ppermute | solution.py:342
  2.3 4.1 %collective-permute-start.10 = (bf16[256,384]{1,0:T(8,128)(2,1)S(1)}, bf16[256,384]{1,0:T(8,128)(2,1)S(1)}, u32[]{:S(2)}, u32[]{:S(2)}) collective-permute-start(bf16[256,384]{1,0:T(8,128)(2,1)S(1)} %get-tuple-element.31.out), channel_id=1, source_target_pairs={{0,4},{4,0},{8,12},{12,8},{1,5},{5,1},{9,13},{13,9},{2,6},{6,2},{1... | collective-permute-start | bytes 589832 | tf_op jit(solution)/shard_map/ppermute | solution.py:339
  6.5 0.0 collective-permute-start.8
  6.5 0.0 copy-start
  6.5 0.0 copy-start.1
  6.5 0.7 %copy-done = s32[256]{0:T(256)S(1)} copy-done((s32[256]{0:T(256)S(1)}, s32[256]{0:T(256)}, u32[]{:S(2)}) %copy-start) | copy-done | bytes 1048
  7.2 0.0 copy-done.1
  7.2 1.9 %shard_map.111 = (bf16[256,256]{1,0:T(8,128)(2,1)S(1)}, bf16[256,128]{1,0:T(8,128)(2,1)S(1)}, bf16[256,384]{1,0:T(8,128)(2,1)S(1)}, bf16[128,384]{1,0:T(8,128)(2...) custom-call(s32[1]{0:T(128)} %bitcast.me_ref, ...), custom_call_target="tpu_custom_call" | custom-call | tf_op jit(solution)/shard_map/pallas_call | solution.py:345
  9.1 0.0 collective-permute-done.across
  9.1 0.0 copy-start.2
  9.2 2.5 %collective-permute-start.13 = (bf16[256,256]{1,0:T(8,128)(2,1)S(1)}, bf16[256,256]{1,0:T(8,128)(2,1)S(1)}, u32[]{:S(2)}, u32[]{:S(2)}) collective-permute-start(bf16[256,256]{1,0:T(8,128)(2,1)S(1)} %slice_select_fusion), channel_id=1, source_target_pairs={{0,4},{4,0},{8,12},{12,8},{1,5},{5,1},{9,13},{13,9},{2,6},{6,2},{1... | collective-permute-start | bytes 393224 | tf_op jit(solution)/shard_map/ppermute | solution.py:339
  11.7 0.0 collective-permute-start.11
  11.7 0.0 copy-done.2
  11.7 0.5 %collective-permute-start.2 = (bf16[128,768]{1,0:T(8,128)(2,1)S(1)}, bf16[128,768]{1,0:T(8,128)(2,1)S(1)}, u32[]{:S(2)}, u32[]{:S(2)}) collective-permute-start(bf16[128,768]{1,0:T(8,128)(2,1)S(1)} %copy-done.2), channel_id=1, source_target_pairs={{0,1},{1,0},{4,8},{5,9},{8,4},{9,5},{12,13},{13,12},{2,3},{3,2},{6... | collective-permute-start | bytes 589832 | tf_op jit(solution)/shard_map/ppermute | solution.py:342
  12.2 0.8 %collective-permute-done.11.refs_4_ = bf16[128,384]{1,0:T(8,128)(2,1)S(1)} collective-permute-done((bf16[128,384]{1,0:T(8,128)(2,1)S(1)}, bf16[128,384]{1,0:T(8,128)(2,1)S(1)}, u32[]{:S(2)}, u32[]{:S(2)}) %collective-permute-start.11) | collective-permute-done | bytes 98336 | tf_op jit(solution)/shard_map/ppermute | solution.py:342
  13.0 4.4 %collective-permute-start.5 = (bf16[256,384]{1,0:T(8,128)(2,1)S(1)}, bf16[256,384]{1,0:T(8,128)(2,1)S(1)}, u32[]{:S(2)}, u32[]{:S(2)}) collective-permute-start(bf16[256,384]{1,0:T(8,128)(2,1)S(1)} %get-tuple-element.28.refs_0_.asks0), channel_id=1, source_target_pairs={{0,4},{4,0},{8,12},{12,8},{1,5},{5,1},{9,13},{13,9},{2,6},{6,2},{1... | collective-permute-start | bytes 589832 | tf_op jit(solution)/shard_map/ppermute | solution.py:339
  17.4 0.0 collective-permute-done.10.refs_2_.first
  17.4 0.0 collective-permute-start.12
  17.4 0.0 collective-permute-done.8.second
  17.4 0.5 %collective-permute-start.9 = (bf16[256,384]{1,0:T(8,128)(2,1)S(1)}, bf16[256,384]{1,0:T(8,128)(2,1)S(1)}, u32[]{:S(2)}, u32[]{:S(2)}) collective-permute-start(bf16[256,384]{1,0:T(8,128)(2,1)S(1)} %collective-permute-done.8.second), channel_id=1, source_target_pairs={{0,1},{1,0},{4,8},{5,9},{8,4},{9,5},{12,13},{13,12},{2,3},{3,2},{6... | collective-permute-start | bytes 589832 | tf_op jit(solution)/shard_map/ppermute | solution.py:342
  17.9 1.4 %collective-permute-done.13.refs_3_.part1 = bf16[256,256]{1,0:T(8,128)(2,1)S(1)} collective-permute-done((bf16[256,256]{1,0:T(8,128)(2,1)S(1)}, bf16[256,256]{1,0:T(8,128)(2,1)S(1)}, u32[]{:S(2)}, u32[]{:S(2)}) %collective-permute-start.13) | collective-permute-done | bytes 131104 | tf_op jit(solution)/shard_map/ppermute | solution.py:339
  19.3 0.0 collective-permute-start.14
  19.3 0.0 collective-permute-done.2.refs_4_.refs_3_
  19.3 2.5 %collective-permute-start.1 = (bf16[256,128]{1,0:T(8,128)(2,1)S(1)}, bf16[256,128]{1,0:T(8,128)(2,1)S(1)}, u32[]{:S(2)}, u32[]{:S(2)}) collective-permute-start(bf16[256,128]{1,0:T(8,128)(2,1)S(1)} %slice_select_fusion.1), channel_id=1, source_target_pairs={{0,4},{4,0},{8,12},{12,8},{1,5},{5,1},{9,13},{13,9},{2,6},{6,2},{1... | collective-permute-start | bytes 196616 | tf_op jit(solution)/shard_map/ppermute | solution.py:339
  21.8 0.5 %collective-permute-done.5.refs_0_.asks0 = bf16[256,384]{1,0:T(8,128)(2,1)S(1)} collective-permute-done((bf16[256,384]{1,0:T(8,128)(2,1)S(1)}, bf16[256,384]{1,0:T(8,128)(2,1)S(1)}, u32[]{:S(2)}, u32[]{:S(2)}) %collective-permute-start.5) | collective-permute-done | bytes 196640 | tf_op jit(solution)/shard_map/ppermute | solution.py:339
  22.4 0.0 collective-permute-start.3
  22.4 0.0 collective-permute-done.12.refs_5_
  22.4 3.5 %collective-permute-start.6 = (bf16[128,384]{1,0:T(8,128)(2,1)S(1)}, bf16[128,384]{1,0:T(8,128)(2,1)S(1)}, u32[]{:S(2)}, u32[]{:S(2)}) collective-permute-start(bf16[128,384]{1,0:T(8,128)(2,1)S(1)} %get-tuple-element.29.refs_1_.asks1), channel_id=1, source_target_pairs={{0,4},{4,0},{8,12},{12,8},{1,5},{5,1},{9,13},{13,9},{2,6},{6,2},{1... | collective-permute-start | bytes 294920 | tf_op jit(solution)/shard_map/ppermute | solution.py:339
  25.8 0.0 collective-permute-done.1.refs_3_.part2
  25.8 0.9 %collective-permute-start.16 = (bf16[192,384]{1,0:T(8,128)(2,1)S(1)}, bf16[192,384]{1,0:T(8,128)(2,1)S(1)}, u32[]{:S(2)}, u32[]{:S(2)}) collective-permute-start(bf16[192,384]{1,0:T(8,128)(2,1)S(1)} %shard_map.119), channel_id=1, source_target_pairs={{0,4},{4,0},{8,12},{12,8},{1,5},{5,1},{9,13},{13,9},{2,6},{6,2},{1... | collective-permute-start | bytes 442376 | tf_op jit(solution)/shard_map/ppermute | solution.py:339
  26.7 0.0 collective-permute-done.9.far
  26.7 0.0 collective-permute-start.4
  26.7 0.0 collective-permute-done.3.refs_5_
  26.7 7.4 %collective-permute-start.15 = (bf16[64,768]{1,0:T(8,128)(2,1)S(1)}, bf16[64,768]{1,0:T(8,128)(2,1)S(1)}, u32[]{:S(2)}, u32[]{:S(2)}) collective-permute-start(bf16[64,768]{1,0:T(8,128)(2,1)S(1)} %shard_map.118), channel_id=1, source_target_pairs={{0,4},{4,0},{8,12},{12,8},{1,5},{5,1},{9,13},{13,9},{2,6},{6,2},{1... | collective-permute-start | bytes 294920 | tf_op jit(solution)/shard_map/ppermute | solution.py:339
  34.1 0.0 collective-permute-done.6.refs_1_
  34.1 0.0 collective-permute-done.14.refs_6_
  34.1 0.7 %collective-permute-start.17 = (bf16[192,256]{1,0:T(8,128)(2,1)S(1)}, bf16[192,256]{1,0:T(8,128)(2,1)S(1)}, u32[]{:S(2)}, u32[]{:S(2)}) collective-permute-start(bf16[192,256]{1,0:T(8,128)(2,1)S(1)} %shard_map.120), channel_id=1, source_target_pairs={{0,4},{4,0},{8,12},{12,8},{1,5},{5,1},{9,13},{13,9},{2,6},{6,2},{1... | collective-permute-start | bytes 294920 | tf_op jit(solution)/shard_map/ppermute | solution.py:339
  34.9 0.0 collective-permute-done.4.refs_6_
  34.9 1.9 %collective-permute-start.7 = (bf16[192,128]{1,0:T(8,128)(2,1)S(1)}, bf16[192,128]{1,0:T(8,128)(2,1)S(1)}, u32[]{:S(2)}, u32[]{:S(2)}) collective-permute-start(bf16[192,128]{1,0:T(8,128)(2,1)S(1)} %shard_map.114), channel_id=1, source_target_pairs={{0,4},{4,0},{8,12},{12,8},{1,5},{5,1},{9,13},{13,9},{2,6},{6,2},{1... | collective-permute-start | bytes 147464 | tf_op jit(solution)/shard_map/ppermute | solution.py:339
  36.7 0.6 %shard_map.121.cross = bf16[128,768]{1,0:T(8,128)(2,1)S(1)} custom-call(s32[1]{0:T(128)} %bitcast.me_ref, f32[192,256]{1,0:T(8,128)S(1)} %get-tuple-element.34.near_ref, bf16[256,384]{1,0:T(8,128)(2,1)S(1)} %get-tuple-element.28.refs_0_.asks0, bf16[128,384]{1,0:T(8,128)(2,1)S(1)} %get-tuple-element.29.refs_1_.asks1, ...), custom_call_target="tpu_custom_call" | custom-call | flops 150994944 | bytes 589824 | tf_op jit(solution)/shard_map/pallas_call | solution.py:345
  37.3 0.7 %shard_map.122 = (bf16[128,768]{1,0:T(8,128)(2,1)}, bf16[128,768]{1,0:T(8,128)(2,1)}, bf16[64,768]{1,0:T(8,128)(2,1)}, bf16[64,768]{1,0:T(8,128)(2,1)}) custom-call(s32[1]{0:T(128)} %bitcast.me_ref, bf16[128,768]{1,0:T(8,128)(2,1)S(1)} %shard_map.121.cross), custom_call_target="tpu_custom_call" | custom-call | tf_op jit(solution)/shard_map/pallas_call | solution.py:345
  38.1 0.0 collective-permute-done.15.back_sound
  38.1 0.0 collective-permute-done.16.back0
  38.1 0.6 %collective-permute-done.17.back1 = bf16[192,256]{1,0:T(8,128)(2,1)S(1)} collective-permute-done((bf16[192,256]{1,0:T(8,128)(2,1)S(1)}, bf16[192,256]{1,0:T(8,128)(2,1)S(1)}, u32[]{:S(2)}, u32[]{:S(2)}) %collective-permute-start.17) | collective-permute-done | bytes 98336 | tf_op jit(solution)/shard_map/ppermute | solution.py:339
  38.7 0.8 %shard_map.123 = (bf16[128,768]{1,0:T(8,128)(2,1)}, bf16[128,768]{1,0:T(8,128)(2,1)}, bf16[64,768]{1,0:T(8,128)(2,1)}, bf16[64,768]{1,0:T(8,128)(2,1)}) custom-call(s32[1]{0:T(128)} %bitcast.me_ref, bf16[128,768]{1,0:T(8,128)(2,1)S(1)} %get-tuple-element.36.own_cross, ...), custom_call_target="tpu_custom_call", output_to_operand_aliasing={{0}: (8, {}), {1}: (9, {}), {2}: (10, {}), {3}: (11, {})} | custom-call | tf_op jit(solution)/shard_map/pallas_call | solution.py:345
  39.5 0.0 collective-permute-done.7.back
  39.5 0.6 %shard_map.124 = (bf16[128,768]{1,0:T(8,128)(2,1)}, bf16[64,768]{1,0:T(8,128)(2,1)}) custom-call(s32[1]{0:T(128)} %bitcast.me_ref, bf16[192,128]{1,0:T(8,128)(2,1)S(1)} %shard_map.113.own, bf16[192,128]{1,0:T(8,128)(2,1)S(1)} %collective-permute-done.7.back, ...), custom_call_target="tpu_custom_call", output_to_operand_aliasing={{0}: (3, {}), {1}: (4, {})} | custom-call | tf_op jit(solution)/shard_map/pallas_call | solution.py:345
  (10 shorter events, 0.1 us)
Async XLA Ops:
  1.8 7.3 %collective-permute-start = (bf16[256,384]{1,0:T(8,128)(2,1)S(1)}, bf16[256,384]{1,0:T(8,128)(2,1)S(1)}, u32[]{:S(2)}, u32[]{:S(2)}) collective-permute-start(bf16[256,384]{1,0:T(8,128)(2,1)S(1)} %get-tuple-element.31.out), channel_id=1, source_target_pairs={{0,1},{1,0},{4,8},{5,9},{8,4},{9,5},{12,13},{13,12},{2,3},{3,2},{6... | collective-permute-start | bytes 589832 | tf_op jit(solution)/shard_map/ppermute | solution.py:342
  2.3 15.1 %collective-permute-start.10 = (bf16[256,384]{1,0:T(8,128)(2,1)S(1)}, bf16[256,384]{1,0:T(8,128)(2,1)S(1)}, u32[]{:S(2)}, u32[]{:S(2)}) collective-permute-start(bf16[256,384]{1,0:T(8,128)(2,1)S(1)} %get-tuple-element.31.out), channel_id=1, source_target_pairs={{0,4},{4,0},{8,12},{12,8},{1,5},{5,1},{9,13},{13,9},{2,6},{6,2},{1... | collective-permute-start | bytes 589832 | tf_op jit(solution)/shard_map/ppermute | solution.py:339
  6.5 10.9 %collective-permute-start.8 = (bf16[256,384]{1,0:T(8,128)(2,1)S(1)}, bf16[256,384]{1,0:T(8,128)(2,1)S(1)}, u32[]{:S(2)}, u32[]{:S(2)}) collective-permute-start(bf16[256,384]{1,0:T(8,128)(2,1)S(1)} %get-tuple-element.35.refs_1_.over), channel_id=1, source_target_pairs={{0,4},{4,0},{8,12},{12,8},{1,5},{5,1},{9,13},{13,9},{2,6},{6,2},{1... | collective-permute-start | bytes 589832 | tf_op jit(solution)/shard_map/ppermute | solution.py:339
  6.5 0.7 %copy-start = (s32[256]{0:T(256)S(1)}, s32[256]{0:T(256)}, u32[]{:S(2)}) copy-start(s32[256]{0:T(256)} %param.14) | copy-start | bytes 3076
  6.5 0.7 %copy-start.1 = (s32[4]{0:T(128)S(1)}, s32[4]{0:T(128)}, u32[]{:S(2)}) copy-start(s32[4]{0:T(128)} %count_ref.1) | copy-start | bytes 52
  9.1 2.5 %copy-start.2 = (bf16[128,768]{1,0:T(8,128)(2,1)S(1)}, bf16[128,768]{1,0:T(8,128)(2,1)}, u32[]{:S(2)}) copy-start(bf16[128,768]{1,0:T(8,128)(2,1)} %video_k.3) | copy-start | bytes 589828
  9.2 10.1 %collective-permute-start.13 = (bf16[256,256]{1,0:T(8,128)(2,1)S(1)}, bf16[256,256]{1,0:T(8,128)(2,1)S(1)}, u32[]{:S(2)}, u32[]{:S(2)}) collective-permute-start(bf16[256,256]{1,0:T(8,128)(2,1)S(1)} %slice_select_fusion), channel_id=1, source_target_pairs={{0,4},{4,0},{8,12},{12,8},{1,5},{5,1},{9,13},{13,9},{2,6},{6,2},{1... | collective-permute-start | bytes 393224 | tf_op jit(solution)/shard_map/ppermute | solution.py:339
  11.7 1.3 %collective-permute-start.11 = (bf16[128,384]{1,0:T(8,128)(2,1)S(1)}, bf16[128,384]{1,0:T(8,128)(2,1)S(1)}, u32[]{:S(2)}, u32[]{:S(2)}) collective-permute-start(bf16[128,384]{1,0:T(8,128)(2,1)S(1)} %get-tuple-element.38), channel_id=1, source_target_pairs={{0,1},{1,0},{4,8},{5,9},{8,4},{9,5},{12,13},{13,12},{2,3},{3,2},{6... | collective-permute-start | bytes 294920 | tf_op jit(solution)/shard_map/ppermute | solution.py:342
  11.7 7.6 %collective-permute-start.2 = (bf16[128,768]{1,0:T(8,128)(2,1)S(1)}, bf16[128,768]{1,0:T(8,128)(2,1)S(1)}, u32[]{:S(2)}, u32[]{:S(2)}) collective-permute-start(bf16[128,768]{1,0:T(8,128)(2,1)S(1)} %copy-done.2), channel_id=1, source_target_pairs={{0,1},{1,0},{4,8},{5,9},{8,4},{9,5},{12,13},{13,12},{2,3},{3,2},{6... | collective-permute-start | bytes 589832 | tf_op jit(solution)/shard_map/ppermute | solution.py:342
  13.0 9.4 %collective-permute-start.5 = (bf16[256,384]{1,0:T(8,128)(2,1)S(1)}, bf16[256,384]{1,0:T(8,128)(2,1)S(1)}, u32[]{:S(2)}, u32[]{:S(2)}) collective-permute-start(bf16[256,384]{1,0:T(8,128)(2,1)S(1)} %get-tuple-element.28.refs_0_.asks0), channel_id=1, source_target_pairs={{0,4},{4,0},{8,12},{12,8},{1,5},{5,1},{9,13},{13,9},{2,6},{6,2},{1... | collective-permute-start | bytes 589832 | tf_op jit(solution)/shard_map/ppermute | solution.py:339
  17.4 5.0 %collective-permute-start.12 = (bf16[256,384]{1,0:T(8,128)(2,1)S(1)}, bf16[256,384]{1,0:T(8,128)(2,1)S(1)}, u32[]{:S(2)}, u32[]{:S(2)}) collective-permute-start(bf16[256,384]{1,0:T(8,128)(2,1)S(1)} %collective-permute-done.10.refs_2_.first), channel_id=1, source_target_pairs={{0,1},{1,0},{4,8},{5,9},{8,4},{9,5},{12,13},{13,12},{2,3},{3,2},{6... | collective-permute-start | bytes 589832 | tf_op jit(solution)/shard_map/ppermute | solution.py:342
  17.4 9.3 %collective-permute-start.9 = (bf16[256,384]{1,0:T(8,128)(2,1)S(1)}, bf16[256,384]{1,0:T(8,128)(2,1)S(1)}, u32[]{:S(2)}, u32[]{:S(2)}) collective-permute-start(bf16[256,384]{1,0:T(8,128)(2,1)S(1)} %collective-permute-done.8.second), channel_id=1, source_target_pairs={{0,1},{1,0},{4,8},{5,9},{8,4},{9,5},{12,13},{13,12},{2,3},{3,2},{6... | collective-permute-start | bytes 589832 | tf_op jit(solution)/shard_map/ppermute | solution.py:342
  19.3 14.8 %collective-permute-start.14 = (bf16[256,256]{1,0:T(8,128)(2,1)S(1)}, bf16[256,256]{1,0:T(8,128)(2,1)S(1)}, u32[]{:S(2)}, u32[]{:S(2)}) collective-permute-start(bf16[256,256]{1,0:T(8,128)(2,1)S(1)} %collective-permute-done.13.refs_3_.part1), channel_id=1, source_target_pairs={{0,1},{1,0},{4,8},{5,9},{8,4},{9,5},{12,13},{13,12},{2,3},{3,2},{6... | collective-permute-start | bytes 393224 | tf_op jit(solution)/shard_map/ppermute | solution.py:342
  19.3 6.5 %collective-permute-start.1 = (bf16[256,128]{1,0:T(8,128)(2,1)S(1)}, bf16[256,128]{1,0:T(8,128)(2,1)S(1)}, u32[]{:S(2)}, u32[]{:S(2)}) collective-permute-start(bf16[256,128]{1,0:T(8,128)(2,1)S(1)} %slice_select_fusion.1), channel_id=1, source_target_pairs={{0,4},{4,0},{8,12},{12,8},{1,5},{5,1},{9,13},{13,9},{2,6},{6,2},{1... | collective-permute-start | bytes 196616 | tf_op jit(solution)/shard_map/ppermute | solution.py:339
  22.4 4.4 %collective-permute-start.3 = (bf16[128,384]{1,0:T(8,128)(2,1)S(1)}, bf16[128,384]{1,0:T(8,128)(2,1)S(1)}, u32[]{:S(2)}, u32[]{:S(2)}) collective-permute-start(bf16[128,384]{1,0:T(8,128)(2,1)S(1)} %get-tuple-element.32), channel_id=1, source_target_pairs={{0,1},{1,0},{4,8},{5,9},{8,4},{9,5},{12,13},{13,12},{2,3},{3,2},{6... | collective-permute-start | bytes 294920 | tf_op jit(solution)/shard_map/ppermute | solution.py:342
  22.4 11.8 %collective-permute-start.6 = (bf16[128,384]{1,0:T(8,128)(2,1)S(1)}, bf16[128,384]{1,0:T(8,128)(2,1)S(1)}, u32[]{:S(2)}, u32[]{:S(2)}) collective-permute-start(bf16[128,384]{1,0:T(8,128)(2,1)S(1)} %get-tuple-element.29.refs_1_.asks1), channel_id=1, source_target_pairs={{0,4},{4,0},{8,12},{12,8},{1,5},{5,1},{9,13},{13,9},{2,6},{6,2},{1... | collective-permute-start | bytes 294920 | tf_op jit(solution)/shard_map/ppermute | solution.py:339
  25.8 12.3 %collective-permute-start.16 = (bf16[192,384]{1,0:T(8,128)(2,1)S(1)}, bf16[192,384]{1,0:T(8,128)(2,1)S(1)}, u32[]{:S(2)}, u32[]{:S(2)}) collective-permute-start(bf16[192,384]{1,0:T(8,128)(2,1)S(1)} %shard_map.119), channel_id=1, source_target_pairs={{0,4},{4,0},{8,12},{12,8},{1,5},{5,1},{9,13},{13,9},{2,6},{6,2},{1... | collective-permute-start | bytes 442376 | tf_op jit(solution)/shard_map/ppermute | solution.py:339
  26.7 8.2 %collective-permute-start.4 = (bf16[256,128]{1,0:T(8,128)(2,1)S(1)}, bf16[256,128]{1,0:T(8,128)(2,1)S(1)}, u32[]{:S(2)}, u32[]{:S(2)}) collective-permute-start(bf16[256,128]{1,0:T(8,128)(2,1)S(1)} %collective-permute-done.1.refs_3_.part2), channel_id=1, source_target_pairs={{0,1},{1,0},{4,8},{5,9},{8,4},{9,5},{12,13},{13,12},{2,3},{3,2},{6... | collective-permute-start | bytes 196616 | tf_op jit(solution)/shard_map/ppermute | solution.py:342
  26.7 11.4 %collective-permute-start.15 = (bf16[64,768]{1,0:T(8,128)(2,1)S(1)}, bf16[64,768]{1,0:T(8,128)(2,1)S(1)}, u32[]{:S(2)}, u32[]{:S(2)}) collective-permute-start(bf16[64,768]{1,0:T(8,128)(2,1)S(1)} %shard_map.118), channel_id=1, source_target_pairs={{0,4},{4,0},{8,12},{12,8},{1,5},{5,1},{9,13},{13,9},{2,6},{6,2},{1... | collective-permute-start | bytes 294920 | tf_op jit(solution)/shard_map/ppermute | solution.py:339
  34.1 4.6 %collective-permute-start.17 = (bf16[192,256]{1,0:T(8,128)(2,1)S(1)}, bf16[192,256]{1,0:T(8,128)(2,1)S(1)}, u32[]{:S(2)}, u32[]{:S(2)}) collective-permute-start(bf16[192,256]{1,0:T(8,128)(2,1)S(1)} %shard_map.120), channel_id=1, source_target_pairs={{0,4},{4,0},{8,12},{12,8},{1,5},{5,1},{9,13},{13,9},{2,6},{6,2},{1... | collective-permute-start | bytes 294920 | tf_op jit(solution)/shard_map/ppermute | solution.py:339
  34.9 4.7 %collective-permute-start.7 = (bf16[192,128]{1,0:T(8,128)(2,1)S(1)}, bf16[192,128]{1,0:T(8,128)(2,1)S(1)}, u32[]{:S(2)}, u32[]{:S(2)}) collective-permute-start(bf16[192,128]{1,0:T(8,128)(2,1)S(1)} %shard_map.114), channel_id=1, source_target_pairs={{0,4},{4,0},{8,12},{12,8},{1,5},{5,1},{9,13},{13,9},{2,6},{6,2},{1... | collective-permute-start | bytes 147464 | tf_op jit(solution)/shard_map/ppermute | solution.py:339

commit v15 on v10

--- a/solution.py
+++ b/solution.py
@@ -397,12 +397,8 @@
     pieces = [(0, chunks[0], 0, 0)]
     sight_far = [cross(sight_mate[0])]
     for source in (1, 2):
-        for i in range(chunks[source]):
-            pieces.append((sum(chunks[:source]) + i, 1, source, i))
-            part = sight_mate[source]
-            if chunks[source] > 1:
-                part = part[:, i * HEAD_DIM : (i + 1) * HEAD_DIM]
-            sight_far.append(cross(part))
+        pieces.append((sum(chunks[:source]), chunks[source], source, 0))
+        sight_far.append(cross(sight_mate[source]))
     last = len(pieces) - 1
     asks_mate = [mate(asks[i]) for i in range(2)]
 
@@ -425,7 +421,8 @@
             cost_estimate=cost(rows, n * video_rows, size),
         )[0]
 
-    back = [mate(look(i, asks_mate, mask1)) for i in range(last + 1)]
+    results = [look(i, asks_mate, mask1) for i in range(last + 1)]
+    back = [mate(result) for result in results]
     mine = [look(i, asks, mask0) for i in range(last + 1)]
     theirs = call(
         functools.partial(audio_mate_kernel, n),
@@ -487,7 +484,7 @@
         scratch_shapes=[pltpu.SemaphoreType.DMA((2 + 2 * last,))],
     )
     video_self, audio_cross = call(
-        functools.partial(place_last_kernel, n, width - HEAD_DIM),
+        functools.partial(place_last_kernel, n, width - chunks[2] * HEAD_DIM),
         (video_shape, audio_shape),
         [SMEM] + [VMEM] * 2 + [HBM] * 2,
         place,

time: 45.3 us -> 39.8 us (0.88)
  starting transfers between devices: 31.2 us -> 21.9 us
  waiting for transfers between devices: 7.86 us -> 11.1 us
  local copies, waits for them, and re-layouts: 0.03 us -> 0.69 us
    ppermute x11 -> x10, starting transfers between devices: 29.4 us -> 20.3 us  [mate(): return lax.ppermute(block, 'seq', mate_pairs)]
    ppermute x11 -> x10, waiting for transfers between devices: 7.84 us -> 10.3 us  [mate(): return lax.ppermute(block, 'seq', mate_pairs)]
    ppermute x9 -> x8, waiting for transfers between devices: 0.02 us -> 0.81 us  [cross(): return lax.ppermute(block, ('seq', 'mp'), cross_pairs)]
    unnamed x6, local copies, waits for them, and re-layouts: 0.02 us -> 0.69 us
    ppermute x9 -> x8, starting transfers between devices: 1.79 us -> 1.58 us  [cross(): return lax.ppermute(block, ('seq', 'mp'), cross_pairs)]
    pallas_call x15 -> x13, Pallas kernels: 5.18 us -> 5.13 us  [call(): pl.pallas_call(kernel, out_shape=tuple((jax.ShapeDtypeStruct(shape, dtype...]
  transfers between devices with their start and end apart: 20 -> 18, of which waited for: 4 -> 7; matrix products, arithmetic and copies ran while one was open for 0% -> 0% of each run, Pallas kernels for 7% -> 8%
where the time goes in v15:
time: 39.8 us; the launch traced here: 39.6 us
  starting transfers between devices  21.9 us (55%)
  waiting for transfers between devices  11.1 us (28%)
  Pallas kernels  5.13 us (13%)
  between operations  0.75 us (2%)
  local copies, waits for them, and re-layouts  0.69 us (2%)
    ppermute x10, starting transfers between devices, mate(): return lax.ppermute(block, 'seq', mate_pairs)  20.3 us
    ppermute x10, waiting for transfers between devices, mate(): return lax.ppermute(block, 'seq', mate_pairs)  10.3 us
    pallas_call x13, Pallas kernels, call(): pl.pallas_call(kernel, out_shape=tuple((jax.ShapeDtypeStruct(shape, dtype...  5.13 us
    ppermute x8, starting transfers between devices, cross(): return lax.ppermute(block, ('seq', 'mp'), cross_pairs)  1.58 us
    ppermute x8, waiting for transfers between devices, cross(): return lax.ppermute(block, ('seq', 'mp'), cross_pairs)  0.81 us
  transfers between devices with their start and end apart: 18, of which 7 were waited for; matrix products, arithmetic and copies ran while one was open for 0% of the time, Pallas kernels for 8%

profile of v15, /device:TPU:0, one launch (start us, length us, event | category | flops | bytes accessed | tf_op | source)
XLA Modules:
  0.0 39.6 jit_solution(3438518632004480359)
XLA Ops:
  0.6 1.1 %shard_map.112 = (bf16[256,384]{1,0:T(8,128)(2,1)S(1)}, bf16[256,384]{1,0:T(8,128)(2,1)S(1)}, bf16[128,384]{1,0:T(8,128)(2,1)S(1)}) custom-call(s32[1]{0:T(128)} %bitcast.me_ref, bf16[128,768]{1,0:T(8,128)(2,1)} %video_k.3, bf16[128,768]{1,0:T(8,128)(2,1)} %video_v.3, bf16[64,768]{1,0:T(8,128)(2,1)} %audio_k.1, bf16[64,768]{1,0:T(8,128)(2,1)} %audio_v.1), custom_call_target="tpu_custom_call" | custom-call | tf_op jit(solution)/shard_map/pallas_call | solution.py:336
  1.8 0.6 %collective-permute-start = (bf16[256,384]{1,0:T(8,128)(2,1)S(1)}, bf16[256,384]{1,0:T(8,128)(2,1)S(1)}, u32[]{:S(2)}, u32[]{:S(2)}) collective-permute-start(bf16[256,384]{1,0:T(8,128)(2,1)S(1)} %get-tuple-element.27.out), channel_id=1, source_target_pairs={{0,1},{1,0},{4,8},{5,9},{8,4},{9,5},{12,13},{13,12},{2,3},{3,2},{6... | collective-permute-start | bytes 589832 | tf_op jit(solution)/shard_map/ppermute | solution.py:333
  2.3 4.1 %collective-permute-start.10 = (bf16[256,384]{1,0:T(8,128)(2,1)S(1)}, bf16[256,384]{1,0:T(8,128)(2,1)S(1)}, u32[]{:S(2)}, u32[]{:S(2)}) collective-permute-start(bf16[256,384]{1,0:T(8,128)(2,1)S(1)} %get-tuple-element.27.out), channel_id=1, source_target_pairs={{0,4},{4,0},{8,12},{12,8},{1,5},{5,1},{9,13},{13,9},{2,6},{6,2},{1... | collective-permute-start | bytes 589832 | tf_op jit(solution)/shard_map/ppermute | solution.py:330
  6.5 0.0 collective-permute-start.8
  6.5 0.0 copy-start
  6.5 0.0 copy-start.1
  6.5 0.7 %copy-done = s32[256]{0:T(256)S(1)} copy-done((s32[256]{0:T(256)S(1)}, s32[256]{0:T(256)}, u32[]{:S(2)}) %copy-start) | copy-done | bytes 1048
  7.2 0.0 copy-done.1
  7.2 1.9 %shard_map.111 = (bf16[256,256]{1,0:T(8,128)(2,1)S(1)}, bf16[256,128]{1,0:T(8,128)(2,1)S(1)}, bf16[256,384]{1,0:T(8,128)(2,1)S(1)}, bf16[128,384]{1,0:T(8,128)(2...) custom-call(s32[1]{0:T(128)} %bitcast.me_ref, ...), custom_call_target="tpu_custom_call" | custom-call | tf_op jit(solution)/shard_map/pallas_call | solution.py:336
  9.1 0.0 collective-permute-done.across
  9.1 0.0 copy-start.2
  9.2 2.5 %collective-permute-start.11 = (bf16[256,256]{1,0:T(8,128)(2,1)S(1)}, bf16[256,256]{1,0:T(8,128)(2,1)S(1)}, u32[]{:S(2)}, u32[]{:S(2)}) collective-permute-start(bf16[256,256]{1,0:T(8,128)(2,1)S(1)} %slice_select_fusion), channel_id=1, source_target_pairs={{0,4},{4,0},{8,12},{12,8},{1,5},{5,1},{9,13},{13,9},{2,6},{6,2},{1... | collective-permute-start | bytes 393224 | tf_op jit(solution)/shard_map/ppermute | solution.py:330
  11.7 0.0 collective-permute-start.12
  11.7 0.0 copy-done.2
  11.7 0.5 %collective-permute-start.2 = (bf16[128,768]{1,0:T(8,128)(2,1)S(1)}, bf16[128,768]{1,0:T(8,128)(2,1)S(1)}, u32[]{:S(2)}, u32[]{:S(2)}) collective-permute-start(bf16[128,768]{1,0:T(8,128)(2,1)S(1)} %copy-done.2), channel_id=1, source_target_pairs={{0,1},{1,0},{4,8},{5,9},{8,4},{9,5},{12,13},{13,12},{2,3},{3,2},{6... | collective-permute-start | bytes 589832 | tf_op jit(solution)/shard_map/ppermute | solution.py:333
  12.2 0.8 %collective-permute-done.12.refs_4_ = bf16[128,384]{1,0:T(8,128)(2,1)S(1)} collective-permute-done((bf16[128,384]{1,0:T(8,128)(2,1)S(1)}, bf16[128,384]{1,0:T(8,128)(2,1)S(1)}, u32[]{:S(2)}, u32[]{:S(2)}) %collective-permute-start.12) | collective-permute-done | bytes 98336 | tf_op jit(solution)/shard_map/ppermute | solution.py:333
  13.0 4.4 %collective-permute-start.5 = (bf16[256,384]{1,0:T(8,128)(2,1)S(1)}, bf16[256,384]{1,0:T(8,128)(2,1)S(1)}, u32[]{:S(2)}, u32[]{:S(2)}) collective-permute-start(bf16[256,384]{1,0:T(8,128)(2,1)S(1)} %get-tuple-element.24.refs_0_.asks0), channel_id=1, source_target_pairs={{0,4},{4,0},{8,12},{12,8},{1,5},{5,1},{9,13},{13,9},{2,6},{6,2},{1... | collective-permute-start | bytes 589832 | tf_op jit(solution)/shard_map/ppermute | solution.py:330
  17.4 0.0 collective-permute-done.10.first.refs_2_
  17.4 0.0 collective-permute-start.13
  17.4 0.0 collective-permute-done.8.second
  17.4 0.5 %collective-permute-start.9 = (bf16[256,384]{1,0:T(8,128)(2,1)S(1)}, bf16[256,384]{1,0:T(8,128)(2,1)S(1)}, u32[]{:S(2)}, u32[]{:S(2)}) collective-permute-start(bf16[256,384]{1,0:T(8,128)(2,1)S(1)} %collective-permute-done.8.second), channel_id=1, source_target_pairs={{0,1},{1,0},{4,8},{5,9},{8,4},{9,5},{12,13},{13,12},{2,3},{3,2},{6... | collective-permute-start | bytes 589832 | tf_op jit(solution)/shard_map/ppermute | solution.py:333
  17.9 1.4 %collective-permute-done.11.part1.refs_3_ = bf16[256,256]{1,0:T(8,128)(2,1)S(1)} collective-permute-done((bf16[256,256]{1,0:T(8,128)(2,1)S(1)}, bf16[256,256]{1,0:T(8,128)(2,1)S(1)}, u32[]{:S(2)}, u32[]{:S(2)}) %collective-permute-start.11) | collective-permute-done | bytes 131104 | tf_op jit(solution)/shard_map/ppermute | solution.py:330
  19.3 0.0 collective-permute-start.14
  19.3 3.1 %collective-permute-done.5.refs_0_.asks0 = bf16[256,384]{1,0:T(8,128)(2,1)S(1)} collective-permute-done((bf16[256,384]{1,0:T(8,128)(2,1)S(1)}, bf16[256,384]{1,0:T(8,128)(2,1)S(1)}, u32[]{:S(2)}, u32[]{:S(2)}) %collective-permute-start.5) | collective-permute-done | bytes 196640 | tf_op jit(solution)/shard_map/ppermute | solution.py:330
  22.4 1.7 %collective-permute-start.1 = (bf16[256,128]{1,0:T(8,128)(2,1)S(1)}, bf16[256,128]{1,0:T(8,128)(2,1)S(1)}, u32[]{:S(2)}, u32[]{:S(2)}) collective-permute-start(bf16[256,128]{1,0:T(8,128)(2,1)S(1)} %slice_select_fusion.1), channel_id=1, source_target_pairs={{0,4},{4,0},{8,12},{12,8},{1,5},{5,1},{9,13},{13,9},{2,6},{6,2},{1... | collective-permute-start | bytes 196616 | tf_op jit(solution)/shard_map/ppermute | solution.py:330
  24.1 0.0 collective-permute-done.2.refs_4_.refs_3_
  24.1 0.3 collective-permute-start.6
  24.4 0.0 collective-permute-done.13.refs_5_
  24.4 0.0 collective-permute-start.3
  24.4 2.5 %collective-permute-done.1.refs_3_.part2 = bf16[256,128]{1,0:T(8,128)(2,1)S(1)} collective-permute-done((bf16[256,128]{1,0:T(8,128)(2,1)S(1)}, bf16[256,128]{1,0:T(8,128)(2,1)S(1)}, u32[]{:S(2)}, u32[]{:S(2)}) %collective-permute-start.1) | collective-permute-done | bytes 65568 | tf_op jit(solution)/shard_map/ppermute | solution.py:330
  26.9 1.5 %collective-permute-start.16 = (bf16[192,384]{1,0:T(8,128)(2,1)S(1)}, bf16[192,384]{1,0:T(8,128)(2,1)S(1)}, u32[]{:S(2)}, u32[]{:S(2)}) collective-permute-start(bf16[192,384]{1,0:T(8,128)(2,1)S(1)} %shard_map.120), channel_id=1, source_target_pairs={{0,4},{4,0},{8,12},{12,8},{1,5},{5,1},{9,13},{13,9},{2,6},{6,2},{1... | collective-permute-start | bytes 442376 | tf_op jit(solution)/shard_map/ppermute | solution.py:330
  28.4 0.0 collective-permute-done.9.far
  28.4 0.0 collective-permute-start.4
  28.4 1.4 %collective-permute-done.6.refs_1_ = bf16[128,384]{1,0:T(8,128)(2,1)S(1)} collective-permute-done((bf16[128,384]{1,0:T(8,128)(2,1)S(1)}, bf16[128,384]{1,0:T(8,128)(2,1)S(1)}, u32[]{:S(2)}, u32[]{:S(2)}) %collective-permute-start.6) | collective-permute-done | bytes 98336 | tf_op jit(solution)/shard_map/ppermute | solution.py:330
  29.8 2.5 %collective-permute-start.15 = (bf16[64,768]{1,0:T(8,128)(2,1)S(1)}, bf16[64,768]{1,0:T(8,128)(2,1)S(1)}, u32[]{:S(2)}, u32[]{:S(2)}) collective-permute-start(bf16[64,768]{1,0:T(8,128)(2,1)S(1)} %shard_map.119), channel_id=1, source_target_pairs={{0,4},{4,0},{8,12},{12,8},{1,5},{5,1},{9,13},{13,9},{2,6},{6,2},{1... | collective-permute-start | bytes 294920 | tf_op jit(solution)/shard_map/ppermute | solution.py:330
  32.3 0.0 collective-permute-done.3.refs_5_
  32.3 0.0 collective-permute-done.14.refs_6_
  32.3 2.6 %collective-permute-start.17 = (bf16[192,256]{1,0:T(8,128)(2,1)S(1)}, bf16[192,256]{1,0:T(8,128)(2,1)S(1)}, u32[]{:S(2)}, u32[]{:S(2)}) collective-permute-start(bf16[192,256]{1,0:T(8,128)(2,1)S(1)} %shard_map.121), channel_id=1, source_target_pairs={{0,4},{4,0},{8,12},{12,8},{1,5},{5,1},{9,13},{13,9},{2,6},{6,2},{1... | collective-permute-start | bytes 294920 | tf_op jit(solution)/shard_map/ppermute | solution.py:330
  34.8 0.0 collective-permute-done.4.refs_6_
  34.8 0.6 %collective-permute-start.7 = (bf16[192,128]{1,0:T(8,128)(2,1)S(1)}, bf16[192,128]{1,0:T(8,128)(2,1)S(1)}, u32[]{:S(2)}, u32[]{:S(2)}) collective-permute-start(bf16[192,128]{1,0:T(8,128)(2,1)S(1)} %shard_map.114), channel_id=1, source_target_pairs={{0,4},{4,0},{8,12},{12,8},{1,5},{5,1},{9,13},{13,9},{2,6},{6,2},{1... | collective-permute-start | bytes 147464 | tf_op jit(solution)/shard_map/ppermute | solution.py:330
  35.5 0.6 %shard_map.116.end_cross = bf16[128,768]{1,0:T(8,128)(2,1)S(1)} custom-call(s32[1]{0:T(128)} %bitcast.me_ref, f32[192,256]{1,0:T(8,128)S(1)} %get-tuple-element.30.near_ref, bf16[256,384]{1,0:T(8,128)(2,1)S(1)} %get-tuple-element.24.refs_0_.asks0, bf16[128,384]{1,0:T(8,128)(2,1)S(1)} %get-tuple-element.25.refs_1_.asks1, ...), custom_call_target="tpu_custom_call" | custom-call | flops 150994944 | bytes 589824 | tf_op jit(solution)/shard_map/pallas_call | solution.py:336
  36.1 0.0 collective-permute-done.15.refs_3_
  36.1 0.0 collective-permute-done.16.refs_4_
  36.1 1.3 %collective-permute-done.17.refs_5_ = bf16[192,256]{1,0:T(8,128)(2,1)S(1)} collective-permute-done((bf16[192,256]{1,0:T(8,128)(2,1)S(1)}, bf16[192,256]{1,0:T(8,128)(2,1)S(1)}, u32[]{:S(2)}, u32[]{:S(2)}) %collective-permute-start.17) | collective-permute-done | bytes 98336 | tf_op jit(solution)/shard_map/ppermute | solution.py:330
  37.4 0.8 %shard_map.122 = (bf16[128,768]{1,0:T(8,128)(2,1)}, bf16[128,768]{1,0:T(8,128)(2,1)}, bf16[64,768]{1,0:T(8,128)(2,1)}, bf16[64,768]{1,0:T(8,128)(2,1)}) custom-call(s32[1]{0:T(128)} %bitcast.me_ref, bf16[128,768]{1,0:T(8,128)(2,1)S(1)} %get-tuple-element.32.own_cross, bf16[128,768]{1,0:T(8,128)(2,1)S(1)} %shard_map.116.end_cross, ...), custom_call_target="tpu_custom_call" | custom-call | tf_op jit(solution)/shard_map/pallas_call | solution.py:336
  38.3 0.7 %collective-permute-done.7.back = bf16[192,128]{1,0:T(8,128)(2,1)S(1)} collective-permute-done((bf16[192,128]{1,0:T(8,128)(2,1)S(1)}, bf16[192,128]{1,0:T(8,128)(2,1)S(1)}, u32[]{:S(2)}, u32[]{:S(2)}) %collective-permute-start.7) | collective-permute-done | bytes 49184 | tf_op jit(solution)/shard_map/ppermute | solution.py:330
  38.9 0.6 %shard_map.123 = (bf16[128,768]{1,0:T(8,128)(2,1)}, bf16[64,768]{1,0:T(8,128)(2,1)}) custom-call(s32[1]{0:T(128)} %bitcast.me_ref, bf16[192,128]{1,0:T(8,128)(2,1)S(1)} %shard_map.113.own, bf16[192,128]{1,0:T(8,128)(2,1)S(1)} %collective-permute-done.7.back, ...), custom_call_target="tpu_custom_call", output_to_operand_aliasing={{0}: (3, {}), {1}: (4, {})} | custom-call | tf_op jit(solution)/shard_map/pallas_call | solution.py:336
  (10 shorter events, 0.1 us)
Async XLA Ops:
  1.8 7.3 %collective-permute-start = (bf16[256,384]{1,0:T(8,128)(2,1)S(1)}, bf16[256,384]{1,0:T(8,128)(2,1)S(1)}, u32[]{:S(2)}, u32[]{:S(2)}) collective-permute-start(bf16[256,384]{1,0:T(8,128)(2,1)S(1)} %get-tuple-element.27.out), channel_id=1, source_target_pairs={{0,1},{1,0},{4,8},{5,9},{8,4},{9,5},{12,13},{13,12},{2,3},{3,2},{6... | collective-permute-start | bytes 589832 | tf_op jit(solution)/shard_map/ppermute | solution.py:333
  2.3 15.1 %collective-permute-start.10 = (bf16[256,384]{1,0:T(8,128)(2,1)S(1)}, bf16[256,384]{1,0:T(8,128)(2,1)S(1)}, u32[]{:S(2)}, u32[]{:S(2)}) collective-permute-start(bf16[256,384]{1,0:T(8,128)(2,1)S(1)} %get-tuple-element.27.out), channel_id=1, source_target_pairs={{0,4},{4,0},{8,12},{12,8},{1,5},{5,1},{9,13},{13,9},{2,6},{6,2},{1... | collective-permute-start | bytes 589832 | tf_op jit(solution)/shard_map/ppermute | solution.py:330
  6.5 10.9 %collective-permute-start.8 = (bf16[256,384]{1,0:T(8,128)(2,1)S(1)}, bf16[256,384]{1,0:T(8,128)(2,1)S(1)}, u32[]{:S(2)}, u32[]{:S(2)}) collective-permute-start(bf16[256,384]{1,0:T(8,128)(2,1)S(1)} %get-tuple-element.31.over.refs_1_), channel_id=1, source_target_pairs={{0,4},{4,0},{8,12},{12,8},{1,5},{5,1},{9,13},{13,9},{2,6},{6,2},{1... | collective-permute-start | bytes 589832 | tf_op jit(solution)/shard_map/ppermute | solution.py:330
  6.5 0.7 %copy-start = (s32[256]{0:T(256)S(1)}, s32[256]{0:T(256)}, u32[]{:S(2)}) copy-start(s32[256]{0:T(256)} %param.14) | copy-start | bytes 3076
  6.5 0.7 %copy-start.1 = (s32[4]{0:T(128)S(1)}, s32[4]{0:T(128)}, u32[]{:S(2)}) copy-start(s32[4]{0:T(128)} %count_ref.1) | copy-start | bytes 52
  9.1 2.5 %copy-start.2 = (bf16[128,768]{1,0:T(8,128)(2,1)S(1)}, bf16[128,768]{1,0:T(8,128)(2,1)}, u32[]{:S(2)}) copy-start(bf16[128,768]{1,0:T(8,128)(2,1)} %video_k.3) | copy-start | bytes 589828
  9.2 10.1 %collective-permute-start.11 = (bf16[256,256]{1,0:T(8,128)(2,1)S(1)}, bf16[256,256]{1,0:T(8,128)(2,1)S(1)}, u32[]{:S(2)}, u32[]{:S(2)}) collective-permute-start(bf16[256,256]{1,0:T(8,128)(2,1)S(1)} %slice_select_fusion), channel_id=1, source_target_pairs={{0,4},{4,0},{8,12},{12,8},{1,5},{5,1},{9,13},{13,9},{2,6},{6,2},{1... | collective-permute-start | bytes 393224 | tf_op jit(solution)/shard_map/ppermute | solution.py:330
  11.7 1.3 %collective-permute-start.12 = (bf16[128,384]{1,0:T(8,128)(2,1)S(1)}, bf16[128,384]{1,0:T(8,128)(2,1)S(1)}, u32[]{:S(2)}, u32[]{:S(2)}) collective-permute-start(bf16[128,384]{1,0:T(8,128)(2,1)S(1)} %get-tuple-element.35), channel_id=1, source_target_pairs={{0,1},{1,0},{4,8},{5,9},{8,4},{9,5},{12,13},{13,12},{2,3},{3,2},{6... | collective-permute-start | bytes 294920 | tf_op jit(solution)/shard_map/ppermute | solution.py:333
  11.7 12.4 %collective-permute-start.2 = (bf16[128,768]{1,0:T(8,128)(2,1)S(1)}, bf16[128,768]{1,0:T(8,128)(2,1)S(1)}, u32[]{:S(2)}, u32[]{:S(2)}) collective-permute-start(bf16[128,768]{1,0:T(8,128)(2,1)S(1)} %copy-done.2), channel_id=1, source_target_pairs={{0,1},{1,0},{4,8},{5,9},{8,4},{9,5},{12,13},{13,12},{2,3},{3,2},{6... | collective-permute-start | bytes 589832 | tf_op jit(solution)/shard_map/ppermute | solution.py:333
  13.0 9.4 %collective-permute-start.5 = (bf16[256,384]{1,0:T(8,128)(2,1)S(1)}, bf16[256,384]{1,0:T(8,128)(2,1)S(1)}, u32[]{:S(2)}, u32[]{:S(2)}) collective-permute-start(bf16[256,384]{1,0:T(8,128)(2,1)S(1)} %get-tuple-element.24.refs_0_.asks0), channel_id=1, source_target_pairs={{0,4},{4,0},{8,12},{12,8},{1,5},{5,1},{9,13},{13,9},{2,6},{6,2},{1... | collective-permute-start | bytes 589832 | tf_op jit(solution)/shard_map/ppermute | solution.py:330
  17.4 7.0 %collective-permute-start.13 = (bf16[256,384]{1,0:T(8,128)(2,1)S(1)}, bf16[256,384]{1,0:T(8,128)(2,1)S(1)}, u32[]{:S(2)}, u32[]{:S(2)}) collective-permute-start(bf16[256,384]{1,0:T(8,128)(2,1)S(1)} %collective-permute-done.10.first.refs_2_), channel_id=1, source_target_pairs={{0,1},{1,0},{4,8},{5,9},{8,4},{9,5},{12,13},{13,12},{2,3},{3,2},{6... | collective-permute-start | bytes 589832 | tf_op jit(solution)/shard_map/ppermute | solution.py:333
  17.4 11.0 %collective-permute-start.9 = (bf16[256,384]{1,0:T(8,128)(2,1)S(1)}, bf16[256,384]{1,0:T(8,128)(2,1)S(1)}, u32[]{:S(2)}, u32[]{:S(2)}) collective-permute-start(bf16[256,384]{1,0:T(8,128)(2,1)S(1)} %collective-permute-done.8.second), channel_id=1, source_target_pairs={{0,1},{1,0},{4,8},{5,9},{8,4},{9,5},{12,13},{13,12},{2,3},{3,2},{6... | collective-permute-start | bytes 589832 | tf_op jit(solution)/shard_map/ppermute | solution.py:333
  19.3 13.0 %collective-permute-start.14 = (bf16[256,256]{1,0:T(8,128)(2,1)S(1)}, bf16[256,256]{1,0:T(8,128)(2,1)S(1)}, u32[]{:S(2)}, u32[]{:S(2)}) collective-permute-start(bf16[256,256]{1,0:T(8,128)(2,1)S(1)} %collective-permute-done.11.part1.refs_3_), channel_id=1, source_target_pairs={{0,1},{1,0},{4,8},{5,9},{8,4},{9,5},{12,13},{13,12},{2,3},{3,2},{6... | collective-permute-start | bytes 393224 | tf_op jit(solution)/shard_map/ppermute | solution.py:333
  22.4 4.5 %collective-permute-start.1 = (bf16[256,128]{1,0:T(8,128)(2,1)S(1)}, bf16[256,128]{1,0:T(8,128)(2,1)S(1)}, u32[]{:S(2)}, u32[]{:S(2)}) collective-permute-start(bf16[256,128]{1,0:T(8,128)(2,1)S(1)} %slice_select_fusion.1), channel_id=1, source_target_pairs={{0,4},{4,0},{8,12},{12,8},{1,5},{5,1},{9,13},{13,9},{2,6},{6,2},{1... | collective-permute-start | bytes 196616 | tf_op jit(solution)/shard_map/ppermute | solution.py:330
  24.1 5.7 %collective-permute-start.6 = (bf16[128,384]{1,0:T(8,128)(2,1)S(1)}, bf16[128,384]{1,0:T(8,128)(2,1)S(1)}, u32[]{:S(2)}, u32[]{:S(2)}) collective-permute-start(bf16[128,384]{1,0:T(8,128)(2,1)S(1)} %get-tuple-element.25.refs_1_.asks1), channel_id=1, source_target_pairs={{0,4},{4,0},{8,12},{12,8},{1,5},{5,1},{9,13},{13,9},{2,6},{6,2},{1... | collective-permute-start | bytes 294920 | tf_op jit(solution)/shard_map/ppermute | solution.py:330
  24.4 7.9 %collective-permute-start.3 = (bf16[128,384]{1,0:T(8,128)(2,1)S(1)}, bf16[128,384]{1,0:T(8,128)(2,1)S(1)}, u32[]{:S(2)}, u32[]{:S(2)}) collective-permute-start(bf16[128,384]{1,0:T(8,128)(2,1)S(1)} %get-tuple-element.28), channel_id=1, source_target_pairs={{0,1},{1,0},{4,8},{5,9},{8,4},{9,5},{12,13},{13,12},{2,3},{3,2},{6... | collective-permute-start | bytes 294920 | tf_op jit(solution)/shard_map/ppermute | solution.py:333
  26.9 9.2 %collective-permute-start.16 = (bf16[192,384]{1,0:T(8,128)(2,1)S(1)}, bf16[192,384]{1,0:T(8,128)(2,1)S(1)}, u32[]{:S(2)}, u32[]{:S(2)}) collective-permute-start(bf16[192,384]{1,0:T(8,128)(2,1)S(1)} %shard_map.120), channel_id=1, source_target_pairs={{0,4},{4,0},{8,12},{12,8},{1,5},{5,1},{9,13},{13,9},{2,6},{6,2},{1... | collective-permute-start | bytes 442376 | tf_op jit(solution)/shard_map/ppermute | solution.py:330
  28.4 6.5 %collective-permute-start.4 = (bf16[256,128]{1,0:T(8,128)(2,1)S(1)}, bf16[256,128]{1,0:T(8,128)(2,1)S(1)}, u32[]{:S(2)}, u32[]{:S(2)}) collective-permute-start(bf16[256,128]{1,0:T(8,128)(2,1)S(1)} %collective-permute-done.1.refs_3_.part2), channel_id=1, source_target_pairs={{0,1},{1,0},{4,8},{5,9},{8,4},{9,5},{12,13},{13,12},{2,3},{3,2},{6... | collective-permute-start | bytes 196616 | tf_op jit(solution)/shard_map/ppermute | solution.py:333
  29.8 6.3 %collective-permute-start.15 = (bf16[64,768]{1,0:T(8,128)(2,1)S(1)}, bf16[64,768]{1,0:T(8,128)(2,1)S(1)}, u32[]{:S(2)}, u32[]{:S(2)}) collective-permute-start(bf16[64,768]{1,0:T(8,128)(2,1)S(1)} %shard_map.119), channel_id=1, source_target_pairs={{0,4},{4,0},{8,12},{12,8},{1,5},{5,1},{9,13},{13,9},{2,6},{6,2},{1... | collective-permute-start | bytes 294920 | tf_op jit(solution)/shard_map/ppermute | solution.py:330
  32.3 5.2 %collective-permute-start.17 = (bf16[192,256]{1,0:T(8,128)(2,1)S(1)}, bf16[192,256]{1,0:T(8,128)(2,1)S(1)}, u32[]{:S(2)}, u32[]{:S(2)}) collective-permute-start(bf16[192,256]{1,0:T(8,128)(2,1)S(1)} %shard_map.121), channel_id=1, source_target_pairs={{0,4},{4,0},{8,12},{12,8},{1,5},{5,1},{9,13},{13,9},{2,6},{6,2},{1... | collective-permute-start | bytes 294920 | tf_op jit(solution)/shard_map/ppermute | solution.py:330
  34.8 4.1 %collective-permute-start.7 = (bf16[192,128]{1,0:T(8,128)(2,1)S(1)}, bf16[192,128]{1,0:T(8,128)(2,1)S(1)}, u32[]{:S(2)}, u32[]{:S(2)}) collective-permute-start(bf16[192,128]{1,0:T(8,128)(2,1)S(1)} %shard_map.114), channel_id=1, source_target_pairs={{0,4},{4,0},{8,12},{12,8},{1,5},{5,1},{9,13},{13,9},{2,6},{6,2},{1... | collective-permute-start | bytes 147464 | tf_op jit(solution)/shard_map/ppermute | solution.py:330
